TPU v7x, 256 devices: a whole 4x4x8 slice. The times are simulated.
256 devices in a mesh: pop: 64 (over y, x, z_lo), tp: 4 (over z_hi, core).
Axes of the slice: x: 4, y: 4, z: 8 (z_hi: 2, z_lo: 4; z = z_hi * 4 + z_lo), core: 2. Of those that a mesh axis runs over, the one named last changes fastest.
Arguments:
- tokens: bfloat16 [64, 256, 4096], P('pop', None, 'tp'), may hold values from -6 to 6
- receptance: bfloat16 [64, 256, 4096], P('pop', None, 'tp'), may hold values from -6 to 6
- keys: bfloat16 [64, 256, 4096], P('pop', None, 'tp'), may hold values from -0.29882812 to 0.29882812
- log_decay: bfloat16 [64, 256, 4096], P('pop', None, 'tp'), may hold values from -1 to 0
- value_weight: bfloat16 [4096, 4096], P('pop', 'tp'), may hold values from -0.09375 to 0.09375
- noise_in: bfloat16 [64, 4096], P('pop'), may hold values from -6 to 6
- noise_out: bfloat16 [64, 4096], P('pop', 'tp'), may hold values from -6 to 6
- utilities: float32 [64], P('pop'), may hold values from -0.5 to 0.5, as said below
- live_length: int32 [64], P('pop'), may hold values from 1 to 256, as said below
Outputs:
- wkv_out: bfloat16 [64, 256, 4096], P('pop', None, 'tp')
- update: float32 [4096, 4096], P('pop', 'tp')
Inputs may be any that keep to these rules, and one draw needn't show every extreme that they name: `utilities`: centered ranks: the values k / 63 - 0.5, each taken once. tokens at positions from live_length on are masked.
All inputs are finite; a program needn't handle non-finite values.
Results may differ from a plain program's by a relative error of at most 0.0049.
Values may be sent and summed in bfloat16 or wider, within the bound.
No kernel may reach another device: no remote copies, remote signals or barrier semaphores. Data moves between devices by JAX's collectives and lax.ppermute only.
A program may use at most 128 MiB of HBM per device.

v0:
```python
import math

import jax
import jax.numpy as jnp
from jax import lax
from jax.sharding import PartitionSpec as P

HEAD = 64


HIGHEST = lax.Precision.HIGHEST
SIGMA = 0.5


def wkv_block(weighted_key_value_state, recept, masked_keys, masked_decay, value_items):
    cum_log = jnp.cumsum(masked_decay, axis=0)
    span_len = recept.shape[0]
    lower_mask = jnp.arange(span_len)[:, None] >= jnp.arange(span_len)[None, :]
    grown_recept = recept * jnp.exp(cum_log)
    shrunk_keys = masked_keys * jnp.exp(-cum_log)
    scores = jnp.where(lower_mask, jnp.dot(grown_recept, shrunk_keys.T, precision=HIGHEST), 0.0)
    block_out = jnp.dot(grown_recept, weighted_key_value_state, precision=HIGHEST) + jnp.dot(
        scores, value_items, precision=HIGHEST
    )
    final_log = cum_log[-1]
    carried = (masked_keys * jnp.exp(final_log[None, :] - cum_log)).T
    weighted_key_value_state = jnp.exp(final_log)[:, None] * weighted_key_value_state + jnp.dot(
        carried, value_items, precision=HIGHEST
    )
    return (weighted_key_value_state, block_out)


def body(
    tokens, receptance, keys, log_decay, value_weight, noise_in, noise_out, utilities, live_length
):
    members, length, local_width = receptance.shape
    all_features = lax.all_gather(tokens, "tp", axis=2, tiled=True)
    full_width = all_features.shape[2]
    flat_tokens = all_features.reshape(members * length, full_width)
    base_value = jnp.dot(
        flat_tokens,
        lax.all_gather(value_weight, "pop", axis=0, tiled=True),
        preferred_element_type=jnp.float32,
    )
    projected = jnp.einsum("mtd,md->mt", all_features, noise_in, preferred_element_type=jnp.float32)
    values = (
        base_value.reshape(members, length, local_width)
        + SIGMA
        / math.sqrt(full_width)
        * projected[:, :, None]
        * noise_out.astype(jnp.float32)[:, None, :]
    ).astype(jnp.bfloat16)
    live_mask = (jnp.arange(length)[None, :] < live_length[:, None]).astype(jnp.float32)
    head_count = local_width // HEAD

    def to_items(array_in):
        return (
            array_in.reshape(members, length, head_count, HEAD)
            .transpose(0, 2, 1, 3)
            .reshape(members * head_count, length, HEAD)
        )

    recept = to_items(receptance.astype(jnp.float32))
    masked_keys = to_items(keys.astype(jnp.float32) * live_mask[:, :, None])
    masked_decay = to_items(log_decay.astype(jnp.float32) * live_mask[:, :, None])
    value_items = to_items(values.astype(jnp.float32))
    block_len = min(32, length)
    weighted_key_value_state = jnp.zeros((members * head_count, HEAD, HEAD), jnp.float32)
    advance_tokens = jax.vmap(wkv_block)
    pieces = []
    for offset in range(0, length, block_len):
        operands = (
            weighted_key_value_state,
            recept[:, offset : offset + block_len],
            masked_keys[:, offset : offset + block_len],
            masked_decay[:, offset : offset + block_len],
            value_items[:, offset : offset + block_len],
        )
        weighted_key_value_state, block_out = advance_tokens(*operands)
        pieces.append(block_out)
    emitted_vector = jnp.concatenate(pieces, 1)
    emitted_vector = (
        emitted_vector.reshape(members, head_count, length, HEAD)
        .transpose(0, 2, 1, 3)
        .reshape(members, length, local_width)
    )
    wkv_out = (emitted_vector * live_mask[:, :, None]).astype(jnp.bfloat16)
    population = members * lax.axis_size("pop")
    weighted = noise_in.astype(jnp.float32) * (utilities / math.sqrt(population))[:, None]
    owned_rows = lax.all_to_all(weighted, "pop", split_axis=1, concat_axis=0, tiled=True)
    owned_columns = lax.all_gather(noise_out, "pop", axis=0, tiled=True)
    update = lax.dot_general(
        owned_rows,
        owned_columns.astype(jnp.float32),
        (((0,), (0,)), ((), ())),
        precision=HIGHEST,
        preferred_element_type=jnp.float32,
    )
    return (wkv_out, update)


def solution(mesh):
    return jax.shard_map(
        body,
        mesh=mesh,
        in_specs=(
            P("pop", None, "tp"),
            P("pop", None, "tp"),
            P("pop", None, "tp"),
            P("pop", None, "tp"),
            P("pop", "tp"),
            P("pop", None),
            P("pop", "tp"),
            P("pop"),
            P("pop"),
        ),
        out_specs=(P("pop", None, "tp"), P("pop", "tp")),
        check_vma=False,
    )
```

profile of v0, /device:TPU:32, one launch (start us, length us, event | category | flops | bytes accessed | tf_op | source)
XLA Modules:
  0.0 461.1 jit_solution(18405937563097400006)
XLA Ops:
  7.2 0.7 all-gather.4.cloned.1.call-update
  8.0 0.7 all-gather.6.cloned.1.call-update
  9.3 0.8 multiply_reduce_fusion
  10.1 0.7 all_to_all.12
  10.8 11.7 %all-to-all-start = ((f32[1,64,64]{2,0,1:T(1,128)}), f32[1,64,64]{2,0,1:T(1,128)S(1)}, u32[]{:S(2)}, u32[]{:S(2)}) async-start(f32[1,64,64]{2,0,1:T(1,128)} %all_to_all.12), calls=%async_computation | async-start | bytes 65536 | tf_op jit(solution)/shard_map/all_to_all | solution.py:90
  23.1 2.1 copy.57
  25.8 2.5 copy.63
  28.3 2.0 copy.58
  30.3 2.8 fusion.85
  33.1 1.3 copy.98
  34.4 2.0 copy.93
  36.4 2.0 copy.88
  38.4 1.9 copy.83
  40.4 1.9 copy.78
  42.3 1.9 copy.73
  44.3 0.9 copy.68
  45.2 0.9 copy.60
  46.1 1.0 fusion.89
  47.2 1.0 fusion.92
  48.2 1.0 fusion.91
  49.2 1.9 fusion.90
  51.1 1.9 fusion.88
  53.0 1.9 fusion.87
  54.9 1.9 fusion.86
  56.8 1.9 fusion.93
  58.7 0.4 slice_multiply_fusion.1
  59.2 1.2 fusion.34
  60.4 0.5 copy-done
  60.9 1.0 exponential_multiply_fusion
  61.9 1.4 convolution_select_fusion.7
  63.3 1.0 exponential_multiply_fusion.2
  64.3 1.4 convolution_select_fusion.2
  65.7 1.4 convolution_select_fusion.6
  67.1 1.4 convolution_select_fusion.5
  68.5 1.4 convolution_select_fusion.4
  69.9 1.4 convolution_select_fusion.3
  71.3 1.4 convolution_select_fusion.1
  72.6 1.4 convolution_select_fusion
  74.0 182.8 %all-gather = bf16[64,1,1024]{2,1,0:T(2,128)(2,1)S(1)} all-gather(bf16[1,1,1024]{2,1,0:T(2,128)(2,1)S(1)} %bitcast.124), channel_id=1, replica_groups=mesh['pop'=64,'tp'=4] {'pop'}, dimensions={0}, use_global_device_ids=true | all-gather | bytes 133120 | tf_op jit(solution)/shard_map/all_gather | solution.py:91
  256.8 1.0 fusion.60
  257.8 2.4 fusion
  260.2 172.2 %all-gather.6.cloned.1.call-done = bf16[4096,1024]{1,0:T(8,128)(2,1)} async-done(((bf16[64,1024]{1,0:T(8,128)(2,1)}), bf16[4096,1024]{1,0:T(8,128)(2,1)}) %all-gather.6.cloned.1.call-update) | async-done | bytes 8388624 | tf_op jit(solution)/shard_map/all_gather | solution.py:42
  432.4 6.5 %fusion.7 = bf16[256,1024]{1,0:T(8,128)(2,1)} fusion(bf16[4096,1024]{1,0:T(8,128)(2,1)} %all-gather.6.cloned.1.call-done, bf16[1,256,4096]{2,1,0:T(8,128)(2,1)S(1)} %copy-done.15, f32[1024]{0:T(1024)S(1)} %bitcast.126, f32[256]{0:T(256)S(1)} %broadcast_multiply_fusion), kind=kOutput, calls=%fused_computation.5 | convolution fusion | flops 2148270080 | bytes 11015168 | tf_op jit(solution)/shard_map/dot_general | solution.py:40
  438.9 1.3 copy.66
  440.2 0.5 copy.67
  440.7 0.6 convolution_add_fusion.6
  441.4 0.7 fusion.55
  442.1 0.6 convolution_add_fusion.5
  442.8 0.7 fusion.52
  443.4 0.6 convolution_add_fusion.4
  444.1 0.7 fusion.49
  444.8 0.6 convolution_add_fusion.3
  445.4 0.7 fusion.46
  446.1 0.6 convolution_add_fusion.2
  446.8 0.7 fusion.43
  447.4 0.6 convolution_add_fusion.1
  448.1 0.7 fusion.40
  448.8 0.6 convolution_add_fusion
  449.4 0.9 fusion.37
  451.2 0.3 fusion.14
  451.8 0.3 fusion.12
  452.0 0.3 fusion.11
  452.6 0.6 copy.103
  453.2 1.0 copy.104
  (99 shorter events, 2.2 us)
Async XLA Ops:
  7.2 18.0 %copy-start.32 = (bf16[1,256,1024]{2,1,0:T(8,128)(2,1)S(1)}, bf16[1,256,1024]{2,1,0:T(8,128)(2,1)}, u32[]{:S(2)}) copy-start(bf16[1,256,1024]{2,1,0:T(8,128)(2,1)} %param.11) | copy-start | bytes 1572868
  7.2 18.2 %copy-start.33 = (bf16[1,256,1024]{2,1,0:T(8,128)(2,1)S(1)}, bf16[1,256,1024]{2,1,0:T(8,128)(2,1)}, u32[]{:S(2)}) copy-start(bf16[1,256,1024]{2,1,0:T(8,128)(2,1)} %param.12) | copy-start | bytes 1572868
  7.2 250.6 %all-gather.4.cloned.1.call-start = ((), (), s32[]{:S(2)}) async-start(), calls=%async_computation.1 | async-start | bytes 2621440 | tf_op jit(solution)/shard_map/all_gather | solution.py:37
  7.9 424.5 %all-gather.6.cloned.1.call-start = ((), (), s32[]{:S(2)}) async-start(), calls=%async_computation.2 | async-start | bytes 8519680 | tf_op jit(solution)/shard_map/all_gather | solution.py:42
  10.8 246.0 %all-to-all-start = ((f32[1,64,64]{2,0,1:T(1,128)}), f32[1,64,64]{2,0,1:T(1,128)S(1)}, u32[]{:S(2)}, u32[]{:S(2)}) async-start(f32[1,64,64]{2,0,1:T(1,128)} %all_to_all.12), calls=%async_computation | async-start | bytes 65536 | tf_op jit(solution)/shard_map/all_to_all | solution.py:90
  34.4 9.9 %copy-start.14 = (f32[16,32,64]{1,2,0:T(8,128)S(1)}, f32[16,32,64]{1,2,0:T(8,128)}, u32[]{:S(2)}) copy-start(f32[16,32,64]{1,2,0:T(8,128)} %get-tuple-element.46) | copy-start | bytes 393220
  36.4 8.8 %copy-start.13 = (f32[16,32,64]{1,2,0:T(8,128)S(1)}, f32[16,32,64]{1,2,0:T(8,128)}, u32[]{:S(2)}) copy-start(f32[16,32,64]{1,2,0:T(8,128)} %get-tuple-element.47) | copy-start | bytes 393220
  45.2 4.0 copy-start.25
  45.2 7.8 %copy-start.26 = (f32[16,32,64]{2,0,1:T(8,128)S(1)}, f32[16,32,64]{2,0,1:T(8,128)}, u32[]{:S(2)}) copy-start(f32[16,32,64]{2,0,1:T(8,128)} %copy.68) | copy-start | bytes 393220
  46.1 5.0 %copy-start.28 = (f32[16,32,64]{2,0,1:T(8,128)S(1)}, f32[16,32,64]{2,0,1:T(8,128)}, u32[]{:S(2)}) copy-start(f32[16,32,64]{2,0,1:T(8,128)} %copy.73) | copy-start | bytes 393220
  46.1 8.8 %copy-start.27 = (f32[16,32,64]{2,0,1:T(8,128)S(1)}, f32[16,32,64]{2,0,1:T(8,128)}, u32[]{:S(2)}) copy-start(f32[16,32,64]{2,0,1:T(8,128)} %copy.60) | copy-start | bytes 393220
  58.7 2.1 copy-start
  59.1 5.2 %copy-start.3 = (f32[16,32,64]{2,0,1:T(8,128)}, f32[16,32,64]{2,0,1:T(8,128)S(1)}, u32[]{:S(2)}) copy-start(f32[16,32,64]{2,0,1:T(8,128)S(1)} %get-tuple-element.23) | copy-start | bytes 393220
  59.1 6.6 %copy-start.11 = (f32[16,32,64]{2,0,1:T(8,128)}, f32[16,32,64]{2,0,1:T(8,128)S(1)}, u32[]{:S(2)}) copy-start(f32[16,32,64]{2,0,1:T(8,128)S(1)} %get-tuple-element.27) | copy-start | bytes 393220
  59.2 7.9 %copy-start.9 = (f32[16,32,64]{2,0,1:T(8,128)}, f32[16,32,64]{2,0,1:T(8,128)S(1)}, u32[]{:S(2)}) copy-start(f32[16,32,64]{2,0,1:T(8,128)S(1)} %get-tuple-element.26) | copy-start | bytes 393220
  59.2 9.3 %copy-start.7 = (f32[16,32,64]{2,0,1:T(8,128)}, f32[16,32,64]{2,0,1:T(8,128)S(1)}, u32[]{:S(2)}) copy-start(f32[16,32,64]{2,0,1:T(8,128)S(1)} %get-tuple-element.25) | copy-start | bytes 393220
  59.2 10.7 %copy-start.5 = (f32[16,32,64]{2,0,1:T(8,128)}, f32[16,32,64]{2,0,1:T(8,128)S(1)}, u32[]{:S(2)}) copy-start(f32[16,32,64]{2,0,1:T(8,128)S(1)} %get-tuple-element.24) | copy-start | bytes 393220
  59.2 12.1 %copy-start.1 = (f32[16,32,64]{2,0,1:T(8,128)}, f32[16,32,64]{2,0,1:T(8,128)S(1)}, u32[]{:S(2)}) copy-start(f32[16,32,64]{2,0,1:T(8,128)S(1)} %get-tuple-element.22) | copy-start | bytes 393220
  67.1 6.9 %copy-start.35 = (bf16[1,1024]{1,0:T(2,128)(2,1)S(1)}, bf16[1,1024]{1,0:T(2,128)(2,1)}, u32[]{:S(2)}) copy-start(bf16[1,1024]{1,0:T(2,128)(2,1)} %param.15) | copy-start | bytes 6148
  68.5 189.4 %copy-start.34 = (bf16[1,4096]{1,0:T(2,128)(2,1)S(1)}, bf16[1,4096]{1,0:T(2,128)(2,1)}, u32[]{:S(2)}) copy-start(bf16[1,4096]{1,0:T(2,128)(2,1)} %param.14) | copy-start | bytes 24580
  257.8 174.6 %copy-start.15 = (bf16[1,256,4096]{2,1,0:T(8,128)(2,1)S(1)}, bf16[1,256,4096]{2,1,0:T(8,128)(2,1)}, u32[]{:S(2)}) copy-start(bf16[1,256,4096]{2,1,0:T(8,128)(2,1)} %all-gather.4.cloned.1.call-done) | copy-start | bytes 6291460
  438.9 2.4 copy-start.12
  438.9 3.1 copy-start.29
  440.7 2.0 copy-start.10
  442.1 2.0 copy-start.8
  442.7 2.0 copy-start.31
  443.4 2.0 copy-start.6
  444.1 2.0 copy-start.30
  444.8 2.0 copy-start.4
  446.1 2.0 copy-start.2
  448.1 2.3 copy-start.16
  448.1 2.3 copy-start.24
  448.1 2.5 copy-start.23
  448.8 2.2 copy-start.22
  449.4 1.8 copy-start.21
  450.4 1.1 copy-start.20
  450.4 1.4 copy-start.17
  450.7 1.4 copy-start.19
  450.9 1.4 copy-start.18
Sparse Core Ops, SparseCore 0:
  9.8 44.6 all-gather.3
  56.3 376.0 all-gather.5
where the time goes:
time: 462 us; the launch traced here: 461 us
  blocking collectives  183 us (40%)
  waiting for transfers between devices  174 us (38%)
  matrix products  33.5 us (7%)
  local copies, waits for them, and re-layouts  27.5 us (6%)
  between operations  16.1 us (3%)
  other arithmetic  15.9 us (3%)
  starting transfers between devices  11.7 us (3%)
    all_gather x1, blocking collectives, body(): owned_columns = lax.all_gather(noise_out, 'pop', axis=0, tiled=True)  183 us
    all_gather x1, waiting for transfers between devices, body(): lax.all_gather(value_weight, 'pop', axis=0, tiled=True)  172 us
    slice x9, local copies, waits for them, and re-layouts, body(): masked_decay[:, offset:offset + block_len]  15.8 us
    another operation x8, other arithmetic, wkv_block(): cum_log = jnp.cumsum(masked_decay, axis=0)  12.4 us
    all_to_all x1, starting transfers between devices, body(): lax.all_to_all(weighted, 'pop', split_axis=1, concat_axis=0, tiled=True)  11.7 us
    dot_general x8, matrix products, wkv_block(): jnp.dot(grown_recept, shrunk_keys.T, precision=HIGHEST)  11.1 us
  transfers between devices with their start and end apart: 3, of which 1 were waited for; matrix products, arithmetic and copies ran while one was open for 12% of the time, Pallas kernels for 0%

commit v1 on v0

v1 whole, which is shorter than its diff:
```python
import functools
import math

import jax
import jax.numpy as jnp
from jax import lax
from jax.experimental import pallas as pl
from jax.experimental.pallas import tpu as pltpu
from jax.sharding import PartitionSpec as P

HEAD = 64
SIGMA = 0.5
HIGHEST = lax.Precision.HIGHEST
F32 = jnp.float32
BF16 = jnp.bfloat16

SIDE = 4
STRIDE = {"y": 16, "x": 4, "z": 1}
SPAN = 64
LANES = 128

VMEM = pl.BlockSpec(memory_space=pltpu.VMEM)
SMEM = pl.BlockSpec(memory_space=pltpu.SMEM)


def fetch(array, axis, step):
    stride = STRIDE[axis]
    pairs = []
    for me in range(SIDE**3):
        at = (me // stride) % SIDE
        pairs.append((me + ((at + step) % SIDE - at) * stride, me))
    return lax.ppermute(array, "pop", pairs)


def swap(array, bit):
    return lax.ppermute(array, "tp", [(i, i ^ bit) for i in range(4)])


def join_kernel(at_ref, p0, p1, p2, p3, left_ref, right_ref):
    rows = p0.shape[0]
    half = left_ref.shape[1]
    for step, part in enumerate((p0, p1, p2, p3)):
        place = pl.ds(pl.multiple_of(lax.rem(at_ref[0] + step, SIDE) * rows, rows), rows)
        left_ref[place, :] = part[:, :half]
        right_ref[place, :] = part[:, half:]


def token_kernel(at_ref, t0, t1, t2, t3, noise_ref, tokens_ref, projected_ref):
    total = None
    for bits, part in enumerate((t0, t1, t2, t3)):
        place = jnp.bitwise_xor(at_ref[0], bits)
        block = part[...]
        tokens_ref[place] = block
        noise = jnp.broadcast_to(noise_ref[place], (8, block.shape[1]))
        term = lax.dot_general(
            block, noise, (((1,), (1,)), ((), ())), preferred_element_type=F32
        )
        total = term if total is None else total + term
    projected_ref[...] = total


def score_kernel(live_ref, recept_ref, keys_ref, decay_ref, high_ref, low_ref):
    length = recept_ref.shape[0]
    live = live_ref[0]
    row = lax.broadcasted_iota(jnp.int32, (length, LANES), 0)
    alive = row < live
    decay = jnp.where(alive, decay_ref[...], jnp.zeros((), BF16))
    keys = jnp.where(alive, keys_ref[...].astype(F32), 0.0)
    lower = (
        lax.broadcasted_iota(jnp.int32, (length, length), 0)
        >= lax.broadcasted_iota(jnp.int32, (length, length), 1)
    ).astype(F32).astype(BF16)
    summed = jnp.dot(lower, decay, preferred_element_type=F32)
    lane = lax.broadcasted_iota(jnp.int32, (SPAN, LANES), 1)
    for chunk in range(length // SPAN):
        first, last = chunk * SPAN, (chunk + 1) * SPAN
        base = summed[first - 1 : first] if chunk else jnp.zeros((1, LANES), F32)
        grown = recept_ref[first:last].astype(F32) * jnp.exp(summed[first:last] - base)
        shrunk = keys[:last] * jnp.exp(base - summed[:last])
        both = jnp.concatenate(
            [jnp.where(lane < HEAD, grown, 0.0), jnp.where(lane < HEAD, 0.0, grown)], 0
        )
        scores = lax.dot_general(
            both, shrunk, (((1,), (1,)), ((), ())), precision=HIGHEST, preferred_element_type=F32
        )
        for head in range(2):
            mine = scores[head * SPAN : (head + 1) * SPAN]
            here = lax.broadcasted_iota(jnp.int32, (SPAN, last), 0) + first
            there = lax.broadcasted_iota(jnp.int32, (SPAN, last), 1)
            mine = jnp.where((here >= there) & (here < live), mine, 0.0)
            high = mine.astype(BF16)
            low = (mine - high.astype(F32)).astype(BF16)
            high_ref[head, first:last, :last] = high
            low_ref[head, first:last, :last] = low
            if last < length:
                rest = jnp.zeros((SPAN, length - last), BF16)
                high_ref[head, first:last, last:] = rest
                low_ref[head, first:last, last:] = rest


def readout_kernel(count, at_ref, *refs):
    pieces = refs[: 2 * count]
    tokens_ref, projected_ref, noise_ref, high_ref, low_ref, out_ref = refs[2 * count :]
    y, x = at_ref[0], at_ref[1]
    depth, half = pieces[0].shape
    projected = projected_ref[...][:, :1]
    lane = lax.broadcasted_iota(jnp.int32, (out_ref.shape[0], LANES), 1)
    for side in range(2):
        total = None
        for dy in range(SIDE):
            for dx in range(SIDE):
                block = tokens_ref[
                    lax.rem(y + dy, SIDE),
                    :,
                    pl.ds(pl.multiple_of(lax.rem(x + dx, SIDE) * depth, depth), depth),
                ]
                term = jnp.dot(
                    block,
                    pieces[side * count + dy * SIDE + dx][...],
                    preferred_element_type=F32,
                )
                total = term if total is None else total + term
        noise = noise_ref[:, side * half : (side + 1) * half].astype(F32)
        values = (total + (SIGMA / math.sqrt(SIDE**3 * 64)) * projected * noise).astype(BF16)
        for pair in range(half // LANES):
            mine = values[:, pair * LANES : (pair + 1) * LANES]
            head = side * (half // HEAD) + 2 * pair
            outs = [
                jnp.dot(high_ref[head + i], mine, preferred_element_type=F32)
                + jnp.dot(low_ref[head + i], mine, preferred_element_type=F32)
                for i in range(2)
            ]
            start = side * half + pair * LANES
            out_ref[:, start : start + LANES] = jnp.where(lane < HEAD, *outs).astype(BF16)


def params(mib):
    return pltpu.CompilerParams(vmem_limit_bytes=mib << 20)


def body(
    tokens, receptance, keys, log_decay, value_weight, noise_in, noise_out, utilities, live_length
):
    _, length, width = receptance.shape
    full = noise_in.shape[1]
    pop = lax.axis_index("pop")
    tp = lax.axis_index("tp")
    y, x, z = pop // 16, (pop // 4) % SIDE, pop % SIDE
    tokens, receptance, keys, log_decay = (
        a.reshape(length, width) for a in (tokens, receptance, keys, log_decay)
    )
    rows = value_weight.shape[0]
    half = width // 2

    near = [value_weight] + [fetch(value_weight, "z", s) for s in (1, 2, 3)]
    left, right = pl.pallas_call(
        join_kernel,
        out_shape=[jax.ShapeDtypeStruct((SIDE * rows, half), BF16)] * 2,
        in_specs=[SMEM] + [VMEM] * 4,
        out_specs=[VMEM] * 2,
        name="join_rows",
    )(z.reshape(1), *near)

    (left, right), tokens = lax.optimization_barrier(((left, right), tokens))
    twin = swap(tokens, 2)
    mate = swap(tokens, 1)
    both = swap(twin, 1)

    lefts = {(0, 0): left}
    rights = {(0, 0): right}
    for s in (1, 3, 2):
        lefts[0, s] = fetch(left, "x", s)
        rights[s, 0] = fetch(right, "y", s)
    for s in (1, 3, 2):
        lefts[s, 0] = fetch(left, "y", s)
        rights[0, s] = fetch(right, "x", s)
    for t in (1, 3, 2):
        for s in (1, 3, 2):
            lefts[s, t] = fetch(lefts[0, t], "y", s)
            rights[t, s] = fetch(rights[t, 0], "x", s)

    all_tokens, projected = pl.pallas_call(
        token_kernel,
        out_shape=[
            jax.ShapeDtypeStruct((4, length, width), BF16),
            jax.ShapeDtypeStruct((length, 8), F32),
        ],
        in_specs=[SMEM] + [VMEM] * 5,
        out_specs=[VMEM] * 2,
        name="member_tokens",
    )(tp.reshape(1), tokens, mate, twin, both, noise_in.reshape(4, 1, width))

    heads = width // HEAD
    strip = pl.BlockSpec((length, LANES), lambda i: (0, i))
    square = pl.BlockSpec((2, length, length), lambda i: (i, 0, 0))
    high, low = pl.pallas_call(
        score_kernel,
        out_shape=[jax.ShapeDtypeStruct((heads, length, length), BF16)] * 2,
        grid=(width // LANES,),
        in_specs=[SMEM, strip, strip, strip],
        out_specs=[square, square],
        name="decayed_scores",
    )(live_length, receptance, keys, log_decay)

    population = lax.axis_size("pop")
    weighted = noise_in.astype(F32) * (utilities / math.sqrt(population))[:, None]
    message = jnp.concatenate(
        [
            weighted.reshape(population, rows),
            jnp.zeros((population, LANES - rows), F32),
            jnp.broadcast_to(noise_out.astype(F32), (population, width)),
        ],
        1,
    )
    message = lax.all_to_all(message, "pop", split_axis=0, concat_axis=0, tiled=True)
    update = lax.dot_general(
        message[:, :rows],
        message[:, LANES:],
        (((0,), (0,)), ((), ())),
        precision=HIGHEST,
        preferred_element_type=F32,
    )

    order = [(a, b) for a in range(SIDE) for b in range(SIDE)]
    wkv_out = pl.pallas_call(
        functools.partial(readout_kernel, len(order)),
        out_shape=jax.ShapeDtypeStruct((length, width), BF16),
        in_specs=[SMEM] + [VMEM] * (2 * len(order) + 5),
        out_specs=VMEM,
        compiler_params=params(40),
        name="values_readout",
    )(
        jnp.stack([y, x]),
        *[lefts[k] for k in order],
        *[rights[k] for k in order],
        all_tokens,
        projected,
        noise_out,
        high,
        low,
    )
    return wkv_out.reshape(1, length, width), update


def solution(mesh):
    return jax.shard_map(
        body,
        mesh=mesh,
        in_specs=(
            P("pop", None, "tp"),
            P("pop", None, "tp"),
            P("pop", None, "tp"),
            P("pop", None, "tp"),
            P("pop", "tp"),
            P("pop", None),
            P("pop", "tp"),
            P("pop"),
            P("pop"),
        ),
        out_specs=(P("pop", None, "tp"), P("pop", "tp")),
        check_vma=False,
    )
```

time: 462 us -> 183 us (0.40)
  the two profiles are of different devices: /device:TPU:32 before, /device:TPU:230 now
where the time goes in v1:
time: 183 us; the launch traced here: 182 us
  starting transfers between devices  64.8 us (35%)
  waiting for transfers between devices  59.1 us (32%)
  local copies, waits for them, and re-layouts  31.2 us (17%)
  Pallas kernels  21.7 us (12%)
  between operations  2.22 us (1%)
    ppermute x33, waiting for transfers between devices, fetch(): return lax.ppermute(array, 'pop', pairs)  59 us
    ppermute x33, starting transfers between devices, fetch(): return lax.ppermute(array, 'pop', pairs)  51.4 us
    unnamed x87, local copies, waits for them, and re-layouts  26.8 us
    all_to_all x1, starting transfers between devices, body(): lax.all_to_all(message, 'pop', split_axis=0, concat_axis=0, tiled=True)  13.2 us
    pallas_call x1, Pallas kernels, body(): pl.pallas_call(score_kernel, out_shape=[jax.ShapeDtypeStruct((heads, leng...  9.32 us
    pallas_call x1, Pallas kernels, body(): pl.pallas_call(functools.partial(readout_kernel, len(order)), out_shape=j...  6.95 us
  transfers between devices with their start and end apart: 37, of which 12 were waited for; matrix products, arithmetic and copies ran while one was open for 3% of the time, Pallas kernels for 7%

profile of v1, /device:TPU:230, one launch (start us, length us, event | category | flops | bytes accessed | tf_op | source)
XLA Modules:
  0.0 181.6 jit_solution(15458275851022083429)
XLA Ops:
  0.6 1.1 collective-permute-start
  1.7 1.5 collective-permute-start.1
  3.2 1.9 %collective-permute-start.2 = (bf16[64,1024]{1,0:T(8,128)(2,1)}, bf16[64,1024]{1,0:T(8,128)(2,1)S(1)}, u32[]{:S(2)}, u32[]{:S(2)}) collective-permute-start(bf16[64,1024]{1,0:T(8,128)(2,1)} %p0.1), channel_id=1, source_target_pairs={{12,0},{0,4},{4,8},{8,12},{28,16},{16,20},{20,24},{24,28},{44,32},... | collective-permute-start | bytes 393224 | tf_op jit(solution)/shard_map/ppermute | solution.py:32
  5.1 4.1 %collective-permute-done.p1 = bf16[64,1024]{1,0:T(8,128)(2,1)S(1)} collective-permute-done((bf16[64,1024]{1,0:T(8,128)(2,1)}, bf16[64,1024]{1,0:T(8,128)(2,1)S(1)}, u32[]{:S(2)}, u32[]{:S(2)}) %collective-permute-start) | collective-permute-done | bytes 131104 | tf_op jit(solution)/shard_map/ppermute | solution.py:32
  9.2 4.5 %collective-permute-done.1.p2 = bf16[64,1024]{1,0:T(8,128)(2,1)S(1)} collective-permute-done((bf16[64,1024]{1,0:T(8,128)(2,1)}, bf16[64,1024]{1,0:T(8,128)(2,1)S(1)}, u32[]{:S(2)}, u32[]{:S(2)}) %collective-permute-start.1) | collective-permute-done | bytes 131104 | tf_op jit(solution)/shard_map/ppermute | solution.py:32
  14.4 1.9 %join_rows.1 = (bf16[256,512]{1,0:T(8,128)(2,1)}, bf16[256,512]{1,0:T(8,128)(2,1)}) custom-call(s32[1]{0:T(128)} %bitcast.2.at_ref, bf16[64,1024]{1,0:T(8,128)(2,1)} %p0.1, bf16[64,1024]{1,0:T(8,128)(2,1)} %copy-done.40, bf16[64,1024]{1,0:T(8,128)(2,1)} %copy-done.41, bf16[64,1024]{1,0:T(8,128)(2,1)} %copy-done.42), custom_call_target="tpu_custom_call" | custom-call | tf_op jit(solution)/shard_map/join_rows/pallas_call | solution.py:156
  16.3 0.8 collective-permute-start.3
  17.1 1.1 collective-permute-start.4
  18.2 2.1 %collective-permute-start.5 = (bf16[256,512]{1,0:T(8,128)(2,1)}, bf16[256,512]{1,0:T(8,128)(2,1)S(1)}, u32[]{:S(2)}, u32[]{:S(2)}) collective-permute-start(bf16[256,512]{1,0:T(8,128)(2,1)} %get-tuple-element.13.refs_0_), channel_id=1, source_target_pairs={{48,0},{52,4},{56,8},{60,12},{0,16},{4,20},{8,24},{12,28},{16,32},... | collective-permute-start | bytes 786440 | tf_op jit(solution)/shard_map/ppermute | solution.py:32
  20.3 3.0 %collective-permute-start.21 = (bf16[256,512]{1,0:T(8,128)(2,1)}, bf16[256,512]{1,0:T(8,128)(2,1)S(1)}, u32[]{:S(2)}, u32[]{:S(2)}) collective-permute-start(bf16[256,512]{1,0:T(8,128)(2,1)} %get-tuple-element.14.refs_16_), channel_id=1, source_target_pairs={{64,0},{68,4},{72,8},{76,12},{80,16},{84,20},{88,24},{92,28},{96,3... | collective-permute-start | bytes 786440 | tf_op jit(solution)/shard_map/ppermute | solution.py:32
  24.0 7.1 %collective-permute-done.3.refs_1_ = bf16[256,512]{1,0:T(8,128)(2,1)S(1)} collective-permute-done((bf16[256,512]{1,0:T(8,128)(2,1)}, bf16[256,512]{1,0:T(8,128)(2,1)S(1)}, u32[]{:S(2)}, u32[]{:S(2)}) %collective-permute-start.3) | collective-permute-done | bytes 262176 | tf_op jit(solution)/shard_map/ppermute | solution.py:32
  31.1 1.6 collective-permute-start.29
  32.7 2.9 %collective-permute-start.10 = (bf16[256,512]{1,0:T(8,128)(2,1)}, bf16[256,512]{1,0:T(8,128)(2,1)S(1)}, u32[]{:S(2)}, u32[]{:S(2)}) collective-permute-start(bf16[256,512]{1,0:T(8,128)(2,1)} %get-tuple-element.13.refs_0_), channel_id=1, source_target_pairs={{128,0},{132,4},{136,8},{140,12},{144,16},{148,20},{152,24},{156,2... | collective-permute-start | bytes 786440 | tf_op jit(solution)/shard_map/ppermute | solution.py:32
  35.6 3.8 %collective-permute-done.21.refs_20_ = bf16[256,512]{1,0:T(8,128)(2,1)S(1)} collective-permute-done((bf16[256,512]{1,0:T(8,128)(2,1)}, bf16[256,512]{1,0:T(8,128)(2,1)S(1)}, u32[]{:S(2)}, u32[]{:S(2)}) %collective-permute-start.21) | collective-permute-done | bytes 262176 | tf_op jit(solution)/shard_map/ppermute | solution.py:32
  39.8 3.2 %collective-permute-done.29.refs_28_ = bf16[256,512]{1,0:T(8,128)(2,1)} collective-permute-done((bf16[256,512]{1,0:T(8,128)(2,1)}, bf16[256,512]{1,0:T(8,128)(2,1)}, u32[]{:S(2)}, u32[]{:S(2)}) %collective-permute-start.29) | collective-permute-done | bytes 262176 | tf_op jit(solution)/shard_map/ppermute | solution.py:32
  43.0 2.8 %collective-permute-done.10.refs_8_ = bf16[256,512]{1,0:T(8,128)(2,1)S(1)} collective-permute-done((bf16[256,512]{1,0:T(8,128)(2,1)}, bf16[256,512]{1,0:T(8,128)(2,1)S(1)}, u32[]{:S(2)}, u32[]{:S(2)}) %collective-permute-start.10) | collective-permute-done | bytes 262176 | tf_op jit(solution)/shard_map/ppermute | solution.py:32
  45.9 1.8 collective-permute-start.19
  47.7 0.9 collective-permute-done.14.refs_12_
  48.6 0.9 collective-permute-start.20
  49.5 6.9 %collective-permute-start.6 = (bf16[256,512]{1,0:T(8,128)(2,1)}, bf16[256,512]{1,0:T(8,128)(2,1)S(1)}, u32[]{:S(2)}, u32[]{:S(2)}) collective-permute-start(bf16[256,512]{1,0:T(8,128)(2,1)} %get-tuple-element.13.refs_0_), channel_id=1, source_target_pairs={{64,0},{68,4},{72,8},{76,12},{80,16},{84,20},{88,24},{92,28},{96,3... | collective-permute-start | bytes 786440 | tf_op jit(solution)/shard_map/ppermute | solution.py:32
  56.4 1.2 collective-permute-done.20.refs_19_
  57.5 2.4 %collective-permute-start.12 = (bf16[256,512]{1,0:T(8,128)(2,1)S(1)}, bf16[256,512]{1,0:T(8,128)(2,1)S(1)}, u32[]{:S(2)}, u32[]{:S(2)}) collective-permute-start(bf16[256,512]{1,0:T(8,128)(2,1)S(1)} %collective-permute-done.4.refs_2_), channel_id=1, source_target_pairs={{128,0},{132,4},{136,8},{140,12},{144,16},{148,20},{152,24},{156,2... | collective-permute-start | bytes 786440 | tf_op jit(solution)/shard_map/ppermute | solution.py:32
  59.9 12.1 %collective-permute-done.6.refs_4_ = bf16[256,512]{1,0:T(8,128)(2,1)S(1)} collective-permute-done((bf16[256,512]{1,0:T(8,128)(2,1)}, bf16[256,512]{1,0:T(8,128)(2,1)S(1)}, u32[]{:S(2)}, u32[]{:S(2)}) %collective-permute-start.6) | collective-permute-done | bytes 262176 | tf_op jit(solution)/shard_map/ppermute | solution.py:32
  72.0 4.4 %collective-permute-start.15 = (bf16[256,512]{1,0:T(8,128)(2,1)S(1)}, bf16[256,512]{1,0:T(8,128)(2,1)S(1)}, u32[]{:S(2)}, u32[]{:S(2)}) collective-permute-start(bf16[256,512]{1,0:T(8,128)(2,1)S(1)} %collective-permute-done.3.refs_1_), channel_id=1, source_target_pairs={{192,0},{196,4},{200,8},{204,12},{208,16},{212,20},{216,24},{220,2... | collective-permute-start | bytes 786440 | tf_op jit(solution)/shard_map/ppermute | solution.py:32
  79.1 1.0 collective-permute-start.22
  80.1 1.3 collective-permute-done.13.refs_11_
  82.1 3.5 %collective-permute-start.23 = (bf16[256,512]{1,0:T(8,128)(2,1)S(1)}, bf16[256,512]{1,0:T(8,128)(2,1)}, u32[]{:S(2)}, u32[]{:S(2)}) collective-permute-start(bf16[256,512]{1,0:T(8,128)(2,1)S(1)} %collective-permute-done.21.refs_20_), channel_id=1, source_target_pairs={{32,0},{36,4},{40,8},{44,12},{48,16},{52,20},{56,24},{60,28},{0,32... | collective-permute-start | bytes 786440 | tf_op jit(solution)/shard_map/ppermute | solution.py:32
  86.4 2.1 %collective-permute-start.24 = (bf16[256,512]{1,0:T(8,128)(2,1)S(1)}, bf16[256,512]{1,0:T(8,128)(2,1)}, u32[]{:S(2)}, u32[]{:S(2)}) collective-permute-start(bf16[256,512]{1,0:T(8,128)(2,1)S(1)} %collective-permute-done.21.refs_20_), channel_id=1, source_target_pairs={{48,0},{52,4},{56,8},{60,12},{0,16},{4,20},{8,24},{12,28},{16,32},... | collective-permute-start | bytes 786440 | tf_op jit(solution)/shard_map/ppermute | solution.py:32
  89.2 0.8 multiply_reduce_fusion
  91.4 1.7 concatenate.3
  93.2 1.9 %all_to_all.8 = f32[64,1,1152]{2,1,0:T(1,128)} reshape(f32[64,1152]{1,0:T(8,128)} %concatenate.3) | data formatting | bytes 589824 | tf_op jit(solution)/shard_map/all_to_all | solution.py:215
  95.1 13.2 %all-to-all-start = ((f32[64,1,1152]{2,1,0:T(1,128)}), f32[64,1,1152]{2,1,0:T(1,128)}, u32[]{:S(2)}, u32[]{:S(2)}) async-start(f32[64,1,1152]{2,1,0:T(1,128)} %all_to_all.8), calls=%async_computation | async-start | bytes 589824 | tf_op jit(solution)/shard_map/all_to_all | solution.py:215
  109.0 0.9 collective-permute-start.26
  110.6 1.2 collective-permute-start.27
  111.8 2.1 %collective-permute-start.28 = (bf16[256,512]{1,0:T(8,128)(2,1)S(1)}, bf16[256,512]{1,0:T(8,128)(2,1)}, u32[]{:S(2)}, u32[]{:S(2)}) collective-permute-start(bf16[256,512]{1,0:T(8,128)(2,1)S(1)} %collective-permute-done.25.refs_24_), channel_id=1, source_target_pairs={{48,0},{52,4},{56,8},{60,12},{0,16},{4,20},{8,24},{12,28},{16,32},... | collective-permute-start | bytes 786440 | tf_op jit(solution)/shard_map/ppermute | solution.py:32
  113.9 11.7 %collective-permute-done.26.refs_25_ = bf16[256,512]{1,0:T(8,128)(2,1)S(1)} collective-permute-done((bf16[256,512]{1,0:T(8,128)(2,1)S(1)}, bf16[256,512]{1,0:T(8,128)(2,1)S(1)}, u32[]{:S(2)}, u32[]{:S(2)}) %collective-permute-start.26) | collective-permute-done | bytes 262176 | tf_op jit(solution)/shard_map/ppermute | solution.py:32
  127.0 2.9 %collective-permute-start.7 = (bf16[256,512]{1,0:T(8,128)(2,1)S(1)}, bf16[256,512]{1,0:T(8,128)(2,1)}, u32[]{:S(2)}, u32[]{:S(2)}) collective-permute-start(bf16[256,512]{1,0:T(8,128)(2,1)S(1)} %collective-permute-done.3.refs_1_), channel_id=1, source_target_pairs={{64,0},{68,4},{72,8},{76,12},{80,16},{84,20},{88,24},{92,28},{96,3... | collective-permute-start | bytes 786440 | tf_op jit(solution)/shard_map/ppermute | solution.py:32
  129.9 6.3 %collective-permute-done.30.refs_29_ = bf16[256,512]{1,0:T(8,128)(2,1)} collective-permute-done((bf16[256,512]{1,0:T(8,128)(2,1)}, bf16[256,512]{1,0:T(8,128)(2,1)}, u32[]{:S(2)}, u32[]{:S(2)}) %collective-permute-start.30) | collective-permute-done | bytes 262176 | tf_op jit(solution)/shard_map/ppermute | solution.py:32
  136.2 3.0 %collective-permute-start.8 = (bf16[256,512]{1,0:T(8,128)(2,1)S(1)}, bf16[256,512]{1,0:T(8,128)(2,1)}, u32[]{:S(2)}, u32[]{:S(2)}) collective-permute-start(bf16[256,512]{1,0:T(8,128)(2,1)S(1)} %collective-permute-done.4.refs_2_), channel_id=1, source_target_pairs={{64,0},{68,4},{72,8},{76,12},{80,16},{84,20},{88,24},{92,28},{96,3... | collective-permute-start | bytes 786440 | tf_op jit(solution)/shard_map/ppermute | solution.py:32
  139.2 0.7 collective-permute-start.9
  140.8 9.3 %decayed_scores.1 = (bf16[16,256,256]{2,1,0:T(8,128)(2,1)}, bf16[16,256,256]{2,1,0:T(8,128)(2,1)}) custom-call(s32[1]{0:T(128)S(6)} %copy.15.live_ref, bf16[256,1024]{1,0:T(8,128)(2,1)} %bitcast.20, bf16[256,1024]{1,0:T(8,128)(2,1)} %bitcast.21, bf16[256,1024]{1,0:T(8,128)(2,1)} %bitcast.22), custom_call_target="tpu_custom_call" | custom-call | tf_op jit(solution)/shard_map/decayed_scores/pallas_call | solution.py:196
  150.1 1.1 copy.13
  151.3 1.1 fusion
  152.4 3.5 %member_tokens.1 = (bf16[4,256,1024]{2,1,0:T(8,128)(2,1)}, f32[256,8]{1,0:T(8,128)}) custom-call(s32[1]{0:T(128)} %bitcast.4.at_ref, bf16[256,1024]{1,0:T(8,128)(2,1)} %bitcast.18, bf16[256,1024]{1,0:T(8,128)(2,1)} %collective-permute-done.33.t1, bf16[256,1024]{1,0:T(8,128)(2,1)} %collective-permute-done.34.t2, ...), custom_call_target="tpu_custom_call" | custom-call | tf_op jit(solution)/shard_map/member_tokens/pallas_call | solution.py:182
  156.0 1.6 copy-done.1
  157.6 0.9 copy-done.5
  158.5 0.9 copy-done.7
  159.5 0.9 copy-done.9
  160.4 0.9 copy-done.11
  161.4 0.9 copy-done.13
  162.3 0.9 copy-done.15
  163.3 0.9 copy-done.17
  164.2 0.9 copy-done.19
  165.2 0.9 copy-done.21
  166.1 0.9 copy-done.23
  167.1 0.9 copy-done.25
  168.0 0.9 copy-done.27
  169.0 0.9 copy-done.29
  169.9 0.9 copy-done.31
  170.9 0.9 copy-done.33
  171.8 0.9 copy-done.35
  172.8 0.9 copy-done.37
  173.7 0.9 copy-done.38
  174.6 6.9 %values_readout.1 = bf16[256,1024]{1,0:T(8,128)(2,1)} custom-call(s32[2]{0:T(128)S(1)} %pad_add_fusion.at_ref, bf16[256,512]{1,0:T(8,128)(2,1)S(1)} %copy-done.2, bf16[256,512]{1,0:T(8,128)(2,1)S(1)} %collective-permute-done.3.refs_1_, bf16[256,512]{1,0:T(8,128)(2,1)S(1)} %collective-permute-done.4.refs_2_, ...), custom_call_target="tpu_custom_call" | custom-call | tf_op jit(solution)/shard_map/values_readout/pallas_call | solution.py:225
  (110 shorter events, 10.5 us)
Async XLA Ops:
  0.6 8.5 %collective-permute-start = (bf16[64,1024]{1,0:T(8,128)(2,1)}, bf16[64,1024]{1,0:T(8,128)(2,1)S(1)}, u32[]{:S(2)}, u32[]{:S(2)}) collective-permute-start(bf16[64,1024]{1,0:T(8,128)(2,1)} %p0.1), channel_id=1, source_target_pairs={{4,0},{8,4},{12,8},{0,12},{20,16},{24,20},{28,24},{16,28},{36,32},... | collective-permute-start | bytes 393224 | tf_op jit(solution)/shard_map/ppermute | solution.py:32
  1.7 12.0 %collective-permute-start.1 = (bf16[64,1024]{1,0:T(8,128)(2,1)}, bf16[64,1024]{1,0:T(8,128)(2,1)S(1)}, u32[]{:S(2)}, u32[]{:S(2)}) collective-permute-start(bf16[64,1024]{1,0:T(8,128)(2,1)} %p0.1), channel_id=1, source_target_pairs={{8,0},{12,4},{0,8},{4,12},{24,16},{28,20},{16,24},{20,28},{40,32},... | collective-permute-start | bytes 393224 | tf_op jit(solution)/shard_map/ppermute | solution.py:32
  3.2 10.5 %collective-permute-start.2 = (bf16[64,1024]{1,0:T(8,128)(2,1)}, bf16[64,1024]{1,0:T(8,128)(2,1)S(1)}, u32[]{:S(2)}, u32[]{:S(2)}) collective-permute-start(bf16[64,1024]{1,0:T(8,128)(2,1)} %p0.1), channel_id=1, source_target_pairs={{12,0},{0,4},{4,8},{8,12},{28,16},{16,20},{20,24},{24,28},{44,32},... | collective-permute-start | bytes 393224 | tf_op jit(solution)/shard_map/ppermute | solution.py:32
  9.2 4.5 %copy-start.40 = (bf16[64,1024]{1,0:T(8,128)(2,1)}, bf16[64,1024]{1,0:T(8,128)(2,1)S(1)}, u32[]{:S(2)}) copy-start(bf16[64,1024]{1,0:T(8,128)(2,1)S(1)} %collective-permute-done.p1) | copy-start | bytes 393220
  16.3 14.8 %collective-permute-start.3 = (bf16[256,512]{1,0:T(8,128)(2,1)}, bf16[256,512]{1,0:T(8,128)(2,1)S(1)}, u32[]{:S(2)}, u32[]{:S(2)}) collective-permute-start(bf16[256,512]{1,0:T(8,128)(2,1)} %get-tuple-element.13.refs_0_), channel_id=1, source_target_pairs={{16,0},{20,4},{24,8},{28,12},{32,16},{36,20},{40,24},{44,28},{48,3... | collective-permute-start | bytes 786440 | tf_op jit(solution)/shard_map/ppermute | solution.py:32
  17.1 15.6 %collective-permute-start.4 = (bf16[256,512]{1,0:T(8,128)(2,1)}, bf16[256,512]{1,0:T(8,128)(2,1)S(1)}, u32[]{:S(2)}, u32[]{:S(2)}) collective-permute-start(bf16[256,512]{1,0:T(8,128)(2,1)} %get-tuple-element.13.refs_0_), channel_id=1, source_target_pairs={{32,0},{36,4},{40,8},{44,12},{48,16},{52,20},{56,24},{60,28},{0,32... | collective-permute-start | bytes 786440 | tf_op jit(solution)/shard_map/ppermute | solution.py:32
  18.2 17.4 %collective-permute-start.5 = (bf16[256,512]{1,0:T(8,128)(2,1)}, bf16[256,512]{1,0:T(8,128)(2,1)S(1)}, u32[]{:S(2)}, u32[]{:S(2)}) collective-permute-start(bf16[256,512]{1,0:T(8,128)(2,1)} %get-tuple-element.13.refs_0_), channel_id=1, source_target_pairs={{48,0},{52,4},{56,8},{60,12},{0,16},{4,20},{8,24},{12,28},{16,32},... | collective-permute-start | bytes 786440 | tf_op jit(solution)/shard_map/ppermute | solution.py:32
  20.3 19.1 %collective-permute-start.21 = (bf16[256,512]{1,0:T(8,128)(2,1)}, bf16[256,512]{1,0:T(8,128)(2,1)S(1)}, u32[]{:S(2)}, u32[]{:S(2)}) collective-permute-start(bf16[256,512]{1,0:T(8,128)(2,1)} %get-tuple-element.14.refs_16_), channel_id=1, source_target_pairs={{64,0},{68,4},{72,8},{76,12},{80,16},{84,20},{88,24},{92,28},{96,3... | collective-permute-start | bytes 786440 | tf_op jit(solution)/shard_map/ppermute | solution.py:32
  23.3 16.4 %collective-permute-start.25 = (bf16[256,512]{1,0:T(8,128)(2,1)}, bf16[256,512]{1,0:T(8,128)(2,1)S(1)}, u32[]{:S(2)}, u32[]{:S(2)}) collective-permute-start(bf16[256,512]{1,0:T(8,128)(2,1)} %get-tuple-element.14.refs_16_), channel_id=1, source_target_pairs={{128,0},{132,4},{136,8},{140,12},{144,16},{148,20},{152,24},{156,2... | collective-permute-start | bytes 786440 | tf_op jit(solution)/shard_map/ppermute | solution.py:32
  31.1 11.9 %collective-permute-start.29 = (bf16[256,512]{1,0:T(8,128)(2,1)}, bf16[256,512]{1,0:T(8,128)(2,1)}, u32[]{:S(2)}, u32[]{:S(2)}) collective-permute-start(bf16[256,512]{1,0:T(8,128)(2,1)} %get-tuple-element.14.refs_16_), channel_id=1, source_target_pairs={{192,0},{196,4},{200,8},{204,12},{208,16},{212,20},{216,24},{220,2... | collective-permute-start | bytes 786440 | tf_op jit(solution)/shard_map/ppermute | solution.py:32
  32.7 13.2 %collective-permute-start.10 = (bf16[256,512]{1,0:T(8,128)(2,1)}, bf16[256,512]{1,0:T(8,128)(2,1)S(1)}, u32[]{:S(2)}, u32[]{:S(2)}) collective-permute-start(bf16[256,512]{1,0:T(8,128)(2,1)} %get-tuple-element.13.refs_0_), channel_id=1, source_target_pairs={{128,0},{132,4},{136,8},{140,12},{144,16},{148,20},{152,24},{156,2... | collective-permute-start | bytes 786440 | tf_op jit(solution)/shard_map/ppermute | solution.py:32
  35.6 13.0 %collective-permute-start.14 = (bf16[256,512]{1,0:T(8,128)(2,1)}, bf16[256,512]{1,0:T(8,128)(2,1)S(1)}, u32[]{:S(2)}, u32[]{:S(2)}) collective-permute-start(bf16[256,512]{1,0:T(8,128)(2,1)} %get-tuple-element.13.refs_0_), channel_id=1, source_target_pairs={{192,0},{196,4},{200,8},{204,12},{208,16},{212,20},{216,24},{220,2... | collective-permute-start | bytes 786440 | tf_op jit(solution)/shard_map/ppermute | solution.py:32
  39.4 101.3 %copy-start.4 = (bf16[256,512]{1,0:T(8,128)(2,1)}, bf16[256,512]{1,0:T(8,128)(2,1)S(1)}, u32[]{:S(2)}) copy-start(bf16[256,512]{1,0:T(8,128)(2,1)S(1)} %collective-permute-done.21.refs_20_) | copy-start | bytes 786436
  39.4 10.1 %collective-permute-start.18 = (bf16[256,512]{1,0:T(8,128)(2,1)}, bf16[256,512]{1,0:T(8,128)(2,1)S(1)}, u32[]{:S(2)}, u32[]{:S(2)}) collective-permute-start(bf16[256,512]{1,0:T(8,128)(2,1)} %get-tuple-element.14.refs_16_), channel_id=1, source_target_pairs={{16,0},{20,4},{24,8},{28,12},{32,16},{36,20},{40,24},{44,28},{48,3... | collective-permute-start | bytes 786440 | tf_op jit(solution)/shard_map/ppermute | solution.py:32
  39.7 101.0 %copy-start.6 = (bf16[256,512]{1,0:T(8,128)(2,1)}, bf16[256,512]{1,0:T(8,128)(2,1)S(1)}, u32[]{:S(2)}) copy-start(bf16[256,512]{1,0:T(8,128)(2,1)S(1)} %collective-permute-done.25.refs_24_) | copy-start | bytes 786436
  39.7 32.3 %collective-permute-start.34 = (bf16[256,1024]{1,0:T(8,128)(2,1)}, bf16[256,1024]{1,0:T(8,128)(2,1)}, u32[]{:S(2)}, u32[]{:S(2)}) collective-permute-start(bf16[256,1024]{1,0:T(8,128)(2,1)} %bitcast.16), channel_id=1, source_target_pairs={{0,2},{1,3},{2,0},{3,1},{4,6},{5,7},{6,4},{7,5},{8,10},{9,11},{10,... | collective-permute-start | bytes 1572872 | tf_op jit(solution)/shard_map/ppermute | solution.py:36
  43.0 33.4 %collective-permute-start.33 = (bf16[256,1024]{1,0:T(8,128)(2,1)}, bf16[256,1024]{1,0:T(8,128)(2,1)}, u32[]{:S(2)}, u32[]{:S(2)}) collective-permute-start(bf16[256,1024]{1,0:T(8,128)(2,1)} %bitcast.17), channel_id=1, source_target_pairs={{0,1},{1,0},{2,3},{3,2},{4,5},{5,4},{6,7},{7,6},{8,9},{9,8},{10,11... | collective-permute-start | bytes 1572872 | tf_op jit(solution)/shard_map/ppermute | solution.py:36
  45.9 94.8 %copy-start.8 = (bf16[256,512]{1,0:T(8,128)(2,1)}, bf16[256,512]{1,0:T(8,128)(2,1)S(1)}, u32[]{:S(2)}) copy-start(bf16[256,512]{1,0:T(8,128)(2,1)S(1)} %collective-permute-done.10.refs_8_) | copy-start | bytes 786436
  45.9 10.4 %collective-permute-start.19 = (bf16[256,512]{1,0:T(8,128)(2,1)}, bf16[256,512]{1,0:T(8,128)(2,1)S(1)}, u32[]{:S(2)}, u32[]{:S(2)}) collective-permute-start(bf16[256,512]{1,0:T(8,128)(2,1)} %get-tuple-element.14.refs_16_), channel_id=1, source_target_pairs={{32,0},{36,4},{40,8},{44,12},{48,16},{52,20},{56,24},{60,28},{0,32... | collective-permute-start | bytes 786440 | tf_op jit(solution)/shard_map/ppermute | solution.py:32
  48.6 92.2 %copy-start.10 = (bf16[256,512]{1,0:T(8,128)(2,1)}, bf16[256,512]{1,0:T(8,128)(2,1)S(1)}, u32[]{:S(2)}) copy-start(bf16[256,512]{1,0:T(8,128)(2,1)S(1)} %collective-permute-done.14.refs_12_) | copy-start | bytes 786436
  48.6 9.0 %collective-permute-start.20 = (bf16[256,512]{1,0:T(8,128)(2,1)}, bf16[256,512]{1,0:T(8,128)(2,1)S(1)}, u32[]{:S(2)}, u32[]{:S(2)}) collective-permute-start(bf16[256,512]{1,0:T(8,128)(2,1)} %get-tuple-element.14.refs_16_), channel_id=1, source_target_pairs={{48,0},{52,4},{56,8},{60,12},{0,16},{4,20},{8,24},{12,28},{16,32},... | collective-permute-start | bytes 786440 | tf_op jit(solution)/shard_map/ppermute | solution.py:32
  49.4 91.3 %copy-start.12 = (bf16[256,512]{1,0:T(8,128)(2,1)}, bf16[256,512]{1,0:T(8,128)(2,1)S(1)}, u32[]{:S(2)}) copy-start(bf16[256,512]{1,0:T(8,128)(2,1)S(1)} %collective-permute-done.18.refs_17_) | copy-start | bytes 786436
  49.5 22.5 %collective-permute-start.6 = (bf16[256,512]{1,0:T(8,128)(2,1)}, bf16[256,512]{1,0:T(8,128)(2,1)S(1)}, u32[]{:S(2)}, u32[]{:S(2)}) collective-permute-start(bf16[256,512]{1,0:T(8,128)(2,1)} %get-tuple-element.13.refs_0_), channel_id=1, source_target_pairs={{64,0},{68,4},{72,8},{76,12},{80,16},{84,20},{88,24},{92,28},{96,3... | collective-permute-start | bytes 786440 | tf_op jit(solution)/shard_map/ppermute | solution.py:32
  56.3 84.4 %copy-start.14 = (bf16[256,512]{1,0:T(8,128)(2,1)}, bf16[256,512]{1,0:T(8,128)(2,1)S(1)}, u32[]{:S(2)}) copy-start(bf16[256,512]{1,0:T(8,128)(2,1)S(1)} %collective-permute-done.19.refs_18_) | copy-start | bytes 786436
  56.3 20.8 %collective-permute-start.11 = (bf16[256,512]{1,0:T(8,128)(2,1)S(1)}, bf16[256,512]{1,0:T(8,128)(2,1)S(1)}, u32[]{:S(2)}, u32[]{:S(2)}) collective-permute-start(bf16[256,512]{1,0:T(8,128)(2,1)S(1)} %collective-permute-done.3.refs_1_), channel_id=1, source_target_pairs={{128,0},{132,4},{136,8},{140,12},{144,16},{148,20},{152,24},{156,2... | collective-permute-start | bytes 786440 | tf_op jit(solution)/shard_map/ppermute | solution.py:32
  57.5 83.2 %copy-start.16 = (bf16[256,512]{1,0:T(8,128)(2,1)}, bf16[256,512]{1,0:T(8,128)(2,1)S(1)}, u32[]{:S(2)}) copy-start(bf16[256,512]{1,0:T(8,128)(2,1)S(1)} %collective-permute-done.20.refs_19_) | copy-start | bytes 786436
  57.5 20.9 %collective-permute-start.12 = (bf16[256,512]{1,0:T(8,128)(2,1)S(1)}, bf16[256,512]{1,0:T(8,128)(2,1)S(1)}, u32[]{:S(2)}, u32[]{:S(2)}) collective-permute-start(bf16[256,512]{1,0:T(8,128)(2,1)S(1)} %collective-permute-done.4.refs_2_), channel_id=1, source_target_pairs={{128,0},{132,4},{136,8},{140,12},{144,16},{148,20},{152,24},{156,2... | collective-permute-start | bytes 786440 | tf_op jit(solution)/shard_map/ppermute | solution.py:32
  72.0 68.8 %copy-start.18 = (bf16[256,512]{1,0:T(8,128)(2,1)}, bf16[256,512]{1,0:T(8,128)(2,1)S(1)}, u32[]{:S(2)}) copy-start(bf16[256,512]{1,0:T(8,128)(2,1)S(1)} %collective-permute-done.6.refs_4_) | copy-start | bytes 786436
  72.0 9.4 %collective-permute-start.13 = (bf16[256,512]{1,0:T(8,128)(2,1)S(1)}, bf16[256,512]{1,0:T(8,128)(2,1)S(1)}, u32[]{:S(2)}, u32[]{:S(2)}) collective-permute-start(bf16[256,512]{1,0:T(8,128)(2,1)S(1)} %collective-permute-done.5.refs_3_), channel_id=1, source_target_pairs={{128,0},{132,4},{136,8},{140,12},{144,16},{148,20},{152,24},{156,2... | collective-permute-start | bytes 786440 | tf_op jit(solution)/shard_map/ppermute | solution.py:32
  72.0 13.7 %collective-permute-start.15 = (bf16[256,512]{1,0:T(8,128)(2,1)S(1)}, bf16[256,512]{1,0:T(8,128)(2,1)S(1)}, u32[]{:S(2)}, u32[]{:S(2)}) collective-permute-start(bf16[256,512]{1,0:T(8,128)(2,1)S(1)} %collective-permute-done.3.refs_1_), channel_id=1, source_target_pairs={{192,0},{196,4},{200,8},{204,12},{208,16},{212,20},{216,24},{220,2... | collective-permute-start | bytes 786440 | tf_op jit(solution)/shard_map/ppermute | solution.py:32
  76.4 12.0 %collective-permute-start.16 = (bf16[256,512]{1,0:T(8,128)(2,1)S(1)}, bf16[256,512]{1,0:T(8,128)(2,1)S(1)}, u32[]{:S(2)}, u32[]{:S(2)}) collective-permute-start(bf16[256,512]{1,0:T(8,128)(2,1)S(1)} %collective-permute-done.4.refs_2_), channel_id=1, source_target_pairs={{192,0},{196,4},{200,8},{204,12},{208,16},{212,20},{216,24},{220,2... | collective-permute-start | bytes 786440 | tf_op jit(solution)/shard_map/ppermute | solution.py:32
  77.9 30.4 %collective-permute-start.17 = (bf16[256,512]{1,0:T(8,128)(2,1)S(1)}, bf16[256,512]{1,0:T(8,128)(2,1)S(1)}, u32[]{:S(2)}, u32[]{:S(2)}) collective-permute-start(bf16[256,512]{1,0:T(8,128)(2,1)S(1)} %collective-permute-done.5.refs_3_), channel_id=1, source_target_pairs={{192,0},{196,4},{200,8},{204,12},{208,16},{212,20},{216,24},{220,2... | collective-permute-start | bytes 786440 | tf_op jit(solution)/shard_map/ppermute | solution.py:32
  79.1 30.7 %collective-permute-start.22 = (bf16[256,512]{1,0:T(8,128)(2,1)S(1)}, bf16[256,512]{1,0:T(8,128)(2,1)S(1)}, u32[]{:S(2)}, u32[]{:S(2)}) collective-permute-start(bf16[256,512]{1,0:T(8,128)(2,1)S(1)} %collective-permute-done.21.refs_20_), channel_id=1, source_target_pairs={{16,0},{20,4},{24,8},{28,12},{32,16},{36,20},{40,24},{44,28},{48,3... | collective-permute-start | bytes 786440 | tf_op jit(solution)/shard_map/ppermute | solution.py:32
  82.1 29.7 %collective-permute-start.23 = (bf16[256,512]{1,0:T(8,128)(2,1)S(1)}, bf16[256,512]{1,0:T(8,128)(2,1)}, u32[]{:S(2)}, u32[]{:S(2)}) collective-permute-start(bf16[256,512]{1,0:T(8,128)(2,1)S(1)} %collective-permute-done.21.refs_20_), channel_id=1, source_target_pairs={{32,0},{36,4},{40,8},{44,12},{48,16},{52,20},{56,24},{60,28},{0,32... | collective-permute-start | bytes 786440 | tf_op jit(solution)/shard_map/ppermute | solution.py:32
  86.4 27.5 %collective-permute-start.24 = (bf16[256,512]{1,0:T(8,128)(2,1)S(1)}, bf16[256,512]{1,0:T(8,128)(2,1)}, u32[]{:S(2)}, u32[]{:S(2)}) collective-permute-start(bf16[256,512]{1,0:T(8,128)(2,1)S(1)} %collective-permute-done.21.refs_20_), channel_id=1, source_target_pairs={{48,0},{52,4},{56,8},{60,12},{0,16},{4,20},{8,24},{12,28},{16,32},... | collective-permute-start | bytes 786440 | tf_op jit(solution)/shard_map/ppermute | solution.py:32
  89.2 50.0 %collective-permute-start.35 = (bf16[256,1024]{1,0:T(8,128)(2,1)}, bf16[256,1024]{1,0:T(8,128)(2,1)}, u32[]{:S(2)}, u32[]{:S(2)}) collective-permute-start(bf16[256,1024]{1,0:T(8,128)(2,1)} %collective-permute-done.34.t2), channel_id=1, source_target_pairs={{0,1},{1,0},{2,3},{3,2},{4,5},{5,4},{6,7},{7,6},{8,9},{9,8},{10,11... | collective-permute-start | bytes 1572872 | tf_op jit(solution)/shard_map/ppermute | solution.py:36
  95.1 55.1 %all-to-all-start = ((f32[64,1,1152]{2,1,0:T(1,128)}), f32[64,1,1152]{2,1,0:T(1,128)}, u32[]{:S(2)}, u32[]{:S(2)}) async-start(f32[64,1,1152]{2,1,0:T(1,128)} %all_to_all.8), calls=%async_computation | async-start | bytes 589824 | tf_op jit(solution)/shard_map/all_to_all | solution.py:215
  109.0 16.5 %collective-permute-start.26 = (bf16[256,512]{1,0:T(8,128)(2,1)S(1)}, bf16[256,512]{1,0:T(8,128)(2,1)S(1)}, u32[]{:S(2)}, u32[]{:S(2)}) collective-permute-start(bf16[256,512]{1,0:T(8,128)(2,1)S(1)} %collective-permute-done.25.refs_24_), channel_id=1, source_target_pairs={{16,0},{20,4},{24,8},{28,12},{32,16},{36,20},{40,24},{44,28},{48,3... | collective-permute-start | bytes 786440 | tf_op jit(solution)/shard_map/ppermute | solution.py:32
  110.6 15.7 %collective-permute-start.27 = (bf16[256,512]{1,0:T(8,128)(2,1)S(1)}, bf16[256,512]{1,0:T(8,128)(2,1)S(1)}, u32[]{:S(2)}, u32[]{:S(2)}) collective-permute-start(bf16[256,512]{1,0:T(8,128)(2,1)S(1)} %collective-permute-done.25.refs_24_), channel_id=1, source_target_pairs={{32,0},{36,4},{40,8},{44,12},{48,16},{52,20},{56,24},{60,28},{0,32... | collective-permute-start | bytes 786440 | tf_op jit(solution)/shard_map/ppermute | solution.py:32
  111.8 15.2 %collective-permute-start.28 = (bf16[256,512]{1,0:T(8,128)(2,1)S(1)}, bf16[256,512]{1,0:T(8,128)(2,1)}, u32[]{:S(2)}, u32[]{:S(2)}) collective-permute-start(bf16[256,512]{1,0:T(8,128)(2,1)S(1)} %collective-permute-done.25.refs_24_), channel_id=1, source_target_pairs={{48,0},{52,4},{56,8},{60,12},{0,16},{4,20},{8,24},{12,28},{16,32},... | collective-permute-start | bytes 786440 | tf_op jit(solution)/shard_map/ppermute | solution.py:32
  113.8 22.4 %collective-permute-start.30 = (bf16[256,512]{1,0:T(8,128)(2,1)}, bf16[256,512]{1,0:T(8,128)(2,1)}, u32[]{:S(2)}, u32[]{:S(2)}) collective-permute-start(bf16[256,512]{1,0:T(8,128)(2,1)} %collective-permute-done.29.refs_28_), channel_id=1, source_target_pairs={{16,0},{20,4},{24,8},{28,12},{32,16},{36,20},{40,24},{44,28},{48,3... | collective-permute-start | bytes 786440 | tf_op jit(solution)/shard_map/ppermute | solution.py:32
  126.3 29.6 %collective-permute-start.31 = (bf16[256,512]{1,0:T(8,128)(2,1)}, bf16[256,512]{1,0:T(8,128)(2,1)}, u32[]{:S(2)}, u32[]{:S(2)}) collective-permute-start(bf16[256,512]{1,0:T(8,128)(2,1)} %collective-permute-done.29.refs_28_), channel_id=1, source_target_pairs={{32,0},{36,4},{40,8},{44,12},{48,16},{52,20},{56,24},{60,28},{0,32... | collective-permute-start | bytes 786440 | tf_op jit(solution)/shard_map/ppermute | solution.py:32
  127.0 28.9 %collective-permute-start.32 = (bf16[256,512]{1,0:T(8,128)(2,1)}, bf16[256,512]{1,0:T(8,128)(2,1)}, u32[]{:S(2)}, u32[]{:S(2)}) collective-permute-start(bf16[256,512]{1,0:T(8,128)(2,1)} %collective-permute-done.29.refs_28_), channel_id=1, source_target_pairs={{48,0},{52,4},{56,8},{60,12},{0,16},{4,20},{8,24},{12,28},{16,32},... | collective-permute-start | bytes 786440 | tf_op jit(solution)/shard_map/ppermute | solution.py:32
  127.0 28.9 %collective-permute-start.7 = (bf16[256,512]{1,0:T(8,128)(2,1)S(1)}, bf16[256,512]{1,0:T(8,128)(2,1)}, u32[]{:S(2)}, u32[]{:S(2)}) collective-permute-start(bf16[256,512]{1,0:T(8,128)(2,1)S(1)} %collective-permute-done.3.refs_1_), channel_id=1, source_target_pairs={{64,0},{68,4},{72,8},{76,12},{80,16},{84,20},{88,24},{92,28},{96,3... | collective-permute-start | bytes 786440 | tf_op jit(solution)/shard_map/ppermute | solution.py:32
  136.2 19.7 %collective-permute-start.8 = (bf16[256,512]{1,0:T(8,128)(2,1)S(1)}, bf16[256,512]{1,0:T(8,128)(2,1)}, u32[]{:S(2)}, u32[]{:S(2)}) collective-permute-start(bf16[256,512]{1,0:T(8,128)(2,1)S(1)} %collective-permute-done.4.refs_2_), channel_id=1, source_target_pairs={{64,0},{68,4},{72,8},{76,12},{80,16},{84,20},{88,24},{92,28},{96,3... | collective-permute-start | bytes 786440 | tf_op jit(solution)/shard_map/ppermute | solution.py:32
  139.2 16.7 %collective-permute-start.9 = (bf16[256,512]{1,0:T(8,128)(2,1)S(1)}, bf16[256,512]{1,0:T(8,128)(2,1)}, u32[]{:S(2)}, u32[]{:S(2)}) collective-permute-start(bf16[256,512]{1,0:T(8,128)(2,1)S(1)} %collective-permute-done.5.refs_3_), channel_id=1, source_target_pairs={{64,0},{68,4},{72,8},{76,12},{80,16},{84,20},{88,24},{92,28},{96,3... | collective-permute-start | bytes 786440 | tf_op jit(solution)/shard_map/ppermute | solution.py:32
  140.8 15.2 %copy-start.2 = (bf16[256,512]{1,0:T(8,128)(2,1)S(1)}, bf16[256,512]{1,0:T(8,128)(2,1)}, u32[]{:S(2)}) copy-start(bf16[256,512]{1,0:T(8,128)(2,1)} %get-tuple-element.13.refs_0_) | copy-start | bytes 786436
  140.8 15.2 %copy-start.3 = (bf16[256,512]{1,0:T(8,128)(2,1)S(1)}, bf16[256,512]{1,0:T(8,128)(2,1)}, u32[]{:S(2)}) copy-start(bf16[256,512]{1,0:T(8,128)(2,1)} %get-tuple-element.14.refs_16_) | copy-start | bytes 786436
  140.8 15.2 %copy-start.39 = (bf16[1,1024]{1,0:T(2,128)(2,1)S(1)}, bf16[1,1024]{1,0:T(2,128)(2,1)}, u32[]{:S(2)}) copy-start(bf16[1,1024]{1,0:T(2,128)(2,1)} %refs_34_.1) | copy-start | bytes 6148
  150.1 5.8 %copy-start = (bf16[16,256,256]{2,1,0:T(8,128)(2,1)S(1)}, bf16[16,256,256]{2,1,0:T(8,128)(2,1)}, u32[]{:S(2)}) copy-start(bf16[16,256,256]{2,1,0:T(8,128)(2,1)} %get-tuple-element.18.refs_35_) | copy-start | bytes 6291460
  156.0 1.6 copy-start.1
  157.6 0.9 copy-start.5
  158.5 0.9 copy-start.7
  159.5 0.9 copy-start.9
  160.4 0.9 copy-start.11
  161.4 0.9 copy-start.13
  162.3 0.9 copy-start.15
  163.3 0.9 copy-start.17
  164.2 0.9 copy-start.19
  165.2 0.9 copy-start.21
  166.1 0.9 copy-start.23
  167.1 0.9 copy-start.25
  168.0 0.9 copy-start.27
  169.0 0.9 copy-start.29
  (16 other events, 12.4 us)

commit v2 on v1

v2 whole, which is shorter than its diff:
```python
import functools
import math

import jax
import jax.numpy as jnp
from jax import lax
from jax.experimental import pallas as pl
from jax.experimental.pallas import tpu as pltpu
from jax.sharding import PartitionSpec as P

HEAD = 64
SIGMA = 0.5
HIGHEST = lax.Precision.HIGHEST
F32 = jnp.float32
BF16 = jnp.bfloat16

SIDE = 4
STRIDE = {"y": 16, "x": 4, "z": 1}
SPAN = 64
LANES = 128

VMEM = pl.BlockSpec(memory_space=pltpu.VMEM)
ANY = pl.BlockSpec(memory_space=pl.ANY)
SMEM = pl.BlockSpec(memory_space=pltpu.SMEM)


def fetch(array, axis, step):
    stride = STRIDE[axis]
    pairs = []
    for me in range(SIDE**3):
        at = (me // stride) % SIDE
        pairs.append((me + ((at + step) % SIDE - at) * stride, me))
    return lax.ppermute(array, "pop", pairs)


def swap(array, bit):
    return lax.ppermute(array, "tp", [(i, i ^ bit) for i in range(4)])


def score_kernel(live_ref, recept_ref, keys_ref, decay_ref, high_ref, low_ref):
    length = recept_ref.shape[0]
    live = live_ref[0]
    row = lax.broadcasted_iota(jnp.int32, (length, LANES), 0)
    alive = row < live
    decay = jnp.where(alive, decay_ref[...], jnp.zeros((), BF16))
    keys = jnp.where(alive, keys_ref[...].astype(F32), 0.0)
    lower = (
        lax.broadcasted_iota(jnp.int32, (length, length), 0)
        >= lax.broadcasted_iota(jnp.int32, (length, length), 1)
    ).astype(F32).astype(BF16)
    summed = jnp.dot(lower, decay, preferred_element_type=F32)
    lane = lax.broadcasted_iota(jnp.int32, (SPAN, LANES), 1)
    for chunk in range(length // SPAN):
        first, last = chunk * SPAN, (chunk + 1) * SPAN
        base = summed[first - 1 : first] if chunk else jnp.zeros((1, LANES), F32)
        grown = recept_ref[first:last].astype(F32) * jnp.exp(summed[first:last] - base)
        shrunk = keys[:last] * jnp.exp(base - summed[:last])
        both = jnp.concatenate(
            [jnp.where(lane < HEAD, grown, 0.0), jnp.where(lane < HEAD, 0.0, grown)], 0
        )
        scores = lax.dot_general(
            both, shrunk, (((1,), (1,)), ((), ())), precision=HIGHEST, preferred_element_type=F32
        )
        for head in range(2):
            mine = scores[head * SPAN : (head + 1) * SPAN]
            here = lax.broadcasted_iota(jnp.int32, (SPAN, last), 0) + first
            there = lax.broadcasted_iota(jnp.int32, (SPAN, last), 1)
            mine = jnp.where((here >= there) & (here < live), mine, 0.0)
            high = mine.astype(BF16)
            low = (mine - high.astype(F32)).astype(BF16)
            high_ref[head, first:last, :last] = high
            low_ref[head, first:last, :last] = low
            if last < length:
                rest = jnp.zeros((SPAN, length - last), BF16)
                high_ref[head, first:last, last:] = rest
                low_ref[head, first:last, last:] = rest


def join_kernel(pop_ref, p0, p1, p2, p3, left_ref, right_ref, sems):
    rows = p0.shape[0]
    half = left_ref.shape[1]
    copies = []
    for step, part in enumerate((p0, p1, p2, p3)):
        place = pl.ds(pl.multiple_of(lax.rem(pop_ref[0] + step, SIDE) * rows, rows), rows)
        for side, out in enumerate((left_ref, right_ref)):
            copies.append(
                pltpu.make_async_copy(
                    part.at[:, side * half : (side + 1) * half], out.at[place], sems.at[step, side]
                )
            )
    for copy in copies:
        copy.start()
    for copy in copies:
        copy.wait()


def join_rows(pop, parts):
    rows, width = parts[0].shape
    return pl.pallas_call(
        join_kernel,
        out_shape=[jax.ShapeDtypeStruct((SIDE * rows, width // 2), BF16)] * 2,
        in_specs=[SMEM] + [ANY] * 4,
        out_specs=[ANY] * 2,
        scratch_shapes=[pltpu.SemaphoreType.DMA((SIDE, 2))],
        name="join_rows",
    )(pop, *parts)


def stack_kernel(*refs):
    parts, out_ref, sems = refs[:-2], refs[-2], refs[-1]
    rows = parts[0].shape[0]
    copies = [
        pltpu.make_async_copy(part, out_ref.at[i * rows : (i + 1) * rows], sems.at[i])
        for i, part in enumerate(parts)
    ]
    for copy in copies:
        copy.start()
    for copy in copies:
        copy.wait()


def stack_rows(parts):
    rows, width = parts[0].shape
    return pl.pallas_call(
        stack_kernel,
        out_shape=jax.ShapeDtypeStruct((len(parts) * rows, width), BF16),
        in_specs=[ANY] * len(parts),
        out_specs=ANY,
        scratch_shapes=[pltpu.SemaphoreType.DMA((len(parts),))],
        name="stack_rows",
    )(*parts)


def token_kernel(at_ref, t0, t1, t2, t3, noise_ref, tokens_ref, projected_ref):
    total = None
    for bits, part in enumerate((t0, t1, t2, t3)):
        place = jnp.bitwise_xor(at_ref[0], bits)
        block = part[...]
        tokens_ref[place] = block
        noise = jnp.broadcast_to(noise_ref[place], (8, block.shape[1]))
        term = lax.dot_general(
            block, noise, (((1,), (1,)), ((), ())), preferred_element_type=F32
        )
        total = term if total is None else total + term
    projected_ref[...] = total


def token_blocks(pop_ref, tokens_ref, side, far, nears):
    y, x = lax.div(pop_ref[0], SIDE * SIDE), lax.rem(lax.div(pop_ref[0], SIDE), SIDE)
    depth = tokens_ref.shape[2] // SIDE
    blocks = []
    for near in nears:
        dy, dx = (far, near) if side == 0 else (near, far)
        place = pl.ds(pl.multiple_of(lax.rem(x + dx, SIDE) * depth, depth), depth)
        blocks.append(tokens_ref[lax.rem(y + dy, SIDE), :, place])
    return jnp.concatenate(blocks, 1)


def product_kernel(plan, added, pop_ref, tokens_ref, *refs):
    refs = list(refs)
    sum_ref = refs.pop(0) if added else None
    count = len(plan)
    pieces, out_ref, held, sems = refs[:count], refs[count], refs[count + 1], refs[count + 2]
    half = out_ref.shape[1] // 2
    copies = [pltpu.make_async_copy(p, held.at[i], sems.at[i]) for i, p in enumerate(pieces)]
    for copy in copies:
        copy.start()
    totals = [None, None]
    for i, (side, far, nears) in enumerate(plan):
        blocks = token_blocks(pop_ref, tokens_ref, side, far, nears)
        copies[i].wait()
        term = jnp.dot(blocks, held[i], preferred_element_type=F32)
        totals[side] = term if totals[side] is None else totals[side] + term
    for side in range(2):
        where = slice(side * half, (side + 1) * half)
        total = totals[side]
        if added:
            total = total + sum_ref[:, where]
        out_ref[:, where] = total


def product(pop, tokens, plan, pieces, before=None):
    length, width = tokens.shape[1:]
    extra = () if before is None else (before,)
    return pl.pallas_call(
        functools.partial(product_kernel, plan, before is not None),
        out_shape=jax.ShapeDtypeStruct((length, width), F32),
        in_specs=[SMEM, VMEM] + [VMEM] * len(extra) + [ANY] * len(pieces),
        out_specs=VMEM,
        scratch_shapes=[
            pltpu.VMEM((len(pieces),) + pieces[0].shape, BF16),
            pltpu.SemaphoreType.DMA((len(pieces),)),
        ],
        compiler_params=params(24),
        cost_estimate=pl.CostEstimate(
            flops=len(pieces) * 2 * length * pieces[0].size,
            bytes_accessed=len(pieces) * 2 * pieces[0].size + 4 * length * width * 2,
            transcendentals=0,
        ),
        name="products",
    )(pop, tokens, *extra, *pieces)


def readout_kernel(plan, pop_ref, *refs):
    count = len(plan)
    tokens_ref, sum_ref, projected_ref, noise_ref, high_ref, low_ref = refs[:6]
    pieces = refs[6 : 6 + count]
    out_ref, held, sems = refs[6 + count :]
    half = out_ref.shape[1] // 2
    copies = [pltpu.make_async_copy(p, held.at[i], sems.at[i]) for i, p in enumerate(pieces)]
    for copy in copies:
        copy.start()
    projected = projected_ref[...][:, :1] * (SIGMA / math.sqrt(SIDE**3 * 64))
    lane = lax.broadcasted_iota(jnp.int32, (out_ref.shape[0], LANES), 1)
    for side in range(2):
        where = slice(side * half, (side + 1) * half)
        total = sum_ref[:, where] + projected * noise_ref[:, where].astype(F32)
        for i, (at, far, nears) in enumerate(plan):
            if at == side:
                blocks = token_blocks(pop_ref, tokens_ref, side, far, nears)
                copies[i].wait()
                total = total + jnp.dot(blocks, held[i], preferred_element_type=F32)
        values = total.astype(BF16)
        for pair in range(half // LANES):
            mine = values[:, pair * LANES : (pair + 1) * LANES]
            head = side * (half // HEAD) + 2 * pair
            outs = [
                jnp.dot(high_ref[head + i], mine, preferred_element_type=F32)
                + jnp.dot(low_ref[head + i], mine, preferred_element_type=F32)
                for i in range(2)
            ]
            start = side * half + pair * LANES
            out_ref[:, start : start + LANES] = jnp.where(lane < HEAD, *outs).astype(BF16)


def params(mib):
    return pltpu.CompilerParams(vmem_limit_bytes=mib << 20)


def after(value, *others):
    return lax.optimization_barrier((value, others))[0]


def body(
    tokens, receptance, keys, log_decay, value_weight, noise_in, noise_out, utilities, live_length
):
    _, length, width = receptance.shape
    pop = lax.axis_index("pop").reshape(1)
    tp = lax.axis_index("tp").reshape(1)
    tokens, receptance, keys, log_decay = (
        a.reshape(length, width) for a in (tokens, receptance, keys, log_decay)
    )
    rows = value_weight.shape[0]

    population = lax.axis_size("pop")
    weighted = noise_in.astype(F32) * (utilities / math.sqrt(population))[:, None]
    message = jnp.concatenate(
        [
            weighted.reshape(population, rows),
            jnp.zeros((population, LANES - rows), F32),
            jnp.broadcast_to(noise_out.astype(F32), (population, width)),
        ],
        1,
    )
    message = lax.all_to_all(message, "pop", split_axis=0, concat_axis=0, tiled=True)

    parts = [value_weight] + [fetch(value_weight, "z", s) for s in (1, 2, 3)]
    left, right = join_rows(pop, parts)

    twin = swap(after(tokens, left), 2)

    lefts, rights = {0: left}, {0: right}
    for s in (1, 3):
        lefts[s] = fetch(left, "x", s)
        rights[s] = fetch(right, "y", s)
    for s in (2,):
        lefts[s] = fetch(left, "x", s)
        rights[s] = fetch(right, "y", s)
    left = stack_rows([lefts[s] for s in range(SIDE)])
    right = stack_rows([rights[s] for s in range(SIDE)])

    l1, l3 = fetch(left, "y", 1), fetch(left, "y", 3)
    r1, r3 = fetch(right, "x", 1), fetch(right, "x", 3)

    mate = swap(after(tokens, twin), 1)
    both = swap(twin, 1)
    all_tokens, projected = pl.pallas_call(
        token_kernel,
        out_shape=[
            jax.ShapeDtypeStruct((4, length, width), BF16),
            jax.ShapeDtypeStruct((length, 8), F32),
        ],
        in_specs=[SMEM] + [VMEM] * 5,
        out_specs=[VMEM] * 2,
        cost_estimate=pl.CostEstimate(flops=0, bytes_accessed=8 << 20, transcendentals=0),
        name="member_tokens",
    )(tp, tokens, mate, twin, both, noise_in.reshape(4, 1, width))

    heads = width // HEAD
    strip = pl.BlockSpec((length, LANES), lambda i: (0, i))
    square = pl.BlockSpec((2, length, length), lambda i: (i, 0, 0))
    recept = after(receptance, left, right)
    high, low = pl.pallas_call(
        score_kernel,
        out_shape=[jax.ShapeDtypeStruct((heads, length, length), BF16)] * 2,
        grid=(width // LANES,),
        in_specs=[SMEM, strip, strip, strip],
        out_specs=[square, square],
        cost_estimate=pl.CostEstimate(flops=0, bytes_accessed=24 << 20, transcendentals=0),
        name="decayed_scores",
    )(live_length, recept, keys, log_decay)

    update = lax.dot_general(
        message[:, :rows],
        message[:, LANES:],
        (((0,), (0,)), ((), ())),
        precision=HIGHEST,
        preferred_element_type=F32,
    )
    every = tuple(range(SIDE))
    total = product(pop, all_tokens, ((0, 0, every), (1, 0, every)), (left, right))

    middle = l1.shape[0] // 2
    l1, l3, r1, r3, high, low, update = lax.optimization_barrier(
        (l1, l3, r1, r3, high, low, update)
    )
    l2a, l2b = fetch(l1[:middle], "y", 1), fetch(l3[middle:], "y", 3)
    r2a, r2b = fetch(r1[:middle], "x", 1), fetch(r3[middle:], "x", 3)

    total = product(
        pop,
        all_tokens,
        ((0, 1, every), (0, 3, every), (1, 1, every), (1, 3, every)),
        (l1, l3, r1, r3),
        total,
    )
    plan = ((0, 2, (0, 1)), (0, 2, (2, 3)), (1, 2, (0, 1)), (1, 2, (2, 3)))
    pieces = (l2a, l2b, r2a, r2b)
    wkv_out = pl.pallas_call(
        functools.partial(readout_kernel, plan),
        out_shape=jax.ShapeDtypeStruct((length, width), BF16),
        in_specs=[SMEM] + [VMEM] * 6 + [ANY] * 4,
        out_specs=VMEM,
        scratch_shapes=[
            pltpu.VMEM((4,) + pieces[0].shape, BF16),
            pltpu.SemaphoreType.DMA((4,)),
        ],
        compiler_params=params(24),
        name="values_readout",
    )(pop, all_tokens, total, projected, noise_out, high, low, *pieces)
    return wkv_out.reshape(1, length, width), update


def solution(mesh):
    return jax.shard_map(
        body,
        mesh=mesh,
        in_specs=(
            P("pop", None, "tp"),
            P("pop", None, "tp"),
            P("pop", None, "tp"),
            P("pop", None, "tp"),
            P("pop", "tp"),
            P("pop", None),
            P("pop", "tp"),
            P("pop"),
            P("pop"),
        ),
        out_specs=(P("pop", None, "tp"), P("pop", "tp")),
        check_vma=False,
    )
```

time: 183 us -> 195 us (1.066)
  the two profiles are of different devices: /device:TPU:230 before, /device:TPU:32 now
where the time goes in v2:
time: 195 us; the launch traced here: 194 us
  Pallas kernels  104 us (53%)
  starting transfers between devices  43.6 us (22%)
  waiting for transfers between devices  29.2 us (15%)
  local copies, waits for them, and re-layouts  14.5 us (7%)
  between operations  2.31 us (1%)
    pallas_call x2, Pallas kernels, stack_rows(): pl.pallas_call(stack_kernel, out_shape=jax.ShapeDtypeStruct((len(parts) *...  65.8 us
    ppermute x17, starting transfers between devices, fetch(): return lax.ppermute(array, 'pop', pairs)  31.2 us
    pallas_call x1, Pallas kernels, join_rows(): pl.pallas_call(join_kernel, out_shape=[jax.ShapeDtypeStruct((SIDE * rows,...  17.1 us
    ppermute x17, waiting for transfers between devices, fetch(): return lax.ppermute(array, 'pop', pairs)  15.1 us
    ppermute x3, waiting for transfers between devices, swap(): return lax.ppermute(array, 'tp', [(i, i ^ bit) for i in range(4)])  14.2 us
    pallas_call x1, Pallas kernels, body(): pl.pallas_call(score_kernel, out_shape=[jax.ShapeDtypeStruct((heads, leng...  9.25 us
    ppermute x3, starting transfers between devices, swap(): return lax.ppermute(array, 'tp', [(i, i ^ bit) for i in range(4)])  6.41 us
    unnamed x43, local copies, waits for them, and re-layouts  6.09 us
  transfers between devices with their start and end apart: 21, of which 6 were waited for; matrix products, arithmetic and copies ran while one was open for 4% of the time, Pallas kernels for 42%

profile of v2, /device:TPU:32, one launch (start us, length us, event | category | flops | bytes accessed | tf_op | source)
XLA Modules:
  0.0 194.5 jit_solution(15460096438511980702)
XLA Ops:
  0.6 3.4 %collective-permute-start.1 = (bf16[64,1024]{1,0:T(8,128)(2,1)}, bf16[64,1024]{1,0:T(8,128)(2,1)S(1)}, u32[]{:S(2)}, u32[]{:S(2)}) collective-permute-start(bf16[64,1024]{1,0:T(8,128)(2,1)} %p0.1), channel_id=1, source_target_pairs={{8,0},{12,4},{0,8},{4,12},{24,16},{28,20},{16,24},{20,28},{40,32},... | collective-permute-start | bytes 393224 | tf_op jit(solution)/shard_map/ppermute | solution.py:33
  4.0 0.1 collective-permute-start
  4.1 1.9 collective-permute-start.2
  6.0 6.3 %collective-permute-done.1.p2 = bf16[64,1024]{1,0:T(8,128)(2,1)S(1)} collective-permute-done((bf16[64,1024]{1,0:T(8,128)(2,1)}, bf16[64,1024]{1,0:T(8,128)(2,1)S(1)}, u32[]{:S(2)}, u32[]{:S(2)}) %collective-permute-start.1) | collective-permute-done | bytes 131104 | tf_op jit(solution)/shard_map/ppermute | solution.py:33
  12.4 2.4 %collective-permute-done.p1 = bf16[64,1024]{1,0:T(8,128)(2,1)S(1)} collective-permute-done((bf16[64,1024]{1,0:T(8,128)(2,1)}, bf16[64,1024]{1,0:T(8,128)(2,1)S(1)}, u32[]{:S(2)}, u32[]{:S(2)}) %collective-permute-start) | collective-permute-done | bytes 131104 | tf_op jit(solution)/shard_map/ppermute | solution.py:33
  14.8 0.3 collective-permute-done.2.p3
  15.1 0.3 copy-done.18
  15.4 0.3 copy-done.19
  15.7 17.1 %join_rows.1 = (bf16[256,512]{1,0:T(8,128)(2,1)}, bf16[256,512]{1,0:T(8,128)(2,1)}) custom-call(s32[1]{0:T(128)} %bitcast.pop_ref, bf16[64,1024]{1,0:T(8,128)(2,1)} %p0.1, bf16[64,1024]{1,0:T(8,128)(2,1)} %copy-done.18, bf16[64,1024]{1,0:T(8,128)(2,1)} %copy-done.17, bf16[64,1024]{1,0:T(8,128)(2,1)} %copy-done.19), custom_call_target="tpu_custom_call" | custom-call | tf_op jit(solution)/shard_map/join_rows/pallas_call | solution.py:99
  32.8 1.6 collective-permute-start.8
  34.4 2.7 %collective-permute-start.7 = (bf16[256,512]{1,0:T(8,128)(2,1)}, bf16[256,512]{1,0:T(8,128)(2,1)S(1)}, u32[]{:S(2)}, u32[]{:S(2)}) collective-permute-start(bf16[256,512]{1,0:T(8,128)(2,1)} %get-tuple-element.18.refs_0_), channel_id=1, source_target_pairs={{32,0},{36,4},{40,8},{44,12},{48,16},{52,20},{56,24},{60,28},{0,32... | collective-permute-start | bytes 786440 | tf_op jit(solution)/shard_map/ppermute | solution.py:33
  37.1 1.4 collective-permute-start.6
  38.5 1.6 collective-permute-start.11
  40.1 2.9 %collective-permute-start.10 = (bf16[256,512]{1,0:T(8,128)(2,1)}, bf16[256,512]{1,0:T(8,128)(2,1)S(1)}, u32[]{:S(2)}, u32[]{:S(2)}) collective-permute-start(bf16[256,512]{1,0:T(8,128)(2,1)} %get-tuple-element.22.refs_0_), channel_id=1, source_target_pairs={{128,0},{132,4},{136,8},{140,12},{144,16},{148,20},{152,24},{156,2... | collective-permute-start | bytes 786440 | tf_op jit(solution)/shard_map/ppermute | solution.py:33
  43.0 0.0 collective-permute-done.8.refs_3_
  43.0 2.5 %collective-permute-start.9 = (bf16[256,512]{1,0:T(8,128)(2,1)}, bf16[256,512]{1,0:T(8,128)(2,1)S(1)}, u32[]{:S(2)}, u32[]{:S(2)}) collective-permute-start(bf16[256,512]{1,0:T(8,128)(2,1)} %get-tuple-element.22.refs_0_), channel_id=1, source_target_pairs={{64,0},{68,4},{72,8},{76,12},{80,16},{84,20},{88,24},{92,28},{96,3... | collective-permute-start | bytes 786440 | tf_op jit(solution)/shard_map/ppermute | solution.py:33
  45.5 3.6 %collective-permute-done.7.refs_2_ = bf16[256,512]{1,0:T(8,128)(2,1)S(1)} collective-permute-done((bf16[256,512]{1,0:T(8,128)(2,1)}, bf16[256,512]{1,0:T(8,128)(2,1)S(1)}, u32[]{:S(2)}, u32[]{:S(2)}) %collective-permute-start.7) | collective-permute-done | bytes 262176 | tf_op jit(solution)/shard_map/ppermute | solution.py:33
  49.1 0.7 copy-done.15
  49.8 0.7 copy-done.16
  50.5 32.9 %stack_rows.2.refs_0_ = bf16[1024,512]{1,0:T(8,128)(2,1)} custom-call(bf16[256,512]{1,0:T(8,128)(2,1)} %get-tuple-element.18.refs_0_, bf16[256,512]{1,0:T(8,128)(2,1)} %copy-done.16, bf16[256,512]{1,0:T(8,128)(2,1)} %copy-done.15, bf16[256,512]{1,0:T(8,128)(2,1)} %copy-done.13), custom_call_target="tpu_custom_call" | custom-call | tf_op jit(solution)/shard_map/stack_rows/pallas_call | solution.py:124
  83.4 1.7 collective-permute-start.13
  85.1 1.7 collective-permute-start.12
  86.7 0.0 collective-permute-done.11.refs_3_
  86.7 0.0 collective-permute-done.10.refs_2_
  86.8 0.7 copy-done.11
  87.5 0.1 copy-done.12
  87.6 0.7 copy-done.14
  88.3 32.9 %stack_rows.3.refs_1_ = bf16[1024,512]{1,0:T(8,128)(2,1)} custom-call(bf16[256,512]{1,0:T(8,128)(2,1)} %get-tuple-element.22.refs_0_, bf16[256,512]{1,0:T(8,128)(2,1)} %copy-done.14, bf16[256,512]{1,0:T(8,128)(2,1)} %copy-done.12, bf16[256,512]{1,0:T(8,128)(2,1)} %copy-done.11), custom_call_target="tpu_custom_call" | custom-call | tf_op jit(solution)/shard_map/stack_rows/pallas_call | solution.py:124
  121.2 0.7 collective-permute-start.15
  121.9 2.6 %collective-permute-start.14 = (bf16[1024,512]{1,0:T(8,128)(2,1)}, bf16[1024,512]{1,0:T(8,128)(2,1)}, u32[]{:S(2)}, u32[]{:S(2)}) collective-permute-start(bf16[1024,512]{1,0:T(8,128)(2,1)} %stack_rows.3.refs_1_), channel_id=1, source_target_pairs={{16,0},{20,4},{24,8},{28,12},{32,16},{36,20},{40,24},{44,28},{48,3... | collective-permute-start | bytes 3145736 | tf_op jit(solution)/shard_map/ppermute | solution.py:33
  124.5 5.8 %collective-permute-start.3 = (bf16[256,1024]{1,0:T(8,128)(2,1)}, bf16[256,1024]{1,0:T(8,128)(2,1)}, u32[]{:S(2)}, u32[]{:S(2)}) collective-permute-start(bf16[256,1024]{1,0:T(8,128)(2,1)} %bitcast.14), channel_id=1, source_target_pairs={{0,2},{1,3},{2,0},{3,1},{4,6},{5,7},{6,4},{7,5},{8,10},{9,11},{10,... | collective-permute-start | bytes 1572872 | tf_op jit(solution)/shard_map/ppermute | solution.py:37
  131.0 0.1 multiply_reduce_fusion
  131.1 0.1 reshape.43
  131.2 0.7 broadcast_in_dim.17
  131.9 1.0 concatenate.3
  132.9 0.9 all_to_all.8
  133.8 5.9 %all-to-all-start = ((f32[64,1,1152]{2,1,0:T(1,128)}), f32[64,1,1152]{2,1,0:T(1,128)S(1)}, u32[]{:S(2)}, u32[]{:S(2)}) async-start(f32[64,1,1152]{2,1,0:T(1,128)} %all_to_all.8), calls=%async_computation | async-start | bytes 589824 | tf_op jit(solution)/shard_map/all_to_all | solution.py:265
  139.8 14.2 %collective-permute-done.3.t2 = bf16[256,1024]{1,0:T(8,128)(2,1)} collective-permute-done((bf16[256,1024]{1,0:T(8,128)(2,1)}, bf16[256,1024]{1,0:T(8,128)(2,1)}, u32[]{:S(2)}, u32[]{:S(2)}) %collective-permute-start.3) | collective-permute-done | bytes 524320 | tf_op jit(solution)/shard_map/ppermute | solution.py:37
  153.9 0.0 collective-permute-start.4
  154.6 9.3 %decayed_scores.1 = (bf16[16,256,256]{2,1,0:T(8,128)(2,1)}, bf16[16,256,256]{2,1,0:T(8,128)(2,1)}) custom-call(s32[1]{0:T(128)S(6)} %copy.15.live_ref, bf16[256,1024]{1,0:T(8,128)(2,1)} %bitcast.18, bf16[256,1024]{1,0:T(8,128)(2,1)} %bitcast.19, bf16[256,1024]{1,0:T(8,128)(2,1)} %bitcast.20), custom_call_target="tpu_custom_call" | custom-call | bytes 25165824 | tf_op jit(solution)/shard_map/decayed_scores/pallas_call | solution.py:303
  163.9 0.0 collective-permute-done.13.refs_2_
  163.9 0.6 collective-permute-start.5
  164.5 1.1 fusion
  165.6 0.0 collective-permute-done.12.refs_1_
  165.6 0.0 collective-permute-done.15.refs_4_
  165.6 0.9 slice.20
  166.5 0.2 copy-done.3
  166.8 0.4 copy-done.5
  167.1 0.8 slice.21
  167.9 2.0 %slice.22 = bf16[512,512]{1,0:T(8,128)(2,1)} slice(bf16[1024,512]{1,0:T(8,128)(2,1)} %collective-permute-done.14.refs_3_), slice={[0:512], [0:512]} | slice | bytes 1048576 | tf_op jit(solution)/shard_map/slice | solution.py:328
  170.0 1.9 slice.23
  171.8 3.2 %collective-permute-start.18 = (bf16[512,512]{1,0:T(8,128)(2,1)}, bf16[512,512]{1,0:T(8,128)(2,1)}, u32[]{:S(2)}, u32[]{:S(2)}) collective-permute-start(bf16[512,512]{1,0:T(8,128)(2,1)} %slice.22), channel_id=1, source_target_pairs={{16,0},{20,4},{24,8},{28,12},{32,16},{36,20},{40,24},{44,28},{48,3... | collective-permute-start | bytes 1572872 | tf_op jit(solution)/shard_map/ppermute | solution.py:33
  175.1 0.0 collective-permute-start.17
  175.1 0.0 collective-permute-done.4.t1
  175.1 3.2 %collective-permute-start.16 = (bf16[512,512]{1,0:T(8,128)(2,1)}, bf16[512,512]{1,0:T(8,128)(2,1)}, u32[]{:S(2)}, u32[]{:S(2)}) collective-permute-start(bf16[512,512]{1,0:T(8,128)(2,1)} %slice.20), channel_id=1, source_target_pairs={{64,0},{68,4},{72,8},{76,12},{80,16},{84,20},{88,24},{92,28},{96,3... | collective-permute-start | bytes 1572872 | tf_op jit(solution)/shard_map/ppermute | solution.py:33
  178.3 3.5 %member_tokens.1 = (bf16[4,256,1024]{2,1,0:T(8,128)(2,1)}, f32[256,8]{1,0:T(8,128)}) custom-call(s32[1]{0:T(128)} %bitcast.1.at_ref, bf16[256,1024]{1,0:T(8,128)(2,1)} %bitcast.16, bf16[256,1024]{1,0:T(8,128)(2,1)} %collective-permute-done.4.t1, bf16[256,1024]{1,0:T(8,128)(2,1)} %collective-permute-done.3.t2, bf16[256,1024]{1,0:T(8,128)(2,1)} %collective-permute-done.5.t3, ...), custom_call_target="tpu_custom_call" | custom-call | bytes 8388608 | tf_op jit(solution)/shard_map/member_tokens/pallas_call | solution.py:287
  181.9 1.6 copy-done
  183.5 1.2 products.2.refs_0_
  184.7 0.3 copy-done.6
  185.0 2.4 %products.3.refs_1_ = f32[256,1024]{1,0:T(8,128)S(1)} custom-call(s32[1]{0:T(128)} %bitcast.pop_ref, bf16[4,256,1024]{2,1,0:T(8,128)(2,1)S(1)} %copy-done, f32[256,1024]{1,0:T(8,128)S(1)} %products.2.refs_0_, bf16[1024,512]{1,0:T(8,128)(2,1)S(1)} %copy-done.4, bf16[1024,512]{1,0:T(8,128)(2,1)S(1)} %collective-permute-done.13.refs_2_, ...), custom_call_target="tpu_custom_call" | custom-call | flops 1073741824 | bytes 6291456 | tf_op jit(solution)/shard_map/products/pallas_call | solution.py:185
  187.4 0.0 collective-permute-done.19.refs_9_
  187.5 2.4 %collective-permute-done.17.refs_7_ = bf16[512,512]{1,0:T(8,128)(2,1)} collective-permute-done((bf16[512,512]{1,0:T(8,128)(2,1)}, bf16[512,512]{1,0:T(8,128)(2,1)}, u32[]{:S(2)}, u32[]{:S(2)}) %collective-permute-start.17) | collective-permute-done | bytes 524320 | tf_op jit(solution)/shard_map/ppermute | solution.py:33
  189.9 0.0 collective-permute-done.16.refs_6_
  189.9 4.4 %values_readout.1 = bf16[256,1024]{1,0:T(8,128)(2,1)} custom-call(s32[1]{0:T(128)} %bitcast.pop_ref, bf16[4,256,1024]{2,1,0:T(8,128)(2,1)S(1)} %copy-done, f32[256,1024]{1,0:T(8,128)S(1)} %products.3.refs_1_, f32[256,8]{1,0:T(8,128)S(1)} %copy-done.9, bf16[1,1024]{1,0:T(2,128)(2,1)S(1)} %copy-done.10, bf16[16,256,256]{2,1,0:T(8,128)(2,1)S(1)} %copy-done.7, ...), custom_call_target="tpu_custom_call" | custom-call | tf_op jit(solution)/shard_map/values_readout/pallas_call | solution.py:339
  (41 shorter events, 0.1 us)
Async XLA Ops:
  0.6 11.7 %collective-permute-start.1 = (bf16[64,1024]{1,0:T(8,128)(2,1)}, bf16[64,1024]{1,0:T(8,128)(2,1)S(1)}, u32[]{:S(2)}, u32[]{:S(2)}) collective-permute-start(bf16[64,1024]{1,0:T(8,128)(2,1)} %p0.1), channel_id=1, source_target_pairs={{8,0},{12,4},{0,8},{4,12},{24,16},{28,20},{16,24},{20,28},{40,32},... | collective-permute-start | bytes 393224 | tf_op jit(solution)/shard_map/ppermute | solution.py:33
  4.0 10.8 %collective-permute-start = (bf16[64,1024]{1,0:T(8,128)(2,1)}, bf16[64,1024]{1,0:T(8,128)(2,1)S(1)}, u32[]{:S(2)}, u32[]{:S(2)}) collective-permute-start(bf16[64,1024]{1,0:T(8,128)(2,1)} %p0.1), channel_id=1, source_target_pairs={{4,0},{8,4},{12,8},{0,12},{20,16},{24,20},{28,24},{16,28},{36,32},... | collective-permute-start | bytes 393224 | tf_op jit(solution)/shard_map/ppermute | solution.py:33
  4.1 11.0 %collective-permute-start.2 = (bf16[64,1024]{1,0:T(8,128)(2,1)}, bf16[64,1024]{1,0:T(8,128)(2,1)S(1)}, u32[]{:S(2)}, u32[]{:S(2)}) collective-permute-start(bf16[64,1024]{1,0:T(8,128)(2,1)} %p0.1), channel_id=1, source_target_pairs={{12,0},{0,4},{4,8},{8,12},{28,16},{16,20},{20,24},{24,28},{44,32},... | collective-permute-start | bytes 393224 | tf_op jit(solution)/shard_map/ppermute | solution.py:33
  12.4 2.7 %copy-start.17 = (bf16[64,1024]{1,0:T(8,128)(2,1)}, bf16[64,1024]{1,0:T(8,128)(2,1)S(1)}, u32[]{:S(2)}) copy-start(bf16[64,1024]{1,0:T(8,128)(2,1)S(1)} %collective-permute-done.1.p2) | copy-start | bytes 393220
  14.8 0.6 copy-start.18
  15.1 0.7 copy-start.19
  32.8 10.2 %collective-permute-start.8 = (bf16[256,512]{1,0:T(8,128)(2,1)}, bf16[256,512]{1,0:T(8,128)(2,1)S(1)}, u32[]{:S(2)}, u32[]{:S(2)}) collective-permute-start(bf16[256,512]{1,0:T(8,128)(2,1)} %get-tuple-element.18.refs_0_), channel_id=1, source_target_pairs={{48,0},{52,4},{56,8},{60,12},{0,16},{4,20},{8,24},{12,28},{16,32},... | collective-permute-start | bytes 786440 | tf_op jit(solution)/shard_map/ppermute | solution.py:33
  34.4 14.8 %collective-permute-start.7 = (bf16[256,512]{1,0:T(8,128)(2,1)}, bf16[256,512]{1,0:T(8,128)(2,1)S(1)}, u32[]{:S(2)}, u32[]{:S(2)}) collective-permute-start(bf16[256,512]{1,0:T(8,128)(2,1)} %get-tuple-element.18.refs_0_), channel_id=1, source_target_pairs={{32,0},{36,4},{40,8},{44,12},{48,16},{52,20},{56,24},{60,28},{0,32... | collective-permute-start | bytes 786440 | tf_op jit(solution)/shard_map/ppermute | solution.py:33
  37.1 12.0 %collective-permute-start.6 = (bf16[256,512]{1,0:T(8,128)(2,1)}, bf16[256,512]{1,0:T(8,128)(2,1)S(1)}, u32[]{:S(2)}, u32[]{:S(2)}) collective-permute-start(bf16[256,512]{1,0:T(8,128)(2,1)} %get-tuple-element.18.refs_0_), channel_id=1, source_target_pairs={{16,0},{20,4},{24,8},{28,12},{32,16},{36,20},{40,24},{44,28},{48,3... | collective-permute-start | bytes 786440 | tf_op jit(solution)/shard_map/ppermute | solution.py:33
  38.5 92.5 %copy-start.10 = (bf16[1,1024]{1,0:T(2,128)(2,1)S(1)}, bf16[1,1024]{1,0:T(2,128)(2,1)}, u32[]{:S(2)}) copy-start(bf16[1,1024]{1,0:T(2,128)(2,1)} %refs_3_.1) | copy-start | bytes 6148
  38.5 92.5 %copy-start.20 = (bf16[1,4096]{1,0:T(2,128)(2,1)S(1)}, bf16[1,4096]{1,0:T(2,128)(2,1)}, u32[]{:S(2)}) copy-start(bf16[1,4096]{1,0:T(2,128)(2,1)} %param.14) | copy-start | bytes 24580
  38.5 48.2 %collective-permute-start.11 = (bf16[256,512]{1,0:T(8,128)(2,1)}, bf16[256,512]{1,0:T(8,128)(2,1)S(1)}, u32[]{:S(2)}, u32[]{:S(2)}) collective-permute-start(bf16[256,512]{1,0:T(8,128)(2,1)} %get-tuple-element.22.refs_0_), channel_id=1, source_target_pairs={{192,0},{196,4},{200,8},{204,12},{208,16},{212,20},{216,24},{220,2... | collective-permute-start | bytes 786440 | tf_op jit(solution)/shard_map/ppermute | solution.py:33
  40.1 46.6 %collective-permute-start.10 = (bf16[256,512]{1,0:T(8,128)(2,1)}, bf16[256,512]{1,0:T(8,128)(2,1)S(1)}, u32[]{:S(2)}, u32[]{:S(2)}) collective-permute-start(bf16[256,512]{1,0:T(8,128)(2,1)} %get-tuple-element.22.refs_0_), channel_id=1, source_target_pairs={{128,0},{132,4},{136,8},{140,12},{144,16},{148,20},{152,24},{156,2... | collective-permute-start | bytes 786440 | tf_op jit(solution)/shard_map/ppermute | solution.py:33
  43.0 6.1 %copy-start.13 = (bf16[256,512]{1,0:T(8,128)(2,1)}, bf16[256,512]{1,0:T(8,128)(2,1)S(1)}, u32[]{:S(2)}) copy-start(bf16[256,512]{1,0:T(8,128)(2,1)S(1)} %collective-permute-done.8.refs_3_) | copy-start | bytes 786436
  43.0 43.8 %collective-permute-start.9 = (bf16[256,512]{1,0:T(8,128)(2,1)}, bf16[256,512]{1,0:T(8,128)(2,1)S(1)}, u32[]{:S(2)}, u32[]{:S(2)}) collective-permute-start(bf16[256,512]{1,0:T(8,128)(2,1)} %get-tuple-element.22.refs_0_), channel_id=1, source_target_pairs={{64,0},{68,4},{72,8},{76,12},{80,16},{84,20},{88,24},{92,28},{96,3... | collective-permute-start | bytes 786440 | tf_op jit(solution)/shard_map/ppermute | solution.py:33
  49.1 0.7 copy-start.15
  49.8 0.7 copy-start.16
  83.4 80.5 %collective-permute-start.13 = (bf16[1024,512]{1,0:T(8,128)(2,1)}, bf16[1024,512]{1,0:T(8,128)(2,1)S(1)}, u32[]{:S(2)}, u32[]{:S(2)}) collective-permute-start(bf16[1024,512]{1,0:T(8,128)(2,1)} %stack_rows.2.refs_0_), channel_id=1, source_target_pairs={{192,0},{196,4},{200,8},{204,12},{208,16},{212,20},{216,24},{220,2... | collective-permute-start | bytes 3145736 | tf_op jit(solution)/shard_map/ppermute | solution.py:33
  85.1 80.5 %collective-permute-start.12 = (bf16[1024,512]{1,0:T(8,128)(2,1)}, bf16[1024,512]{1,0:T(8,128)(2,1)S(1)}, u32[]{:S(2)}, u32[]{:S(2)}) collective-permute-start(bf16[1024,512]{1,0:T(8,128)(2,1)} %stack_rows.2.refs_0_), channel_id=1, source_target_pairs={{64,0},{68,4},{72,8},{76,12},{80,16},{84,20},{88,24},{92,28},{96,3... | collective-permute-start | bytes 3145736 | tf_op jit(solution)/shard_map/ppermute | solution.py:33
  86.7 0.7 copy-start.11
  86.8 0.8 copy-start.12
  87.6 0.7 copy-start.14
  121.2 44.4 %collective-permute-start.15 = (bf16[1024,512]{1,0:T(8,128)(2,1)}, bf16[1024,512]{1,0:T(8,128)(2,1)S(1)}, u32[]{:S(2)}, u32[]{:S(2)}) collective-permute-start(bf16[1024,512]{1,0:T(8,128)(2,1)} %stack_rows.3.refs_1_), channel_id=1, source_target_pairs={{48,0},{52,4},{56,8},{60,12},{0,16},{4,20},{8,24},{12,28},{16,32},... | collective-permute-start | bytes 3145736 | tf_op jit(solution)/shard_map/ppermute | solution.py:33
  121.9 43.7 %collective-permute-start.14 = (bf16[1024,512]{1,0:T(8,128)(2,1)}, bf16[1024,512]{1,0:T(8,128)(2,1)}, u32[]{:S(2)}, u32[]{:S(2)}) collective-permute-start(bf16[1024,512]{1,0:T(8,128)(2,1)} %stack_rows.3.refs_1_), channel_id=1, source_target_pairs={{16,0},{20,4},{24,8},{28,12},{32,16},{36,20},{40,24},{44,28},{48,3... | collective-permute-start | bytes 3145736 | tf_op jit(solution)/shard_map/ppermute | solution.py:33
  124.5 29.4 %collective-permute-start.3 = (bf16[256,1024]{1,0:T(8,128)(2,1)}, bf16[256,1024]{1,0:T(8,128)(2,1)}, u32[]{:S(2)}, u32[]{:S(2)}) collective-permute-start(bf16[256,1024]{1,0:T(8,128)(2,1)} %bitcast.14), channel_id=1, source_target_pairs={{0,2},{1,3},{2,0},{3,1},{4,6},{5,7},{6,4},{7,5},{8,10},{9,11},{10,... | collective-permute-start | bytes 1572872 | tf_op jit(solution)/shard_map/ppermute | solution.py:37
  133.8 30.0 %all-to-all-start = ((f32[64,1,1152]{2,1,0:T(1,128)}), f32[64,1,1152]{2,1,0:T(1,128)S(1)}, u32[]{:S(2)}, u32[]{:S(2)}) async-start(f32[64,1,1152]{2,1,0:T(1,128)} %all_to_all.8), calls=%async_computation | async-start | bytes 589824 | tf_op jit(solution)/shard_map/all_to_all | solution.py:265
  153.9 21.1 %collective-permute-start.4 = (bf16[256,1024]{1,0:T(8,128)(2,1)}, bf16[256,1024]{1,0:T(8,128)(2,1)}, u32[]{:S(2)}, u32[]{:S(2)}) collective-permute-start(bf16[256,1024]{1,0:T(8,128)(2,1)} %bitcast.15), channel_id=1, source_target_pairs={{0,1},{1,0},{2,3},{3,2},{4,5},{5,4},{6,7},{7,6},{8,9},{9,8},{10,11... | collective-permute-start | bytes 1572872 | tf_op jit(solution)/shard_map/ppermute | solution.py:37
  163.9 14.4 %collective-permute-start.5 = (bf16[256,1024]{1,0:T(8,128)(2,1)}, bf16[256,1024]{1,0:T(8,128)(2,1)}, u32[]{:S(2)}, u32[]{:S(2)}) collective-permute-start(bf16[256,1024]{1,0:T(8,128)(2,1)} %collective-permute-done.3.t2), channel_id=1, source_target_pairs={{0,1},{1,0},{2,3},{3,2},{4,5},{5,4},{6,7},{7,6},{8,9},{9,8},{10,11... | collective-permute-start | bytes 1572872 | tf_op jit(solution)/shard_map/ppermute | solution.py:37
  165.6 1.2 copy-start.3
  165.6 1.5 copy-start.5
  167.9 13.9 %copy-start.1 = (bf16[1024,512]{1,0:T(8,128)(2,1)S(1)}, bf16[1024,512]{1,0:T(8,128)(2,1)}, u32[]{:S(2)}) copy-start(bf16[1024,512]{1,0:T(8,128)(2,1)} %stack_rows.2.refs_0_) | copy-start | bytes 3145732
  167.9 13.9 %copy-start.2 = (bf16[1024,512]{1,0:T(8,128)(2,1)S(1)}, bf16[1024,512]{1,0:T(8,128)(2,1)}, u32[]{:S(2)}) copy-start(bf16[1024,512]{1,0:T(8,128)(2,1)} %stack_rows.3.refs_1_) | copy-start | bytes 3145732
  171.8 15.6 %collective-permute-start.19 = (bf16[512,512]{1,0:T(8,128)(2,1)}, bf16[512,512]{1,0:T(8,128)(2,1)}, u32[]{:S(2)}, u32[]{:S(2)}) collective-permute-start(bf16[512,512]{1,0:T(8,128)(2,1)} %slice.23), channel_id=1, source_target_pairs={{48,0},{52,4},{56,8},{60,12},{0,16},{4,20},{8,24},{12,28},{16,32},... | collective-permute-start | bytes 1572872 | tf_op jit(solution)/shard_map/ppermute | solution.py:33
  171.8 15.6 %collective-permute-start.18 = (bf16[512,512]{1,0:T(8,128)(2,1)}, bf16[512,512]{1,0:T(8,128)(2,1)}, u32[]{:S(2)}, u32[]{:S(2)}) collective-permute-start(bf16[512,512]{1,0:T(8,128)(2,1)} %slice.22), channel_id=1, source_target_pairs={{16,0},{20,4},{24,8},{28,12},{32,16},{36,20},{40,24},{44,28},{48,3... | collective-permute-start | bytes 1572872 | tf_op jit(solution)/shard_map/ppermute | solution.py:33
  175.1 14.8 %collective-permute-start.17 = (bf16[512,512]{1,0:T(8,128)(2,1)}, bf16[512,512]{1,0:T(8,128)(2,1)}, u32[]{:S(2)}, u32[]{:S(2)}) collective-permute-start(bf16[512,512]{1,0:T(8,128)(2,1)} %slice.21), channel_id=1, source_target_pairs={{192,0},{196,4},{200,8},{204,12},{208,16},{212,20},{216,24},{220,2... | collective-permute-start | bytes 1572872 | tf_op jit(solution)/shard_map/ppermute | solution.py:33
  175.1 14.8 %collective-permute-start.16 = (bf16[512,512]{1,0:T(8,128)(2,1)}, bf16[512,512]{1,0:T(8,128)(2,1)}, u32[]{:S(2)}, u32[]{:S(2)}) collective-permute-start(bf16[512,512]{1,0:T(8,128)(2,1)} %slice.20), channel_id=1, source_target_pairs={{64,0},{68,4},{72,8},{76,12},{80,16},{84,20},{88,24},{92,28},{96,3... | collective-permute-start | bytes 1572872 | tf_op jit(solution)/shard_map/ppermute | solution.py:33
  181.9 1.6 copy-start
  183.4 1.2 copy-start.4
  183.5 1.5 copy-start.6
  185.0 4.9 %copy-start.7 = (bf16[16,256,256]{2,1,0:T(8,128)(2,1)S(1)}, bf16[16,256,256]{2,1,0:T(8,128)(2,1)}, u32[]{:S(2)}) copy-start(bf16[16,256,256]{2,1,0:T(8,128)(2,1)} %get-tuple-element.31.refs_4_) | copy-start | bytes 6291460
  185.0 4.9 %copy-start.8 = (bf16[16,256,256]{2,1,0:T(8,128)(2,1)S(1)}, bf16[16,256,256]{2,1,0:T(8,128)(2,1)}, u32[]{:S(2)}) copy-start(bf16[16,256,256]{2,1,0:T(8,128)(2,1)} %get-tuple-element.32.refs_5_) | copy-start | bytes 6291460
  185.0 4.9 %copy-start.9 = (f32[256,8]{1,0:T(8,128)S(1)}, f32[256,8]{1,0:T(8,128)}, u32[]{:S(2)}) copy-start(f32[256,8]{1,0:T(8,128)} %get-tuple-element.30.refs_2_) | copy-start | bytes 24580

commit v3 on v1

v3 whole, which is shorter than its diff:
```python
import functools
import math

import jax
import jax.numpy as jnp
from jax import lax
from jax.experimental import pallas as pl
from jax.experimental.pallas import tpu as pltpu
from jax.sharding import Mesh, PartitionSpec as P

HEAD = 64
SIGMA = 0.5
HIGHEST = lax.Precision.HIGHEST
F32 = jnp.float32
BF16 = jnp.bfloat16

SIDE = 4
SPAN = 64
LANES = 128
POP = ("y", "x", "z")
TP = ("twin", "core")

LINKS = {"a": ("x", 1), "b": ("x", 3), "c": ("y", 1), "d": ("y", 3)}
ROUTES = ("acbd", "cadb", "bdac", "dbca")

VMEM = pl.BlockSpec(memory_space=pltpu.VMEM)
SMEM = pl.BlockSpec(memory_space=pltpu.SMEM)


def swap(array, axis, mask):
    size = lax.axis_size(axis)
    return lax.ppermute(array, axis, [(i, i ^ mask) for i in range(size)])


def fetch(array, axis, step):
    size = lax.axis_size(axis)
    return lax.ppermute(array, axis, [((i + step) % size, i) for i in range(size)])


def masks(route, last):
    steps = [LINKS[s] for s in route]
    found = []
    for i in range(2 ** (len(steps) - 1)):
        y = x = 0
        for k, (axis, mask) in enumerate(steps):
            if (i >> k) & 1 or (last and k == len(steps) - 1):
                y, x = (y ^ mask, x) if axis == "y" else (y, x ^ mask)
        found.append((y, x))
    return found


def token_kernel(at_ref, t0, t1, t2, t3, noise_ref, tokens_ref, projected_ref):
    total = None
    for bits, part in enumerate((t0, t1, t2, t3)):
        place = jnp.bitwise_xor(at_ref[0], bits)
        block = part[...]
        tokens_ref[place] = block
        noise = jnp.broadcast_to(noise_ref[place], (8, block.shape[1]))
        term = lax.dot_general(
            block, noise, (((1,), (1,)), ((), ())), preferred_element_type=F32
        )
        total = term if total is None else total + term
    projected_ref[...] = total


def score_kernel(live_ref, recept_ref, keys_ref, decay_ref, high_ref, low_ref):
    length = recept_ref.shape[0]
    live = live_ref[0]
    row = lax.broadcasted_iota(jnp.int32, (length, LANES), 0)
    alive = row < live
    decay = jnp.where(alive, decay_ref[...], jnp.zeros((), BF16))
    keys = jnp.where(alive, keys_ref[...].astype(F32), 0.0)
    lower = (
        lax.broadcasted_iota(jnp.int32, (length, length), 0)
        >= lax.broadcasted_iota(jnp.int32, (length, length), 1)
    ).astype(F32).astype(BF16)
    summed = jnp.dot(lower, decay, preferred_element_type=F32)
    lane = lax.broadcasted_iota(jnp.int32, (SPAN, LANES), 1)
    for chunk in range(length // SPAN):
        first, last = chunk * SPAN, (chunk + 1) * SPAN
        base = summed[first - 1 : first] if chunk else jnp.zeros((1, LANES), F32)
        grown = recept_ref[first:last].astype(F32) * jnp.exp(summed[first:last] - base)
        shrunk = keys[:last] * jnp.exp(base - summed[:last])
        both = jnp.concatenate(
            [jnp.where(lane < HEAD, grown, 0.0), jnp.where(lane < HEAD, 0.0, grown)], 0
        )
        scores = lax.dot_general(
            both, shrunk, (((1,), (1,)), ((), ())), precision=HIGHEST, preferred_element_type=F32
        )
        for head in range(2):
            mine = scores[head * SPAN : (head + 1) * SPAN]
            here = lax.broadcasted_iota(jnp.int32, (SPAN, last), 0) + first
            there = lax.broadcasted_iota(jnp.int32, (SPAN, last), 1)
            mine = jnp.where((here >= there) & (here < live), mine, 0.0)
            high = mine.astype(BF16)
            low = (mine - high.astype(F32)).astype(BF16)
            high_ref[head, first:last, :last] = high
            low_ref[head, first:last, :last] = low
            if last < length:
                rest = jnp.zeros((SPAN, length - last), BF16)
                high_ref[head, first:last, last:] = rest
                low_ref[head, first:last, last:] = rest


def chunk_product(at_ref, tokens_ref, piece_ref, blocks):
    depth = piece_ref.shape[0] // len(blocks)
    group = 4
    total = None
    for first in range(0, len(blocks), group):
        columns = []
        for y, x in blocks[first : first + group]:
            place = pl.multiple_of(jnp.bitwise_xor(at_ref[1], x) * depth, depth)
            columns.append(tokens_ref[jnp.bitwise_xor(at_ref[0], y), :, pl.ds(place, depth)])
        term = jnp.dot(
            jnp.concatenate(columns, 1),
            piece_ref[first * depth : (first + group) * depth],
            preferred_element_type=F32,
        )
        total = term if total is None else total + term
    return total


def held_kernel(at_ref, tokens_ref, *refs):
    pieces, out_ref = refs[:-1], refs[-1]
    wide = pieces[0].shape[1]
    for c, piece in enumerate(pieces):
        out_ref[:, c * wide : (c + 1) * wide] = chunk_product(
            at_ref, tokens_ref, piece, masks(ROUTES[c], False)
        )


def readout_kernel(at_ref, tokens_ref, sum_ref, projected_ref, noise_ref, high_ref, low_ref, *refs):
    pieces, out_ref = refs[:-1], refs[-1]
    wide = pieces[0].shape[1]
    projected = projected_ref[...][:, :1] * (
        SIGMA / math.sqrt(tokens_ref.shape[0] * tokens_ref.shape[2])
    )
    lane = lax.broadcasted_iota(jnp.int32, (out_ref.shape[0], LANES), 1)
    for c, piece in enumerate(pieces):
        where = slice(c * wide, (c + 1) * wide)
        total = sum_ref[:, where] + projected * noise_ref[:, where].astype(F32)
        total = total + chunk_product(at_ref, tokens_ref, piece, masks(ROUTES[c], True))
        values = total.astype(BF16)
        for pair in range(wide // LANES):
            mine = values[:, pair * LANES : (pair + 1) * LANES]
            head = c * (wide // HEAD) + 2 * pair
            outs = [
                jnp.dot(high_ref[head + i], mine, preferred_element_type=F32)
                + jnp.dot(low_ref[head + i], mine, preferred_element_type=F32)
                for i in range(2)
            ]
            start = c * wide + pair * LANES
            out_ref[:, start : start + LANES] = jnp.where(lane < HEAD, *outs).astype(BF16)


def params(mib):
    return pltpu.CompilerParams(vmem_limit_bytes=mib << 20)


def cost(flops, moved):
    return pl.CostEstimate(flops=flops, bytes_accessed=moved, transcendentals=0)


def after(value, *others):
    return lax.optimization_barrier((value, others))[0]


def body(
    tokens, receptance, keys, log_decay, value_weight, noise_in, noise_out, utilities, live_length
):
    _, length, width = receptance.shape
    tokens, receptance, keys, log_decay = (
        a.reshape(length, width) for a in (tokens, receptance, keys, log_decay)
    )
    rows = value_weight.shape[0]
    wide = width // len(ROUTES)

    z = lax.axis_index("z")
    near = jnp.zeros((SIDE * rows, width), BF16)
    for step in (0, 1, 3, 2):
        part = fetch(value_weight, "z", step) if step else value_weight
        near = lax.dynamic_update_slice(near, part, (lax.rem(z + step, SIDE) * rows, 0))

    population = lax.axis_size(POP)
    weighted = noise_in.astype(F32) * (utilities / math.sqrt(population))[:, None]
    message = jnp.concatenate(
        [
            weighted.reshape(population, rows),
            jnp.zeros((population, LANES - rows), F32),
            jnp.broadcast_to(noise_out.astype(F32), (population, width)),
        ],
        1,
    )
    message = lax.all_to_all(message, POP, split_axis=0, concat_axis=0, tiled=True)

    twin = swap(after(tokens, near), "twin", 1)

    held = [near[:, c * wide : (c + 1) * wide] for c in range(len(ROUTES))]
    for step in range(3):
        if step == 2:
            held, message = lax.optimization_barrier((held, message))
        came = [swap(held[c], *LINKS[ROUTES[c][step]]) for c in range(len(ROUTES))]
        held = [jnp.concatenate([a, b], 0) for a, b in zip(held, came)]
    came = [swap(held[c], *LINKS[ROUTES[c][3]]) for c in range(len(ROUTES))]

    mate = swap(after(tokens, twin), "core", 1)
    both = swap(twin, "core", 1)
    tp = lax.axis_index(TP).reshape(1)
    all_tokens, projected = pl.pallas_call(
        token_kernel,
        out_shape=[
            jax.ShapeDtypeStruct((4, length, width), BF16),
            jax.ShapeDtypeStruct((length, 8), F32),
        ],
        in_specs=[SMEM] + [VMEM] * 5,
        out_specs=[VMEM] * 2,
        cost_estimate=cost(0, 8 << 20),
        compiler_params=params(16),
        name="member_tokens",
    )(tp, tokens, mate, twin, both, noise_in.reshape(4, 1, width))

    heads = width // HEAD
    strip = pl.BlockSpec((length, LANES), lambda i: (0, i))
    square = pl.BlockSpec((2, length, length), lambda i: (i, 0, 0))
    high, low = pl.pallas_call(
        score_kernel,
        out_shape=[jax.ShapeDtypeStruct((heads, length, length), BF16)] * 2,
        grid=(width // LANES,),
        in_specs=[SMEM, strip, strip, strip],
        out_specs=[square, square],
        cost_estimate=cost(0, 24 << 20),
        compiler_params=params(16),
        name="decayed_scores",
    )(live_length, after(receptance, *held), keys, log_decay)

    update = lax.dot_general(
        message[:, :rows],
        message[:, LANES:],
        (((0,), (0,)), ((), ())),
        precision=HIGHEST,
        preferred_element_type=F32,
    )

    at = jnp.stack([lax.axis_index("y"), lax.axis_index("x")])
    flops = length * width * 2 * 2048
    total = pl.pallas_call(
        held_kernel,
        out_shape=jax.ShapeDtypeStruct((length, width), F32),
        in_specs=[SMEM] + [VMEM] * 5,
        out_specs=VMEM,
        cost_estimate=cost(flops, 8 << 20),
        compiler_params=params(16),
        name="held_products",
    )(at, all_tokens, *held)
    wkv_out = pl.pallas_call(
        readout_kernel,
        out_shape=jax.ShapeDtypeStruct((length, width), BF16),
        in_specs=[SMEM] + [VMEM] * 10,
        out_specs=VMEM,
        cost_estimate=cost(flops, 12 << 20),
        compiler_params=params(20),
        name="values_readout",
    )(at, all_tokens, total, projected, noise_out, high, low, *came)
    return wkv_out.reshape(1, length, width), update


def solution(mesh):
    mesh = Mesh(mesh.devices.reshape(SIDE, SIDE, SIDE, 2, 2), POP + TP)
    return jax.shard_map(
        body,
        mesh=mesh,
        in_specs=(
            P(POP, None, TP),
            P(POP, None, TP),
            P(POP, None, TP),
            P(POP, None, TP),
            P(POP, TP),
            P(POP, None),
            P(POP, TP),
            P(POP),
            P(POP),
        ),
        out_specs=(P(POP, None, TP), P(POP, TP)),
        check_vma=False,
    )
```

time: 183 us -> 111 us (0.61)
  the two profiles are of different devices: /device:TPU:230 before, /device:TPU:128 now
where the time goes in v3:
time: 111 us; the launch traced here: 110 us
  waiting for transfers between devices  40.2 us (36%)
  starting transfers between devices  32.5 us (29%)
  Pallas kernels  18.4 us (17%)
  local copies, waits for them, and re-layouts  12.2 us (11%)
  other arithmetic  3.55 us (3%)
  between operations  2.16 us (2%)
  matrix products  1.12 us (1%)
    ppermute x19, starting transfers between devices, swap(): return lax.ppermute(array, axis, [(i, i ^ mask) for i in range(size)])  24.1 us
    all_to_all x1, waiting for transfers between devices, body(): lax.all_to_all(message, POP, split_axis=0, concat_axis=0, tiled=True)  18.7 us
    ppermute x19, waiting for transfers between devices, swap(): return lax.ppermute(array, axis, [(i, i ^ mask) for i in range(size)])  11.7 us
    ppermute x3, waiting for transfers between devices, fetch(): lax.ppermute(array, axis, [((i + step) % size, i) for i in range(size)])  9.79 us
    unnamed x19, local copies, waits for them, and re-layouts  9.11 us
    pallas_call x1, Pallas kernels, body(): pl.pallas_call(score_kernel, out_shape=[jax.ShapeDtypeStruct((heads, leng...  7.07 us
    pallas_call x1, Pallas kernels, body(): pl.pallas_call(readout_kernel, out_shape=jax.ShapeDtypeStruct((length, wi...  6.68 us
    all_to_all x1, starting transfers between devices, body(): lax.all_to_all(message, POP, split_axis=0, concat_axis=0, tiled=True)  4.82 us
  transfers between devices with their start and end apart: 23, of which 13 were waited for; matrix products, arithmetic and copies ran while one was open for 11% of the time, Pallas kernels for 11%

profile of v3, /device:TPU:128, one launch (start us, length us, event | category | flops | bytes accessed | tf_op | source)
XLA Modules:
  0.0 110.1 jit_solution(14237971626735561498)
XLA Ops:
  0.6 2.0 %collective-permute-start = (bf16[64,1024]{1,0:T(8,128)(2,1)}, bf16[64,1024]{1,0:T(8,128)(2,1)S(1)}, u32[]{:S(2)}, u32[]{:S(2)}) collective-permute-start(bf16[64,1024]{1,0:T(8,128)(2,1)} %param.13), channel_id=1, source_target_pairs={{4,0},{8,4},{12,8},{0,12},{5,1},{9,5},{13,9},{1,13},{6,2},{10,6},{... | collective-permute-start | bytes 393224 | tf_op jit(solution)/shard_map/ppermute | solution.py:37
  2.7 0.6 collective-permute-start.2
  3.2 1.0 collective-permute-start.1
  4.2 0.1 broadcast_in_dim.17
  4.3 0.9 constant_dynamic-update-slice_fusion.11
  5.2 1.6 %collective-permute-done = bf16[64,1024]{1,0:T(8,128)(2,1)S(1)} collective-permute-done((bf16[64,1024]{1,0:T(8,128)(2,1)}, bf16[64,1024]{1,0:T(8,128)(2,1)S(1)}, u32[]{:S(2)}, u32[]{:S(2)}) %collective-permute-start) | collective-permute-done | bytes 131104 | tf_op jit(solution)/shard_map/ppermute | solution.py:37
  6.9 5.9 %collective-permute-done.1 = bf16[64,1024]{1,0:T(8,128)(2,1)S(1)} collective-permute-done((bf16[64,1024]{1,0:T(8,128)(2,1)}, bf16[64,1024]{1,0:T(8,128)(2,1)S(1)}, u32[]{:S(2)}, u32[]{:S(2)}) %collective-permute-start.1) | collective-permute-done | bytes 131104 | tf_op jit(solution)/shard_map/ppermute | solution.py:37
  12.8 2.2 %collective-permute-done.2 = bf16[64,1024]{1,0:T(8,128)(2,1)S(1)} collective-permute-done((bf16[64,1024]{1,0:T(8,128)(2,1)}, bf16[64,1024]{1,0:T(8,128)(2,1)S(1)}, u32[]{:S(2)}, u32[]{:S(2)}) %collective-permute-start.2) | collective-permute-done | bytes 131104 | tf_op jit(solution)/shard_map/ppermute | solution.py:37
  15.1 3.1 %collective-permute-start.12 = (bf16[256,256]{1,0:T(8,128)(2,1)S(1)}, bf16[256,256]{1,0:T(8,128)(2,1)S(1)}, u32[]{:S(2)}, u32[]{:S(2)}) collective-permute-start(bf16[256,256]{1,0:T(8,128)(2,1)S(1)} %get-tuple-element.26), channel_id=1, source_target_pairs={{0,192},{64,128},{128,64},{192,0},{1,193},{65,129},{129,65},{193,1... | collective-permute-start | bytes 393224 | tf_op jit(solution)/shard_map/ppermute | solution.py:32
  18.9 2.8 %collective-permute-start.10 = (bf16[256,256]{1,0:T(8,128)(2,1)S(1)}, bf16[256,256]{1,0:T(8,128)(2,1)S(1)}, u32[]{:S(2)}, u32[]{:S(2)}) collective-permute-start(bf16[256,256]{1,0:T(8,128)(2,1)S(1)} %get-tuple-element.27), channel_id=1, source_target_pairs={{0,48},{16,32},{32,16},{48,0},{1,49},{17,33},{33,17},{49,1},{2,50}... | collective-permute-start | bytes 393224 | tf_op jit(solution)/shard_map/ppermute | solution.py:32
  21.8 0.1 reshape.36
  21.9 0.1 concatenate.51
  22.0 0.9 all_to_all.8
  22.9 4.8 %all-to-all-start = ((f32[64,1,1152]{2,1,0:T(1,128)}), f32[64,1,1152]{2,1,0:T(1,128)S(1)}, u32[]{:S(2)}, u32[]{:S(2)}) async-start(f32[64,1,1152]{2,1,0:T(1,128)} %all_to_all.8), calls=%async_computation | async-start | bytes 589824 | tf_op jit(solution)/shard_map/all_to_all | solution.py:194
  27.7 1.7 %collective-permute-start.8 = (bf16[256,256]{1,0:T(8,128)(2,1)S(1)}, bf16[256,256]{1,0:T(8,128)(2,1)S(1)}, u32[]{:S(2)}, u32[]{:S(2)}) collective-permute-start(bf16[256,256]{1,0:T(8,128)(2,1)S(1)} %get-tuple-element.28), channel_id=1, source_target_pairs={{0,64},{64,0},{128,192},{192,128},{1,65},{65,1},{129,193},{193,129... | collective-permute-start | bytes 393224 | tf_op jit(solution)/shard_map/ppermute | solution.py:32
  29.4 1.5 %collective-permute-start.6 = (bf16[256,256]{1,0:T(8,128)(2,1)S(1)}, bf16[256,256]{1,0:T(8,128)(2,1)S(1)}, u32[]{:S(2)}, u32[]{:S(2)}) collective-permute-start(bf16[256,256]{1,0:T(8,128)(2,1)S(1)} %get-tuple-element.29), channel_id=1, source_target_pairs={{0,16},{16,0},{32,48},{48,32},{1,17},{17,1},{33,49},{49,33},{2,18}... | collective-permute-start | bytes 393224 | tf_op jit(solution)/shard_map/ppermute | solution.py:32
  30.9 0.8 collective-permute-start.3
  31.7 0.0 collective-permute-done.12
  31.7 2.2 %collective-permute-start.13 = (bf16[512,256]{1,0:T(8,128)(2,1)S(1)}, bf16[512,256]{1,0:T(8,128)(2,1)S(1)}, u32[]{:S(2)}, u32[]{:S(2)}) collective-permute-start(bf16[512,256]{1,0:T(8,128)(2,1)S(1)} %pad_maximum_fusion.7), channel_id=1, source_target_pairs={{0,48},{16,32},{32,16},{48,0},{1,49},{17,33},{33,17},{49,1},{2,50}... | collective-permute-start | bytes 786440 | tf_op jit(solution)/shard_map/ppermute | solution.py:32
  33.9 0.0 collective-permute-done.10
  33.9 2.3 %collective-permute-start.11 = (bf16[512,256]{1,0:T(8,128)(2,1)S(1)}, bf16[512,256]{1,0:T(8,128)(2,1)S(1)}, u32[]{:S(2)}, u32[]{:S(2)}) collective-permute-start(bf16[512,256]{1,0:T(8,128)(2,1)S(1)} %pad_maximum_fusion.6), channel_id=1, source_target_pairs={{0,192},{64,128},{128,64},{192,0},{1,193},{65,129},{129,65},{193,1... | collective-permute-start | bytes 786440 | tf_op jit(solution)/shard_map/ppermute | solution.py:32
  36.2 0.7 collective-permute-start.9
  36.9 0.0 collective-permute-done.6
  36.9 0.8 collective-permute-start.7
  37.7 2.3 %collective-permute-done.13 = bf16[512,256]{1,0:T(8,128)(2,1)S(1)} collective-permute-done((bf16[512,256]{1,0:T(8,128)(2,1)S(1)}, bf16[512,256]{1,0:T(8,128)(2,1)S(1)}, u32[]{:S(2)}, u32[]{:S(2)}) %collective-permute-start.13) | collective-permute-done | bytes 262176 | tf_op jit(solution)/shard_map/ppermute | solution.py:32
  40.0 0.8 pad_maximum_fusion.3
  40.8 1.1 collective-permute-done.11
  41.8 0.8 pad_maximum_fusion.2
  42.7 0.1 collective-permute-done.9
  42.8 0.8 pad_maximum_fusion.1
  43.6 0.0 collective-permute-done.7
  43.6 0.8 pad_maximum_fusion
  44.4 18.7 %all-to-all-done = f32[64,1,1152]{2,1,0:T(1,128)S(1)} async-done(((f32[64,1,1152]{2,1,0:T(1,128)}), f32[64,1,1152]{2,1,0:T(1,128)S(1)}, u32[]{:S(2)}, u32[]{:S(2)}) %all-to-all-start) | async-done | bytes 294944 | tf_op jit(solution)/shard_map/all_to_all | solution.py:194
  63.2 0.6 collective-permute-start.17
  63.8 0.5 collective-permute-start.14
  64.2 0.2 collective-permute-start.16
  64.4 1.1 constant_dynamic-update-slice_fusion.1
  65.5 1.8 %collective-permute-start.15 = (bf16[1024,256]{1,0:T(8,128)(2,1)}, bf16[1024,256]{1,0:T(8,128)(2,1)S(1)}, u32[]{:S(2)}, u32[]{:S(2)}) collective-permute-start(bf16[1024,256]{1,0:T(8,128)(2,1)} %pad_maximum_fusion.1), channel_id=1, source_target_pairs={{0,192},{64,128},{128,64},{192,0},{1,193},{65,129},{129,65},{193,1... | collective-permute-start | bytes 1572872 | tf_op jit(solution)/shard_map/ppermute | solution.py:32
  67.3 1.1 %constant_dynamic-update-slice_fusion.3 = bf16[2048,256]{1,0:T(8,128)(2,1)S(1)} fusion(bf16[1024,256]{1,0:T(8,128)(2,1)} %pad_maximum_fusion.1), kind=kLoop, calls=%fused_computation.15 | loop fusion | bytes 1048576
  68.4 1.1 constant_dynamic-update-slice_fusion.5
  69.5 1.9 %constant_dynamic-update-slice_fusion.7 = bf16[2048,256]{1,0:T(8,128)(2,1)} fusion(bf16[1024,256]{1,0:T(8,128)(2,1)} %pad_maximum_fusion.3), kind=kLoop, calls=%fused_computation.19 | loop fusion | bytes 1048576
  71.4 1.2 %collective-permute-done.17 = bf16[1024,256]{1,0:T(8,128)(2,1)S(1)} collective-permute-done((bf16[1024,256]{1,0:T(8,128)(2,1)}, bf16[1024,256]{1,0:T(8,128)(2,1)S(1)}, u32[]{:S(2)}, u32[]{:S(2)}) %collective-permute-start.17) | collective-permute-done | bytes 524320 | tf_op jit(solution)/shard_map/ppermute | solution.py:32
  72.6 0.8 constant_dynamic-update-slice_fusion.6.refs_3_
  73.5 0.7 collective-permute-start.21
  74.3 1.0 collective-permute-start.20
  75.3 0.9 collective-permute-done.15
  76.2 2.7 %collective-permute-start.19 = (bf16[2048,256]{1,0:T(8,128)(2,1)S(1)}, bf16[2048,256]{1,0:T(8,128)(2,1)}, u32[]{:S(2)}, u32[]{:S(2)}) collective-permute-start(bf16[2048,256]{1,0:T(8,128)(2,1)S(1)} %constant_dynamic-update-slice_fusion.2.refs_1_), channel_id=1, source_target_pairs={{0,48},{16,32},{32,16},{48,0},{1,49},{17,33},{33,17},{49,1},{2,50}... | collective-permute-start | bytes 3145736 | tf_op jit(solution)/shard_map/ppermute | solution.py:32
  79.0 0.8 collective-permute-start.18
  79.8 0.8 copy-done
  80.5 0.0 collective-permute-start.5
  81.2 0.0 copy-start.1
  81.2 0.1 pad_add_fusion.at_ref
  81.3 1.1 %fusion = f32[64,1024]{1,0:T(8,128)} fusion(f32[64,1152]{1,0:T(8,128)S(1)} %bitcast.18), kind=kOutput, calls=%fused_computation.9 | convolution fusion | flops 50331648 | bytes 557056 | tf_op jit(solution)/shard_map/dot_general | solution.py:236
  82.4 1.0 copy-done.2
  83.5 1.0 copy-done.3
  84.5 1.0 copy-done.4
  85.5 7.1 %decayed_scores.1 = (bf16[16,256,256]{2,1,0:T(8,128)(2,1)S(1)}, bf16[16,256,256]{2,1,0:T(8,128)(2,1)S(1)}) custom-call(s32[1]{0:T(128)S(6)} %copy.23.live_ref, bf16[256,1024]{1,0:T(8,128)(2,1)S(1)} %bitcast.14, bf16[256,1024]{1,0:T(8,128)(2,1)S(1)} %bitcast.15, bf16[256,1024]{1,0:T(8,128)(2,1)S(1)} %bitcast.16), custom_call_target="tpu_custom_call" | custom-call | bytes 25165824 | tf_op jit(solution)/shard_map/decayed_scores/pallas_call | solution.py:225
  92.6 2.1 %member_tokens.1 = (bf16[4,256,1024]{2,1,0:T(8,128)(2,1)S(1)}, f32[256,8]{1,0:T(8,128)S(1)}) custom-call(s32[1]{0:T(128)} %bitcast.2.at_ref, bf16[256,1024]{1,0:T(8,128)(2,1)} %bitcast.3.t0, bf16[256,1024]{1,0:T(8,128)(2,1)S(1)} %copy-done.1, bf16[256,1024]{1,0:T(8,128)(2,1)} %collective-permute-done.3.t2, bf16[256,1024]{1,0:T(8,128)(2,1)} %collective-permute-done.5.t3, ...), custom_call_target="tpu_custom_call" | custom-call | bytes 8388608 | tf_op jit(solution)/shard_map/member_tokens/pallas_call | solution.py:209
  94.8 2.5 %held_products.1.sum_ref = f32[256,1024]{1,0:T(8,128)S(1)} custom-call(s32[2]{0:T(128)S(1)} %pad_add_fusion.at_ref, bf16[4,256,1024]{2,1,0:T(8,128)(2,1)S(1)} %get-tuple-element.16.tokens_ref, bf16[2048,256]{1,0:T(8,128)(2,1)S(1)} %constant_dynamic-update-slice_fusion.refs_0_, bf16[2048,256]{1,0:T(8,128)(2,1)S(1)} %constant_dynamic-update-slice_fusion.2.refs_1_, ...), custom_call_target="tpu_custom_call" | custom-call | flops 1073741824 | bytes 8388608 | tf_op jit(solution)/shard_map/held_products/pallas_call | solution.py:246
  97.3 1.0 collective-permute-done.21.refs_3_
  98.4 1.4 %collective-permute-done.20.refs_2_ = bf16[2048,256]{1,0:T(8,128)(2,1)} collective-permute-done((bf16[2048,256]{1,0:T(8,128)(2,1)S(1)}, bf16[2048,256]{1,0:T(8,128)(2,1)}, u32[]{:S(2)}, u32[]{:S(2)}) %collective-permute-start.20) | collective-permute-done | bytes 1048608 | tf_op jit(solution)/shard_map/ppermute | solution.py:32
  99.7 1.4 %collective-permute-done.19.refs_1_ = bf16[2048,256]{1,0:T(8,128)(2,1)} collective-permute-done((bf16[2048,256]{1,0:T(8,128)(2,1)S(1)}, bf16[2048,256]{1,0:T(8,128)(2,1)}, u32[]{:S(2)}, u32[]{:S(2)}) %collective-permute-start.19) | collective-permute-done | bytes 1048608 | tf_op jit(solution)/shard_map/ppermute | solution.py:32
  101.1 2.3 %collective-permute-done.18.refs_0_ = bf16[2048,256]{1,0:T(8,128)(2,1)} collective-permute-done((bf16[2048,256]{1,0:T(8,128)(2,1)S(1)}, bf16[2048,256]{1,0:T(8,128)(2,1)}, u32[]{:S(2)}, u32[]{:S(2)}) %collective-permute-start.18) | collective-permute-done | bytes 1048608 | tf_op jit(solution)/shard_map/ppermute | solution.py:32
  103.4 6.7 %values_readout.1 = bf16[256,1024]{1,0:T(8,128)(2,1)} custom-call(s32[2]{0:T(128)S(1)} %pad_add_fusion.at_ref, bf16[4,256,1024]{2,1,0:T(8,128)(2,1)S(1)} %get-tuple-element.16.tokens_ref, f32[256,1024]{1,0:T(8,128)S(1)} %held_products.1.sum_ref, f32[256,8]{1,0:T(8,128)S(1)} %get-tuple-element.21.projected_ref, bf16[1,1024]{1,0:T(2,128)(2,1)S(1)} %copy-done.6, ...), custom_call_target="tpu_custom_call" | custom-call | flops 1073741824 | bytes 12582912 | tf_op jit(solution)/shard_map/values_readout/pallas_call | solution.py:255
  (32 shorter events, 0.4 us)
Async XLA Ops:
  0.6 21.1 %copy-start.5 = (bf16[1,4096]{1,0:T(2,128)(2,1)S(1)}, bf16[1,4096]{1,0:T(2,128)(2,1)}, u32[]{:S(2)}) copy-start(bf16[1,4096]{1,0:T(2,128)(2,1)} %param.14) | copy-start | bytes 24580
  0.6 21.1 %copy-start.6 = (bf16[1,1024]{1,0:T(2,128)(2,1)S(1)}, bf16[1,1024]{1,0:T(2,128)(2,1)}, u32[]{:S(2)}) copy-start(bf16[1,1024]{1,0:T(2,128)(2,1)} %noise_ref.1) | copy-start | bytes 6148
  0.6 6.2 %collective-permute-start = (bf16[64,1024]{1,0:T(8,128)(2,1)}, bf16[64,1024]{1,0:T(8,128)(2,1)S(1)}, u32[]{:S(2)}, u32[]{:S(2)}) collective-permute-start(bf16[64,1024]{1,0:T(8,128)(2,1)} %param.13), channel_id=1, source_target_pairs={{4,0},{8,4},{12,8},{0,12},{5,1},{9,5},{13,9},{1,13},{6,2},{10,6},{... | collective-permute-start | bytes 393224 | tf_op jit(solution)/shard_map/ppermute | solution.py:37
  2.7 12.4 %collective-permute-start.2 = (bf16[64,1024]{1,0:T(8,128)(2,1)}, bf16[64,1024]{1,0:T(8,128)(2,1)S(1)}, u32[]{:S(2)}, u32[]{:S(2)}) collective-permute-start(bf16[64,1024]{1,0:T(8,128)(2,1)} %param.13), channel_id=1, source_target_pairs={{8,0},{12,4},{0,8},{4,12},{9,1},{13,5},{1,9},{5,13},{10,2},{14,6},... | collective-permute-start | bytes 393224 | tf_op jit(solution)/shard_map/ppermute | solution.py:37
  3.2 9.6 %collective-permute-start.1 = (bf16[64,1024]{1,0:T(8,128)(2,1)}, bf16[64,1024]{1,0:T(8,128)(2,1)S(1)}, u32[]{:S(2)}, u32[]{:S(2)}) collective-permute-start(bf16[64,1024]{1,0:T(8,128)(2,1)} %param.13), channel_id=1, source_target_pairs={{12,0},{0,4},{4,8},{8,12},{13,1},{1,5},{5,9},{9,13},{14,2},{2,6},{... | collective-permute-start | bytes 393224 | tf_op jit(solution)/shard_map/ppermute | solution.py:37
  15.1 16.6 %collective-permute-start.12 = (bf16[256,256]{1,0:T(8,128)(2,1)S(1)}, bf16[256,256]{1,0:T(8,128)(2,1)S(1)}, u32[]{:S(2)}, u32[]{:S(2)}) collective-permute-start(bf16[256,256]{1,0:T(8,128)(2,1)S(1)} %get-tuple-element.26), channel_id=1, source_target_pairs={{0,192},{64,128},{128,64},{192,0},{1,193},{65,129},{129,65},{193,1... | collective-permute-start | bytes 393224 | tf_op jit(solution)/shard_map/ppermute | solution.py:32
  18.9 15.0 %collective-permute-start.10 = (bf16[256,256]{1,0:T(8,128)(2,1)S(1)}, bf16[256,256]{1,0:T(8,128)(2,1)S(1)}, u32[]{:S(2)}, u32[]{:S(2)}) collective-permute-start(bf16[256,256]{1,0:T(8,128)(2,1)S(1)} %get-tuple-element.27), channel_id=1, source_target_pairs={{0,48},{16,32},{32,16},{48,0},{1,49},{17,33},{33,17},{49,1},{2,50}... | collective-permute-start | bytes 393224 | tf_op jit(solution)/shard_map/ppermute | solution.py:32
  22.9 40.2 %all-to-all-start = ((f32[64,1,1152]{2,1,0:T(1,128)}), f32[64,1,1152]{2,1,0:T(1,128)S(1)}, u32[]{:S(2)}, u32[]{:S(2)}) async-start(f32[64,1,1152]{2,1,0:T(1,128)} %all_to_all.8), calls=%async_computation | async-start | bytes 589824 | tf_op jit(solution)/shard_map/all_to_all | solution.py:194
  27.7 8.5 %collective-permute-start.8 = (bf16[256,256]{1,0:T(8,128)(2,1)S(1)}, bf16[256,256]{1,0:T(8,128)(2,1)S(1)}, u32[]{:S(2)}, u32[]{:S(2)}) collective-permute-start(bf16[256,256]{1,0:T(8,128)(2,1)S(1)} %get-tuple-element.28), channel_id=1, source_target_pairs={{0,64},{64,0},{128,192},{192,128},{1,65},{65,1},{129,193},{193,129... | collective-permute-start | bytes 393224 | tf_op jit(solution)/shard_map/ppermute | solution.py:32
  29.4 7.5 %collective-permute-start.6 = (bf16[256,256]{1,0:T(8,128)(2,1)S(1)}, bf16[256,256]{1,0:T(8,128)(2,1)S(1)}, u32[]{:S(2)}, u32[]{:S(2)}) collective-permute-start(bf16[256,256]{1,0:T(8,128)(2,1)S(1)} %get-tuple-element.29), channel_id=1, source_target_pairs={{0,16},{16,0},{32,48},{48,32},{1,17},{17,1},{33,49},{49,33},{2,18}... | collective-permute-start | bytes 393224 | tf_op jit(solution)/shard_map/ppermute | solution.py:32
  30.9 40.5 %collective-permute-start.3 = (bf16[256,1024]{1,0:T(8,128)(2,1)}, bf16[256,1024]{1,0:T(8,128)(2,1)}, u32[]{:S(2)}, u32[]{:S(2)}) collective-permute-start(bf16[256,1024]{1,0:T(8,128)(2,1)} %bitcast.3.t0), channel_id=1, source_target_pairs={{0,2},{2,0},{1,3},{3,1},{4,6},{6,4},{5,7},{7,5},{8,10},{10,8},{9,1... | collective-permute-start | bytes 1572872 | tf_op jit(solution)/shard_map/ppermute | solution.py:32
  31.7 8.2 %collective-permute-start.13 = (bf16[512,256]{1,0:T(8,128)(2,1)S(1)}, bf16[512,256]{1,0:T(8,128)(2,1)S(1)}, u32[]{:S(2)}, u32[]{:S(2)}) collective-permute-start(bf16[512,256]{1,0:T(8,128)(2,1)S(1)} %pad_maximum_fusion.7), channel_id=1, source_target_pairs={{0,48},{16,32},{32,16},{48,0},{1,49},{17,33},{33,17},{49,1},{2,50}... | collective-permute-start | bytes 786440 | tf_op jit(solution)/shard_map/ppermute | solution.py:32
  33.9 7.9 %collective-permute-start.11 = (bf16[512,256]{1,0:T(8,128)(2,1)S(1)}, bf16[512,256]{1,0:T(8,128)(2,1)S(1)}, u32[]{:S(2)}, u32[]{:S(2)}) collective-permute-start(bf16[512,256]{1,0:T(8,128)(2,1)S(1)} %pad_maximum_fusion.6), channel_id=1, source_target_pairs={{0,192},{64,128},{128,64},{192,0},{1,193},{65,129},{129,65},{193,1... | collective-permute-start | bytes 786440 | tf_op jit(solution)/shard_map/ppermute | solution.py:32
  36.2 6.5 %collective-permute-start.9 = (bf16[512,256]{1,0:T(8,128)(2,1)S(1)}, bf16[512,256]{1,0:T(8,128)(2,1)S(1)}, u32[]{:S(2)}, u32[]{:S(2)}) collective-permute-start(bf16[512,256]{1,0:T(8,128)(2,1)S(1)} %pad_maximum_fusion.5), channel_id=1, source_target_pairs={{0,16},{16,0},{32,48},{48,32},{1,17},{17,1},{33,49},{49,33},{2,18}... | collective-permute-start | bytes 786440 | tf_op jit(solution)/shard_map/ppermute | solution.py:32
  36.9 6.7 %collective-permute-start.7 = (bf16[512,256]{1,0:T(8,128)(2,1)S(1)}, bf16[512,256]{1,0:T(8,128)(2,1)S(1)}, u32[]{:S(2)}, u32[]{:S(2)}) collective-permute-start(bf16[512,256]{1,0:T(8,128)(2,1)S(1)} %pad_maximum_fusion.4), channel_id=1, source_target_pairs={{0,64},{64,0},{128,192},{192,128},{1,65},{65,1},{129,193},{193,129... | collective-permute-start | bytes 786440 | tf_op jit(solution)/shard_map/ppermute | solution.py:32
  63.2 9.5 %collective-permute-start.17 = (bf16[1024,256]{1,0:T(8,128)(2,1)}, bf16[1024,256]{1,0:T(8,128)(2,1)S(1)}, u32[]{:S(2)}, u32[]{:S(2)}) collective-permute-start(bf16[1024,256]{1,0:T(8,128)(2,1)} %pad_maximum_fusion.3), channel_id=1, source_target_pairs={{0,64},{64,0},{128,192},{192,128},{1,65},{65,1},{129,193},{193,129... | collective-permute-start | bytes 1572872 | tf_op jit(solution)/shard_map/ppermute | solution.py:32
  63.8 15.2 %collective-permute-start.14 = (bf16[1024,256]{1,0:T(8,128)(2,1)}, bf16[1024,256]{1,0:T(8,128)(2,1)S(1)}, u32[]{:S(2)}, u32[]{:S(2)}) collective-permute-start(bf16[1024,256]{1,0:T(8,128)(2,1)} %pad_maximum_fusion), channel_id=1, source_target_pairs={{0,48},{16,32},{32,16},{48,0},{1,49},{17,33},{33,17},{49,1},{2,50}... | collective-permute-start | bytes 1572872 | tf_op jit(solution)/shard_map/ppermute | solution.py:32
  64.2 10.0 %collective-permute-start.16 = (bf16[1024,256]{1,0:T(8,128)(2,1)}, bf16[1024,256]{1,0:T(8,128)(2,1)S(1)}, u32[]{:S(2)}, u32[]{:S(2)}) collective-permute-start(bf16[1024,256]{1,0:T(8,128)(2,1)} %pad_maximum_fusion.2), channel_id=1, source_target_pairs={{0,16},{16,0},{32,48},{48,32},{1,17},{17,1},{33,49},{49,33},{2,18}... | collective-permute-start | bytes 1572872 | tf_op jit(solution)/shard_map/ppermute | solution.py:32
  65.5 10.7 %collective-permute-start.15 = (bf16[1024,256]{1,0:T(8,128)(2,1)}, bf16[1024,256]{1,0:T(8,128)(2,1)S(1)}, u32[]{:S(2)}, u32[]{:S(2)}) collective-permute-start(bf16[1024,256]{1,0:T(8,128)(2,1)} %pad_maximum_fusion.1), channel_id=1, source_target_pairs={{0,192},{64,128},{128,64},{192,0},{1,193},{65,129},{129,65},{193,1... | collective-permute-start | bytes 1572872 | tf_op jit(solution)/shard_map/ppermute | solution.py:32
  71.4 8.3 %collective-permute-start.4 = (bf16[256,1024]{1,0:T(8,128)(2,1)}, bf16[256,1024]{1,0:T(8,128)(2,1)S(1)}, u32[]{:S(2)}, u32[]{:S(2)}) collective-permute-start(bf16[256,1024]{1,0:T(8,128)(2,1)} %bitcast.3.t0), channel_id=1, source_target_pairs={{0,1},{1,0},{2,3},{3,2},{4,5},{5,4},{6,7},{7,6},{8,9},{9,8},{10,11... | collective-permute-start | bytes 1572872 | tf_op jit(solution)/shard_map/ppermute | solution.py:32
  73.5 24.9 %collective-permute-start.21 = (bf16[2048,256]{1,0:T(8,128)(2,1)}, bf16[2048,256]{1,0:T(8,128)(2,1)}, u32[]{:S(2)}, u32[]{:S(2)}) collective-permute-start(bf16[2048,256]{1,0:T(8,128)(2,1)} %constant_dynamic-update-slice_fusion.6.refs_3_), channel_id=1, source_target_pairs={{0,16},{16,0},{32,48},{48,32},{1,17},{17,1},{33,49},{49,33},{2,18}... | collective-permute-start | bytes 3145736 | tf_op jit(solution)/shard_map/ppermute | solution.py:32
  74.3 25.5 %collective-permute-start.20 = (bf16[2048,256]{1,0:T(8,128)(2,1)S(1)}, bf16[2048,256]{1,0:T(8,128)(2,1)}, u32[]{:S(2)}, u32[]{:S(2)}) collective-permute-start(bf16[2048,256]{1,0:T(8,128)(2,1)S(1)} %constant_dynamic-update-slice_fusion.4.refs_2_), channel_id=1, source_target_pairs={{0,64},{64,0},{128,192},{192,128},{1,65},{65,1},{129,193},{193,129... | collective-permute-start | bytes 3145736 | tf_op jit(solution)/shard_map/ppermute | solution.py:32
  76.2 24.9 %collective-permute-start.19 = (bf16[2048,256]{1,0:T(8,128)(2,1)S(1)}, bf16[2048,256]{1,0:T(8,128)(2,1)}, u32[]{:S(2)}, u32[]{:S(2)}) collective-permute-start(bf16[2048,256]{1,0:T(8,128)(2,1)S(1)} %constant_dynamic-update-slice_fusion.2.refs_1_), channel_id=1, source_target_pairs={{0,48},{16,32},{32,16},{48,0},{1,49},{17,33},{33,17},{49,1},{2,50}... | collective-permute-start | bytes 3145736 | tf_op jit(solution)/shard_map/ppermute | solution.py:32
  79.0 24.4 %collective-permute-start.18 = (bf16[2048,256]{1,0:T(8,128)(2,1)S(1)}, bf16[2048,256]{1,0:T(8,128)(2,1)}, u32[]{:S(2)}, u32[]{:S(2)}) collective-permute-start(bf16[2048,256]{1,0:T(8,128)(2,1)S(1)} %constant_dynamic-update-slice_fusion.refs_0_), channel_id=1, source_target_pairs={{0,192},{64,128},{128,64},{192,0},{1,193},{65,129},{129,65},{193,1... | collective-permute-start | bytes 3145736 | tf_op jit(solution)/shard_map/ppermute | solution.py:32
  79.8 0.8 copy-start
  80.5 12.1 %collective-permute-start.5 = (bf16[256,1024]{1,0:T(8,128)(2,1)}, bf16[256,1024]{1,0:T(8,128)(2,1)}, u32[]{:S(2)}, u32[]{:S(2)}) collective-permute-start(bf16[256,1024]{1,0:T(8,128)(2,1)} %collective-permute-done.3.t2), channel_id=1, source_target_pairs={{0,1},{1,0},{2,3},{3,2},{4,5},{5,4},{6,7},{7,6},{8,9},{9,8},{10,11... | collective-permute-start | bytes 1572872 | tf_op jit(solution)/shard_map/ppermute | solution.py:32
  81.2 11.4 %copy-start.1 = (bf16[256,1024]{1,0:T(8,128)(2,1)S(1)}, bf16[256,1024]{1,0:T(8,128)(2,1)}, u32[]{:S(2)}) copy-start(bf16[256,1024]{1,0:T(8,128)(2,1)} %copy-done) | copy-start | bytes 1572868
  82.4 1.0 copy-start.2
  83.5 1.0 copy-start.3
  84.5 1.0 copy-start.4

commit v4 on v3

--- a/solution.py
+++ b/solution.py
@@ -23,6 +23,7 @@
 LINKS = {"a": ("x", 1), "b": ("x", 3), "c": ("y", 1), "d": ("y", 3)}
 ROUTES = ("acbd", "cadb", "bdac", "dbca")
 
+ANY = pl.BlockSpec(memory_space=pl.ANY)
 VMEM = pl.BlockSpec(memory_space=pltpu.VMEM)
 SMEM = pl.BlockSpec(memory_space=pltpu.SMEM)
 
@@ -37,14 +38,13 @@
     return lax.ppermute(array, axis, [((i + step) % size, i) for i in range(size)])
 
 
-def masks(route, last):
-    steps = [LINKS[s] for s in route]
+def masks(route, steps):
     found = []
-    for i in range(2 ** (len(steps) - 1)):
+    for i in range(4):
         y = x = 0
-        for k, (axis, mask) in enumerate(steps):
-            if (i >> k) & 1 or (last and k == len(steps) - 1):
-                y, x = (y ^ mask, x) if axis == "y" else (y, x ^ mask)
+        for link in [route[k] for k in range(2) if (i >> k) & 1] + [route[k] for k in steps]:
+            axis, mask = LINKS[link]
+            y, x = (y ^ mask, x) if axis == "y" else (y, x ^ mask)
         found.append((y, x))
     return found
 
@@ -102,44 +102,70 @@
                 low_ref[head, first:last, last:] = rest
 
 
-def chunk_product(at_ref, tokens_ref, piece_ref, blocks):
-    depth = piece_ref.shape[0] // len(blocks)
-    group = 4
-    total = None
-    for first in range(0, len(blocks), group):
-        columns = []
-        for y, x in blocks[first : first + group]:
-            place = pl.multiple_of(jnp.bitwise_xor(at_ref[1], x) * depth, depth)
-            columns.append(tokens_ref[jnp.bitwise_xor(at_ref[0], y), :, pl.ds(place, depth)])
-        term = jnp.dot(
-            jnp.concatenate(columns, 1),
-            piece_ref[first * depth : (first + group) * depth],
-            preferred_element_type=F32,
-        )
-        total = term if total is None else total + term
-    return total
-
-
-def held_kernel(at_ref, tokens_ref, *refs):
-    pieces, out_ref = refs[:-1], refs[-1]
-    wide = pieces[0].shape[1]
-    for c, piece in enumerate(pieces):
-        out_ref[:, c * wide : (c + 1) * wide] = chunk_product(
-            at_ref, tokens_ref, piece, masks(ROUTES[c], False)
-        )
+def chunk_product(at_ref, tokens_ref, piece, blocks):
+    depth = piece.shape[0] // len(blocks)
+    columns = []
+    for y, x in blocks:
+        place = pl.multiple_of(jnp.bitwise_xor(at_ref[1], x) * depth, depth)
+        columns.append(tokens_ref[jnp.bitwise_xor(at_ref[0], y), :, pl.ds(place, depth)])
+    return jnp.dot(jnp.concatenate(columns, 1), piece[...], preferred_element_type=F32)
+
+
+def copies_of(pieces, held, sems):
+    copies = [pltpu.make_async_copy(p, held.at[i], sems.at[i]) for i, p in enumerate(pieces)]
+    for copy in copies:
+        copy.start()
+    return copies
+
+
+def product_kernel(ways, added, at_ref, tokens_ref, *refs):
+    refs = list(refs)
+    sum_ref = refs.pop(0) if added else None
+    out_ref, held, sems = refs[-3:]
+    wide = held.shape[2]
+    copies = copies_of(refs[:-3], held, sems)
+    for c, route in enumerate(ROUTES):
+        where = slice(c * wide, (c + 1) * wide)
+        total = sum_ref[:, where] if added else None
+        for i, steps in enumerate(ways):
+            at = c * len(ways) + i
+            copies[at].wait()
+            term = chunk_product(at_ref, tokens_ref, held.at[at], masks(route, steps))
+            total = term if total is None else total + term
+        out_ref[:, where] = total
+
+
+def product(at, tokens, ways, pieces, before=None):
+    length, width = tokens.shape[1:]
+    extra = () if before is None else (before,)
+    return pl.pallas_call(
+        functools.partial(product_kernel, ways, before is not None),
+        out_shape=jax.ShapeDtypeStruct((length, width), F32),
+        in_specs=[SMEM, VMEM] + [VMEM] * len(extra) + [ANY] * len(pieces),
+        out_specs=VMEM,
+        scratch_shapes=[
+            pltpu.VMEM((len(pieces),) + pieces[0].shape, BF16),
+            pltpu.SemaphoreType.DMA((len(pieces),)),
+        ],
+        cost_estimate=cost(len(pieces) * 2 * length * pieces[0].size, 8 << 20),
+        compiler_params=params(20),
+        name="products",
+    )(at, tokens, *extra, *pieces)
 
 
 def readout_kernel(at_ref, tokens_ref, sum_ref, projected_ref, noise_ref, high_ref, low_ref, *refs):
-    pieces, out_ref = refs[:-1], refs[-1]
-    wide = pieces[0].shape[1]
+    out_ref, held, sems = refs[-3:]
+    wide = held.shape[2]
+    copies = copies_of(refs[:-3], held, sems)
     projected = projected_ref[...][:, :1] * (
         SIGMA / math.sqrt(tokens_ref.shape[0] * tokens_ref.shape[2])
     )
     lane = lax.broadcasted_iota(jnp.int32, (out_ref.shape[0], LANES), 1)
-    for c, piece in enumerate(pieces):
+    for c, route in enumerate(ROUTES):
         where = slice(c * wide, (c + 1) * wide)
         total = sum_ref[:, where] + projected * noise_ref[:, where].astype(F32)
-        total = total + chunk_product(at_ref, tokens_ref, piece, masks(ROUTES[c], True))
+        copies[c].wait()
+        total = total + chunk_product(at_ref, tokens_ref, held.at[c], masks(route, (2, 3)))
         values = total.astype(BF16)
         for pair in range(wide // LANES):
             mine = values[:, pair * LANES : (pair + 1) * LANES]
@@ -175,36 +201,38 @@
     rows = value_weight.shape[0]
     wide = width // len(ROUTES)
 
+    heads = width // HEAD
+    strip = pl.BlockSpec((length, LANES), lambda i: (0, i))
+    square = pl.BlockSpec((2, length, length), lambda i: (i, 0, 0))
+    high, low = pl.pallas_call(
+        score_kernel,
+        out_shape=[jax.ShapeDtypeStruct((heads, length, length), BF16)] * 2,
+        grid=(width // LANES,),
+        in_specs=[SMEM, strip, strip, strip],
+        out_specs=[square, square],
+        cost_estimate=cost(0, 24 << 20),
+        name="decayed_scores",
+    )(live_length, receptance, keys, log_decay)
     z = lax.axis_index("z")
     near = jnp.zeros((SIDE * rows, width), BF16)
     for step in (0, 1, 3, 2):
         part = fetch(value_weight, "z", step) if step else value_weight
         near = lax.dynamic_update_slice(near, part, (lax.rem(z + step, SIDE) * rows, 0))
-
-    population = lax.axis_size(POP)
-    weighted = noise_in.astype(F32) * (utilities / math.sqrt(population))[:, None]
-    message = jnp.concatenate(
-        [
-            weighted.reshape(population, rows),
-            jnp.zeros((population, LANES - rows), F32),
-            jnp.broadcast_to(noise_out.astype(F32), (population, width)),
-        ],
-        1,
-    )
-    message = lax.all_to_all(message, POP, split_axis=0, concat_axis=0, tiled=True)
+    mate = swap(tokens, "core", 1)
+    near, high, low, mate = lax.optimization_barrier((near, high, low, mate))
 
     twin = swap(after(tokens, near), "twin", 1)
 
-    held = [near[:, c * wide : (c + 1) * wide] for c in range(len(ROUTES))]
-    for step in range(3):
-        if step == 2:
-            held, message = lax.optimization_barrier((held, message))
-        came = [swap(held[c], *LINKS[ROUTES[c][step]]) for c in range(len(ROUTES))]
+    chunks = range(len(ROUTES))
+    held = [near[:, c * wide : (c + 1) * wide] for c in chunks]
+    for step in range(2):
+        came = [swap(held[c], *LINKS[ROUTES[c][step]]) for c in chunks]
         held = [jnp.concatenate([a, b], 0) for a, b in zip(held, came)]
-    came = [swap(held[c], *LINKS[ROUTES[c][3]]) for c in range(len(ROUTES))]
-
-    mate = swap(after(tokens, twin), "core", 1)
-    both = swap(twin, "core", 1)
+    third = [swap(held[c], *LINKS[ROUTES[c][2]]) for c in chunks]
+    fourth = [swap(held[c], *LINKS[ROUTES[c][3]]) for c in chunks]
+    last = [swap(third[c], *LINKS[ROUTES[c][3]]) for c in chunks]
+
+    both = swap(after(twin, *third), "core", 1)
     tp = lax.axis_index(TP).reshape(1)
     all_tokens, projected = pl.pallas_call(
         token_kernel,
@@ -219,20 +247,19 @@
         name="member_tokens",
     )(tp, tokens, mate, twin, both, noise_in.reshape(4, 1, width))
 
-    heads = width // HEAD
-    strip = pl.BlockSpec((length, LANES), lambda i: (0, i))
-    square = pl.BlockSpec((2, length, length), lambda i: (i, 0, 0))
-    high, low = pl.pallas_call(
-        score_kernel,
-        out_shape=[jax.ShapeDtypeStruct((heads, length, length), BF16)] * 2,
-        grid=(width // LANES,),
-        in_specs=[SMEM, strip, strip, strip],
-        out_specs=[square, square],
-        cost_estimate=cost(0, 24 << 20),
-        compiler_params=params(16),
-        name="decayed_scores",
-    )(live_length, after(receptance, *held), keys, log_decay)
-
+    population = lax.axis_size(POP)
+    weighted = noise_in.astype(F32) * (utilities / math.sqrt(population))[:, None]
+    message = jnp.concatenate(
+        [
+            weighted.reshape(population, rows),
+            jnp.zeros((population, LANES - rows), F32),
+            jnp.broadcast_to(noise_out.astype(F32), (population, width)),
+        ],
+        1,
+    )
+    message = lax.all_to_all(
+        after(message, *third), POP, split_axis=0, concat_axis=0, tiled=True
+    )
     update = lax.dot_general(
         message[:, :rows],
         message[:, LANES:],
@@ -242,25 +269,23 @@
     )
 
     at = jnp.stack([lax.axis_index("y"), lax.axis_index("x")])
-    flops = length * width * 2 * 2048
-    total = pl.pallas_call(
-        held_kernel,
-        out_shape=jax.ShapeDtypeStruct((length, width), F32),
-        in_specs=[SMEM] + [VMEM] * 5,
-        out_specs=VMEM,
-        cost_estimate=cost(flops, 8 << 20),
-        compiler_params=params(16),
-        name="held_products",
-    )(at, all_tokens, *held)
+    total = product(
+        at, all_tokens, ((), (2,)), [p for c in chunks for p in (held[c], third[c])]
+    )
+    total = product(at, all_tokens, ((3,),), fourth, total)
     wkv_out = pl.pallas_call(
         readout_kernel,
         out_shape=jax.ShapeDtypeStruct((length, width), BF16),
-        in_specs=[SMEM] + [VMEM] * 10,
+        in_specs=[SMEM] + [VMEM] * 6 + [ANY] * len(last),
         out_specs=VMEM,
-        cost_estimate=cost(flops, 12 << 20),
+        scratch_shapes=[
+            pltpu.VMEM((len(last),) + last[0].shape, BF16),
+            pltpu.SemaphoreType.DMA((len(last),)),
+        ],
+        cost_estimate=cost(length * width * 2 * 1024, 12 << 20),
         compiler_params=params(20),
         name="values_readout",
-    )(at, all_tokens, total, projected, noise_out, high, low, *came)
+    )(at, all_tokens, total, projected, noise_out, high, low, *last)
     return wkv_out.reshape(1, length, width), update
 
 

time: 111 us -> 97.3 us (0.88)
  the two profiles are of different devices: /device:TPU:128 before, /device:TPU:32 now
where the time goes in v4:
time: 97.3 us; the launch traced here: 96.3 us
  starting transfers between devices  50.3 us (52%)
  Pallas kernels  25.4 us (26%)
  waiting for transfers between devices  12.2 us (13%)
  local copies, waits for them, and re-layouts  4.72 us (5%)
  between operations  2.29 us (2%)
  matrix products  1.12 us (1%)
    ppermute x23, starting transfers between devices, swap(): return lax.ppermute(array, axis, [(i, i ^ mask) for i in range(size)])  34.6 us
    ppermute x23, waiting for transfers between devices, swap(): return lax.ppermute(array, axis, [(i, i ^ mask) for i in range(size)])  12.2 us
    pallas_call x1, Pallas kernels, body(): pl.pallas_call(score_kernel, out_shape=[jax.ShapeDtypeStruct((heads, leng...  9.26 us
    all_to_all x1, starting transfers between devices, body(): lax.all_to_all(after(message, *third), POP, split_axis=0, concat_axis=0,...  8.52 us
    pallas_call x2, Pallas kernels, product(): pl.pallas_call(functools.partial(product_kernel, ways, before is not None...  7.67 us
    ppermute x3, starting transfers between devices, fetch(): lax.ppermute(array, axis, [((i + step) % size, i) for i in range(size)])  7.17 us
    pallas_call x1, Pallas kernels, body(): pl.pallas_call(readout_kernel, out_shape=jax.ShapeDtypeStruct((length, wi...  6.3 us
    pallas_call x1, Pallas kernels, body(): pl.pallas_call(token_kernel, out_shape=[jax.ShapeDtypeStruct((4, length,...  2.12 us
  transfers between devices with their start and end apart: 27, of which 9 were waited for; matrix products, arithmetic and copies ran while one was open for 3% of the time, Pallas kernels for 26%

profile of v4, /device:TPU:32, one launch (start us, length us, event | category | flops | bytes accessed | tf_op | source)
XLA Modules:
  0.0 96.3 jit_solution(7535292167626774491)
XLA Ops:
  0.6 0.1 collective-permute-start.3
  0.7 1.9 %collective-permute-start = (bf16[64,1024]{1,0:T(8,128)(2,1)}, bf16[64,1024]{1,0:T(8,128)(2,1)S(1)}, u32[]{:S(2)}, u32[]{:S(2)}) collective-permute-start(bf16[64,1024]{1,0:T(8,128)(2,1)} %param.13), channel_id=1, source_target_pairs={{4,0},{8,4},{12,8},{0,12},{5,1},{9,5},{13,9},{1,13},{6,2},{10,6},{... | collective-permute-start | bytes 393224 | tf_op jit(solution)/shard_map/ppermute | solution.py:38
  2.7 0.2 collective-permute-start.1
  2.8 5.1 %collective-permute-start.2 = (bf16[64,1024]{1,0:T(8,128)(2,1)}, bf16[64,1024]{1,0:T(8,128)(2,1)S(1)}, u32[]{:S(2)}, u32[]{:S(2)}) collective-permute-start(bf16[64,1024]{1,0:T(8,128)(2,1)} %param.13), channel_id=1, source_target_pairs={{8,0},{12,4},{0,8},{4,12},{9,1},{13,5},{1,9},{5,13},{10,2},{14,6},... | collective-permute-start | bytes 393224 | tf_op jit(solution)/shard_map/ppermute | solution.py:38
  7.9 0.1 broadcast_in_dim.17
  8.0 1.0 %constant_dynamic-update-slice_fusion.3 = bf16[256,1024]{1,0:T(8,128)(2,1)S(1)} fusion(bf16[256,1024]{1,0:T(8,128)(2,1)S(1)} %broadcast_in_dim.17, bf16[64,1024]{1,0:T(8,128)(2,1)} %param.13, s32[]{:T(128)S(6)} %select_n.12), kind=kLoop, calls=%fused_computation.16 | loop fusion | bytes 262148 | tf_op jit(solution)/shard_map/dynamic_update_slice | solution.py:220
  9.6 9.3 %decayed_scores.1 = (bf16[16,256,256]{2,1,0:T(8,128)(2,1)}, bf16[16,256,256]{2,1,0:T(8,128)(2,1)}) custom-call(s32[1]{0:T(128)S(6)} %copy.19.live_ref, bf16[256,1024]{1,0:T(8,128)(2,1)} %bitcast.20, bf16[256,1024]{1,0:T(8,128)(2,1)} %bitcast.21, bf16[256,1024]{1,0:T(8,128)(2,1)} %bitcast.22), custom_call_target="tpu_custom_call" | custom-call | bytes 25165824 | tf_op jit(solution)/shard_map/decayed_scores/pallas_call | solution.py:207
  18.9 0.0 collective-permute-done
  18.9 0.0 collective-permute-done.1
  18.9 0.0 collective-permute-done.2
  18.9 0.0 collective-permute-done.3.t1
  19.0 1.6 %collective-permute-start.5 = (bf16[256,256]{1,0:T(8,128)(2,1)S(1)}, bf16[256,256]{1,0:T(8,128)(2,1)S(1)}, u32[]{:S(2)}, u32[]{:S(2)}) collective-permute-start(bf16[256,256]{1,0:T(8,128)(2,1)S(1)} %get-tuple-element.27), channel_id=1, source_target_pairs={{0,16},{16,0},{32,48},{48,32},{1,17},{17,1},{33,49},{49,33},{2,18}... | collective-permute-start | bytes 393224 | tf_op jit(solution)/shard_map/ppermute | solution.py:33
  20.6 1.6 %collective-permute-start.8 = (bf16[256,256]{1,0:T(8,128)(2,1)S(1)}, bf16[256,256]{1,0:T(8,128)(2,1)S(1)}, u32[]{:S(2)}, u32[]{:S(2)}) collective-permute-start(bf16[256,256]{1,0:T(8,128)(2,1)S(1)} %get-tuple-element.26), channel_id=1, source_target_pairs={{0,64},{64,0},{128,192},{192,128},{1,65},{65,1},{129,193},{193,129... | collective-permute-start | bytes 393224 | tf_op jit(solution)/shard_map/ppermute | solution.py:33
  22.2 4.5 %collective-permute-start.4 = (bf16[256,1024]{1,0:T(8,128)(2,1)S(1)}, bf16[256,1024]{1,0:T(8,128)(2,1)}, u32[]{:S(2)}, u32[]{:S(2)}) collective-permute-start(bf16[256,1024]{1,0:T(8,128)(2,1)S(1)} %bitcast.15), channel_id=1, source_target_pairs={{0,2},{2,0},{1,3},{3,1},{4,6},{6,4},{5,7},{7,5},{8,10},{10,8},{9,1... | collective-permute-start | bytes 1572872 | tf_op jit(solution)/shard_map/ppermute | solution.py:33
  26.7 2.1 %collective-permute-start.11 = (bf16[256,256]{1,0:T(8,128)(2,1)S(1)}, bf16[256,256]{1,0:T(8,128)(2,1)S(1)}, u32[]{:S(2)}, u32[]{:S(2)}) collective-permute-start(bf16[256,256]{1,0:T(8,128)(2,1)S(1)} %get-tuple-element.25), channel_id=1, source_target_pairs={{0,48},{16,32},{32,16},{48,0},{1,49},{17,33},{33,17},{49,1},{2,50}... | collective-permute-start | bytes 393224 | tf_op jit(solution)/shard_map/ppermute | solution.py:33
  28.8 2.2 %collective-permute-start.14 = (bf16[256,256]{1,0:T(8,128)(2,1)S(1)}, bf16[256,256]{1,0:T(8,128)(2,1)S(1)}, u32[]{:S(2)}, u32[]{:S(2)}) collective-permute-start(bf16[256,256]{1,0:T(8,128)(2,1)S(1)} %get-tuple-element.24), channel_id=1, source_target_pairs={{0,192},{64,128},{128,64},{192,0},{1,193},{65,129},{129,65},{193,1... | collective-permute-start | bytes 393224 | tf_op jit(solution)/shard_map/ppermute | solution.py:33
  30.9 0.0 collective-permute-done.5
  31.0 0.8 collective-permute-start.6
  31.7 0.0 collective-permute-done.8
  31.7 0.7 collective-permute-start.9
  32.4 0.4 collective-permute-done.11
  32.9 2.3 %collective-permute-start.12 = (bf16[512,256]{1,0:T(8,128)(2,1)S(1)}, bf16[512,256]{1,0:T(8,128)(2,1)S(1)}, u32[]{:S(2)}, u32[]{:S(2)}) collective-permute-start(bf16[512,256]{1,0:T(8,128)(2,1)S(1)} %pad_maximum_fusion.6), channel_id=1, source_target_pairs={{0,192},{64,128},{128,64},{192,0},{1,193},{65,129},{129,65},{193,1... | collective-permute-start | bytes 786440 | tf_op jit(solution)/shard_map/ppermute | solution.py:33
  35.1 0.4 collective-permute-done.14
  35.6 0.0 copy-start.11
  35.6 0.0 copy-start.12
  35.6 1.8 %collective-permute-start.15 = (bf16[512,256]{1,0:T(8,128)(2,1)S(1)}, bf16[512,256]{1,0:T(8,128)(2,1)S(1)}, u32[]{:S(2)}, u32[]{:S(2)}) collective-permute-start(bf16[512,256]{1,0:T(8,128)(2,1)S(1)} %pad_maximum_fusion.7), channel_id=1, source_target_pairs={{0,48},{16,32},{32,16},{48,0},{1,49},{17,33},{33,17},{49,1},{2,50}... | collective-permute-start | bytes 786440 | tf_op jit(solution)/shard_map/ppermute | solution.py:33
  37.4 0.1 collective-permute-done.6
  37.5 1.5 %collective-permute-start.7 = (bf16[1024,256]{1,0:T(8,128)(2,1)S(1)}, bf16[1024,256]{1,0:T(8,128)(2,1)S(1)}, u32[]{:S(2)}, u32[]{:S(2)}) collective-permute-start(bf16[1024,256]{1,0:T(8,128)(2,1)S(1)} %pad_maximum_fusion.refs_0_), channel_id=1, source_target_pairs={{0,48},{16,32},{32,16},{48,0},{1,49},{17,33},{33,17},{49,1},{2,50}... | collective-permute-start | bytes 1572872 | tf_op jit(solution)/shard_map/ppermute | solution.py:33
  39.0 0.0 collective-permute-done.9
  39.1 2.3 %collective-permute-start.10 = (bf16[1024,256]{1,0:T(8,128)(2,1)S(1)}, bf16[1024,256]{1,0:T(8,128)(2,1)S(1)}, u32[]{:S(2)}, u32[]{:S(2)}) collective-permute-start(bf16[1024,256]{1,0:T(8,128)(2,1)S(1)} %pad_maximum_fusion.1.refs_2_), channel_id=1, source_target_pairs={{0,192},{64,128},{128,64},{192,0},{1,193},{65,129},{129,65},{193,1... | collective-permute-start | bytes 1572872 | tf_op jit(solution)/shard_map/ppermute | solution.py:33
  41.3 0.0 collective-permute-done.12
  41.4 1.9 %collective-permute-start.13 = (bf16[1024,256]{1,0:T(8,128)(2,1)S(1)}, bf16[1024,256]{1,0:T(8,128)(2,1)S(1)}, u32[]{:S(2)}, u32[]{:S(2)}) collective-permute-start(bf16[1024,256]{1,0:T(8,128)(2,1)S(1)} %pad_maximum_fusion.2.refs_4_), channel_id=1, source_target_pairs={{0,16},{16,0},{32,48},{48,32},{1,17},{17,1},{33,49},{49,33},{2,18}... | collective-permute-start | bytes 1572872 | tf_op jit(solution)/shard_map/ppermute | solution.py:33
  43.3 2.8 %collective-permute-done.15 = bf16[512,256]{1,0:T(8,128)(2,1)S(1)} collective-permute-done((bf16[512,256]{1,0:T(8,128)(2,1)S(1)}, bf16[512,256]{1,0:T(8,128)(2,1)S(1)}, u32[]{:S(2)}, u32[]{:S(2)}) %collective-permute-start.15) | collective-permute-done | bytes 262176 | tf_op jit(solution)/shard_map/ppermute | solution.py:33
  46.2 0.4 collective-permute-start.16
  46.5 3.5 %collective-permute-done.4.t2 = bf16[256,1024]{1,0:T(8,128)(2,1)} collective-permute-done((bf16[256,1024]{1,0:T(8,128)(2,1)S(1)}, bf16[256,1024]{1,0:T(8,128)(2,1)}, u32[]{:S(2)}, u32[]{:S(2)}) %collective-permute-start.4) | collective-permute-done | bytes 524320 | tf_op jit(solution)/shard_map/ppermute | solution.py:33
  50.0 2.2 %collective-permute-start.18 = (bf16[1024,256]{1,0:T(8,128)(2,1)S(1)}, bf16[1024,256]{1,0:T(8,128)(2,1)}, u32[]{:S(2)}, u32[]{:S(2)}) collective-permute-start(bf16[1024,256]{1,0:T(8,128)(2,1)S(1)} %pad_maximum_fusion.refs_0_), channel_id=1, source_target_pairs={{0,192},{64,128},{128,64},{192,0},{1,193},{65,129},{129,65},{193,1... | collective-permute-start | bytes 1572872 | tf_op jit(solution)/shard_map/ppermute | solution.py:33
  52.2 1.3 %collective-permute-done.7.refs_1_ = bf16[1024,256]{1,0:T(8,128)(2,1)S(1)} collective-permute-done((bf16[1024,256]{1,0:T(8,128)(2,1)S(1)}, bf16[1024,256]{1,0:T(8,128)(2,1)S(1)}, u32[]{:S(2)}, u32[]{:S(2)}) %collective-permute-start.7) | collective-permute-done | bytes 524320 | tf_op jit(solution)/shard_map/ppermute | solution.py:33
  53.4 1.9 %collective-permute-start.19 = (bf16[1024,256]{1,0:T(8,128)(2,1)S(1)}, bf16[1024,256]{1,0:T(8,128)(2,1)}, u32[]{:S(2)}, u32[]{:S(2)}) collective-permute-start(bf16[1024,256]{1,0:T(8,128)(2,1)S(1)} %pad_maximum_fusion.1.refs_2_), channel_id=1, source_target_pairs={{0,48},{16,32},{32,16},{48,0},{1,49},{17,33},{33,17},{49,1},{2,50}... | collective-permute-start | bytes 1572872 | tf_op jit(solution)/shard_map/ppermute | solution.py:33
  55.3 0.7 collective-permute-start.20
  56.0 0.8 copy-done.9
  56.9 0.0 collective-permute-start.17
  57.5 0.1 collective-permute-start.21
  57.6 0.1 multiply_reduce_fusion
  57.7 0.1 reshape.40
  57.8 0.7 broadcast_in_dim.21
  58.5 1.0 %concatenate.39 = f32[64,1152]{1,0:T(8,128)S(1)} concatenate(f32[64,64]{1,0:T(8,128)S(1)} %reshape.40, f32[64,64]{1,0:T(8,128)S(1)} %broadcast_in_dim.18, f32[64,1024]{1,0:T(8,128)} %broadcast_in_dim.21), dimensions={1} | concatenate | bytes 589824 | tf_op jit(solution)/shard_map/concatenate | solution.py:252
  59.5 0.9 all_to_all.8
  60.5 8.5 %all-to-all-start = ((f32[64,1,1152]{2,1,0:T(1,128)}), f32[64,1,1152]{2,1,0:T(1,128)S(1)}, u32[]{:S(2)}, u32[]{:S(2)}) async-start(f32[64,1,1152]{2,1,0:T(1,128)} %all_to_all.8), calls=%async_computation | async-start | bytes 589824 | tf_op jit(solution)/shard_map/all_to_all | solution.py:260
  69.0 3.0 %collective-permute-start.22 = (bf16[1024,256]{1,0:T(8,128)(2,1)}, bf16[1024,256]{1,0:T(8,128)(2,1)}, u32[]{:S(2)}, u32[]{:S(2)}) collective-permute-start(bf16[1024,256]{1,0:T(8,128)(2,1)} %copy-done.3), channel_id=1, source_target_pairs={{0,192},{64,128},{128,64},{192,0},{1,193},{65,129},{129,65},{193,1... | collective-permute-start | bytes 1572872 | tf_op jit(solution)/shard_map/ppermute | solution.py:33
  72.0 0.0 collective-permute-done.19.refs_2_
  72.0 2.8 %collective-permute-start.23 = (bf16[1024,256]{1,0:T(8,128)(2,1)}, bf16[1024,256]{1,0:T(8,128)(2,1)}, u32[]{:S(2)}, u32[]{:S(2)}) collective-permute-start(bf16[1024,256]{1,0:T(8,128)(2,1)} %copy-done.5), channel_id=1, source_target_pairs={{0,48},{16,32},{32,16},{48,0},{1,49},{17,33},{33,17},{49,1},{2,50}... | collective-permute-start | bytes 1572872 | tf_op jit(solution)/shard_map/ppermute | solution.py:33
  74.7 0.1 collective-permute-start.24
  74.9 0.2 collective-permute-start.25
  75.1 0.1 pad_add_fusion.at_ref
  75.2 2.1 %member_tokens.1 = (bf16[4,256,1024]{2,1,0:T(8,128)(2,1)S(1)}, f32[256,8]{1,0:T(8,128)S(1)}) custom-call(s32[1]{0:T(128)} %bitcast.2.at_ref, bf16[256,1024]{1,0:T(8,128)(2,1)S(1)} %bitcast.16, bf16[256,1024]{1,0:T(8,128)(2,1)S(1)} %collective-permute-done.3.t1, bf16[256,1024]{1,0:T(8,128)(2,1)} %collective-permute-done.4.t2, ...), custom_call_target="tpu_custom_call" | custom-call | bytes 8388608 | tf_op jit(solution)/shard_map/member_tokens/pallas_call | solution.py:237
  77.4 4.0 %products.2.refs_0_ = f32[256,1024]{1,0:T(8,128)S(1)} custom-call(s32[2]{0:T(128)S(1)} %pad_add_fusion.at_ref, bf16[4,256,1024]{2,1,0:T(8,128)(2,1)S(1)} %get-tuple-element.19.tokens_ref, bf16[1024,256]{1,0:T(8,128)(2,1)S(1)} %pad_maximum_fusion.refs_0_, bf16[1024,256]{1,0:T(8,128)(2,1)S(1)} %copy-done.4, bf16[1024,256]{1,0:T(8,128)(2,1)S(1)} %pad_maximum_fusion.1.refs_2_, ...), custom_call_target="tpu_custom_call" | custom-call | flops 1073741824 | bytes 8388608 | tf_op jit(solution)/shard_map/products/pallas_call | solution.py:141
  81.4 0.0 collective-permute-done.21.refs_4_
  81.4 3.6 %products.3.sum_ref = f32[256,1024]{1,0:T(8,128)S(1)} custom-call(s32[2]{0:T(128)S(1)} %pad_add_fusion.at_ref, bf16[4,256,1024]{2,1,0:T(8,128)(2,1)S(1)} %get-tuple-element.19.tokens_ref, f32[256,1024]{1,0:T(8,128)S(1)} %products.2.refs_0_, bf16[1024,256]{1,0:T(8,128)(2,1)} %collective-permute-done.18.refs_1_, ...), custom_call_target="tpu_custom_call" | custom-call | flops 536870912 | bytes 8388608 | tf_op jit(solution)/shard_map/products/pallas_call | solution.py:141
  85.1 2.1 %collective-permute-done.22.refs_0_ = bf16[1024,256]{1,0:T(8,128)(2,1)} collective-permute-done((bf16[1024,256]{1,0:T(8,128)(2,1)}, bf16[1024,256]{1,0:T(8,128)(2,1)}, u32[]{:S(2)}, u32[]{:S(2)}) %collective-permute-start.22) | collective-permute-done | bytes 524320 | tf_op jit(solution)/shard_map/ppermute | solution.py:33
  87.2 0.9 collective-permute-done.23.refs_1_
  88.0 0.8 collective-permute-done.24.refs_2_
  88.8 0.0 collective-permute-done.25.refs_3_
  88.8 6.3 %values_readout.1 = bf16[256,1024]{1,0:T(8,128)(2,1)} custom-call(s32[2]{0:T(128)S(1)} %pad_add_fusion.at_ref, bf16[4,256,1024]{2,1,0:T(8,128)(2,1)S(1)} %get-tuple-element.19.tokens_ref, f32[256,1024]{1,0:T(8,128)S(1)} %products.3.sum_ref, f32[256,8]{1,0:T(8,128)S(1)} %get-tuple-element.20.projected_ref, bf16[1,1024]{1,0:T(2,128)(2,1)S(1)} %copy-done.12, ...), custom_call_target="tpu_custom_call" | custom-call | flops 536870912 | bytes 12582912 | tf_op jit(solution)/shard_map/values_readout/pallas_call | solution.py:276
  95.1 1.1 %fusion = f32[64,1024]{1,0:T(8,128)} fusion(f32[64,1152]{1,0:T(8,128)S(1)} %bitcast.18), kind=kOutput, calls=%fused_computation.5 | convolution fusion | flops 50331648 | bytes 557056 | tf_op jit(solution)/shard_map/dot_general | solution.py:263
  (45 shorter events, 0.4 us)
Async XLA Ops:
  0.6 18.3 %collective-permute-start.3 = (bf16[256,1024]{1,0:T(8,128)(2,1)}, bf16[256,1024]{1,0:T(8,128)(2,1)S(1)}, u32[]{:S(2)}, u32[]{:S(2)}) collective-permute-start(bf16[256,1024]{1,0:T(8,128)(2,1)} %bitcast.14), channel_id=1, source_target_pairs={{0,1},{1,0},{2,3},{3,2},{4,5},{5,4},{6,7},{7,6},{8,9},{9,8},{10,11... | collective-permute-start | bytes 1572872 | tf_op jit(solution)/shard_map/ppermute | solution.py:33
  0.7 18.1 %collective-permute-start = (bf16[64,1024]{1,0:T(8,128)(2,1)}, bf16[64,1024]{1,0:T(8,128)(2,1)S(1)}, u32[]{:S(2)}, u32[]{:S(2)}) collective-permute-start(bf16[64,1024]{1,0:T(8,128)(2,1)} %param.13), channel_id=1, source_target_pairs={{4,0},{8,4},{12,8},{0,12},{5,1},{9,5},{13,9},{1,13},{6,2},{10,6},{... | collective-permute-start | bytes 393224 | tf_op jit(solution)/shard_map/ppermute | solution.py:38
  2.7 16.2 %collective-permute-start.1 = (bf16[64,1024]{1,0:T(8,128)(2,1)}, bf16[64,1024]{1,0:T(8,128)(2,1)S(1)}, u32[]{:S(2)}, u32[]{:S(2)}) collective-permute-start(bf16[64,1024]{1,0:T(8,128)(2,1)} %param.13), channel_id=1, source_target_pairs={{12,0},{0,4},{4,8},{8,12},{13,1},{1,5},{5,9},{9,13},{14,2},{2,6},{... | collective-permute-start | bytes 393224 | tf_op jit(solution)/shard_map/ppermute | solution.py:38
  2.8 16.1 %collective-permute-start.2 = (bf16[64,1024]{1,0:T(8,128)(2,1)}, bf16[64,1024]{1,0:T(8,128)(2,1)S(1)}, u32[]{:S(2)}, u32[]{:S(2)}) collective-permute-start(bf16[64,1024]{1,0:T(8,128)(2,1)} %param.13), channel_id=1, source_target_pairs={{8,0},{12,4},{0,8},{4,12},{9,1},{13,5},{1,9},{5,13},{10,2},{14,6},... | collective-permute-start | bytes 393224 | tf_op jit(solution)/shard_map/ppermute | solution.py:38
  7.9 14.3 %copy-start.2 = (bf16[1,256,1024]{2,1,0:T(8,128)(2,1)S(1)}, bf16[1,256,1024]{2,1,0:T(8,128)(2,1)}, u32[]{:S(2)}) copy-start(bf16[1,256,1024]{2,1,0:T(8,128)(2,1)} %param.9) | copy-start | bytes 1572868
  19.0 11.9 %collective-permute-start.5 = (bf16[256,256]{1,0:T(8,128)(2,1)S(1)}, bf16[256,256]{1,0:T(8,128)(2,1)S(1)}, u32[]{:S(2)}, u32[]{:S(2)}) collective-permute-start(bf16[256,256]{1,0:T(8,128)(2,1)S(1)} %get-tuple-element.27), channel_id=1, source_target_pairs={{0,16},{16,0},{32,48},{48,32},{1,17},{17,1},{33,49},{49,33},{2,18}... | collective-permute-start | bytes 393224 | tf_op jit(solution)/shard_map/ppermute | solution.py:33
  20.6 11.1 %collective-permute-start.8 = (bf16[256,256]{1,0:T(8,128)(2,1)S(1)}, bf16[256,256]{1,0:T(8,128)(2,1)S(1)}, u32[]{:S(2)}, u32[]{:S(2)}) collective-permute-start(bf16[256,256]{1,0:T(8,128)(2,1)S(1)} %get-tuple-element.26), channel_id=1, source_target_pairs={{0,64},{64,0},{128,192},{192,128},{1,65},{65,1},{129,193},{193,129... | collective-permute-start | bytes 393224 | tf_op jit(solution)/shard_map/ppermute | solution.py:33
  22.2 27.8 %collective-permute-start.4 = (bf16[256,1024]{1,0:T(8,128)(2,1)S(1)}, bf16[256,1024]{1,0:T(8,128)(2,1)}, u32[]{:S(2)}, u32[]{:S(2)}) collective-permute-start(bf16[256,1024]{1,0:T(8,128)(2,1)S(1)} %bitcast.15), channel_id=1, source_target_pairs={{0,2},{2,0},{1,3},{3,1},{4,6},{6,4},{5,7},{7,5},{8,10},{10,8},{9,1... | collective-permute-start | bytes 1572872 | tf_op jit(solution)/shard_map/ppermute | solution.py:33
  26.7 6.2 %collective-permute-start.11 = (bf16[256,256]{1,0:T(8,128)(2,1)S(1)}, bf16[256,256]{1,0:T(8,128)(2,1)S(1)}, u32[]{:S(2)}, u32[]{:S(2)}) collective-permute-start(bf16[256,256]{1,0:T(8,128)(2,1)S(1)} %get-tuple-element.25), channel_id=1, source_target_pairs={{0,48},{16,32},{32,16},{48,0},{1,49},{17,33},{33,17},{49,1},{2,50}... | collective-permute-start | bytes 393224 | tf_op jit(solution)/shard_map/ppermute | solution.py:33
  28.8 6.8 %collective-permute-start.14 = (bf16[256,256]{1,0:T(8,128)(2,1)S(1)}, bf16[256,256]{1,0:T(8,128)(2,1)S(1)}, u32[]{:S(2)}, u32[]{:S(2)}) collective-permute-start(bf16[256,256]{1,0:T(8,128)(2,1)S(1)} %get-tuple-element.24), channel_id=1, source_target_pairs={{0,192},{64,128},{128,64},{192,0},{1,193},{65,129},{129,65},{193,1... | collective-permute-start | bytes 393224 | tf_op jit(solution)/shard_map/ppermute | solution.py:33
  31.0 6.5 %collective-permute-start.6 = (bf16[512,256]{1,0:T(8,128)(2,1)S(1)}, bf16[512,256]{1,0:T(8,128)(2,1)S(1)}, u32[]{:S(2)}, u32[]{:S(2)}) collective-permute-start(bf16[512,256]{1,0:T(8,128)(2,1)S(1)} %pad_maximum_fusion.4), channel_id=1, source_target_pairs={{0,64},{64,0},{128,192},{192,128},{1,65},{65,1},{129,193},{193,129... | collective-permute-start | bytes 786440 | tf_op jit(solution)/shard_map/ppermute | solution.py:33
  31.7 7.3 %collective-permute-start.9 = (bf16[512,256]{1,0:T(8,128)(2,1)S(1)}, bf16[512,256]{1,0:T(8,128)(2,1)S(1)}, u32[]{:S(2)}, u32[]{:S(2)}) collective-permute-start(bf16[512,256]{1,0:T(8,128)(2,1)S(1)} %pad_maximum_fusion.5), channel_id=1, source_target_pairs={{0,16},{16,0},{32,48},{48,32},{1,17},{17,1},{33,49},{49,33},{2,18}... | collective-permute-start | bytes 786440 | tf_op jit(solution)/shard_map/ppermute | solution.py:33
  32.9 8.5 %collective-permute-start.12 = (bf16[512,256]{1,0:T(8,128)(2,1)S(1)}, bf16[512,256]{1,0:T(8,128)(2,1)S(1)}, u32[]{:S(2)}, u32[]{:S(2)}) collective-permute-start(bf16[512,256]{1,0:T(8,128)(2,1)S(1)} %pad_maximum_fusion.6), channel_id=1, source_target_pairs={{0,192},{64,128},{128,64},{192,0},{1,193},{65,129},{129,65},{193,1... | collective-permute-start | bytes 786440 | tf_op jit(solution)/shard_map/ppermute | solution.py:33
  35.6 22.1 %copy-start.11 = (bf16[1,4096]{1,0:T(2,128)(2,1)S(1)}, bf16[1,4096]{1,0:T(2,128)(2,1)}, u32[]{:S(2)}) copy-start(bf16[1,4096]{1,0:T(2,128)(2,1)} %param.14) | copy-start | bytes 24580
  35.6 22.2 %copy-start.12 = (bf16[1,1024]{1,0:T(2,128)(2,1)S(1)}, bf16[1,1024]{1,0:T(2,128)(2,1)}, u32[]{:S(2)}) copy-start(bf16[1,1024]{1,0:T(2,128)(2,1)} %noise_ref.1) | copy-start | bytes 6148
  35.6 10.5 %collective-permute-start.15 = (bf16[512,256]{1,0:T(8,128)(2,1)S(1)}, bf16[512,256]{1,0:T(8,128)(2,1)S(1)}, u32[]{:S(2)}, u32[]{:S(2)}) collective-permute-start(bf16[512,256]{1,0:T(8,128)(2,1)S(1)} %pad_maximum_fusion.7), channel_id=1, source_target_pairs={{0,48},{16,32},{32,16},{48,0},{1,49},{17,33},{33,17},{49,1},{2,50}... | collective-permute-start | bytes 786440 | tf_op jit(solution)/shard_map/ppermute | solution.py:33
  37.5 15.9 %collective-permute-start.7 = (bf16[1024,256]{1,0:T(8,128)(2,1)S(1)}, bf16[1024,256]{1,0:T(8,128)(2,1)S(1)}, u32[]{:S(2)}, u32[]{:S(2)}) collective-permute-start(bf16[1024,256]{1,0:T(8,128)(2,1)S(1)} %pad_maximum_fusion.refs_0_), channel_id=1, source_target_pairs={{0,48},{16,32},{32,16},{48,0},{1,49},{17,33},{33,17},{49,1},{2,50}... | collective-permute-start | bytes 1572872 | tf_op jit(solution)/shard_map/ppermute | solution.py:33
  39.1 16.3 %collective-permute-start.10 = (bf16[1024,256]{1,0:T(8,128)(2,1)S(1)}, bf16[1024,256]{1,0:T(8,128)(2,1)S(1)}, u32[]{:S(2)}, u32[]{:S(2)}) collective-permute-start(bf16[1024,256]{1,0:T(8,128)(2,1)S(1)} %pad_maximum_fusion.1.refs_2_), channel_id=1, source_target_pairs={{0,192},{64,128},{128,64},{192,0},{1,193},{65,129},{129,65},{193,1... | collective-permute-start | bytes 1572872 | tf_op jit(solution)/shard_map/ppermute | solution.py:33
  41.4 14.6 %collective-permute-start.13 = (bf16[1024,256]{1,0:T(8,128)(2,1)S(1)}, bf16[1024,256]{1,0:T(8,128)(2,1)S(1)}, u32[]{:S(2)}, u32[]{:S(2)}) collective-permute-start(bf16[1024,256]{1,0:T(8,128)(2,1)S(1)} %pad_maximum_fusion.2.refs_4_), channel_id=1, source_target_pairs={{0,16},{16,0},{32,48},{48,32},{1,17},{17,1},{33,49},{49,33},{2,18}... | collective-permute-start | bytes 1572872 | tf_op jit(solution)/shard_map/ppermute | solution.py:33
  46.2 9.9 %collective-permute-start.16 = (bf16[1024,256]{1,0:T(8,128)(2,1)S(1)}, bf16[1024,256]{1,0:T(8,128)(2,1)S(1)}, u32[]{:S(2)}, u32[]{:S(2)}) collective-permute-start(bf16[1024,256]{1,0:T(8,128)(2,1)S(1)} %pad_maximum_fusion.3.refs_6_), channel_id=1, source_target_pairs={{0,64},{64,0},{128,192},{192,128},{1,65},{65,1},{129,193},{193,129... | collective-permute-start | bytes 1572872 | tf_op jit(solution)/shard_map/ppermute | solution.py:33
  50.0 19.0 %collective-permute-start.18 = (bf16[1024,256]{1,0:T(8,128)(2,1)S(1)}, bf16[1024,256]{1,0:T(8,128)(2,1)}, u32[]{:S(2)}, u32[]{:S(2)}) collective-permute-start(bf16[1024,256]{1,0:T(8,128)(2,1)S(1)} %pad_maximum_fusion.refs_0_), channel_id=1, source_target_pairs={{0,192},{64,128},{128,64},{192,0},{1,193},{65,129},{129,65},{193,1... | collective-permute-start | bytes 1572872 | tf_op jit(solution)/shard_map/ppermute | solution.py:33
  53.4 4.1 %copy-start.3 = (bf16[1024,256]{1,0:T(8,128)(2,1)}, bf16[1024,256]{1,0:T(8,128)(2,1)S(1)}, u32[]{:S(2)}) copy-start(bf16[1024,256]{1,0:T(8,128)(2,1)S(1)} %collective-permute-done.7.refs_1_) | copy-start | bytes 1572868
  53.4 18.5 %collective-permute-start.19 = (bf16[1024,256]{1,0:T(8,128)(2,1)S(1)}, bf16[1024,256]{1,0:T(8,128)(2,1)}, u32[]{:S(2)}, u32[]{:S(2)}) collective-permute-start(bf16[1024,256]{1,0:T(8,128)(2,1)S(1)} %pad_maximum_fusion.1.refs_2_), channel_id=1, source_target_pairs={{0,48},{16,32},{32,16},{48,0},{1,49},{17,33},{33,17},{49,1},{2,50}... | collective-permute-start | bytes 1572872 | tf_op jit(solution)/shard_map/ppermute | solution.py:33
  55.3 2.2 %copy-start.5 = (bf16[1024,256]{1,0:T(8,128)(2,1)}, bf16[1024,256]{1,0:T(8,128)(2,1)S(1)}, u32[]{:S(2)}) copy-start(bf16[1024,256]{1,0:T(8,128)(2,1)S(1)} %collective-permute-done.10.refs_3_) | copy-start | bytes 1572868
  55.3 19.4 %collective-permute-start.20 = (bf16[1024,256]{1,0:T(8,128)(2,1)S(1)}, bf16[1024,256]{1,0:T(8,128)(2,1)}, u32[]{:S(2)}, u32[]{:S(2)}) collective-permute-start(bf16[1024,256]{1,0:T(8,128)(2,1)S(1)} %pad_maximum_fusion.2.refs_4_), channel_id=1, source_target_pairs={{0,64},{64,0},{128,192},{192,128},{1,65},{65,1},{129,193},{193,129... | collective-permute-start | bytes 1572872 | tf_op jit(solution)/shard_map/ppermute | solution.py:33
  56.0 1.6 %copy-start.7 = (bf16[1024,256]{1,0:T(8,128)(2,1)}, bf16[1024,256]{1,0:T(8,128)(2,1)S(1)}, u32[]{:S(2)}) copy-start(bf16[1024,256]{1,0:T(8,128)(2,1)S(1)} %collective-permute-done.13.refs_5_) | copy-start | bytes 1572868
  56.0 0.8 copy-start.9
  56.9 18.0 %collective-permute-start.17 = (bf16[256,1024]{1,0:T(8,128)(2,1)}, bf16[256,1024]{1,0:T(8,128)(2,1)}, u32[]{:S(2)}, u32[]{:S(2)}) collective-permute-start(bf16[256,1024]{1,0:T(8,128)(2,1)} %collective-permute-done.4.t2), channel_id=1, source_target_pairs={{0,1},{1,0},{2,3},{3,2},{4,5},{5,4},{6,7},{7,6},{8,9},{9,8},{10,11... | collective-permute-start | bytes 1572872 | tf_op jit(solution)/shard_map/ppermute | solution.py:33
  57.5 23.9 %collective-permute-start.21 = (bf16[1024,256]{1,0:T(8,128)(2,1)S(1)}, bf16[1024,256]{1,0:T(8,128)(2,1)}, u32[]{:S(2)}, u32[]{:S(2)}) collective-permute-start(bf16[1024,256]{1,0:T(8,128)(2,1)S(1)} %pad_maximum_fusion.3.refs_6_), channel_id=1, source_target_pairs={{0,16},{16,0},{32,48},{48,32},{1,17},{17,1},{33,49},{49,33},{2,18}... | collective-permute-start | bytes 1572872 | tf_op jit(solution)/shard_map/ppermute | solution.py:33
  60.5 34.6 %all-to-all-start = ((f32[64,1,1152]{2,1,0:T(1,128)}), f32[64,1,1152]{2,1,0:T(1,128)S(1)}, u32[]{:S(2)}, u32[]{:S(2)}) async-start(f32[64,1,1152]{2,1,0:T(1,128)} %all_to_all.8), calls=%async_computation | async-start | bytes 589824 | tf_op jit(solution)/shard_map/all_to_all | solution.py:260
  69.0 18.2 %collective-permute-start.22 = (bf16[1024,256]{1,0:T(8,128)(2,1)}, bf16[1024,256]{1,0:T(8,128)(2,1)}, u32[]{:S(2)}, u32[]{:S(2)}) collective-permute-start(bf16[1024,256]{1,0:T(8,128)(2,1)} %copy-done.3), channel_id=1, source_target_pairs={{0,192},{64,128},{128,64},{192,0},{1,193},{65,129},{129,65},{193,1... | collective-permute-start | bytes 1572872 | tf_op jit(solution)/shard_map/ppermute | solution.py:33
  72.0 16.0 %collective-permute-start.23 = (bf16[1024,256]{1,0:T(8,128)(2,1)}, bf16[1024,256]{1,0:T(8,128)(2,1)}, u32[]{:S(2)}, u32[]{:S(2)}) collective-permute-start(bf16[1024,256]{1,0:T(8,128)(2,1)} %copy-done.5), channel_id=1, source_target_pairs={{0,48},{16,32},{32,16},{48,0},{1,49},{17,33},{33,17},{49,1},{2,50}... | collective-permute-start | bytes 1572872 | tf_op jit(solution)/shard_map/ppermute | solution.py:33
  74.7 14.0 %collective-permute-start.24 = (bf16[1024,256]{1,0:T(8,128)(2,1)}, bf16[1024,256]{1,0:T(8,128)(2,1)}, u32[]{:S(2)}, u32[]{:S(2)}) collective-permute-start(bf16[1024,256]{1,0:T(8,128)(2,1)} %copy-done.7), channel_id=1, source_target_pairs={{0,64},{64,0},{128,192},{192,128},{1,65},{65,1},{129,193},{193,129... | collective-permute-start | bytes 1572872 | tf_op jit(solution)/shard_map/ppermute | solution.py:33
  74.9 13.9 %collective-permute-start.25 = (bf16[1024,256]{1,0:T(8,128)(2,1)}, bf16[1024,256]{1,0:T(8,128)(2,1)}, u32[]{:S(2)}, u32[]{:S(2)}) collective-permute-start(bf16[1024,256]{1,0:T(8,128)(2,1)} %copy-done.9), channel_id=1, source_target_pairs={{0,16},{16,0},{32,48},{48,32},{1,17},{17,1},{33,49},{49,33},{2,18}... | collective-permute-start | bytes 1572872 | tf_op jit(solution)/shard_map/ppermute | solution.py:33
  75.1 2.2 %copy-start.4 = (bf16[1024,256]{1,0:T(8,128)(2,1)S(1)}, bf16[1024,256]{1,0:T(8,128)(2,1)}, u32[]{:S(2)}) copy-start(bf16[1024,256]{1,0:T(8,128)(2,1)} %copy-done.3) | copy-start | bytes 1572868
  75.1 2.2 %copy-start.6 = (bf16[1024,256]{1,0:T(8,128)(2,1)S(1)}, bf16[1024,256]{1,0:T(8,128)(2,1)}, u32[]{:S(2)}) copy-start(bf16[1024,256]{1,0:T(8,128)(2,1)} %copy-done.5) | copy-start | bytes 1572868
  75.1 2.2 %copy-start.8 = (bf16[1024,256]{1,0:T(8,128)(2,1)S(1)}, bf16[1024,256]{1,0:T(8,128)(2,1)}, u32[]{:S(2)}) copy-start(bf16[1024,256]{1,0:T(8,128)(2,1)} %copy-done.7) | copy-start | bytes 1572868
  75.1 2.2 %copy-start.10 = (bf16[1024,256]{1,0:T(8,128)(2,1)S(1)}, bf16[1024,256]{1,0:T(8,128)(2,1)}, u32[]{:S(2)}) copy-start(bf16[1024,256]{1,0:T(8,128)(2,1)} %copy-done.9) | copy-start | bytes 1572868
  81.4 7.4 %copy-start = (bf16[16,256,256]{2,1,0:T(8,128)(2,1)S(1)}, bf16[16,256,256]{2,1,0:T(8,128)(2,1)}, u32[]{:S(2)}) copy-start(bf16[16,256,256]{2,1,0:T(8,128)(2,1)} %get-tuple-element.21.high_ref) | copy-start | bytes 6291460
  81.4 7.4 %copy-start.1 = (bf16[16,256,256]{2,1,0:T(8,128)(2,1)S(1)}, bf16[16,256,256]{2,1,0:T(8,128)(2,1)}, u32[]{:S(2)}) copy-start(bf16[16,256,256]{2,1,0:T(8,128)(2,1)} %get-tuple-element.22.low_ref) | copy-start | bytes 6291460

commit v5 on v4

--- a/solution.py
+++ b/solution.py
@@ -63,7 +63,12 @@
     projected_ref[...] = total
 
 
-def score_kernel(live_ref, recept_ref, keys_ref, decay_ref, high_ref, low_ref):
+def halves(value):
+    high = value.astype(BF16)
+    return high, (value - high.astype(F32)).astype(BF16)
+
+
+def score_kernel(live_ref, recept_ref, keys_ref, decay_ref, out_ref):
     length = recept_ref.shape[0]
     live = live_ref[0]
     row = lax.broadcasted_iota(jnp.int32, (length, LANES), 0)
@@ -76,30 +81,34 @@
     ).astype(F32).astype(BF16)
     summed = jnp.dot(lower, decay, preferred_element_type=F32)
     lane = lax.broadcasted_iota(jnp.int32, (SPAN, LANES), 1)
+    across = (((1,), (1,)), ((), ()))
     for chunk in range(length // SPAN):
         first, last = chunk * SPAN, (chunk + 1) * SPAN
         base = summed[first - 1 : first] if chunk else jnp.zeros((1, LANES), F32)
         grown = recept_ref[first:last].astype(F32) * jnp.exp(summed[first:last] - base)
-        shrunk = keys[:last] * jnp.exp(base - summed[:last])
+        shrunk_high, shrunk_low = halves(keys[:last] * jnp.exp(base - summed[:last]))
         both = jnp.concatenate(
             [jnp.where(lane < HEAD, grown, 0.0), jnp.where(lane < HEAD, 0.0, grown)], 0
         )
+        both_high, both_low = halves(both)
         scores = lax.dot_general(
-            both, shrunk, (((1,), (1,)), ((), ())), precision=HIGHEST, preferred_element_type=F32
+            jnp.concatenate([both_high, both_low], 0), shrunk_high, across, preferred_element_type=F32
         )
+        scores = (
+            scores[: 2 * SPAN]
+            + scores[2 * SPAN :]
+            + lax.dot_general(both_high, shrunk_low, across, preferred_element_type=F32)
+        )
+        here = lax.broadcasted_iota(jnp.int32, (SPAN, last), 0) + first
+        there = lax.broadcasted_iota(jnp.int32, (SPAN, last), 1)
+        kept = (here >= there) & (here < live)
         for head in range(2):
-            mine = scores[head * SPAN : (head + 1) * SPAN]
-            here = lax.broadcasted_iota(jnp.int32, (SPAN, last), 0) + first
-            there = lax.broadcasted_iota(jnp.int32, (SPAN, last), 1)
-            mine = jnp.where((here >= there) & (here < live), mine, 0.0)
-            high = mine.astype(BF16)
-            low = (mine - high.astype(F32)).astype(BF16)
-            high_ref[head, first:last, :last] = high
-            low_ref[head, first:last, :last] = low
-            if last < length:
-                rest = jnp.zeros((SPAN, length - last), BF16)
-                high_ref[head, first:last, last:] = rest
-                low_ref[head, first:last, last:] = rest
+            parts = halves(jnp.where(kept, scores[head * SPAN : (head + 1) * SPAN], 0.0))
+            for i, part in enumerate(parts):
+                start = (2 * i + head) * length + first
+                out_ref[0, start : start + SPAN, :last] = part
+                if last < length:
+                    out_ref[0, start : start + SPAN, last:] = jnp.zeros((SPAN, length - last), BF16)
 
 
 def chunk_product(at_ref, tokens_ref, piece, blocks):
@@ -153,14 +162,15 @@
     )(at, tokens, *extra, *pieces)
 
 
-def readout_kernel(at_ref, tokens_ref, sum_ref, projected_ref, noise_ref, high_ref, low_ref, *refs):
+def readout_kernel(at_ref, tokens_ref, sum_ref, projected_ref, noise_ref, scores_ref, *refs):
     out_ref, held, sems = refs[-3:]
     wide = held.shape[2]
     copies = copies_of(refs[:-3], held, sems)
     projected = projected_ref[...][:, :1] * (
         SIGMA / math.sqrt(tokens_ref.shape[0] * tokens_ref.shape[2])
     )
-    lane = lax.broadcasted_iota(jnp.int32, (out_ref.shape[0], LANES), 1)
+    length = out_ref.shape[0]
+    lane = lax.broadcasted_iota(jnp.int32, (length, LANES), 1)
     for c, route in enumerate(ROUTES):
         where = slice(c * wide, (c + 1) * wide)
         total = sum_ref[:, where] + projected * noise_ref[:, where].astype(F32)
@@ -169,14 +179,14 @@
         values = total.astype(BF16)
         for pair in range(wide // LANES):
             mine = values[:, pair * LANES : (pair + 1) * LANES]
-            head = c * (wide // HEAD) + 2 * pair
-            outs = [
-                jnp.dot(high_ref[head + i], mine, preferred_element_type=F32)
-                + jnp.dot(low_ref[head + i], mine, preferred_element_type=F32)
-                for i in range(2)
-            ]
+            outs = jnp.dot(
+                scores_ref[c * (wide // LANES) + pair], mine, preferred_element_type=F32
+            )
+            outs = outs[: 2 * length] + outs[2 * length :]
             start = c * wide + pair * LANES
-            out_ref[:, start : start + LANES] = jnp.where(lane < HEAD, *outs).astype(BF16)
+            out_ref[:, start : start + LANES] = jnp.where(
+                lane < HEAD, outs[:length], outs[length:]
+            ).astype(BF16)
 
 
 def params(mib):
@@ -189,6 +199,21 @@
 
 def after(value, *others):
     return lax.optimization_barrier((value, others))[0]
+
+
+def score_heads(live_length, receptance, keys, log_decay):
+    length, width = receptance.shape
+    count = width // LANES
+    strip = pl.BlockSpec((length, LANES), lambda i: (0, i))
+    return pl.pallas_call(
+        score_kernel,
+        out_shape=jax.ShapeDtypeStruct((count, 4 * length, length), BF16),
+        grid=(count,),
+        in_specs=[SMEM, strip, strip, strip],
+        out_specs=pl.BlockSpec((1, 4 * length, length), lambda i: (i, 0, 0)),
+        cost_estimate=cost(0, 20 << 20),
+        name="decayed_scores",
+    )(live_length, receptance, keys, log_decay)
 
 
 def body(
@@ -201,25 +226,24 @@
     rows = value_weight.shape[0]
     wide = width // len(ROUTES)
 
-    heads = width // HEAD
-    strip = pl.BlockSpec((length, LANES), lambda i: (0, i))
-    square = pl.BlockSpec((2, length, length), lambda i: (i, 0, 0))
-    high, low = pl.pallas_call(
-        score_kernel,
-        out_shape=[jax.ShapeDtypeStruct((heads, length, length), BF16)] * 2,
-        grid=(width // LANES,),
-        in_specs=[SMEM, strip, strip, strip],
-        out_specs=[square, square],
-        cost_estimate=cost(0, 24 << 20),
-        name="decayed_scores",
-    )(live_length, receptance, keys, log_decay)
     z = lax.axis_index("z")
     near = jnp.zeros((SIDE * rows, width), BF16)
     for step in (0, 1, 3, 2):
         part = fetch(value_weight, "z", step) if step else value_weight
         near = lax.dynamic_update_slice(near, part, (lax.rem(z + step, SIDE) * rows, 0))
     mate = swap(tokens, "core", 1)
-    near, high, low, mate = lax.optimization_barrier((near, high, low, mate))
+    population = lax.axis_size(POP)
+    weighted = noise_in.astype(F32) * (utilities / math.sqrt(population))[:, None]
+    message = jnp.concatenate(
+        [
+            weighted.reshape(population, rows),
+            jnp.zeros((population, LANES - rows), F32),
+            jnp.broadcast_to(noise_out.astype(F32), (population, width)),
+        ],
+        1,
+    )
+    scores = score_heads(live_length, receptance, keys, log_decay)
+    near, mate, message, scores = lax.optimization_barrier((near, mate, message, scores))
 
     twin = swap(after(tokens, near), "twin", 1)
 
@@ -228,9 +252,14 @@
     for step in range(2):
         came = [swap(held[c], *LINKS[ROUTES[c][step]]) for c in chunks]
         held = [jnp.concatenate([a, b], 0) for a, b in zip(held, came)]
+    message = lax.all_to_all(
+        after(message, *held), POP, split_axis=0, concat_axis=0, tiled=True
+    )
     third = [swap(held[c], *LINKS[ROUTES[c][2]]) for c in chunks]
     fourth = [swap(held[c], *LINKS[ROUTES[c][3]]) for c in chunks]
-    last = [swap(third[c], *LINKS[ROUTES[c][3]]) for c in chunks]
+    ready = list(third)
+    ready[3] = after(third[3], message)
+    last = [swap(ready[c], *LINKS[ROUTES[c][3]]) for c in chunks]
 
     both = swap(after(twin, *third), "core", 1)
     tp = lax.axis_index(TP).reshape(1)
@@ -247,19 +276,6 @@
         name="member_tokens",
     )(tp, tokens, mate, twin, both, noise_in.reshape(4, 1, width))
 
-    population = lax.axis_size(POP)
-    weighted = noise_in.astype(F32) * (utilities / math.sqrt(population))[:, None]
-    message = jnp.concatenate(
-        [
-            weighted.reshape(population, rows),
-            jnp.zeros((population, LANES - rows), F32),
-            jnp.broadcast_to(noise_out.astype(F32), (population, width)),
-        ],
-        1,
-    )
-    message = lax.all_to_all(
-        after(message, *third), POP, split_axis=0, concat_axis=0, tiled=True
-    )
     update = lax.dot_general(
         message[:, :rows],
         message[:, LANES:],
@@ -276,7 +292,7 @@
     wkv_out = pl.pallas_call(
         readout_kernel,
         out_shape=jax.ShapeDtypeStruct((length, width), BF16),
-        in_specs=[SMEM] + [VMEM] * 6 + [ANY] * len(last),
+        in_specs=[SMEM] + [VMEM] * 5 + [ANY] * len(last),
         out_specs=VMEM,
         scratch_shapes=[
             pltpu.VMEM((len(last),) + last[0].shape, BF16),
@@ -285,7 +301,7 @@
         cost_estimate=cost(length * width * 2 * 1024, 12 << 20),
         compiler_params=params(20),
         name="values_readout",
-    )(at, all_tokens, total, projected, noise_out, high, low, *last)
+    )(at, all_tokens, total, projected, noise_out, scores, *last)
     return wkv_out.reshape(1, length, width), update
 
 

time: 97.3 us -> 93.3 us (0.959)
  starting transfers between devices: 50.3 us -> 44.5 us
  waiting for transfers between devices: 12.2 us -> 15.7 us
  local copies, waits for them, and re-layouts: 4.72 us -> 3.15 us
  other arithmetic: 0.34 us -> 1.75 us
  Pallas kernels: 25.4 us -> 24 us
    ppermute x23, starting transfers between devices: 34.6 us -> 30.3 us  [swap(): return lax.ppermute(array, axis, [(i, i ^ mask) for i in range(size)])]
    all_to_all x1, waiting for transfers between devices: 0.01 us -> 3.15 us  [body(): lax.all_to_all(after(message, *held), POP, split_axis=0, concat_axis=0, t...]
    all_to_all x1, starting transfers between devices: 8.52 us -> 7.05 us  [body(): lax.all_to_all(after(message, *held), POP, split_axis=0, concat_axis=0, t...]
    pallas_call x1, Pallas kernels: 9.26 us -> 7.87 us  [score_heads(): pl.pallas_call(score_kernel, out_shape=jax.ShapeDtypeStruct((count, 4 * l...]
  transfers between devices with their start and end apart: 27 -> 27, of which waited for: 9 -> 6; matrix products, arithmetic and copies ran while one was open for 3% -> 5% of each run, Pallas kernels for 26% -> 20%
where the time goes in v5:
time: 93.3 us; the launch traced here: 92.6 us
  starting transfers between devices  44.5 us (48%)
  Pallas kernels  24 us (26%)
  waiting for transfers between devices  15.7 us (17%)
  local copies, waits for them, and re-layouts  3.15 us (3%)
  between operations  2.34 us (3%)
  other arithmetic  1.75 us (2%)
  matrix products  1.12 us (1%)
    ppermute x23, starting transfers between devices, swap(): return lax.ppermute(array, axis, [(i, i ^ mask) for i in range(size)])  30.3 us
    ppermute x23, waiting for transfers between devices, swap(): return lax.ppermute(array, axis, [(i, i ^ mask) for i in range(size)])  12.5 us
    pallas_call x2, Pallas kernels, product(): pl.pallas_call(functools.partial(product_kernel, ways, before is not None...  8.38 us
    pallas_call x1, Pallas kernels, score_heads(): pl.pallas_call(score_kernel, out_shape=jax.ShapeDtypeStruct((count, 4 * l...  7.87 us
    ppermute x3, starting transfers between devices, fetch(): lax.ppermute(array, axis, [((i + step) % size, i) for i in range(size)])  7.17 us
    all_to_all x1, starting transfers between devices, body(): lax.all_to_all(after(message, *held), POP, split_axis=0, concat_axis=0, t...  7.05 us
    pallas_call x1, Pallas kernels, body(): pl.pallas_call(readout_kernel, out_shape=jax.ShapeDtypeStruct((length, wi...  5.76 us
    all_to_all x1, waiting for transfers between devices, body(): lax.all_to_all(after(message, *held), POP, split_axis=0, concat_axis=0, t...  3.15 us
  transfers between devices with their start and end apart: 27, of which 6 were waited for; matrix products, arithmetic and copies ran while one was open for 5% of the time, Pallas kernels for 20%

profile of v5, /device:TPU:32, one launch (start us, length us, event | category | flops | bytes accessed | tf_op | source)
XLA Modules:
  0.0 92.6 jit_solution(3899815472867598006)
XLA Ops:
  0.6 1.9 %collective-permute-start = (bf16[64,1024]{1,0:T(8,128)(2,1)}, bf16[64,1024]{1,0:T(8,128)(2,1)S(1)}, u32[]{:S(2)}, u32[]{:S(2)}) collective-permute-start(bf16[64,1024]{1,0:T(8,128)(2,1)} %param.13), channel_id=1, source_target_pairs={{4,0},{8,4},{12,8},{0,12},{5,1},{9,5},{13,9},{1,13},{6,2},{10,6},{... | collective-permute-start | bytes 393224 | tf_op jit(solution)/shard_map/ppermute | solution.py:38
  2.6 0.2 collective-permute-start.1
  2.7 5.1 %collective-permute-start.2 = (bf16[64,1024]{1,0:T(8,128)(2,1)}, bf16[64,1024]{1,0:T(8,128)(2,1)S(1)}, u32[]{:S(2)}, u32[]{:S(2)}) collective-permute-start(bf16[64,1024]{1,0:T(8,128)(2,1)} %param.13), channel_id=1, source_target_pairs={{8,0},{12,4},{0,8},{4,12},{9,1},{13,5},{1,9},{5,13},{10,2},{14,6},... | collective-permute-start | bytes 393224 | tf_op jit(solution)/shard_map/ppermute | solution.py:38
  7.8 0.0 collective-permute-start.3
  7.8 0.1 broadcast_in_dim.17
  7.9 0.9 constant_dynamic-update-slice_fusion.3
  9.4 0.8 multiply_reduce_fusion
  10.9 0.7 broadcast_in_dim.22
  11.6 0.1 reshape.35
  11.7 0.0 copy-start.1
  11.7 0.1 concatenate.31
  11.8 7.9 %decayed_scores.1.scores_ref = bf16[8,1024,256]{2,1,0:T(8,128)(2,1)} custom-call(s32[1]{0:T(128)S(6)} %copy.19.live_ref, bf16[256,1024]{1,0:T(8,128)(2,1)} %bitcast.19, bf16[256,1024]{1,0:T(8,128)(2,1)} %bitcast.20, bf16[256,1024]{1,0:T(8,128)(2,1)} %bitcast.21), custom_call_target="tpu_custom_call" | custom-call | bytes 20971520 | tf_op jit(solution)/shard_map/decayed_scores/pallas_call | solution.py:208
  19.6 0.0 collective-permute-done
  19.7 0.0 collective-permute-done.1
  19.7 0.0 collective-permute-done.2
  19.7 0.0 collective-permute-done.3.t1
  19.8 3.1 %collective-permute-start.14 = (bf16[256,256]{1,0:T(8,128)(2,1)S(1)}, bf16[256,256]{1,0:T(8,128)(2,1)S(1)}, u32[]{:S(2)}, u32[]{:S(2)}) collective-permute-start(bf16[256,256]{1,0:T(8,128)(2,1)S(1)} %get-tuple-element.22), channel_id=1, source_target_pairs={{0,192},{64,128},{128,64},{192,0},{1,193},{65,129},{129,65},{193,1... | collective-permute-start | bytes 393224 | tf_op jit(solution)/shard_map/ppermute | solution.py:33
  22.9 2.8 %collective-permute-start.11 = (bf16[256,256]{1,0:T(8,128)(2,1)S(1)}, bf16[256,256]{1,0:T(8,128)(2,1)S(1)}, u32[]{:S(2)}, u32[]{:S(2)}) collective-permute-start(bf16[256,256]{1,0:T(8,128)(2,1)S(1)} %get-tuple-element.23), channel_id=1, source_target_pairs={{0,48},{16,32},{32,16},{48,0},{1,49},{17,33},{33,17},{49,1},{2,50}... | collective-permute-start | bytes 393224 | tf_op jit(solution)/shard_map/ppermute | solution.py:33
  25.6 0.1 collective-permute-start.8
  25.8 0.2 collective-permute-start.5
  26.0 4.5 %collective-permute-start.4 = (bf16[256,1024]{1,0:T(8,128)(2,1)S(1)}, bf16[256,1024]{1,0:T(8,128)(2,1)}, u32[]{:S(2)}, u32[]{:S(2)}) collective-permute-start(bf16[256,1024]{1,0:T(8,128)(2,1)S(1)} %bitcast.15), channel_id=1, source_target_pairs={{0,2},{2,0},{1,3},{3,1},{4,6},{6,4},{5,7},{7,5},{8,10},{10,8},{9,1... | collective-permute-start | bytes 1572872 | tf_op jit(solution)/shard_map/ppermute | solution.py:33
  30.5 0.0 copy-start.2
  30.5 1.2 %collective-permute-start.15 = (bf16[512,256]{1,0:T(8,128)(2,1)S(1)}, bf16[512,256]{1,0:T(8,128)(2,1)S(1)}, u32[]{:S(2)}, u32[]{:S(2)}) collective-permute-start(bf16[512,256]{1,0:T(8,128)(2,1)S(1)} %pad_maximum_fusion.7), channel_id=1, source_target_pairs={{0,48},{16,32},{32,16},{48,0},{1,49},{17,33},{33,17},{49,1},{2,50}... | collective-permute-start | bytes 786440 | tf_op jit(solution)/shard_map/ppermute | solution.py:33
  31.8 1.2 %collective-permute-start.12 = (bf16[512,256]{1,0:T(8,128)(2,1)S(1)}, bf16[512,256]{1,0:T(8,128)(2,1)S(1)}, u32[]{:S(2)}, u32[]{:S(2)}) collective-permute-start(bf16[512,256]{1,0:T(8,128)(2,1)S(1)} %pad_maximum_fusion.6), channel_id=1, source_target_pairs={{0,192},{64,128},{128,64},{192,0},{1,193},{65,129},{129,65},{193,1... | collective-permute-start | bytes 786440 | tf_op jit(solution)/shard_map/ppermute | solution.py:33
  33.0 0.7 collective-permute-start.9
  33.7 0.0 collective-permute-done.5
  33.8 0.9 %collective-permute-start.6 = (bf16[512,256]{1,0:T(8,128)(2,1)S(1)}, bf16[512,256]{1,0:T(8,128)(2,1)S(1)}, u32[]{:S(2)}, u32[]{:S(2)}) collective-permute-start(bf16[512,256]{1,0:T(8,128)(2,1)S(1)} %pad_maximum_fusion.4), channel_id=1, source_target_pairs={{0,64},{64,0},{128,192},{192,128},{1,65},{65,1},{129,193},{193,129... | collective-permute-start | bytes 786440 | tf_op jit(solution)/shard_map/ppermute | solution.py:33
  34.7 4.7 %collective-permute-done.15 = bf16[512,256]{1,0:T(8,128)(2,1)S(1)} collective-permute-done((bf16[512,256]{1,0:T(8,128)(2,1)S(1)}, bf16[512,256]{1,0:T(8,128)(2,1)S(1)}, u32[]{:S(2)}, u32[]{:S(2)}) %collective-permute-start.15) | collective-permute-done | bytes 262176 | tf_op jit(solution)/shard_map/ppermute | solution.py:33
  39.5 1.7 %collective-permute-start.16 = (bf16[1024,256]{1,0:T(8,128)(2,1)S(1)}, bf16[1024,256]{1,0:T(8,128)(2,1)}, u32[]{:S(2)}, u32[]{:S(2)}) collective-permute-start(bf16[1024,256]{1,0:T(8,128)(2,1)S(1)} %pad_maximum_fusion.3.refs_6_), channel_id=1, source_target_pairs={{0,64},{64,0},{128,192},{192,128},{1,65},{65,1},{129,193},{193,129... | collective-permute-start | bytes 1572872 | tf_op jit(solution)/shard_map/ppermute | solution.py:33
  41.2 0.0 collective-permute-done.12
  41.3 0.6 collective-permute-start.13
  41.9 0.0 collective-permute-done.9
  41.9 0.5 collective-permute-start.10
  42.4 2.4 %collective-permute-start.7 = (bf16[1024,256]{1,0:T(8,128)(2,1)S(1)}, bf16[1024,256]{1,0:T(8,128)(2,1)}, u32[]{:S(2)}, u32[]{:S(2)}) collective-permute-start(bf16[1024,256]{1,0:T(8,128)(2,1)S(1)} %pad_maximum_fusion.refs_0_), channel_id=1, source_target_pairs={{0,48},{16,32},{32,16},{48,0},{1,49},{17,33},{33,17},{49,1},{2,50}... | collective-permute-start | bytes 1572872 | tf_op jit(solution)/shard_map/ppermute | solution.py:33
  44.9 0.9 all_to_all.8
  45.8 7.0 %all-to-all-start = ((f32[64,1,1152]{2,1,0:T(1,128)}), f32[64,1,1152]{2,1,0:T(1,128)}, u32[]{:S(2)}, u32[]{:S(2)}) async-start(f32[64,1,1152]{2,1,0:T(1,128)} %all_to_all.8), calls=%async_computation | async-start | bytes 589824 | tf_op jit(solution)/shard_map/all_to_all | solution.py:255
  52.8 1.5 %collective-permute-done.4.t2 = bf16[256,1024]{1,0:T(8,128)(2,1)} collective-permute-done((bf16[256,1024]{1,0:T(8,128)(2,1)S(1)}, bf16[256,1024]{1,0:T(8,128)(2,1)}, u32[]{:S(2)}, u32[]{:S(2)}) %collective-permute-start.4) | collective-permute-done | bytes 524320 | tf_op jit(solution)/shard_map/ppermute | solution.py:33
  54.4 1.7 %collective-permute-start.21 = (bf16[1024,256]{1,0:T(8,128)(2,1)S(1)}, bf16[1024,256]{1,0:T(8,128)(2,1)}, u32[]{:S(2)}, u32[]{:S(2)}) collective-permute-start(bf16[1024,256]{1,0:T(8,128)(2,1)S(1)} %pad_maximum_fusion.3.refs_6_), channel_id=1, source_target_pairs={{0,16},{16,0},{32,48},{48,32},{1,17},{17,1},{33,49},{49,33},{2,18}... | collective-permute-start | bytes 1572872 | tf_op jit(solution)/shard_map/ppermute | solution.py:33
  56.0 1.7 %collective-permute-start.20 = (bf16[1024,256]{1,0:T(8,128)(2,1)S(1)}, bf16[1024,256]{1,0:T(8,128)(2,1)}, u32[]{:S(2)}, u32[]{:S(2)}) collective-permute-start(bf16[1024,256]{1,0:T(8,128)(2,1)S(1)} %pad_maximum_fusion.2.refs_4_), channel_id=1, source_target_pairs={{0,64},{64,0},{128,192},{192,128},{1,65},{65,1},{129,193},{193,129... | collective-permute-start | bytes 1572872 | tf_op jit(solution)/shard_map/ppermute | solution.py:33
  57.8 0.0 collective-permute-done.13.refs_5_
  57.8 0.4 collective-permute-start.19
  58.2 0.0 collective-permute-done.10.refs_3_
  58.2 0.0 collective-permute-done.7.refs_1_
  58.2 0.0 collective-permute-start.17
  58.2 2.2 %collective-permute-start.18 = (bf16[1024,256]{1,0:T(8,128)(2,1)S(1)}, bf16[1024,256]{1,0:T(8,128)(2,1)}, u32[]{:S(2)}, u32[]{:S(2)}) collective-permute-start(bf16[1024,256]{1,0:T(8,128)(2,1)S(1)} %pad_maximum_fusion.refs_0_), channel_id=1, source_target_pairs={{0,192},{64,128},{128,64},{192,0},{1,193},{65,129},{129,65},{193,1... | collective-permute-start | bytes 1572872 | tf_op jit(solution)/shard_map/ppermute | solution.py:33
  60.4 3.1 %all-to-all-done = f32[64,1,1152]{2,1,0:T(1,128)} async-done(((f32[64,1,1152]{2,1,0:T(1,128)}), f32[64,1,1152]{2,1,0:T(1,128)}, u32[]{:S(2)}, u32[]{:S(2)}) %all-to-all-start) | async-done | bytes 294944 | tf_op jit(solution)/shard_map/all_to_all | solution.py:255
  63.6 1.0 %copy.13 = f32[64,1,1152]{2,0,1:T(8,128)S(1)} copy(f32[64,1,1152]{2,1,0:T(1,128)} %all-to-all-done) | data formatting | bytes 589824
  64.6 5.0 %collective-permute-done.21.refs_4_ = bf16[1024,256]{1,0:T(8,128)(2,1)} collective-permute-done((bf16[1024,256]{1,0:T(8,128)(2,1)S(1)}, bf16[1024,256]{1,0:T(8,128)(2,1)}, u32[]{:S(2)}, u32[]{:S(2)}) %collective-permute-start.21) | collective-permute-done | bytes 524320 | tf_op jit(solution)/shard_map/ppermute | solution.py:33
  69.5 1.7 %collective-permute-start.24 = (bf16[1024,256]{1,0:T(8,128)(2,1)}, bf16[1024,256]{1,0:T(8,128)(2,1)}, u32[]{:S(2)}, u32[]{:S(2)}) collective-permute-start(bf16[1024,256]{1,0:T(8,128)(2,1)} %collective-permute-done.13.refs_5_), channel_id=1, source_target_pairs={{0,64},{64,0},{128,192},{192,128},{1,65},{65,1},{129,193},{193,129... | collective-permute-start | bytes 1572872 | tf_op jit(solution)/shard_map/ppermute | solution.py:33
  71.3 1.2 %collective-permute-start.23 = (bf16[1024,256]{1,0:T(8,128)(2,1)}, bf16[1024,256]{1,0:T(8,128)(2,1)}, u32[]{:S(2)}, u32[]{:S(2)}) collective-permute-start(bf16[1024,256]{1,0:T(8,128)(2,1)} %collective-permute-done.10.refs_3_), channel_id=1, source_target_pairs={{0,48},{16,32},{32,16},{48,0},{1,49},{17,33},{33,17},{49,1},{2,50}... | collective-permute-start | bytes 1572872 | tf_op jit(solution)/shard_map/ppermute | solution.py:33
  72.4 0.0 collective-permute-done.19.refs_2_
  72.4 1.1 %collective-permute-start.22 = (bf16[1024,256]{1,0:T(8,128)(2,1)}, bf16[1024,256]{1,0:T(8,128)(2,1)}, u32[]{:S(2)}, u32[]{:S(2)}) collective-permute-start(bf16[1024,256]{1,0:T(8,128)(2,1)} %collective-permute-done.7.refs_1_), channel_id=1, source_target_pairs={{0,192},{64,128},{128,64},{192,0},{1,193},{65,129},{129,65},{193,1... | collective-permute-start | bytes 1572872 | tf_op jit(solution)/shard_map/ppermute | solution.py:33
  73.5 0.0 collective-permute-done.17.t3
  73.5 0.2 collective-permute-start.25
  73.7 0.1 pad_add_fusion.at_ref
  73.8 1.1 %fusion = f32[64,1024]{1,0:T(8,128)} fusion(f32[64,1152]{1,0:T(8,128)S(1)} %bitcast.18), kind=kOutput, calls=%fused_computation.5 | convolution fusion | flops 50331648 | bytes 557056 | tf_op jit(solution)/shard_map/dot_general | solution.py:279
  74.9 2.0 %member_tokens.1 = (bf16[4,256,1024]{2,1,0:T(8,128)(2,1)S(1)}, f32[256,8]{1,0:T(8,128)S(1)}) custom-call(s32[1]{0:T(128)} %bitcast.2.at_ref, bf16[256,1024]{1,0:T(8,128)(2,1)S(1)} %bitcast.16, bf16[256,1024]{1,0:T(8,128)(2,1)S(1)} %collective-permute-done.3.t1, bf16[256,1024]{1,0:T(8,128)(2,1)} %collective-permute-done.4.t2, ...), custom_call_target="tpu_custom_call" | custom-call | bytes 8388608 | tf_op jit(solution)/shard_map/member_tokens/pallas_call | solution.py:266
  76.9 4.7 %products.2.refs_0_ = f32[256,1024]{1,0:T(8,128)S(1)} custom-call(s32[2]{0:T(128)S(1)} %pad_add_fusion.at_ref, bf16[4,256,1024]{2,1,0:T(8,128)(2,1)S(1)} %get-tuple-element.16.tokens_ref, bf16[1024,256]{1,0:T(8,128)(2,1)S(1)} %pad_maximum_fusion.refs_0_, bf16[1024,256]{1,0:T(8,128)(2,1)} %collective-permute-done.7.refs_1_, ...), custom_call_target="tpu_custom_call" | custom-call | flops 1073741824 | bytes 8388608 | tf_op jit(solution)/shard_map/products/pallas_call | solution.py:150
  81.7 0.0 copy-start.3
  81.7 3.6 %products.3.sum_ref = f32[256,1024]{1,0:T(8,128)S(1)} custom-call(s32[2]{0:T(128)S(1)} %pad_add_fusion.at_ref, bf16[4,256,1024]{2,1,0:T(8,128)(2,1)S(1)} %get-tuple-element.16.tokens_ref, f32[256,1024]{1,0:T(8,128)S(1)} %products.2.refs_0_, bf16[1024,256]{1,0:T(8,128)(2,1)} %collective-permute-done.18.refs_1_, ...), custom_call_target="tpu_custom_call" | custom-call | flops 536870912 | bytes 8388608 | tf_op jit(solution)/shard_map/products/pallas_call | solution.py:150
  85.4 0.0 collective-permute-done.24.refs_2_
  85.4 0.5 collective-permute-done.23.refs_1_
  85.9 0.7 collective-permute-done.22.refs_0_
  86.6 5.8 %values_readout.1 = bf16[256,1024]{1,0:T(8,128)(2,1)} custom-call(s32[2]{0:T(128)S(1)} %pad_add_fusion.at_ref, bf16[4,256,1024]{2,1,0:T(8,128)(2,1)S(1)} %get-tuple-element.16.tokens_ref, f32[256,1024]{1,0:T(8,128)S(1)} %products.3.sum_ref, f32[256,8]{1,0:T(8,128)S(1)} %get-tuple-element.17.projected_ref, bf16[1,1024]{1,0:T(2,128)(2,1)S(1)} %copy-done.3, ...), custom_call_target="tpu_custom_call" | custom-call | flops 536870912 | bytes 12582912 | tf_op jit(solution)/shard_map/values_readout/pallas_call | solution.py:292
  (27 shorter events, 0.3 us)
Async XLA Ops:
  0.6 19.0 %collective-permute-start = (bf16[64,1024]{1,0:T(8,128)(2,1)}, bf16[64,1024]{1,0:T(8,128)(2,1)S(1)}, u32[]{:S(2)}, u32[]{:S(2)}) collective-permute-start(bf16[64,1024]{1,0:T(8,128)(2,1)} %param.13), channel_id=1, source_target_pairs={{4,0},{8,4},{12,8},{0,12},{5,1},{9,5},{13,9},{1,13},{6,2},{10,6},{... | collective-permute-start | bytes 393224 | tf_op jit(solution)/shard_map/ppermute | solution.py:38
  2.6 17.1 %collective-permute-start.1 = (bf16[64,1024]{1,0:T(8,128)(2,1)}, bf16[64,1024]{1,0:T(8,128)(2,1)S(1)}, u32[]{:S(2)}, u32[]{:S(2)}) collective-permute-start(bf16[64,1024]{1,0:T(8,128)(2,1)} %param.13), channel_id=1, source_target_pairs={{12,0},{0,4},{4,8},{8,12},{13,1},{1,5},{5,9},{9,13},{14,2},{2,6},{... | collective-permute-start | bytes 393224 | tf_op jit(solution)/shard_map/ppermute | solution.py:38
  2.7 17.0 %collective-permute-start.2 = (bf16[64,1024]{1,0:T(8,128)(2,1)}, bf16[64,1024]{1,0:T(8,128)(2,1)S(1)}, u32[]{:S(2)}, u32[]{:S(2)}) collective-permute-start(bf16[64,1024]{1,0:T(8,128)(2,1)} %param.13), channel_id=1, source_target_pairs={{8,0},{12,4},{0,8},{4,12},{9,1},{13,5},{1,9},{5,13},{10,2},{14,6},... | collective-permute-start | bytes 393224 | tf_op jit(solution)/shard_map/ppermute | solution.py:38
  7.8 11.9 %collective-permute-start.3 = (bf16[256,1024]{1,0:T(8,128)(2,1)}, bf16[256,1024]{1,0:T(8,128)(2,1)S(1)}, u32[]{:S(2)}, u32[]{:S(2)}) collective-permute-start(bf16[256,1024]{1,0:T(8,128)(2,1)} %bitcast.14), channel_id=1, source_target_pairs={{0,1},{1,0},{2,3},{3,2},{4,5},{5,4},{6,7},{7,6},{8,9},{9,8},{10,11... | collective-permute-start | bytes 1572872 | tf_op jit(solution)/shard_map/ppermute | solution.py:33
  11.7 14.4 %copy-start.1 = (bf16[1,256,1024]{2,1,0:T(8,128)(2,1)S(1)}, bf16[1,256,1024]{2,1,0:T(8,128)(2,1)}, u32[]{:S(2)}) copy-start(bf16[1,256,1024]{2,1,0:T(8,128)(2,1)} %param.9) | copy-start | bytes 1572868
  19.8 10.7 %collective-permute-start.14 = (bf16[256,256]{1,0:T(8,128)(2,1)S(1)}, bf16[256,256]{1,0:T(8,128)(2,1)S(1)}, u32[]{:S(2)}, u32[]{:S(2)}) collective-permute-start(bf16[256,256]{1,0:T(8,128)(2,1)S(1)} %get-tuple-element.22), channel_id=1, source_target_pairs={{0,192},{64,128},{128,64},{192,0},{1,193},{65,129},{129,65},{193,1... | collective-permute-start | bytes 393224 | tf_op jit(solution)/shard_map/ppermute | solution.py:33
  22.9 8.9 %collective-permute-start.11 = (bf16[256,256]{1,0:T(8,128)(2,1)S(1)}, bf16[256,256]{1,0:T(8,128)(2,1)S(1)}, u32[]{:S(2)}, u32[]{:S(2)}) collective-permute-start(bf16[256,256]{1,0:T(8,128)(2,1)S(1)} %get-tuple-element.23), channel_id=1, source_target_pairs={{0,48},{16,32},{32,16},{48,0},{1,49},{17,33},{33,17},{49,1},{2,50}... | collective-permute-start | bytes 393224 | tf_op jit(solution)/shard_map/ppermute | solution.py:33
  25.6 7.4 %collective-permute-start.8 = (bf16[256,256]{1,0:T(8,128)(2,1)S(1)}, bf16[256,256]{1,0:T(8,128)(2,1)S(1)}, u32[]{:S(2)}, u32[]{:S(2)}) collective-permute-start(bf16[256,256]{1,0:T(8,128)(2,1)S(1)} %get-tuple-element.24), channel_id=1, source_target_pairs={{0,64},{64,0},{128,192},{192,128},{1,65},{65,1},{129,193},{193,129... | collective-permute-start | bytes 393224 | tf_op jit(solution)/shard_map/ppermute | solution.py:33
  25.8 8.0 %collective-permute-start.5 = (bf16[256,256]{1,0:T(8,128)(2,1)S(1)}, bf16[256,256]{1,0:T(8,128)(2,1)S(1)}, u32[]{:S(2)}, u32[]{:S(2)}) collective-permute-start(bf16[256,256]{1,0:T(8,128)(2,1)S(1)} %get-tuple-element.25), channel_id=1, source_target_pairs={{0,16},{16,0},{32,48},{48,32},{1,17},{17,1},{33,49},{49,33},{2,18}... | collective-permute-start | bytes 393224 | tf_op jit(solution)/shard_map/ppermute | solution.py:33
  26.0 28.3 %collective-permute-start.4 = (bf16[256,1024]{1,0:T(8,128)(2,1)S(1)}, bf16[256,1024]{1,0:T(8,128)(2,1)}, u32[]{:S(2)}, u32[]{:S(2)}) collective-permute-start(bf16[256,1024]{1,0:T(8,128)(2,1)S(1)} %bitcast.15), channel_id=1, source_target_pairs={{0,2},{2,0},{1,3},{3,1},{4,6},{6,4},{5,7},{7,5},{8,10},{10,8},{9,1... | collective-permute-start | bytes 1572872 | tf_op jit(solution)/shard_map/ppermute | solution.py:33
  30.5 44.4 %copy-start.2 = (bf16[1,4096]{1,0:T(2,128)(2,1)S(1)}, bf16[1,4096]{1,0:T(2,128)(2,1)}, u32[]{:S(2)}) copy-start(bf16[1,4096]{1,0:T(2,128)(2,1)} %param.14) | copy-start | bytes 24580
  30.5 8.9 %collective-permute-start.15 = (bf16[512,256]{1,0:T(8,128)(2,1)S(1)}, bf16[512,256]{1,0:T(8,128)(2,1)S(1)}, u32[]{:S(2)}, u32[]{:S(2)}) collective-permute-start(bf16[512,256]{1,0:T(8,128)(2,1)S(1)} %pad_maximum_fusion.7), channel_id=1, source_target_pairs={{0,48},{16,32},{32,16},{48,0},{1,49},{17,33},{33,17},{49,1},{2,50}... | collective-permute-start | bytes 786440 | tf_op jit(solution)/shard_map/ppermute | solution.py:33
  31.8 9.4 %collective-permute-start.12 = (bf16[512,256]{1,0:T(8,128)(2,1)S(1)}, bf16[512,256]{1,0:T(8,128)(2,1)S(1)}, u32[]{:S(2)}, u32[]{:S(2)}) collective-permute-start(bf16[512,256]{1,0:T(8,128)(2,1)S(1)} %pad_maximum_fusion.6), channel_id=1, source_target_pairs={{0,192},{64,128},{128,64},{192,0},{1,193},{65,129},{129,65},{193,1... | collective-permute-start | bytes 786440 | tf_op jit(solution)/shard_map/ppermute | solution.py:33
  33.0 8.9 %collective-permute-start.9 = (bf16[512,256]{1,0:T(8,128)(2,1)S(1)}, bf16[512,256]{1,0:T(8,128)(2,1)S(1)}, u32[]{:S(2)}, u32[]{:S(2)}) collective-permute-start(bf16[512,256]{1,0:T(8,128)(2,1)S(1)} %pad_maximum_fusion.5), channel_id=1, source_target_pairs={{0,16},{16,0},{32,48},{48,32},{1,17},{17,1},{33,49},{49,33},{2,18}... | collective-permute-start | bytes 786440 | tf_op jit(solution)/shard_map/ppermute | solution.py:33
  33.8 8.6 %collective-permute-start.6 = (bf16[512,256]{1,0:T(8,128)(2,1)S(1)}, bf16[512,256]{1,0:T(8,128)(2,1)S(1)}, u32[]{:S(2)}, u32[]{:S(2)}) collective-permute-start(bf16[512,256]{1,0:T(8,128)(2,1)S(1)} %pad_maximum_fusion.4), channel_id=1, source_target_pairs={{0,64},{64,0},{128,192},{192,128},{1,65},{65,1},{129,193},{193,129... | collective-permute-start | bytes 786440 | tf_op jit(solution)/shard_map/ppermute | solution.py:33
  39.5 16.5 %collective-permute-start.16 = (bf16[1024,256]{1,0:T(8,128)(2,1)S(1)}, bf16[1024,256]{1,0:T(8,128)(2,1)}, u32[]{:S(2)}, u32[]{:S(2)}) collective-permute-start(bf16[1024,256]{1,0:T(8,128)(2,1)S(1)} %pad_maximum_fusion.3.refs_6_), channel_id=1, source_target_pairs={{0,64},{64,0},{128,192},{192,128},{1,65},{65,1},{129,193},{193,129... | collective-permute-start | bytes 1572872 | tf_op jit(solution)/shard_map/ppermute | solution.py:33
  41.3 16.5 %collective-permute-start.13 = (bf16[1024,256]{1,0:T(8,128)(2,1)S(1)}, bf16[1024,256]{1,0:T(8,128)(2,1)}, u32[]{:S(2)}, u32[]{:S(2)}) collective-permute-start(bf16[1024,256]{1,0:T(8,128)(2,1)S(1)} %pad_maximum_fusion.2.refs_4_), channel_id=1, source_target_pairs={{0,16},{16,0},{32,48},{48,32},{1,17},{17,1},{33,49},{49,33},{2,18}... | collective-permute-start | bytes 1572872 | tf_op jit(solution)/shard_map/ppermute | solution.py:33
  41.9 16.3 %collective-permute-start.10 = (bf16[1024,256]{1,0:T(8,128)(2,1)S(1)}, bf16[1024,256]{1,0:T(8,128)(2,1)}, u32[]{:S(2)}, u32[]{:S(2)}) collective-permute-start(bf16[1024,256]{1,0:T(8,128)(2,1)S(1)} %pad_maximum_fusion.1.refs_2_), channel_id=1, source_target_pairs={{0,192},{64,128},{128,64},{192,0},{1,193},{65,129},{129,65},{193,1... | collective-permute-start | bytes 1572872 | tf_op jit(solution)/shard_map/ppermute | solution.py:33
  42.4 15.8 %collective-permute-start.7 = (bf16[1024,256]{1,0:T(8,128)(2,1)S(1)}, bf16[1024,256]{1,0:T(8,128)(2,1)}, u32[]{:S(2)}, u32[]{:S(2)}) collective-permute-start(bf16[1024,256]{1,0:T(8,128)(2,1)S(1)} %pad_maximum_fusion.refs_0_), channel_id=1, source_target_pairs={{0,48},{16,32},{32,16},{48,0},{1,49},{17,33},{33,17},{49,1},{2,50}... | collective-permute-start | bytes 1572872 | tf_op jit(solution)/shard_map/ppermute | solution.py:33
  45.8 17.8 %all-to-all-start = ((f32[64,1,1152]{2,1,0:T(1,128)}), f32[64,1,1152]{2,1,0:T(1,128)}, u32[]{:S(2)}, u32[]{:S(2)}) async-start(f32[64,1,1152]{2,1,0:T(1,128)} %all_to_all.8), calls=%async_computation | async-start | bytes 589824 | tf_op jit(solution)/shard_map/all_to_all | solution.py:255
  54.4 15.2 %collective-permute-start.21 = (bf16[1024,256]{1,0:T(8,128)(2,1)S(1)}, bf16[1024,256]{1,0:T(8,128)(2,1)}, u32[]{:S(2)}, u32[]{:S(2)}) collective-permute-start(bf16[1024,256]{1,0:T(8,128)(2,1)S(1)} %pad_maximum_fusion.3.refs_6_), channel_id=1, source_target_pairs={{0,16},{16,0},{32,48},{48,32},{1,17},{17,1},{33,49},{49,33},{2,18}... | collective-permute-start | bytes 1572872 | tf_op jit(solution)/shard_map/ppermute | solution.py:33
  56.0 15.2 %collective-permute-start.20 = (bf16[1024,256]{1,0:T(8,128)(2,1)S(1)}, bf16[1024,256]{1,0:T(8,128)(2,1)}, u32[]{:S(2)}, u32[]{:S(2)}) collective-permute-start(bf16[1024,256]{1,0:T(8,128)(2,1)S(1)} %pad_maximum_fusion.2.refs_4_), channel_id=1, source_target_pairs={{0,64},{64,0},{128,192},{192,128},{1,65},{65,1},{129,193},{193,129... | collective-permute-start | bytes 1572872 | tf_op jit(solution)/shard_map/ppermute | solution.py:33
  57.8 14.7 %collective-permute-start.19 = (bf16[1024,256]{1,0:T(8,128)(2,1)S(1)}, bf16[1024,256]{1,0:T(8,128)(2,1)}, u32[]{:S(2)}, u32[]{:S(2)}) collective-permute-start(bf16[1024,256]{1,0:T(8,128)(2,1)S(1)} %pad_maximum_fusion.1.refs_2_), channel_id=1, source_target_pairs={{0,48},{16,32},{32,16},{48,0},{1,49},{17,33},{33,17},{49,1},{2,50}... | collective-permute-start | bytes 1572872 | tf_op jit(solution)/shard_map/ppermute | solution.py:33
  58.2 15.3 %collective-permute-start.17 = (bf16[256,1024]{1,0:T(8,128)(2,1)}, bf16[256,1024]{1,0:T(8,128)(2,1)}, u32[]{:S(2)}, u32[]{:S(2)}) collective-permute-start(bf16[256,1024]{1,0:T(8,128)(2,1)} %collective-permute-done.4.t2), channel_id=1, source_target_pairs={{0,1},{1,0},{2,3},{3,2},{4,5},{5,4},{6,7},{7,6},{8,9},{9,8},{10,11... | collective-permute-start | bytes 1572872 | tf_op jit(solution)/shard_map/ppermute | solution.py:33
  58.2 23.5 %collective-permute-start.18 = (bf16[1024,256]{1,0:T(8,128)(2,1)S(1)}, bf16[1024,256]{1,0:T(8,128)(2,1)}, u32[]{:S(2)}, u32[]{:S(2)}) collective-permute-start(bf16[1024,256]{1,0:T(8,128)(2,1)S(1)} %pad_maximum_fusion.refs_0_), channel_id=1, source_target_pairs={{0,192},{64,128},{128,64},{192,0},{1,193},{65,129},{129,65},{193,1... | collective-permute-start | bytes 1572872 | tf_op jit(solution)/shard_map/ppermute | solution.py:33
  69.5 15.8 %collective-permute-start.24 = (bf16[1024,256]{1,0:T(8,128)(2,1)}, bf16[1024,256]{1,0:T(8,128)(2,1)}, u32[]{:S(2)}, u32[]{:S(2)}) collective-permute-start(bf16[1024,256]{1,0:T(8,128)(2,1)} %collective-permute-done.13.refs_5_), channel_id=1, source_target_pairs={{0,64},{64,0},{128,192},{192,128},{1,65},{65,1},{129,193},{193,129... | collective-permute-start | bytes 1572872 | tf_op jit(solution)/shard_map/ppermute | solution.py:33
  71.3 14.6 %collective-permute-start.23 = (bf16[1024,256]{1,0:T(8,128)(2,1)}, bf16[1024,256]{1,0:T(8,128)(2,1)}, u32[]{:S(2)}, u32[]{:S(2)}) collective-permute-start(bf16[1024,256]{1,0:T(8,128)(2,1)} %collective-permute-done.10.refs_3_), channel_id=1, source_target_pairs={{0,48},{16,32},{32,16},{48,0},{1,49},{17,33},{33,17},{49,1},{2,50}... | collective-permute-start | bytes 1572872 | tf_op jit(solution)/shard_map/ppermute | solution.py:33
  72.4 14.2 %collective-permute-start.22 = (bf16[1024,256]{1,0:T(8,128)(2,1)}, bf16[1024,256]{1,0:T(8,128)(2,1)}, u32[]{:S(2)}, u32[]{:S(2)}) collective-permute-start(bf16[1024,256]{1,0:T(8,128)(2,1)} %collective-permute-done.7.refs_1_), channel_id=1, source_target_pairs={{0,192},{64,128},{128,64},{192,0},{1,193},{65,129},{129,65},{193,1... | collective-permute-start | bytes 1572872 | tf_op jit(solution)/shard_map/ppermute | solution.py:33
  73.5 13.1 %collective-permute-start.25 = (bf16[1024,256]{1,0:T(8,128)(2,1)}, bf16[1024,256]{1,0:T(8,128)(2,1)}, u32[]{:S(2)}, u32[]{:S(2)}) collective-permute-start(bf16[1024,256]{1,0:T(8,128)(2,1)} %collective-permute-done.16.refs_7_), channel_id=1, source_target_pairs={{0,16},{16,0},{32,48},{48,32},{1,17},{17,1},{33,49},{49,33},{2,18}... | collective-permute-start | bytes 1572872 | tf_op jit(solution)/shard_map/ppermute | solution.py:33
  81.7 4.9 %copy-start = (bf16[8,1024,256]{2,1,0:T(8,128)(2,1)S(1)}, bf16[8,1024,256]{2,1,0:T(8,128)(2,1)}, u32[]{:S(2)}) copy-start(bf16[8,1024,256]{2,1,0:T(8,128)(2,1)} %decayed_scores.1.scores_ref) | copy-start | bytes 12582916
  81.7 4.9 %copy-start.3 = (bf16[1,1024]{1,0:T(2,128)(2,1)S(1)}, bf16[1,1024]{1,0:T(2,128)(2,1)}, u32[]{:S(2)}) copy-start(bf16[1,1024]{1,0:T(2,128)(2,1)} %noise_ref.1) | copy-start | bytes 6148

commit v6 on v5

--- a/solution.py
+++ b/solution.py
@@ -189,6 +189,56 @@
             ).astype(BF16)
 
 
+def pack_kernel(utility_ref, weight_ref, noise_in_ref, noise_out_ref, out_ref):
+    rows, width = weight_ref.shape
+    out_ref[:rows] = weight_ref[...]
+    line = lax.broadcasted_iota(jnp.int32, (8, width), 0)
+    lane = lax.broadcasted_iota(jnp.int32, (8, width), 1)
+    packed = jnp.where(line == 0, noise_out_ref[...].astype(F32), 0.0)
+    for i in range(SIDE):
+        part = noise_in_ref[:, i * width : (i + 1) * width].astype(F32)
+        packed = jnp.where(line == 1 + i, part, packed)
+    rest = jnp.full((8, width), utility_ref[0], F32)
+    for i in range(3):
+        term = rest.astype(BF16).astype(F32)
+        packed = jnp.where((line == 5) & (lane == i), term, packed)
+        rest = rest - term
+    out_ref[rows:] = packed.astype(BF16)
+
+
+def message_kernel(p0, p1, p2, p3, out_ref):
+    rows, width = p0.shape[0] - 8, p0.shape[1]
+    wide = width // SIDE
+    scale = 1 / math.sqrt(SIDE**3)
+    weighted, plain = [], []
+    for part in (p0, p1, p2, p3):
+        noise = part[rows:].astype(F32)
+        utility = (noise[5:6, 0:1] + noise[5:6, 1:2]) + noise[5:6, 2:3]
+        weighted.append(noise[1:5] * (utility * scale))
+        plain.append(noise[0:1])
+    plain = jnp.concatenate(plain, 0)
+    for y in range(SIDE):
+        line = jnp.concatenate([w[y : y + 1] for w in weighted], 0)
+        for x in range(SIDE):
+            out_ref[y * SIDE + x, :, :wide] = line[:, x * wide : (x + 1) * wide]
+            out_ref[y * SIDE + x, :, wide:] = plain
+
+
+def update_kernel(z_ref, message_ref, out_ref, held):
+    rows, width = out_ref.shape
+    wide = message_ref.shape[2] - width
+    for i in range(message_ref.shape[0]):
+        held[i * SIDE : (i + 1) * SIDE] = message_ref[i]
+    weighted = pltpu.roll(held[:, :wide], lax.rem(SIDE - z_ref[0], SIDE) * rows, 1)[:, :LANES]
+    out_ref[...] = lax.dot_general(
+        weighted,
+        held[:, wide:],
+        (((0,), (0,)), ((), ())),
+        precision=HIGHEST,
+        preferred_element_type=F32,
+    )[:rows]
+
+
 def params(mib):
     return pltpu.CompilerParams(vmem_limit_bytes=mib << 20)
 
@@ -227,23 +277,23 @@
     wide = width // len(ROUTES)
 
     z = lax.axis_index("z")
+    packed = pl.pallas_call(
+        pack_kernel,
+        out_shape=jax.ShapeDtypeStruct((rows + 8, width), BF16),
+        in_specs=[SMEM] + [VMEM] * 3,
+        out_specs=VMEM,
+        name="weight_and_noise",
+    )(utilities, value_weight, noise_in, noise_out)
     near = jnp.zeros((SIDE * rows, width), BF16)
+    parts = []
     for step in (0, 1, 3, 2):
-        part = fetch(value_weight, "z", step) if step else value_weight
-        near = lax.dynamic_update_slice(near, part, (lax.rem(z + step, SIDE) * rows, 0))
+        parts.append(fetch(packed, "z", step) if step else packed)
+        near = lax.dynamic_update_slice(
+            near, parts[-1][:rows], (lax.rem(z + step, SIDE) * rows, 0)
+        )
     mate = swap(tokens, "core", 1)
-    population = lax.axis_size(POP)
-    weighted = noise_in.astype(F32) * (utilities / math.sqrt(population))[:, None]
-    message = jnp.concatenate(
-        [
-            weighted.reshape(population, rows),
-            jnp.zeros((population, LANES - rows), F32),
-            jnp.broadcast_to(noise_out.astype(F32), (population, width)),
-        ],
-        1,
-    )
     scores = score_heads(live_length, receptance, keys, log_decay)
-    near, mate, message, scores = lax.optimization_barrier((near, mate, message, scores))
+    near, mate, scores = lax.optimization_barrier((near, mate, scores))
 
     twin = swap(after(tokens, near), "twin", 1)
 
@@ -252,14 +302,20 @@
     for step in range(2):
         came = [swap(held[c], *LINKS[ROUTES[c][step]]) for c in chunks]
         held = [jnp.concatenate([a, b], 0) for a, b in zip(held, came)]
-    message = lax.all_to_all(
-        after(message, *held), POP, split_axis=0, concat_axis=0, tiled=True
-    )
     third = [swap(held[c], *LINKS[ROUTES[c][2]]) for c in chunks]
+    parts = after(parts, *held)
+    message = pl.pallas_call(
+        message_kernel,
+        out_shape=jax.ShapeDtypeStruct((SIDE * SIDE, SIDE, wide + width), F32),
+        in_specs=[VMEM] * SIDE,
+        out_specs=VMEM,
+        compiler_params=params(60),
+        cost_estimate=cost(0, 1 << 20),
+        name="noise_message",
+    )(*parts)
+    held[0] = after(held[0], message)
+    message = lax.all_to_all(message, ("y", "x"), split_axis=0, concat_axis=0, tiled=True)
     fourth = [swap(held[c], *LINKS[ROUTES[c][3]]) for c in chunks]
-    ready = list(third)
-    ready[3] = after(third[3], message)
-    last = [swap(ready[c], *LINKS[ROUTES[c][3]]) for c in chunks]
 
     both = swap(after(twin, *third), "core", 1)
     tp = lax.axis_index(TP).reshape(1)
@@ -276,15 +332,20 @@
         name="member_tokens",
     )(tp, tokens, mate, twin, both, noise_in.reshape(4, 1, width))
 
-    update = lax.dot_general(
-        message[:, :rows],
-        message[:, LANES:],
-        (((0,), (0,)), ((), ())),
-        precision=HIGHEST,
-        preferred_element_type=F32,
-    )
+    update = pl.pallas_call(
+        update_kernel,
+        out_shape=jax.ShapeDtypeStruct((rows, width), F32),
+        in_specs=[SMEM, VMEM],
+        out_specs=VMEM,
+        scratch_shapes=[pltpu.VMEM((SIDE**3, wide + width), F32)],
+        compiler_params=params(8),
+        cost_estimate=cost(0, 2 << 20),
+        name="update_product",
+    )(z.reshape(1), message)
 
     at = jnp.stack([lax.axis_index("y"), lax.axis_index("x")])
+    ready = [after(third[0], message)] + third[1:]
+    last = [swap(ready[c], *LINKS[ROUTES[c][3]]) for c in chunks]
     total = product(
         at, all_tokens, ((), (2,)), [p for c in chunks for p in (held[c], third[c])]
     )

time: 93.3 us -> 103 us (1.10)
  the two profiles are of different devices: /device:TPU:32 before, /device:TPU:1 now
where the time goes in v6:
time: 103 us; the launch traced here: 102 us
  starting transfers between devices  47.7 us (46%)
  Pallas kernels  28.3 us (27%)
  waiting for transfers between devices  22.5 us (22%)
  between operations  2.38 us (2%)
  local copies, waits for them, and re-layouts  1.23 us (1%)
    ppermute x23, starting transfers between devices, swap(): return lax.ppermute(array, axis, [(i, i ^ mask) for i in range(size)])  38 us
    ppermute x23, waiting for transfers between devices, swap(): return lax.ppermute(array, axis, [(i, i ^ mask) for i in range(size)])  13 us
    pallas_call x1, Pallas kernels, score_heads(): pl.pallas_call(score_kernel, out_shape=jax.ShapeDtypeStruct((count, 4 * l...  7.88 us
    pallas_call x2, Pallas kernels, product(): pl.pallas_call(functools.partial(product_kernel, ways, before is not None...  7.66 us
    all_to_all x1, waiting for transfers between devices, body(): lax.all_to_all(message, ('y', 'x'), split_axis=0, concat_axis=0, tiled=True)  7.61 us
    pallas_call x1, Pallas kernels, body(): pl.pallas_call(readout_kernel, out_shape=jax.ShapeDtypeStruct((length, wi...  5.76 us
    ppermute x3, starting transfers between devices, fetch(): lax.ppermute(array, axis, [((i + step) % size, i) for i in range(size)])  5.46 us
    all_to_all x1, starting transfers between devices, body(): lax.all_to_all(message, ('y', 'x'), split_axis=0, concat_axis=0, tiled=True)  4.2 us
  transfers between devices with their start and end apart: 27, of which 10 were waited for; matrix products, arithmetic and copies ran while one was open for 0% of the time, Pallas kernels for 20%

profile of v6, /device:TPU:1, one launch (start us, length us, event | category | flops | bytes accessed | tf_op | source)
XLA Modules:
  0.0 102.4 jit_solution(9767413717287339811)
XLA Ops:
  1.3 1.6 %weight_and_noise.1.p0 = bf16[72,1024]{1,0:T(8,128)(2,1)} custom-call(f32[1]{0:T(128)S(6)} %copy.15.utility_ref, bf16[64,1024]{1,0:T(8,128)(2,1)} %weight_ref.1, bf16[1,4096]{1,0:T(2,128)(2,1)} %noise_in_ref.1, bf16[1,1024]{1,0:T(2,128)(2,1)} %noise_ref.1), custom_call_target="tpu_custom_call" | custom-call | tf_op jit(solution)/shard_map/weight_and_noise/pallas_call | solution.py:280
  2.9 5.2 %collective-permute-start = (bf16[72,1024]{1,0:T(8,128)(2,1)}, bf16[72,1024]{1,0:T(8,128)(2,1)S(1)}, u32[]{:S(2)}, u32[]{:S(2)}) collective-permute-start(bf16[72,1024]{1,0:T(8,128)(2,1)} %weight_and_noise.1.p0), channel_id=1, source_target_pairs={{4,0},{8,4},{12,8},{0,12},{5,1},{9,5},{13,9},{1,13},{6,2},{10,6},{... | collective-permute-start | bytes 442376 | tf_op jit(solution)/shard_map/ppermute | solution.py:38
  8.1 0.0 collective-permute-start.1
  8.1 0.3 collective-permute-start.2
  8.4 1.3 %collective-permute-start.3 = (bf16[256,1024]{1,0:T(8,128)(2,1)}, bf16[256,1024]{1,0:T(8,128)(2,1)S(1)}, u32[]{:S(2)}, u32[]{:S(2)}) collective-permute-start(bf16[256,1024]{1,0:T(8,128)(2,1)} %bitcast.10), channel_id=1, source_target_pairs={{0,1},{1,0},{2,3},{3,2},{4,5},{5,4},{6,7},{7,6},{8,9},{9,8},{10,11... | collective-permute-start | bytes 1572872 | tf_op jit(solution)/shard_map/ppermute | solution.py:33
  10.4 7.9 %decayed_scores.1.scores_ref = bf16[8,1024,256]{2,1,0:T(8,128)(2,1)} custom-call(s32[1]{0:T(128)S(6)} %copy.16.live_ref, bf16[256,1024]{1,0:T(8,128)(2,1)} %bitcast.14, bf16[256,1024]{1,0:T(8,128)(2,1)} %bitcast.15, bf16[256,1024]{1,0:T(8,128)(2,1)} %bitcast.16), custom_call_target="tpu_custom_call" | custom-call | bytes 20971520 | tf_op jit(solution)/shard_map/decayed_scores/pallas_call | solution.py:258
  18.3 0.1 broadcast_in_dim.3
  18.3 0.0 collective-permute-done.p1
  18.4 0.0 copy-start.7
  18.4 0.0 collective-permute-done.1.p2
  18.4 1.9 %collective-permute-done.2.p3 = bf16[72,1024]{1,0:T(8,128)(2,1)S(1)} collective-permute-done((bf16[72,1024]{1,0:T(8,128)(2,1)}, bf16[72,1024]{1,0:T(8,128)(2,1)S(1)}, u32[]{:S(2)}, u32[]{:S(2)}) %collective-permute-start.2) | collective-permute-done | bytes 147488 | tf_op jit(solution)/shard_map/ppermute | solution.py:38
  20.3 0.0 collective-permute-done.3.t1
  20.4 1.3 %collective-permute-start.5 = (bf16[256,256]{1,0:T(8,128)(2,1)S(1)}, bf16[256,256]{1,0:T(8,128)(2,1)S(1)}, u32[]{:S(2)}, u32[]{:S(2)}) collective-permute-start(bf16[256,256]{1,0:T(8,128)(2,1)S(1)} %get-tuple-element.31), channel_id=1, source_target_pairs={{0,16},{16,0},{32,48},{48,32},{1,17},{17,1},{33,49},{49,33},{2,18}... | collective-permute-start | bytes 393224 | tf_op jit(solution)/shard_map/ppermute | solution.py:33
  21.7 1.3 %collective-permute-start.8 = (bf16[256,256]{1,0:T(8,128)(2,1)S(1)}, bf16[256,256]{1,0:T(8,128)(2,1)S(1)}, u32[]{:S(2)}, u32[]{:S(2)}) collective-permute-start(bf16[256,256]{1,0:T(8,128)(2,1)S(1)} %get-tuple-element.30), channel_id=1, source_target_pairs={{0,64},{64,0},{128,192},{192,128},{1,65},{65,1},{129,193},{193,129... | collective-permute-start | bytes 393224 | tf_op jit(solution)/shard_map/ppermute | solution.py:33
  23.0 5.3 %collective-permute-start.4 = (bf16[256,1024]{1,0:T(8,128)(2,1)S(1)}, bf16[256,1024]{1,0:T(8,128)(2,1)}, u32[]{:S(2)}, u32[]{:S(2)}) collective-permute-start(bf16[256,1024]{1,0:T(8,128)(2,1)S(1)} %bitcast.11), channel_id=1, source_target_pairs={{0,2},{2,0},{1,3},{3,1},{4,6},{6,4},{5,7},{7,5},{8,10},{10,8},{9,1... | collective-permute-start | bytes 1572872 | tf_op jit(solution)/shard_map/ppermute | solution.py:33
  28.3 1.8 %collective-permute-start.11 = (bf16[256,256]{1,0:T(8,128)(2,1)S(1)}, bf16[256,256]{1,0:T(8,128)(2,1)S(1)}, u32[]{:S(2)}, u32[]{:S(2)}) collective-permute-start(bf16[256,256]{1,0:T(8,128)(2,1)S(1)} %get-tuple-element.29), channel_id=1, source_target_pairs={{0,48},{16,32},{32,16},{48,0},{1,49},{17,33},{33,17},{49,1},{2,50}... | collective-permute-start | bytes 393224 | tf_op jit(solution)/shard_map/ppermute | solution.py:33
  30.1 1.9 %collective-permute-start.14 = (bf16[256,256]{1,0:T(8,128)(2,1)S(1)}, bf16[256,256]{1,0:T(8,128)(2,1)S(1)}, u32[]{:S(2)}, u32[]{:S(2)}) collective-permute-start(bf16[256,256]{1,0:T(8,128)(2,1)S(1)} %get-tuple-element.28), channel_id=1, source_target_pairs={{0,192},{64,128},{128,64},{192,0},{1,193},{65,129},{129,65},{193,1... | collective-permute-start | bytes 393224 | tf_op jit(solution)/shard_map/ppermute | solution.py:33
  32.0 0.0 collective-permute-done.5
  32.0 0.5 collective-permute-start.6
  32.5 0.0 collective-permute-done.8
  32.5 0.4 collective-permute-start.9
  32.9 0.4 collective-permute-done.11
  33.3 2.0 %collective-permute-start.12 = (bf16[512,256]{1,0:T(8,128)(2,1)S(1)}, bf16[512,256]{1,0:T(8,128)(2,1)S(1)}, u32[]{:S(2)}, u32[]{:S(2)}) collective-permute-start(bf16[512,256]{1,0:T(8,128)(2,1)S(1)} %pad_maximum_fusion.6), channel_id=1, source_target_pairs={{0,192},{64,128},{128,64},{192,0},{1,193},{65,129},{129,65},{193,1... | collective-permute-start | bytes 786440 | tf_op jit(solution)/shard_map/ppermute | solution.py:33
  35.3 0.2 collective-permute-done.14
  35.5 1.7 %collective-permute-start.15 = (bf16[512,256]{1,0:T(8,128)(2,1)S(1)}, bf16[512,256]{1,0:T(8,128)(2,1)S(1)}, u32[]{:S(2)}, u32[]{:S(2)}) collective-permute-start(bf16[512,256]{1,0:T(8,128)(2,1)S(1)} %pad_maximum_fusion.7), channel_id=1, source_target_pairs={{0,48},{16,32},{32,16},{48,0},{1,49},{17,33},{33,17},{49,1},{2,50}... | collective-permute-start | bytes 786440 | tf_op jit(solution)/shard_map/ppermute | solution.py:33
  37.2 0.5 collective-permute-done.6
  37.7 0.9 collective-permute-start.7
  38.7 1.7 %collective-permute-start.10 = (bf16[1024,256]{1,0:T(8,128)(2,1)S(1)}, bf16[1024,256]{1,0:T(8,128)(2,1)}, u32[]{:S(2)}, u32[]{:S(2)}) collective-permute-start(bf16[1024,256]{1,0:T(8,128)(2,1)S(1)} %pad_maximum_fusion.1.refs_2_), channel_id=1, source_target_pairs={{0,192},{64,128},{128,64},{192,0},{1,193},{65,129},{129,65},{193,1... | collective-permute-start | bytes 1572872 | tf_op jit(solution)/shard_map/ppermute | solution.py:33
  40.4 0.9 collective-permute-done.12
  41.4 0.4 collective-permute-start.13
  41.8 0.7 collective-permute-done.15
  42.5 0.3 collective-permute-start.16
  42.8 2.0 %noise_message.1 = f32[16,4,1280]{2,1,0:T(4,128)} custom-call(bf16[72,1024]{1,0:T(8,128)(2,1)} %weight_and_noise.1.p0, bf16[72,1024]{1,0:T(8,128)(2,1)} %copy-done.7, bf16[72,1024]{1,0:T(8,128)(2,1)} %copy-done.8, bf16[72,1024]{1,0:T(8,128)(2,1)} %copy-done.9), custom_call_target="tpu_custom_call" | custom-call | bytes 1048576 | tf_op jit(solution)/shard_map/noise_message/pallas_call | solution.py:307
  44.8 2.6 %collective-permute-done.4.t2 = bf16[256,1024]{1,0:T(8,128)(2,1)} collective-permute-done((bf16[256,1024]{1,0:T(8,128)(2,1)S(1)}, bf16[256,1024]{1,0:T(8,128)(2,1)}, u32[]{:S(2)}, u32[]{:S(2)}) %collective-permute-start.4) | collective-permute-done | bytes 524320 | tf_op jit(solution)/shard_map/ppermute | solution.py:33
  47.3 1.8 %collective-permute-start.19 = (bf16[1024,256]{1,0:T(8,128)(2,1)S(1)}, bf16[1024,256]{1,0:T(8,128)(2,1)}, u32[]{:S(2)}, u32[]{:S(2)}) collective-permute-start(bf16[1024,256]{1,0:T(8,128)(2,1)S(1)} %pad_maximum_fusion.1.refs_2_), channel_id=1, source_target_pairs={{0,48},{16,32},{32,16},{48,0},{1,49},{17,33},{33,17},{49,1},{2,50}... | collective-permute-start | bytes 1572872 | tf_op jit(solution)/shard_map/ppermute | solution.py:33
  49.1 2.4 %collective-permute-done.7.refs_1_ = bf16[1024,256]{1,0:T(8,128)(2,1)S(1)} collective-permute-done((bf16[1024,256]{1,0:T(8,128)(2,1)S(1)}, bf16[1024,256]{1,0:T(8,128)(2,1)S(1)}, u32[]{:S(2)}, u32[]{:S(2)}) %collective-permute-start.7) | collective-permute-done | bytes 524320 | tf_op jit(solution)/shard_map/ppermute | solution.py:33
  51.5 1.9 %collective-permute-start.18 = (bf16[1024,256]{1,0:T(8,128)(2,1)S(1)}, bf16[1024,256]{1,0:T(8,128)(2,1)}, u32[]{:S(2)}, u32[]{:S(2)}) collective-permute-start(bf16[1024,256]{1,0:T(8,128)(2,1)S(1)} %pad_maximum_fusion.refs_0_), channel_id=1, source_target_pairs={{0,192},{64,128},{128,64},{192,0},{1,193},{65,129},{129,65},{193,1... | collective-permute-start | bytes 1572872 | tf_op jit(solution)/shard_map/ppermute | solution.py:33
  53.4 0.0 collective-permute-done.10.refs_3_
  53.4 0.0 collective-permute-start.20
  53.4 0.0 collective-permute-done.13.refs_5_
  53.4 10.6 %collective-permute-start.17 = (bf16[256,1024]{1,0:T(8,128)(2,1)}, bf16[256,1024]{1,0:T(8,128)(2,1)}, u32[]{:S(2)}, u32[]{:S(2)}) collective-permute-start(bf16[256,1024]{1,0:T(8,128)(2,1)} %collective-permute-done.4.t2), channel_id=1, source_target_pairs={{0,1},{1,0},{2,3},{3,2},{4,5},{5,4},{6,7},{7,6},{8,9},{9,8},{10,11... | collective-permute-start | bytes 1572872 | tf_op jit(solution)/shard_map/ppermute | solution.py:33
  64.1 4.2 %all-to-all-start = ((f32[16,4,1280]{2,1,0:T(4,128)}), f32[16,4,1280]{2,1,0:T(4,128)S(1)}, u32[]{:S(2)}, u32[]{:S(2)}) async-start(f32[16,4,1280]{2,1,0:T(4,128)} %noise_message.1), calls=%async_computation | async-start | bytes 655360 | tf_op jit(solution)/shard_map/all_to_all | solution.py:317
  68.3 1.4 %collective-permute-start.21 = (bf16[1024,256]{1,0:T(8,128)(2,1)S(1)}, bf16[1024,256]{1,0:T(8,128)(2,1)}, u32[]{:S(2)}, u32[]{:S(2)}) collective-permute-start(bf16[1024,256]{1,0:T(8,128)(2,1)S(1)} %pad_maximum_fusion.3.refs_6_), channel_id=1, source_target_pairs={{0,16},{16,0},{32,48},{48,32},{1,17},{17,1},{33,49},{49,33},{2,18}... | collective-permute-start | bytes 1572872 | tf_op jit(solution)/shard_map/ppermute | solution.py:33
  69.6 7.6 %all-to-all-done.message_ref = f32[16,4,1280]{2,1,0:T(4,128)S(1)} async-done(((f32[16,4,1280]{2,1,0:T(4,128)}), f32[16,4,1280]{2,1,0:T(4,128)S(1)}, u32[]{:S(2)}, u32[]{:S(2)}) %all-to-all-start) | async-done | bytes 327712 | tf_op jit(solution)/shard_map/all_to_all | solution.py:317
  77.3 0.0 collective-permute-done.18.refs_1_
  77.3 0.8 collective-permute-start.22
  78.1 0.6 collective-permute-start.23
  78.7 0.0 collective-permute-done.20.refs_3_
  78.7 0.0 collective-permute-start.24
  78.7 0.0 collective-permute-done.17.t3
  78.7 0.1 collective-permute-start.25
  78.8 0.1 pad_add_fusion.at_ref
  78.9 1.4 %update_product.1 = f32[64,1024]{1,0:T(8,128)} custom-call(s32[1]{0:T(128)} %bitcast.9.z_ref, f32[16,4,1280]{2,1,0:T(4,128)S(1)} %all-to-all-done.message_ref), custom_call_target="tpu_custom_call" | custom-call | bytes 2097152 | tf_op jit(solution)/shard_map/update_product/pallas_call | solution.py:335
  80.3 2.0 %member_tokens.1 = (bf16[4,256,1024]{2,1,0:T(8,128)(2,1)S(1)}, f32[256,8]{1,0:T(8,128)S(1)}) custom-call(s32[1]{0:T(128)} %bitcast.2.at_ref, bf16[256,1024]{1,0:T(8,128)(2,1)S(1)} %bitcast.12, bf16[256,1024]{1,0:T(8,128)(2,1)S(1)} %collective-permute-done.3.t1, bf16[256,1024]{1,0:T(8,128)(2,1)} %collective-permute-done.4.t2, ...), custom_call_target="tpu_custom_call" | custom-call | bytes 8388608 | tf_op jit(solution)/shard_map/member_tokens/pallas_call | solution.py:322
  82.2 0.0 copy-start.3
  82.2 1.0 %copy-done.3 = bf16[1024,256]{1,0:T(8,128)(2,1)S(1)} copy-done((bf16[1024,256]{1,0:T(8,128)(2,1)S(1)}, bf16[1024,256]{1,0:T(8,128)(2,1)}, u32[]{:S(2)}) %copy-start.3) | copy-done | bytes 524312
  83.3 4.0 %products.2.refs_0_ = f32[256,1024]{1,0:T(8,128)S(1)} custom-call(s32[2]{0:T(128)S(1)} %pad_add_fusion.at_ref, bf16[4,256,1024]{2,1,0:T(8,128)(2,1)S(1)} %get-tuple-element.19.tokens_ref, bf16[1024,256]{1,0:T(8,128)(2,1)S(1)} %pad_maximum_fusion.refs_0_, bf16[1024,256]{1,0:T(8,128)(2,1)S(1)} %copy-done.3, bf16[1024,256]{1,0:T(8,128)(2,1)S(1)} %pad_maximum_fusion.1.refs_2_, ...), custom_call_target="tpu_custom_call" | custom-call | flops 1073741824 | bytes 8388608 | tf_op jit(solution)/shard_map/products/pallas_call | solution.py:150
  87.3 0.0 copy-start.5
  87.3 0.0 collective-permute-done.21.refs_4_
  87.3 3.6 %products.3.sum_ref = f32[256,1024]{1,0:T(8,128)S(1)} custom-call(s32[2]{0:T(128)S(1)} %pad_add_fusion.at_ref, bf16[4,256,1024]{2,1,0:T(8,128)(2,1)S(1)} %get-tuple-element.19.tokens_ref, f32[256,1024]{1,0:T(8,128)S(1)} %products.2.refs_0_, bf16[1024,256]{1,0:T(8,128)(2,1)} %collective-permute-done.18.refs_1_, ...), custom_call_target="tpu_custom_call" | custom-call | flops 536870912 | bytes 8388608 | tf_op jit(solution)/shard_map/products/pallas_call | solution.py:150
  91.0 0.0 collective-permute-done.23.refs_1_
  91.0 0.0 collective-permute-done.24.refs_2_
  91.0 5.4 %collective-permute-done.25.refs_3_ = bf16[1024,256]{1,0:T(8,128)(2,1)} collective-permute-done((bf16[1024,256]{1,0:T(8,128)(2,1)}, bf16[1024,256]{1,0:T(8,128)(2,1)}, u32[]{:S(2)}, u32[]{:S(2)}) %collective-permute-start.25) | collective-permute-done | bytes 524320 | tf_op jit(solution)/shard_map/ppermute | solution.py:33
  96.4 5.8 %values_readout.1 = bf16[256,1024]{1,0:T(8,128)(2,1)} custom-call(s32[2]{0:T(128)S(1)} %pad_add_fusion.at_ref, bf16[4,256,1024]{2,1,0:T(8,128)(2,1)S(1)} %get-tuple-element.19.tokens_ref, f32[256,1024]{1,0:T(8,128)S(1)} %products.3.sum_ref, f32[256,8]{1,0:T(8,128)S(1)} %get-tuple-element.25.projected_ref, bf16[1,1024]{1,0:T(2,128)(2,1)S(1)} %copy-done.5, ...), custom_call_target="tpu_custom_call" | custom-call | flops 536870912 | bytes 12582912 | tf_op jit(solution)/shard_map/values_readout/pallas_call | solution.py:353
  (33 shorter events, 0.4 us)
Async XLA Ops:
  2.9 15.4 %copy-start.6 = (bf16[72,1024]{1,0:T(8,128)(2,1)S(1)}, bf16[72,1024]{1,0:T(8,128)(2,1)}, u32[]{:S(2)}) copy-start(bf16[72,1024]{1,0:T(8,128)(2,1)} %weight_and_noise.1.p0) | copy-start | bytes 442372
  2.9 15.5 %collective-permute-start = (bf16[72,1024]{1,0:T(8,128)(2,1)}, bf16[72,1024]{1,0:T(8,128)(2,1)S(1)}, u32[]{:S(2)}, u32[]{:S(2)}) collective-permute-start(bf16[72,1024]{1,0:T(8,128)(2,1)} %weight_and_noise.1.p0), channel_id=1, source_target_pairs={{4,0},{8,4},{12,8},{0,12},{5,1},{9,5},{13,9},{1,13},{6,2},{10,6},{... | collective-permute-start | bytes 442376 | tf_op jit(solution)/shard_map/ppermute | solution.py:38
  8.1 10.3 %collective-permute-start.1 = (bf16[72,1024]{1,0:T(8,128)(2,1)}, bf16[72,1024]{1,0:T(8,128)(2,1)S(1)}, u32[]{:S(2)}, u32[]{:S(2)}) collective-permute-start(bf16[72,1024]{1,0:T(8,128)(2,1)} %weight_and_noise.1.p0), channel_id=1, source_target_pairs={{12,0},{0,4},{4,8},{8,12},{13,1},{1,5},{5,9},{9,13},{14,2},{2,6},{... | collective-permute-start | bytes 442376 | tf_op jit(solution)/shard_map/ppermute | solution.py:38
  8.1 12.2 %collective-permute-start.2 = (bf16[72,1024]{1,0:T(8,128)(2,1)}, bf16[72,1024]{1,0:T(8,128)(2,1)S(1)}, u32[]{:S(2)}, u32[]{:S(2)}) collective-permute-start(bf16[72,1024]{1,0:T(8,128)(2,1)} %weight_and_noise.1.p0), channel_id=1, source_target_pairs={{8,0},{12,4},{0,8},{4,12},{9,1},{13,5},{1,9},{5,13},{10,2},{14,6},... | collective-permute-start | bytes 442376 | tf_op jit(solution)/shard_map/ppermute | solution.py:38
  8.4 12.0 %collective-permute-start.3 = (bf16[256,1024]{1,0:T(8,128)(2,1)}, bf16[256,1024]{1,0:T(8,128)(2,1)S(1)}, u32[]{:S(2)}, u32[]{:S(2)}) collective-permute-start(bf16[256,1024]{1,0:T(8,128)(2,1)} %bitcast.10), channel_id=1, source_target_pairs={{0,1},{1,0},{2,3},{3,2},{4,5},{5,4},{6,7},{7,6},{8,9},{9,8},{10,11... | collective-permute-start | bytes 1572872 | tf_op jit(solution)/shard_map/ppermute | solution.py:33
  10.4 12.6 %copy-start.1 = (bf16[1,256,1024]{2,1,0:T(8,128)(2,1)S(1)}, bf16[1,256,1024]{2,1,0:T(8,128)(2,1)}, u32[]{:S(2)}) copy-start(bf16[1,256,1024]{2,1,0:T(8,128)(2,1)} %param.9) | copy-start | bytes 1572868
  18.4 24.4 %copy-start.7 = (bf16[72,1024]{1,0:T(8,128)(2,1)}, bf16[72,1024]{1,0:T(8,128)(2,1)S(1)}, u32[]{:S(2)}) copy-start(bf16[72,1024]{1,0:T(8,128)(2,1)S(1)} %collective-permute-done.p1) | copy-start | bytes 442372
  18.4 11.7 %copy-start.8 = (bf16[72,1024]{1,0:T(8,128)(2,1)}, bf16[72,1024]{1,0:T(8,128)(2,1)S(1)}, u32[]{:S(2)}) copy-start(bf16[72,1024]{1,0:T(8,128)(2,1)S(1)} %collective-permute-done.1.p2) | copy-start | bytes 442372
  20.3 16.9 %copy-start.9 = (bf16[72,1024]{1,0:T(8,128)(2,1)}, bf16[72,1024]{1,0:T(8,128)(2,1)S(1)}, u32[]{:S(2)}) copy-start(bf16[72,1024]{1,0:T(8,128)(2,1)S(1)} %collective-permute-done.2.p3) | copy-start | bytes 442372
  20.4 11.6 %collective-permute-start.5 = (bf16[256,256]{1,0:T(8,128)(2,1)S(1)}, bf16[256,256]{1,0:T(8,128)(2,1)S(1)}, u32[]{:S(2)}, u32[]{:S(2)}) collective-permute-start(bf16[256,256]{1,0:T(8,128)(2,1)S(1)} %get-tuple-element.31), channel_id=1, source_target_pairs={{0,16},{16,0},{32,48},{48,32},{1,17},{17,1},{33,49},{49,33},{2,18}... | collective-permute-start | bytes 393224 | tf_op jit(solution)/shard_map/ppermute | solution.py:33
  21.7 10.8 %collective-permute-start.8 = (bf16[256,256]{1,0:T(8,128)(2,1)S(1)}, bf16[256,256]{1,0:T(8,128)(2,1)S(1)}, u32[]{:S(2)}, u32[]{:S(2)}) collective-permute-start(bf16[256,256]{1,0:T(8,128)(2,1)S(1)} %get-tuple-element.30), channel_id=1, source_target_pairs={{0,64},{64,0},{128,192},{192,128},{1,65},{65,1},{129,193},{193,129... | collective-permute-start | bytes 393224 | tf_op jit(solution)/shard_map/ppermute | solution.py:33
  23.0 24.3 %collective-permute-start.4 = (bf16[256,1024]{1,0:T(8,128)(2,1)S(1)}, bf16[256,1024]{1,0:T(8,128)(2,1)}, u32[]{:S(2)}, u32[]{:S(2)}) collective-permute-start(bf16[256,1024]{1,0:T(8,128)(2,1)S(1)} %bitcast.11), channel_id=1, source_target_pairs={{0,2},{2,0},{1,3},{3,1},{4,6},{6,4},{5,7},{7,5},{8,10},{10,8},{9,1... | collective-permute-start | bytes 1572872 | tf_op jit(solution)/shard_map/ppermute | solution.py:33
  28.3 5.0 %collective-permute-start.11 = (bf16[256,256]{1,0:T(8,128)(2,1)S(1)}, bf16[256,256]{1,0:T(8,128)(2,1)S(1)}, u32[]{:S(2)}, u32[]{:S(2)}) collective-permute-start(bf16[256,256]{1,0:T(8,128)(2,1)S(1)} %get-tuple-element.29), channel_id=1, source_target_pairs={{0,48},{16,32},{32,16},{48,0},{1,49},{17,33},{33,17},{49,1},{2,50}... | collective-permute-start | bytes 393224 | tf_op jit(solution)/shard_map/ppermute | solution.py:33
  30.1 50.2 %copy-start.4 = (bf16[1,4096]{1,0:T(2,128)(2,1)S(1)}, bf16[1,4096]{1,0:T(2,128)(2,1)}, u32[]{:S(2)}) copy-start(bf16[1,4096]{1,0:T(2,128)(2,1)} %noise_in_ref.1) | copy-start | bytes 24580
  30.1 5.4 %collective-permute-start.14 = (bf16[256,256]{1,0:T(8,128)(2,1)S(1)}, bf16[256,256]{1,0:T(8,128)(2,1)S(1)}, u32[]{:S(2)}, u32[]{:S(2)}) collective-permute-start(bf16[256,256]{1,0:T(8,128)(2,1)S(1)} %get-tuple-element.28), channel_id=1, source_target_pairs={{0,192},{64,128},{128,64},{192,0},{1,193},{65,129},{129,65},{193,1... | collective-permute-start | bytes 393224 | tf_op jit(solution)/shard_map/ppermute | solution.py:33
  32.0 5.7 %collective-permute-start.6 = (bf16[512,256]{1,0:T(8,128)(2,1)S(1)}, bf16[512,256]{1,0:T(8,128)(2,1)S(1)}, u32[]{:S(2)}, u32[]{:S(2)}) collective-permute-start(bf16[512,256]{1,0:T(8,128)(2,1)S(1)} %pad_maximum_fusion.4), channel_id=1, source_target_pairs={{0,64},{64,0},{128,192},{192,128},{1,65},{65,1},{129,193},{193,129... | collective-permute-start | bytes 786440 | tf_op jit(solution)/shard_map/ppermute | solution.py:33
  32.5 6.2 %collective-permute-start.9 = (bf16[512,256]{1,0:T(8,128)(2,1)S(1)}, bf16[512,256]{1,0:T(8,128)(2,1)S(1)}, u32[]{:S(2)}, u32[]{:S(2)}) collective-permute-start(bf16[512,256]{1,0:T(8,128)(2,1)S(1)} %pad_maximum_fusion.5), channel_id=1, source_target_pairs={{0,16},{16,0},{32,48},{48,32},{1,17},{17,1},{33,49},{49,33},{2,18}... | collective-permute-start | bytes 786440 | tf_op jit(solution)/shard_map/ppermute | solution.py:33
  33.3 8.1 %collective-permute-start.12 = (bf16[512,256]{1,0:T(8,128)(2,1)S(1)}, bf16[512,256]{1,0:T(8,128)(2,1)S(1)}, u32[]{:S(2)}, u32[]{:S(2)}) collective-permute-start(bf16[512,256]{1,0:T(8,128)(2,1)S(1)} %pad_maximum_fusion.6), channel_id=1, source_target_pairs={{0,192},{64,128},{128,64},{192,0},{1,193},{65,129},{129,65},{193,1... | collective-permute-start | bytes 786440 | tf_op jit(solution)/shard_map/ppermute | solution.py:33
  35.5 6.9 %collective-permute-start.15 = (bf16[512,256]{1,0:T(8,128)(2,1)S(1)}, bf16[512,256]{1,0:T(8,128)(2,1)S(1)}, u32[]{:S(2)}, u32[]{:S(2)}) collective-permute-start(bf16[512,256]{1,0:T(8,128)(2,1)S(1)} %pad_maximum_fusion.7), channel_id=1, source_target_pairs={{0,48},{16,32},{32,16},{48,0},{1,49},{17,33},{33,17},{49,1},{2,50}... | collective-permute-start | bytes 786440 | tf_op jit(solution)/shard_map/ppermute | solution.py:33
  37.7 13.7 %collective-permute-start.7 = (bf16[1024,256]{1,0:T(8,128)(2,1)S(1)}, bf16[1024,256]{1,0:T(8,128)(2,1)S(1)}, u32[]{:S(2)}, u32[]{:S(2)}) collective-permute-start(bf16[1024,256]{1,0:T(8,128)(2,1)S(1)} %pad_maximum_fusion.refs_0_), channel_id=1, source_target_pairs={{0,48},{16,32},{32,16},{48,0},{1,49},{17,33},{33,17},{49,1},{2,50}... | collective-permute-start | bytes 1572872 | tf_op jit(solution)/shard_map/ppermute | solution.py:33
  38.7 14.7 %collective-permute-start.10 = (bf16[1024,256]{1,0:T(8,128)(2,1)S(1)}, bf16[1024,256]{1,0:T(8,128)(2,1)}, u32[]{:S(2)}, u32[]{:S(2)}) collective-permute-start(bf16[1024,256]{1,0:T(8,128)(2,1)S(1)} %pad_maximum_fusion.1.refs_2_), channel_id=1, source_target_pairs={{0,192},{64,128},{128,64},{192,0},{1,193},{65,129},{129,65},{193,1... | collective-permute-start | bytes 1572872 | tf_op jit(solution)/shard_map/ppermute | solution.py:33
  41.4 12.0 %collective-permute-start.13 = (bf16[1024,256]{1,0:T(8,128)(2,1)S(1)}, bf16[1024,256]{1,0:T(8,128)(2,1)}, u32[]{:S(2)}, u32[]{:S(2)}) collective-permute-start(bf16[1024,256]{1,0:T(8,128)(2,1)S(1)} %pad_maximum_fusion.2.refs_4_), channel_id=1, source_target_pairs={{0,16},{16,0},{32,48},{48,32},{1,17},{17,1},{33,49},{49,33},{2,18}... | collective-permute-start | bytes 1572872 | tf_op jit(solution)/shard_map/ppermute | solution.py:33
  42.5 10.9 %collective-permute-start.16 = (bf16[1024,256]{1,0:T(8,128)(2,1)S(1)}, bf16[1024,256]{1,0:T(8,128)(2,1)}, u32[]{:S(2)}, u32[]{:S(2)}) collective-permute-start(bf16[1024,256]{1,0:T(8,128)(2,1)S(1)} %pad_maximum_fusion.3.refs_6_), channel_id=1, source_target_pairs={{0,64},{64,0},{128,192},{192,128},{1,65},{65,1},{129,193},{193,129... | collective-permute-start | bytes 1572872 | tf_op jit(solution)/shard_map/ppermute | solution.py:33
  47.3 30.7 %collective-permute-start.19 = (bf16[1024,256]{1,0:T(8,128)(2,1)S(1)}, bf16[1024,256]{1,0:T(8,128)(2,1)}, u32[]{:S(2)}, u32[]{:S(2)}) collective-permute-start(bf16[1024,256]{1,0:T(8,128)(2,1)S(1)} %pad_maximum_fusion.1.refs_2_), channel_id=1, source_target_pairs={{0,48},{16,32},{32,16},{48,0},{1,49},{17,33},{33,17},{49,1},{2,50}... | collective-permute-start | bytes 1572872 | tf_op jit(solution)/shard_map/ppermute | solution.py:33
  51.5 1.9 %copy-start.2 = (bf16[1024,256]{1,0:T(8,128)(2,1)}, bf16[1024,256]{1,0:T(8,128)(2,1)S(1)}, u32[]{:S(2)}) copy-start(bf16[1024,256]{1,0:T(8,128)(2,1)S(1)} %collective-permute-done.7.refs_1_) | copy-start | bytes 1572868
  51.5 25.8 %collective-permute-start.18 = (bf16[1024,256]{1,0:T(8,128)(2,1)S(1)}, bf16[1024,256]{1,0:T(8,128)(2,1)}, u32[]{:S(2)}, u32[]{:S(2)}) collective-permute-start(bf16[1024,256]{1,0:T(8,128)(2,1)S(1)} %pad_maximum_fusion.refs_0_), channel_id=1, source_target_pairs={{0,192},{64,128},{128,64},{192,0},{1,193},{65,129},{129,65},{193,1... | collective-permute-start | bytes 1572872 | tf_op jit(solution)/shard_map/ppermute | solution.py:33
  53.4 25.3 %collective-permute-start.20 = (bf16[1024,256]{1,0:T(8,128)(2,1)S(1)}, bf16[1024,256]{1,0:T(8,128)(2,1)}, u32[]{:S(2)}, u32[]{:S(2)}) collective-permute-start(bf16[1024,256]{1,0:T(8,128)(2,1)S(1)} %pad_maximum_fusion.2.refs_4_), channel_id=1, source_target_pairs={{0,64},{64,0},{128,192},{192,128},{1,65},{65,1},{129,193},{193,129... | collective-permute-start | bytes 1572872 | tf_op jit(solution)/shard_map/ppermute | solution.py:33
  53.4 25.2 %collective-permute-start.17 = (bf16[256,1024]{1,0:T(8,128)(2,1)}, bf16[256,1024]{1,0:T(8,128)(2,1)}, u32[]{:S(2)}, u32[]{:S(2)}) collective-permute-start(bf16[256,1024]{1,0:T(8,128)(2,1)} %collective-permute-done.4.t2), channel_id=1, source_target_pairs={{0,1},{1,0},{2,3},{3,2},{4,5},{5,4},{6,7},{7,6},{8,9},{9,8},{10,11... | collective-permute-start | bytes 1572872 | tf_op jit(solution)/shard_map/ppermute | solution.py:33
  64.1 13.2 %all-to-all-start = ((f32[16,4,1280]{2,1,0:T(4,128)}), f32[16,4,1280]{2,1,0:T(4,128)S(1)}, u32[]{:S(2)}, u32[]{:S(2)}) async-start(f32[16,4,1280]{2,1,0:T(4,128)} %noise_message.1), calls=%async_computation | async-start | bytes 655360 | tf_op jit(solution)/shard_map/all_to_all | solution.py:317
  68.3 19.1 %collective-permute-start.21 = (bf16[1024,256]{1,0:T(8,128)(2,1)S(1)}, bf16[1024,256]{1,0:T(8,128)(2,1)}, u32[]{:S(2)}, u32[]{:S(2)}) collective-permute-start(bf16[1024,256]{1,0:T(8,128)(2,1)S(1)} %pad_maximum_fusion.3.refs_6_), channel_id=1, source_target_pairs={{0,16},{16,0},{32,48},{48,32},{1,17},{17,1},{33,49},{49,33},{2,18}... | collective-permute-start | bytes 1572872 | tf_op jit(solution)/shard_map/ppermute | solution.py:33
  77.3 13.7 %collective-permute-start.22 = (bf16[1024,256]{1,0:T(8,128)(2,1)}, bf16[1024,256]{1,0:T(8,128)(2,1)}, u32[]{:S(2)}, u32[]{:S(2)}) collective-permute-start(bf16[1024,256]{1,0:T(8,128)(2,1)} %copy-done.2), channel_id=1, source_target_pairs={{0,192},{64,128},{128,64},{192,0},{1,193},{65,129},{129,65},{193,1... | collective-permute-start | bytes 1572872 | tf_op jit(solution)/shard_map/ppermute | solution.py:33
  78.1 12.9 %collective-permute-start.23 = (bf16[1024,256]{1,0:T(8,128)(2,1)}, bf16[1024,256]{1,0:T(8,128)(2,1)}, u32[]{:S(2)}, u32[]{:S(2)}) collective-permute-start(bf16[1024,256]{1,0:T(8,128)(2,1)} %collective-permute-done.10.refs_3_), channel_id=1, source_target_pairs={{0,48},{16,32},{32,16},{48,0},{1,49},{17,33},{33,17},{49,1},{2,50}... | collective-permute-start | bytes 1572872 | tf_op jit(solution)/shard_map/ppermute | solution.py:33
  78.7 12.3 %collective-permute-start.24 = (bf16[1024,256]{1,0:T(8,128)(2,1)}, bf16[1024,256]{1,0:T(8,128)(2,1)}, u32[]{:S(2)}, u32[]{:S(2)}) collective-permute-start(bf16[1024,256]{1,0:T(8,128)(2,1)} %collective-permute-done.13.refs_5_), channel_id=1, source_target_pairs={{0,64},{64,0},{128,192},{192,128},{1,65},{65,1},{129,193},{193,129... | collective-permute-start | bytes 1572872 | tf_op jit(solution)/shard_map/ppermute | solution.py:33
  78.7 17.8 %collective-permute-start.25 = (bf16[1024,256]{1,0:T(8,128)(2,1)}, bf16[1024,256]{1,0:T(8,128)(2,1)}, u32[]{:S(2)}, u32[]{:S(2)}) collective-permute-start(bf16[1024,256]{1,0:T(8,128)(2,1)} %collective-permute-done.16.refs_7_), channel_id=1, source_target_pairs={{0,16},{16,0},{32,48},{48,32},{1,17},{17,1},{33,49},{49,33},{2,18}... | collective-permute-start | bytes 1572872 | tf_op jit(solution)/shard_map/ppermute | solution.py:33
  82.2 1.0 %copy-start.3 = (bf16[1024,256]{1,0:T(8,128)(2,1)S(1)}, bf16[1024,256]{1,0:T(8,128)(2,1)}, u32[]{:S(2)}) copy-start(bf16[1024,256]{1,0:T(8,128)(2,1)} %copy-done.2) | copy-start | bytes 1572868
  87.3 9.1 %copy-start = (bf16[8,1024,256]{2,1,0:T(8,128)(2,1)S(1)}, bf16[8,1024,256]{2,1,0:T(8,128)(2,1)}, u32[]{:S(2)}) copy-start(bf16[8,1024,256]{2,1,0:T(8,128)(2,1)} %decayed_scores.1.scores_ref) | copy-start | bytes 12582916
  87.3 9.1 %copy-start.5 = (bf16[1,1024]{1,0:T(2,128)(2,1)S(1)}, bf16[1,1024]{1,0:T(2,128)(2,1)}, u32[]{:S(2)}) copy-start(bf16[1,1024]{1,0:T(2,128)(2,1)} %noise_ref.1) | copy-start | bytes 6148

commit v7 on v5

--- a/solution.py
+++ b/solution.py
@@ -189,6 +189,28 @@
             ).astype(BF16)
 
 
+def message_kernel(utility_ref, noise_in_ref, noise_out_ref, out_ref):
+    weighted = noise_in_ref[...].astype(F32) * (utility_ref[0] / math.sqrt(SIDE**3))
+    plain = noise_out_ref[...].astype(F32)
+    for i in range(out_ref.shape[0]):
+        first = i // 2 * LANES
+        out_ref[i, :, :LANES] = weighted[:, first : first + LANES]
+        out_ref[i, :, LANES:] = plain
+
+
+def update_kernel(z_ref, message_ref, out_ref):
+    rows = out_ref.shape[0]
+    message = message_ref[:, 0, :]
+    weighted = pltpu.roll(message[:, :LANES], lax.rem(z_ref[0], 2) * rows, 1)
+    out_ref[...] = lax.dot_general(
+        weighted,
+        message[:, LANES:],
+        (((0,), (0,)), ((), ())),
+        precision=HIGHEST,
+        preferred_element_type=F32,
+    )[:rows]
+
+
 def params(mib):
     return pltpu.CompilerParams(vmem_limit_bytes=mib << 20)
 
@@ -233,15 +255,14 @@
         near = lax.dynamic_update_slice(near, part, (lax.rem(z + step, SIDE) * rows, 0))
     mate = swap(tokens, "core", 1)
     population = lax.axis_size(POP)
-    weighted = noise_in.astype(F32) * (utilities / math.sqrt(population))[:, None]
-    message = jnp.concatenate(
-        [
-            weighted.reshape(population, rows),
-            jnp.zeros((population, LANES - rows), F32),
-            jnp.broadcast_to(noise_out.astype(F32), (population, width)),
-        ],
-        1,
-    )
+    message = pl.pallas_call(
+        message_kernel,
+        out_shape=jax.ShapeDtypeStruct((population, 1, LANES + width), F32),
+        in_specs=[SMEM, VMEM, VMEM],
+        out_specs=VMEM,
+        cost_estimate=cost(0, 1 << 19),
+        name="noise_message",
+    )(utilities, noise_in, noise_out)
     scores = score_heads(live_length, receptance, keys, log_decay)
     near, mate, message, scores = lax.optimization_barrier((near, mate, message, scores))
 
@@ -276,13 +297,14 @@
         name="member_tokens",
     )(tp, tokens, mate, twin, both, noise_in.reshape(4, 1, width))
 
-    update = lax.dot_general(
-        message[:, :rows],
-        message[:, LANES:],
-        (((0,), (0,)), ((), ())),
-        precision=HIGHEST,
-        preferred_element_type=F32,
-    )
+    update = pl.pallas_call(
+        update_kernel,
+        out_shape=jax.ShapeDtypeStruct((rows, width), F32),
+        in_specs=[SMEM, VMEM],
+        out_specs=VMEM,
+        cost_estimate=cost(0, 1 << 20),
+        name="update_product",
+    )(z.reshape(1), message)
 
     at = jnp.stack([lax.axis_index("y"), lax.axis_index("x")])
     total = product(

time: 93.3 us -> 92.9 us (level)
  Pallas kernels: 24 us -> 27.7 us
  local copies, waits for them, and re-layouts: 3.15 us -> 1.14 us
  other arithmetic: 1.75 us -> 0.29 us
  starting transfers between devices: 44.5 us -> 45.7 us
  matrix products: 1.12 us -> 0 us
    pallas_call x0 -> x2, Pallas kernels: none -> 3.81 us  [the longest x1 2.34 us: body(): pl.pallas_call(update_kernel, out_shape=jax.ShapeDtypeStruct((rows, width...]
    ppermute x23, starting transfers between devices: 30.3 us -> 32 us  [swap(): return lax.ppermute(array, axis, [(i, i ^ mask) for i in range(size)])]
    dot_general x1 -> x0, matrix products: 1.12 us -> none  [body(): lax.dot_general(message[:, :rows], message[:, LANES:], (((0,), (0,)), (()...]
    unnamed x9 -> x10, local copies, waits for them, and re-layouts: 1 us -> 0.03 us
  transfers between devices with their start and end apart: 27 -> 27, of which waited for: 6 -> 5; matrix products, arithmetic and copies ran while one was open for 5% -> 1% of each run, Pallas kernels for 20% -> 24%
where the time goes in v7:
time: 92.9 us; the launch traced here: 92.1 us
  starting transfers between devices  45.7 us (49%)
  Pallas kernels  27.7 us (30%)
  waiting for transfers between devices  14.9 us (16%)
  between operations  2.33 us (3%)
  local copies, waits for them, and re-layouts  1.14 us (1%)
    ppermute x23, starting transfers between devices, swap(): return lax.ppermute(array, axis, [(i, i ^ mask) for i in range(size)])  32 us
    ppermute x23, waiting for transfers between devices, swap(): return lax.ppermute(array, axis, [(i, i ^ mask) for i in range(size)])  11.7 us
    pallas_call x2, Pallas kernels, product(): pl.pallas_call(functools.partial(product_kernel, ways, before is not None...  8.37 us
    pallas_call x1, Pallas kernels, score_heads(): pl.pallas_call(score_kernel, out_shape=jax.ShapeDtypeStruct((count, 4 * l...  7.8 us
    ppermute x3, starting transfers between devices, fetch(): lax.ppermute(array, axis, [((i + step) % size, i) for i in range(size)])  7.17 us
    all_to_all x1, starting transfers between devices, body(): lax.all_to_all(after(message, *held), POP, split_axis=0, concat_axis=0, t...  6.58 us
    pallas_call x1, Pallas kernels, body(): pl.pallas_call(readout_kernel, out_shape=jax.ShapeDtypeStruct((length, wi...  5.74 us
    all_to_all x1, waiting for transfers between devices, body(): lax.all_to_all(after(message, *held), POP, split_axis=0, concat_axis=0, t...  3.21 us
  transfers between devices with their start and end apart: 27, of which 5 were waited for; matrix products, arithmetic and copies ran while one was open for 1% of the time, Pallas kernels for 24%

profile of v7, /device:TPU:32, one launch (start us, length us, event | category | flops | bytes accessed | tf_op | source)
XLA Modules:
  0.0 92.1 jit_solution(17162326334568922732)
XLA Ops:
  0.6 0.1 collective-permute-start.3
  0.7 1.9 %collective-permute-start = (bf16[64,1024]{1,0:T(8,128)(2,1)}, bf16[64,1024]{1,0:T(8,128)(2,1)S(1)}, u32[]{:S(2)}, u32[]{:S(2)}) collective-permute-start(bf16[64,1024]{1,0:T(8,128)(2,1)} %param.13), channel_id=1, source_target_pairs={{4,0},{8,4},{12,8},{0,12},{5,1},{9,5},{13,9},{1,13},{6,2},{10,6},{... | collective-permute-start | bytes 393224 | tf_op jit(solution)/shard_map/ppermute | solution.py:38
  2.7 0.2 collective-permute-start.1
  2.8 5.1 %collective-permute-start.2 = (bf16[64,1024]{1,0:T(8,128)(2,1)}, bf16[64,1024]{1,0:T(8,128)(2,1)S(1)}, u32[]{:S(2)}, u32[]{:S(2)}) collective-permute-start(bf16[64,1024]{1,0:T(8,128)(2,1)} %param.13), channel_id=1, source_target_pairs={{8,0},{12,4},{0,8},{4,12},{9,1},{13,5},{1,9},{5,13},{10,2},{14,6},... | collective-permute-start | bytes 393224 | tf_op jit(solution)/shard_map/ppermute | solution.py:38
  7.9 0.1 broadcast_in_dim.3
  8.0 0.0 copy-start.1
  8.0 1.0 %constant_dynamic-update-slice_fusion.3 = bf16[256,1024]{1,0:T(8,128)(2,1)S(1)} fusion(bf16[256,1024]{1,0:T(8,128)(2,1)S(1)} %broadcast_in_dim.3, bf16[64,1024]{1,0:T(8,128)(2,1)} %param.13, s32[]{:T(128)S(6)} %select_n.12), kind=kLoop, calls=%fused_computation.11 | loop fusion | bytes 262148 | tf_op jit(solution)/shard_map/dynamic_update_slice | solution.py:255
  10.3 1.5 %noise_message.1 = f32[64,1,1152]{2,1,0:T(1,128)} custom-call(f32[1]{0:T(128)S(6)} %copy.15.utility_ref, bf16[1,4096]{1,0:T(2,128)(2,1)} %noise_in_ref.1, bf16[1,1024]{1,0:T(2,128)(2,1)} %noise_ref.1), custom_call_target="tpu_custom_call" | custom-call | bytes 524288 | tf_op jit(solution)/shard_map/noise_message/pallas_call | solution.py:258
  11.7 7.8 %decayed_scores.1.scores_ref = bf16[8,1024,256]{2,1,0:T(8,128)(2,1)} custom-call(s32[1]{0:T(128)S(6)} %copy.16.live_ref, bf16[256,1024]{1,0:T(8,128)(2,1)} %bitcast.14, bf16[256,1024]{1,0:T(8,128)(2,1)} %bitcast.15, bf16[256,1024]{1,0:T(8,128)(2,1)} %bitcast.16), custom_call_target="tpu_custom_call" | custom-call | bytes 20971520 | tf_op jit(solution)/shard_map/decayed_scores/pallas_call | solution.py:230
  19.5 0.0 collective-permute-done
  19.6 0.0 collective-permute-done.1
  19.6 0.0 collective-permute-done.2
  19.6 0.0 copy-start.2
  19.6 0.0 collective-permute-done.3.t1
  19.7 3.1 %collective-permute-start.14 = (bf16[256,256]{1,0:T(8,128)(2,1)S(1)}, bf16[256,256]{1,0:T(8,128)(2,1)S(1)}, u32[]{:S(2)}, u32[]{:S(2)}) collective-permute-start(bf16[256,256]{1,0:T(8,128)(2,1)S(1)} %get-tuple-element.22), channel_id=1, source_target_pairs={{0,192},{64,128},{128,64},{192,0},{1,193},{65,129},{129,65},{193,1... | collective-permute-start | bytes 393224 | tf_op jit(solution)/shard_map/ppermute | solution.py:33
  22.8 2.8 %collective-permute-start.11 = (bf16[256,256]{1,0:T(8,128)(2,1)S(1)}, bf16[256,256]{1,0:T(8,128)(2,1)S(1)}, u32[]{:S(2)}, u32[]{:S(2)}) collective-permute-start(bf16[256,256]{1,0:T(8,128)(2,1)S(1)} %get-tuple-element.23), channel_id=1, source_target_pairs={{0,48},{16,32},{32,16},{48,0},{1,49},{17,33},{33,17},{49,1},{2,50}... | collective-permute-start | bytes 393224 | tf_op jit(solution)/shard_map/ppermute | solution.py:33
  25.6 0.1 collective-permute-start.8
  25.7 0.2 collective-permute-start.5
  25.9 4.5 %collective-permute-start.4 = (bf16[256,1024]{1,0:T(8,128)(2,1)S(1)}, bf16[256,1024]{1,0:T(8,128)(2,1)}, u32[]{:S(2)}, u32[]{:S(2)}) collective-permute-start(bf16[256,1024]{1,0:T(8,128)(2,1)S(1)} %bitcast.11), channel_id=1, source_target_pairs={{0,2},{2,0},{1,3},{3,1},{4,6},{6,4},{5,7},{7,5},{8,10},{10,8},{9,1... | collective-permute-start | bytes 1572872 | tf_op jit(solution)/shard_map/ppermute | solution.py:33
  30.4 0.0 collective-permute-done.14
  30.5 1.2 %collective-permute-start.15 = (bf16[512,256]{1,0:T(8,128)(2,1)S(1)}, bf16[512,256]{1,0:T(8,128)(2,1)S(1)}, u32[]{:S(2)}, u32[]{:S(2)}) collective-permute-start(bf16[512,256]{1,0:T(8,128)(2,1)S(1)} %pad_maximum_fusion.7), channel_id=1, source_target_pairs={{0,48},{16,32},{32,16},{48,0},{1,49},{17,33},{33,17},{49,1},{2,50}... | collective-permute-start | bytes 786440 | tf_op jit(solution)/shard_map/ppermute | solution.py:33
  31.7 0.0 collective-permute-done.11
  31.7 1.1 %collective-permute-start.12 = (bf16[512,256]{1,0:T(8,128)(2,1)S(1)}, bf16[512,256]{1,0:T(8,128)(2,1)S(1)}, u32[]{:S(2)}, u32[]{:S(2)}) collective-permute-start(bf16[512,256]{1,0:T(8,128)(2,1)S(1)} %pad_maximum_fusion.6), channel_id=1, source_target_pairs={{0,192},{64,128},{128,64},{192,0},{1,193},{65,129},{129,65},{193,1... | collective-permute-start | bytes 786440 | tf_op jit(solution)/shard_map/ppermute | solution.py:33
  32.8 0.0 collective-permute-done.8
  32.9 0.8 collective-permute-start.9
  33.6 0.0 collective-permute-done.5
  33.7 0.9 %collective-permute-start.6 = (bf16[512,256]{1,0:T(8,128)(2,1)S(1)}, bf16[512,256]{1,0:T(8,128)(2,1)S(1)}, u32[]{:S(2)}, u32[]{:S(2)}) collective-permute-start(bf16[512,256]{1,0:T(8,128)(2,1)S(1)} %pad_maximum_fusion.4), channel_id=1, source_target_pairs={{0,64},{64,0},{128,192},{192,128},{1,65},{65,1},{129,193},{193,129... | collective-permute-start | bytes 786440 | tf_op jit(solution)/shard_map/ppermute | solution.py:33
  34.6 3.8 %collective-permute-done.15 = bf16[512,256]{1,0:T(8,128)(2,1)S(1)} collective-permute-done((bf16[512,256]{1,0:T(8,128)(2,1)S(1)}, bf16[512,256]{1,0:T(8,128)(2,1)S(1)}, u32[]{:S(2)}, u32[]{:S(2)}) %collective-permute-start.15) | collective-permute-done | bytes 262176 | tf_op jit(solution)/shard_map/ppermute | solution.py:33
  38.5 1.7 %collective-permute-start.16 = (bf16[1024,256]{1,0:T(8,128)(2,1)S(1)}, bf16[1024,256]{1,0:T(8,128)(2,1)}, u32[]{:S(2)}, u32[]{:S(2)}) collective-permute-start(bf16[1024,256]{1,0:T(8,128)(2,1)S(1)} %pad_maximum_fusion.3.refs_6_), channel_id=1, source_target_pairs={{0,64},{64,0},{128,192},{192,128},{1,65},{65,1},{129,193},{193,129... | collective-permute-start | bytes 1572872 | tf_op jit(solution)/shard_map/ppermute | solution.py:33
  40.2 0.0 collective-permute-done.12
  40.3 0.6 collective-permute-start.13
  40.9 0.0 collective-permute-done.9
  40.9 1.5 %collective-permute-start.10 = (bf16[1024,256]{1,0:T(8,128)(2,1)S(1)}, bf16[1024,256]{1,0:T(8,128)(2,1)}, u32[]{:S(2)}, u32[]{:S(2)}) collective-permute-start(bf16[1024,256]{1,0:T(8,128)(2,1)S(1)} %pad_maximum_fusion.1.refs_2_), channel_id=1, source_target_pairs={{0,192},{64,128},{128,64},{192,0},{1,193},{65,129},{129,65},{193,1... | collective-permute-start | bytes 1572872 | tf_op jit(solution)/shard_map/ppermute | solution.py:33
  42.5 3.1 %collective-permute-start.7 = (bf16[1024,256]{1,0:T(8,128)(2,1)S(1)}, bf16[1024,256]{1,0:T(8,128)(2,1)}, u32[]{:S(2)}, u32[]{:S(2)}) collective-permute-start(bf16[1024,256]{1,0:T(8,128)(2,1)S(1)} %pad_maximum_fusion.refs_0_), channel_id=1, source_target_pairs={{0,48},{16,32},{32,16},{48,0},{1,49},{17,33},{33,17},{49,1},{2,50}... | collective-permute-start | bytes 1572872 | tf_op jit(solution)/shard_map/ppermute | solution.py:33
  45.6 6.6 %all-to-all-start = ((f32[64,1,1152]{2,1,0:T(1,128)}), f32[64,1,1152]{2,1,0:T(1,128)S(1)}, u32[]{:S(2)}, u32[]{:S(2)}) async-start(f32[64,1,1152]{2,1,0:T(1,128)} %noise_message.1), calls=%async_computation | async-start | bytes 589824 | tf_op jit(solution)/shard_map/all_to_all | solution.py:276
  52.2 1.6 %collective-permute-done.4.t2 = bf16[256,1024]{1,0:T(8,128)(2,1)} collective-permute-done((bf16[256,1024]{1,0:T(8,128)(2,1)S(1)}, bf16[256,1024]{1,0:T(8,128)(2,1)}, u32[]{:S(2)}, u32[]{:S(2)}) %collective-permute-start.4) | collective-permute-done | bytes 524320 | tf_op jit(solution)/shard_map/ppermute | solution.py:33
  53.7 1.7 %collective-permute-start.21 = (bf16[1024,256]{1,0:T(8,128)(2,1)S(1)}, bf16[1024,256]{1,0:T(8,128)(2,1)}, u32[]{:S(2)}, u32[]{:S(2)}) collective-permute-start(bf16[1024,256]{1,0:T(8,128)(2,1)S(1)} %pad_maximum_fusion.3.refs_6_), channel_id=1, source_target_pairs={{0,16},{16,0},{32,48},{48,32},{1,17},{17,1},{33,49},{49,33},{2,18}... | collective-permute-start | bytes 1572872 | tf_op jit(solution)/shard_map/ppermute | solution.py:33
  55.4 0.0 collective-permute-done.16.refs_7_
  55.4 1.7 %collective-permute-start.20 = (bf16[1024,256]{1,0:T(8,128)(2,1)S(1)}, bf16[1024,256]{1,0:T(8,128)(2,1)}, u32[]{:S(2)}, u32[]{:S(2)}) collective-permute-start(bf16[1024,256]{1,0:T(8,128)(2,1)S(1)} %pad_maximum_fusion.2.refs_4_), channel_id=1, source_target_pairs={{0,64},{64,0},{128,192},{192,128},{1,65},{65,1},{129,193},{193,129... | collective-permute-start | bytes 1572872 | tf_op jit(solution)/shard_map/ppermute | solution.py:33
  57.1 0.0 collective-permute-done.13.refs_5_
  57.1 0.5 collective-permute-start.19
  57.6 0.0 collective-permute-done.10.refs_3_
  57.6 0.0 collective-permute-done.7.refs_1_
  57.6 0.0 collective-permute-start.17
  57.6 2.1 %collective-permute-start.18 = (bf16[1024,256]{1,0:T(8,128)(2,1)S(1)}, bf16[1024,256]{1,0:T(8,128)(2,1)}, u32[]{:S(2)}, u32[]{:S(2)}) collective-permute-start(bf16[1024,256]{1,0:T(8,128)(2,1)S(1)} %pad_maximum_fusion.refs_0_), channel_id=1, source_target_pairs={{0,192},{64,128},{128,64},{192,0},{1,193},{65,129},{129,65},{193,1... | collective-permute-start | bytes 1572872 | tf_op jit(solution)/shard_map/ppermute | solution.py:33
  59.8 3.2 %all-to-all-done.message_ref = f32[64,1,1152]{2,1,0:T(1,128)S(1)} async-done(((f32[64,1,1152]{2,1,0:T(1,128)}), f32[64,1,1152]{2,1,0:T(1,128)S(1)}, u32[]{:S(2)}, u32[]{:S(2)}) %all-to-all-start) | async-done | bytes 294944 | tf_op jit(solution)/shard_map/all_to_all | solution.py:276
  63.0 5.8 %collective-permute-done.21.refs_4_ = bf16[1024,256]{1,0:T(8,128)(2,1)} collective-permute-done((bf16[1024,256]{1,0:T(8,128)(2,1)S(1)}, bf16[1024,256]{1,0:T(8,128)(2,1)}, u32[]{:S(2)}, u32[]{:S(2)}) %collective-permute-start.21) | collective-permute-done | bytes 524320 | tf_op jit(solution)/shard_map/ppermute | solution.py:33
  68.8 1.8 %collective-permute-start.24 = (bf16[1024,256]{1,0:T(8,128)(2,1)}, bf16[1024,256]{1,0:T(8,128)(2,1)}, u32[]{:S(2)}, u32[]{:S(2)}) collective-permute-start(bf16[1024,256]{1,0:T(8,128)(2,1)} %collective-permute-done.13.refs_5_), channel_id=1, source_target_pairs={{0,64},{64,0},{128,192},{192,128},{1,65},{65,1},{129,193},{193,129... | collective-permute-start | bytes 1572872 | tf_op jit(solution)/shard_map/ppermute | solution.py:33
  70.6 0.0 collective-permute-done.20.refs_3_
  70.6 1.3 %collective-permute-start.23 = (bf16[1024,256]{1,0:T(8,128)(2,1)}, bf16[1024,256]{1,0:T(8,128)(2,1)}, u32[]{:S(2)}, u32[]{:S(2)}) collective-permute-start(bf16[1024,256]{1,0:T(8,128)(2,1)} %collective-permute-done.10.refs_3_), channel_id=1, source_target_pairs={{0,48},{16,32},{32,16},{48,0},{1,49},{17,33},{33,17},{49,1},{2,50}... | collective-permute-start | bytes 1572872 | tf_op jit(solution)/shard_map/ppermute | solution.py:33
  71.9 0.0 collective-permute-done.19.refs_2_
  71.9 1.0 %collective-permute-start.22 = (bf16[1024,256]{1,0:T(8,128)(2,1)}, bf16[1024,256]{1,0:T(8,128)(2,1)}, u32[]{:S(2)}, u32[]{:S(2)}) collective-permute-start(bf16[1024,256]{1,0:T(8,128)(2,1)} %collective-permute-done.7.refs_1_), channel_id=1, source_target_pairs={{0,192},{64,128},{128,64},{192,0},{1,193},{65,129},{129,65},{193,1... | collective-permute-start | bytes 1572872 | tf_op jit(solution)/shard_map/ppermute | solution.py:33
  72.8 0.0 collective-permute-start.25
  72.9 0.1 pad_add_fusion.at_ref
  73.0 2.3 %update_product.1 = f32[64,1024]{1,0:T(8,128)} custom-call(s32[1]{0:T(128)} %bitcast.9.z_ref, f32[64,1,1152]{2,1,0:T(1,128)} %copy-done.4), custom_call_target="tpu_custom_call" | custom-call | bytes 1048576 | tf_op jit(solution)/shard_map/update_product/pallas_call | solution.py:300
  75.3 2.0 %member_tokens.1 = (bf16[4,256,1024]{2,1,0:T(8,128)(2,1)S(1)}, f32[256,8]{1,0:T(8,128)S(1)}) custom-call(s32[1]{0:T(128)} %bitcast.2.at_ref, bf16[256,1024]{1,0:T(8,128)(2,1)S(1)} %bitcast.12, bf16[256,1024]{1,0:T(8,128)(2,1)S(1)} %collective-permute-done.3.t1, bf16[256,1024]{1,0:T(8,128)(2,1)} %collective-permute-done.4.t2, ...), custom_call_target="tpu_custom_call" | custom-call | bytes 8388608 | tf_op jit(solution)/shard_map/member_tokens/pallas_call | solution.py:287
  77.3 4.7 %products.2.refs_0_ = f32[256,1024]{1,0:T(8,128)S(1)} custom-call(s32[2]{0:T(128)S(1)} %pad_add_fusion.at_ref, bf16[4,256,1024]{2,1,0:T(8,128)(2,1)S(1)} %get-tuple-element.16.tokens_ref, bf16[1024,256]{1,0:T(8,128)(2,1)S(1)} %pad_maximum_fusion.refs_0_, bf16[1024,256]{1,0:T(8,128)(2,1)} %collective-permute-done.7.refs_1_, ...), custom_call_target="tpu_custom_call" | custom-call | flops 1073741824 | bytes 8388608 | tf_op jit(solution)/shard_map/products/pallas_call | solution.py:150
  82.1 0.0 copy-start.3
  82.1 0.0 collective-permute-done.18.refs_1_
  82.1 3.6 %products.3.sum_ref = f32[256,1024]{1,0:T(8,128)S(1)} custom-call(s32[2]{0:T(128)S(1)} %pad_add_fusion.at_ref, bf16[4,256,1024]{2,1,0:T(8,128)(2,1)S(1)} %get-tuple-element.16.tokens_ref, f32[256,1024]{1,0:T(8,128)S(1)} %products.2.refs_0_, bf16[1024,256]{1,0:T(8,128)(2,1)} %collective-permute-done.18.refs_1_, ...), custom_call_target="tpu_custom_call" | custom-call | flops 536870912 | bytes 8388608 | tf_op jit(solution)/shard_map/products/pallas_call | solution.py:150
  85.7 0.0 collective-permute-done.23.refs_1_
  85.7 0.4 collective-permute-done.22.refs_0_
  86.1 0.0 collective-permute-done.25.refs_3_
  86.2 5.7 %values_readout.1 = bf16[256,1024]{1,0:T(8,128)(2,1)} custom-call(s32[2]{0:T(128)S(1)} %pad_add_fusion.at_ref, bf16[4,256,1024]{2,1,0:T(8,128)(2,1)S(1)} %get-tuple-element.16.tokens_ref, f32[256,1024]{1,0:T(8,128)S(1)} %products.3.sum_ref, f32[256,8]{1,0:T(8,128)S(1)} %get-tuple-element.17.projected_ref, bf16[1,1024]{1,0:T(2,128)(2,1)S(1)} %copy-done.3, ...), custom_call_target="tpu_custom_call" | custom-call | flops 536870912 | bytes 12582912 | tf_op jit(solution)/shard_map/values_readout/pallas_call | solution.py:314
  (22 shorter events, 0.3 us)
Async XLA Ops:
  0.6 19.0 %collective-permute-start.3 = (bf16[256,1024]{1,0:T(8,128)(2,1)}, bf16[256,1024]{1,0:T(8,128)(2,1)S(1)}, u32[]{:S(2)}, u32[]{:S(2)}) collective-permute-start(bf16[256,1024]{1,0:T(8,128)(2,1)} %bitcast.10), channel_id=1, source_target_pairs={{0,1},{1,0},{2,3},{3,2},{4,5},{5,4},{6,7},{7,6},{8,9},{9,8},{10,11... | collective-permute-start | bytes 1572872 | tf_op jit(solution)/shard_map/ppermute | solution.py:33
  0.7 18.8 %collective-permute-start = (bf16[64,1024]{1,0:T(8,128)(2,1)}, bf16[64,1024]{1,0:T(8,128)(2,1)S(1)}, u32[]{:S(2)}, u32[]{:S(2)}) collective-permute-start(bf16[64,1024]{1,0:T(8,128)(2,1)} %param.13), channel_id=1, source_target_pairs={{4,0},{8,4},{12,8},{0,12},{5,1},{9,5},{13,9},{1,13},{6,2},{10,6},{... | collective-permute-start | bytes 393224 | tf_op jit(solution)/shard_map/ppermute | solution.py:38
  2.7 16.9 %collective-permute-start.1 = (bf16[64,1024]{1,0:T(8,128)(2,1)}, bf16[64,1024]{1,0:T(8,128)(2,1)S(1)}, u32[]{:S(2)}, u32[]{:S(2)}) collective-permute-start(bf16[64,1024]{1,0:T(8,128)(2,1)} %param.13), channel_id=1, source_target_pairs={{12,0},{0,4},{4,8},{8,12},{13,1},{1,5},{5,9},{9,13},{14,2},{2,6},{... | collective-permute-start | bytes 393224 | tf_op jit(solution)/shard_map/ppermute | solution.py:38
  2.8 16.8 %collective-permute-start.2 = (bf16[64,1024]{1,0:T(8,128)(2,1)}, bf16[64,1024]{1,0:T(8,128)(2,1)S(1)}, u32[]{:S(2)}, u32[]{:S(2)}) collective-permute-start(bf16[64,1024]{1,0:T(8,128)(2,1)} %param.13), channel_id=1, source_target_pairs={{8,0},{12,4},{0,8},{4,12},{9,1},{13,5},{1,9},{5,13},{10,2},{14,6},... | collective-permute-start | bytes 393224 | tf_op jit(solution)/shard_map/ppermute | solution.py:38
  8.0 18.0 %copy-start.1 = (bf16[1,256,1024]{2,1,0:T(8,128)(2,1)S(1)}, bf16[1,256,1024]{2,1,0:T(8,128)(2,1)}, u32[]{:S(2)}) copy-start(bf16[1,256,1024]{2,1,0:T(8,128)(2,1)} %param.9) | copy-start | bytes 1572868
  19.6 55.7 %copy-start.2 = (bf16[1,4096]{1,0:T(2,128)(2,1)S(1)}, bf16[1,4096]{1,0:T(2,128)(2,1)}, u32[]{:S(2)}) copy-start(bf16[1,4096]{1,0:T(2,128)(2,1)} %noise_in_ref.1) | copy-start | bytes 24580
  19.7 10.7 %collective-permute-start.14 = (bf16[256,256]{1,0:T(8,128)(2,1)S(1)}, bf16[256,256]{1,0:T(8,128)(2,1)S(1)}, u32[]{:S(2)}, u32[]{:S(2)}) collective-permute-start(bf16[256,256]{1,0:T(8,128)(2,1)S(1)} %get-tuple-element.22), channel_id=1, source_target_pairs={{0,192},{64,128},{128,64},{192,0},{1,193},{65,129},{129,65},{193,1... | collective-permute-start | bytes 393224 | tf_op jit(solution)/shard_map/ppermute | solution.py:33
  22.8 8.9 %collective-permute-start.11 = (bf16[256,256]{1,0:T(8,128)(2,1)S(1)}, bf16[256,256]{1,0:T(8,128)(2,1)S(1)}, u32[]{:S(2)}, u32[]{:S(2)}) collective-permute-start(bf16[256,256]{1,0:T(8,128)(2,1)S(1)} %get-tuple-element.23), channel_id=1, source_target_pairs={{0,48},{16,32},{32,16},{48,0},{1,49},{17,33},{33,17},{49,1},{2,50}... | collective-permute-start | bytes 393224 | tf_op jit(solution)/shard_map/ppermute | solution.py:33
  25.6 7.3 %collective-permute-start.8 = (bf16[256,256]{1,0:T(8,128)(2,1)S(1)}, bf16[256,256]{1,0:T(8,128)(2,1)S(1)}, u32[]{:S(2)}, u32[]{:S(2)}) collective-permute-start(bf16[256,256]{1,0:T(8,128)(2,1)S(1)} %get-tuple-element.24), channel_id=1, source_target_pairs={{0,64},{64,0},{128,192},{192,128},{1,65},{65,1},{129,193},{193,129... | collective-permute-start | bytes 393224 | tf_op jit(solution)/shard_map/ppermute | solution.py:33
  25.7 7.9 %collective-permute-start.5 = (bf16[256,256]{1,0:T(8,128)(2,1)S(1)}, bf16[256,256]{1,0:T(8,128)(2,1)S(1)}, u32[]{:S(2)}, u32[]{:S(2)}) collective-permute-start(bf16[256,256]{1,0:T(8,128)(2,1)S(1)} %get-tuple-element.25), channel_id=1, source_target_pairs={{0,16},{16,0},{32,48},{48,32},{1,17},{17,1},{33,49},{49,33},{2,18}... | collective-permute-start | bytes 393224 | tf_op jit(solution)/shard_map/ppermute | solution.py:33
  25.9 27.8 %collective-permute-start.4 = (bf16[256,1024]{1,0:T(8,128)(2,1)S(1)}, bf16[256,1024]{1,0:T(8,128)(2,1)}, u32[]{:S(2)}, u32[]{:S(2)}) collective-permute-start(bf16[256,1024]{1,0:T(8,128)(2,1)S(1)} %bitcast.11), channel_id=1, source_target_pairs={{0,2},{2,0},{1,3},{3,1},{4,6},{6,4},{5,7},{7,5},{8,10},{10,8},{9,1... | collective-permute-start | bytes 1572872 | tf_op jit(solution)/shard_map/ppermute | solution.py:33
  30.5 8.0 %collective-permute-start.15 = (bf16[512,256]{1,0:T(8,128)(2,1)S(1)}, bf16[512,256]{1,0:T(8,128)(2,1)S(1)}, u32[]{:S(2)}, u32[]{:S(2)}) collective-permute-start(bf16[512,256]{1,0:T(8,128)(2,1)S(1)} %pad_maximum_fusion.7), channel_id=1, source_target_pairs={{0,48},{16,32},{32,16},{48,0},{1,49},{17,33},{33,17},{49,1},{2,50}... | collective-permute-start | bytes 786440 | tf_op jit(solution)/shard_map/ppermute | solution.py:33
  31.7 8.5 %collective-permute-start.12 = (bf16[512,256]{1,0:T(8,128)(2,1)S(1)}, bf16[512,256]{1,0:T(8,128)(2,1)S(1)}, u32[]{:S(2)}, u32[]{:S(2)}) collective-permute-start(bf16[512,256]{1,0:T(8,128)(2,1)S(1)} %pad_maximum_fusion.6), channel_id=1, source_target_pairs={{0,192},{64,128},{128,64},{192,0},{1,193},{65,129},{129,65},{193,1... | collective-permute-start | bytes 786440 | tf_op jit(solution)/shard_map/ppermute | solution.py:33
  32.9 8.0 %collective-permute-start.9 = (bf16[512,256]{1,0:T(8,128)(2,1)S(1)}, bf16[512,256]{1,0:T(8,128)(2,1)S(1)}, u32[]{:S(2)}, u32[]{:S(2)}) collective-permute-start(bf16[512,256]{1,0:T(8,128)(2,1)S(1)} %pad_maximum_fusion.5), channel_id=1, source_target_pairs={{0,16},{16,0},{32,48},{48,32},{1,17},{17,1},{33,49},{49,33},{2,18}... | collective-permute-start | bytes 786440 | tf_op jit(solution)/shard_map/ppermute | solution.py:33
  33.7 8.8 %collective-permute-start.6 = (bf16[512,256]{1,0:T(8,128)(2,1)S(1)}, bf16[512,256]{1,0:T(8,128)(2,1)S(1)}, u32[]{:S(2)}, u32[]{:S(2)}) collective-permute-start(bf16[512,256]{1,0:T(8,128)(2,1)S(1)} %pad_maximum_fusion.4), channel_id=1, source_target_pairs={{0,64},{64,0},{128,192},{192,128},{1,65},{65,1},{129,193},{193,129... | collective-permute-start | bytes 786440 | tf_op jit(solution)/shard_map/ppermute | solution.py:33
  38.5 16.9 %collective-permute-start.16 = (bf16[1024,256]{1,0:T(8,128)(2,1)S(1)}, bf16[1024,256]{1,0:T(8,128)(2,1)}, u32[]{:S(2)}, u32[]{:S(2)}) collective-permute-start(bf16[1024,256]{1,0:T(8,128)(2,1)S(1)} %pad_maximum_fusion.3.refs_6_), channel_id=1, source_target_pairs={{0,64},{64,0},{128,192},{192,128},{1,65},{65,1},{129,193},{193,129... | collective-permute-start | bytes 1572872 | tf_op jit(solution)/shard_map/ppermute | solution.py:33
  40.3 16.9 %collective-permute-start.13 = (bf16[1024,256]{1,0:T(8,128)(2,1)S(1)}, bf16[1024,256]{1,0:T(8,128)(2,1)}, u32[]{:S(2)}, u32[]{:S(2)}) collective-permute-start(bf16[1024,256]{1,0:T(8,128)(2,1)S(1)} %pad_maximum_fusion.2.refs_4_), channel_id=1, source_target_pairs={{0,16},{16,0},{32,48},{48,32},{1,17},{17,1},{33,49},{49,33},{2,18}... | collective-permute-start | bytes 1572872 | tf_op jit(solution)/shard_map/ppermute | solution.py:33
  40.9 16.7 %collective-permute-start.10 = (bf16[1024,256]{1,0:T(8,128)(2,1)S(1)}, bf16[1024,256]{1,0:T(8,128)(2,1)}, u32[]{:S(2)}, u32[]{:S(2)}) collective-permute-start(bf16[1024,256]{1,0:T(8,128)(2,1)S(1)} %pad_maximum_fusion.1.refs_2_), channel_id=1, source_target_pairs={{0,192},{64,128},{128,64},{192,0},{1,193},{65,129},{129,65},{193,1... | collective-permute-start | bytes 1572872 | tf_op jit(solution)/shard_map/ppermute | solution.py:33
  42.5 15.1 %collective-permute-start.7 = (bf16[1024,256]{1,0:T(8,128)(2,1)S(1)}, bf16[1024,256]{1,0:T(8,128)(2,1)}, u32[]{:S(2)}, u32[]{:S(2)}) collective-permute-start(bf16[1024,256]{1,0:T(8,128)(2,1)S(1)} %pad_maximum_fusion.refs_0_), channel_id=1, source_target_pairs={{0,48},{16,32},{32,16},{48,0},{1,49},{17,33},{33,17},{49,1},{2,50}... | collective-permute-start | bytes 1572872 | tf_op jit(solution)/shard_map/ppermute | solution.py:33
  45.6 17.4 %all-to-all-start = ((f32[64,1,1152]{2,1,0:T(1,128)}), f32[64,1,1152]{2,1,0:T(1,128)S(1)}, u32[]{:S(2)}, u32[]{:S(2)}) async-start(f32[64,1,1152]{2,1,0:T(1,128)} %noise_message.1), calls=%async_computation | async-start | bytes 589824 | tf_op jit(solution)/shard_map/all_to_all | solution.py:276
  53.7 15.1 %collective-permute-start.21 = (bf16[1024,256]{1,0:T(8,128)(2,1)S(1)}, bf16[1024,256]{1,0:T(8,128)(2,1)}, u32[]{:S(2)}, u32[]{:S(2)}) collective-permute-start(bf16[1024,256]{1,0:T(8,128)(2,1)S(1)} %pad_maximum_fusion.3.refs_6_), channel_id=1, source_target_pairs={{0,16},{16,0},{32,48},{48,32},{1,17},{17,1},{33,49},{49,33},{2,18}... | collective-permute-start | bytes 1572872 | tf_op jit(solution)/shard_map/ppermute | solution.py:33
  55.4 15.2 %collective-permute-start.20 = (bf16[1024,256]{1,0:T(8,128)(2,1)S(1)}, bf16[1024,256]{1,0:T(8,128)(2,1)}, u32[]{:S(2)}, u32[]{:S(2)}) collective-permute-start(bf16[1024,256]{1,0:T(8,128)(2,1)S(1)} %pad_maximum_fusion.2.refs_4_), channel_id=1, source_target_pairs={{0,64},{64,0},{128,192},{192,128},{1,65},{65,1},{129,193},{193,129... | collective-permute-start | bytes 1572872 | tf_op jit(solution)/shard_map/ppermute | solution.py:33
  57.1 14.7 %collective-permute-start.19 = (bf16[1024,256]{1,0:T(8,128)(2,1)S(1)}, bf16[1024,256]{1,0:T(8,128)(2,1)}, u32[]{:S(2)}, u32[]{:S(2)}) collective-permute-start(bf16[1024,256]{1,0:T(8,128)(2,1)S(1)} %pad_maximum_fusion.1.refs_2_), channel_id=1, source_target_pairs={{0,48},{16,32},{32,16},{48,0},{1,49},{17,33},{33,17},{49,1},{2,50}... | collective-permute-start | bytes 1572872 | tf_op jit(solution)/shard_map/ppermute | solution.py:33
  57.6 15.2 %collective-permute-start.17 = (bf16[256,1024]{1,0:T(8,128)(2,1)}, bf16[256,1024]{1,0:T(8,128)(2,1)}, u32[]{:S(2)}, u32[]{:S(2)}) collective-permute-start(bf16[256,1024]{1,0:T(8,128)(2,1)} %collective-permute-done.4.t2), channel_id=1, source_target_pairs={{0,1},{1,0},{2,3},{3,2},{4,5},{5,4},{6,7},{7,6},{8,9},{9,8},{10,11... | collective-permute-start | bytes 1572872 | tf_op jit(solution)/shard_map/ppermute | solution.py:33
  57.6 24.4 %collective-permute-start.18 = (bf16[1024,256]{1,0:T(8,128)(2,1)S(1)}, bf16[1024,256]{1,0:T(8,128)(2,1)}, u32[]{:S(2)}, u32[]{:S(2)}) collective-permute-start(bf16[1024,256]{1,0:T(8,128)(2,1)S(1)} %pad_maximum_fusion.refs_0_), channel_id=1, source_target_pairs={{0,192},{64,128},{128,64},{192,0},{1,193},{65,129},{129,65},{193,1... | collective-permute-start | bytes 1572872 | tf_op jit(solution)/shard_map/ppermute | solution.py:33
  63.0 10.0 %copy-start.4 = (f32[64,1,1152]{2,1,0:T(1,128)}, f32[64,1,1152]{2,1,0:T(1,128)S(1)}, u32[]{:S(2)}) copy-start(f32[64,1,1152]{2,1,0:T(1,128)S(1)} %all-to-all-done.message_ref) | copy-start | bytes 884740
  68.8 16.9 %collective-permute-start.24 = (bf16[1024,256]{1,0:T(8,128)(2,1)}, bf16[1024,256]{1,0:T(8,128)(2,1)}, u32[]{:S(2)}, u32[]{:S(2)}) collective-permute-start(bf16[1024,256]{1,0:T(8,128)(2,1)} %collective-permute-done.13.refs_5_), channel_id=1, source_target_pairs={{0,64},{64,0},{128,192},{192,128},{1,65},{65,1},{129,193},{193,129... | collective-permute-start | bytes 1572872 | tf_op jit(solution)/shard_map/ppermute | solution.py:33
  70.6 15.1 %collective-permute-start.23 = (bf16[1024,256]{1,0:T(8,128)(2,1)}, bf16[1024,256]{1,0:T(8,128)(2,1)}, u32[]{:S(2)}, u32[]{:S(2)}) collective-permute-start(bf16[1024,256]{1,0:T(8,128)(2,1)} %collective-permute-done.10.refs_3_), channel_id=1, source_target_pairs={{0,48},{16,32},{32,16},{48,0},{1,49},{17,33},{33,17},{49,1},{2,50}... | collective-permute-start | bytes 1572872 | tf_op jit(solution)/shard_map/ppermute | solution.py:33
  71.9 14.3 %collective-permute-start.22 = (bf16[1024,256]{1,0:T(8,128)(2,1)}, bf16[1024,256]{1,0:T(8,128)(2,1)}, u32[]{:S(2)}, u32[]{:S(2)}) collective-permute-start(bf16[1024,256]{1,0:T(8,128)(2,1)} %collective-permute-done.7.refs_1_), channel_id=1, source_target_pairs={{0,192},{64,128},{128,64},{192,0},{1,193},{65,129},{129,65},{193,1... | collective-permute-start | bytes 1572872 | tf_op jit(solution)/shard_map/ppermute | solution.py:33
  72.8 13.3 %collective-permute-start.25 = (bf16[1024,256]{1,0:T(8,128)(2,1)}, bf16[1024,256]{1,0:T(8,128)(2,1)}, u32[]{:S(2)}, u32[]{:S(2)}) collective-permute-start(bf16[1024,256]{1,0:T(8,128)(2,1)} %collective-permute-done.16.refs_7_), channel_id=1, source_target_pairs={{0,16},{16,0},{32,48},{48,32},{1,17},{17,1},{33,49},{49,33},{2,18}... | collective-permute-start | bytes 1572872 | tf_op jit(solution)/shard_map/ppermute | solution.py:33
  82.0 4.1 %copy-start = (bf16[8,1024,256]{2,1,0:T(8,128)(2,1)S(1)}, bf16[8,1024,256]{2,1,0:T(8,128)(2,1)}, u32[]{:S(2)}) copy-start(bf16[8,1024,256]{2,1,0:T(8,128)(2,1)} %decayed_scores.1.scores_ref) | copy-start | bytes 12582916
  82.1 4.1 %copy-start.3 = (bf16[1,1024]{1,0:T(2,128)(2,1)S(1)}, bf16[1,1024]{1,0:T(2,128)(2,1)}, u32[]{:S(2)}) copy-start(bf16[1,1024]{1,0:T(2,128)(2,1)} %noise_ref.1) | copy-start | bytes 6148

commit v8 on v7

--- a/solution.py
+++ b/solution.py
@@ -278,9 +278,6 @@
     )
     third = [swap(held[c], *LINKS[ROUTES[c][2]]) for c in chunks]
     fourth = [swap(held[c], *LINKS[ROUTES[c][3]]) for c in chunks]
-    ready = list(third)
-    ready[3] = after(third[3], message)
-    last = [swap(ready[c], *LINKS[ROUTES[c][3]]) for c in chunks]
 
     both = swap(after(twin, *third), "core", 1)
     tp = lax.axis_index(TP).reshape(1)
@@ -293,7 +290,7 @@
         in_specs=[SMEM] + [VMEM] * 5,
         out_specs=[VMEM] * 2,
         cost_estimate=cost(0, 8 << 20),
-        compiler_params=params(16),
+        compiler_params=params(60),
         name="member_tokens",
     )(tp, tokens, mate, twin, both, noise_in.reshape(4, 1, width))
 
@@ -310,6 +307,9 @@
     total = product(
         at, all_tokens, ((), (2,)), [p for c in chunks for p in (held[c], third[c])]
     )
+    ready = [after(t, total) for t in third[:2]] + third[2:]
+    ready[3] = after(ready[3], message)
+    last = [swap(ready[c], *LINKS[ROUTES[c][3]]) for c in chunks]
     total = product(at, all_tokens, ((3,),), fourth, total)
     wkv_out = pl.pallas_call(
         readout_kernel,

time: 92.9 us -> 97.5 us (1.050)
  starting transfers between devices: 45.7 us -> 41.5 us
  other arithmetic: 0.29 us -> 3.53 us
  waiting for transfers between devices: 14.9 us -> 17 us
  local copies, waits for them, and re-layouts: 1.14 us -> 2.95 us
  Pallas kernels: 27.7 us -> 29.4 us
    ppermute x23, starting transfers between devices: 32 us -> 27 us  [swap(): return lax.ppermute(array, axis, [(i, i ^ mask) for i in range(size)])]
    ppermute x23, waiting for transfers between devices: 11.7 us -> 15 us  [swap(): return lax.ppermute(array, axis, [(i, i ^ mask) for i in range(size)])]
    concatenate x8, other arithmetic: 0.21 us -> 3.46 us  [body(): held = [jnp.concatenate([a, b], 0) for a, b in zip(held, came)]]
    unnamed x10 -> x20, local copies, waits for them, and re-layouts: 0.03 us -> 1.85 us
    pallas_call x1, Pallas kernels: 1.98 us -> 3.51 us  [body(): pl.pallas_call(token_kernel, out_shape=[jax.ShapeDtypeStruct((4, length,...]
    all_to_all x1, waiting for transfers between devices: 3.21 us -> 2.02 us  [body(): lax.all_to_all(after(message, *held), POP, split_axis=0, concat_axis=0, t...]
  transfers between devices with their start and end apart: 27 -> 27, of which waited for: 5 -> 8; matrix products, arithmetic and copies ran while one was open for 1% -> 5% of each run, Pallas kernels for 24% -> 24%
where the time goes in v8:
time: 97.5 us; the launch traced here: 96.8 us
  starting transfers between devices  41.5 us (43%)
  Pallas kernels  29.4 us (30%)
  waiting for transfers between devices  17 us (17%)
  other arithmetic  3.53 us (4%)
  local copies, waits for them, and re-layouts  2.95 us (3%)
  between operations  2.32 us (2%)
    ppermute x23, starting transfers between devices, swap(): return lax.ppermute(array, axis, [(i, i ^ mask) for i in range(size)])  27 us
    ppermute x23, waiting for transfers between devices, swap(): return lax.ppermute(array, axis, [(i, i ^ mask) for i in range(size)])  15 us
    pallas_call x2, Pallas kernels, product(): pl.pallas_call(functools.partial(product_kernel, ways, before is not None...  8.56 us
    pallas_call x1, Pallas kernels, score_heads(): pl.pallas_call(score_kernel, out_shape=jax.ShapeDtypeStruct((count, 4 * l...  7.81 us
    all_to_all x1, starting transfers between devices, body(): lax.all_to_all(after(message, *held), POP, split_axis=0, concat_axis=0, t...  7.3 us
    ppermute x3, starting transfers between devices, fetch(): lax.ppermute(array, axis, [((i + step) % size, i) for i in range(size)])  7.17 us
    pallas_call x1, Pallas kernels, body(): pl.pallas_call(readout_kernel, out_shape=jax.ShapeDtypeStruct((length, wi...  5.74 us
    pallas_call x1, Pallas kernels, body(): pl.pallas_call(token_kernel, out_shape=[jax.ShapeDtypeStruct((4, length,...  3.51 us
  transfers between devices with their start and end apart: 27, of which 8 were waited for; matrix products, arithmetic and copies ran while one was open for 5% of the time, Pallas kernels for 24%

profile of v8, /device:TPU:32, one launch (start us, length us, event | category | flops | bytes accessed | tf_op | source)
XLA Modules:
  0.0 96.8 jit_solution(4596562592445351622)
XLA Ops:
  0.6 0.1 collective-permute-start.3
  0.7 1.9 %collective-permute-start = (bf16[64,1024]{1,0:T(8,128)(2,1)}, bf16[64,1024]{1,0:T(8,128)(2,1)S(1)}, u32[]{:S(2)}, u32[]{:S(2)}) collective-permute-start(bf16[64,1024]{1,0:T(8,128)(2,1)} %param.13), channel_id=1, source_target_pairs={{4,0},{8,4},{12,8},{0,12},{5,1},{9,5},{13,9},{1,13},{6,2},{10,6},{... | collective-permute-start | bytes 393224 | tf_op jit(solution)/shard_map/ppermute | solution.py:38
  2.7 0.2 collective-permute-start.1
  2.8 5.1 %collective-permute-start.2 = (bf16[64,1024]{1,0:T(8,128)(2,1)}, bf16[64,1024]{1,0:T(8,128)(2,1)S(1)}, u32[]{:S(2)}, u32[]{:S(2)}) collective-permute-start(bf16[64,1024]{1,0:T(8,128)(2,1)} %param.13), channel_id=1, source_target_pairs={{8,0},{12,4},{0,8},{4,12},{9,1},{13,5},{1,9},{5,13},{10,2},{14,6},... | collective-permute-start | bytes 393224 | tf_op jit(solution)/shard_map/ppermute | solution.py:38
  7.9 0.1 broadcast_in_dim.3
  8.0 0.0 copy-start.6
  8.0 1.0 %constant_dynamic-update-slice_fusion.3 = bf16[256,1024]{1,0:T(8,128)(2,1)S(1)} fusion(bf16[256,1024]{1,0:T(8,128)(2,1)S(1)} %broadcast_in_dim.3, bf16[64,1024]{1,0:T(8,128)(2,1)} %param.13, s32[]{:T(128)S(6)} %select_n.12), kind=kLoop, calls=%fused_computation.11 | loop fusion | bytes 262148 | tf_op jit(solution)/shard_map/dynamic_update_slice | solution.py:255
  10.3 1.5 %noise_message.1 = f32[64,1,1152]{2,1,0:T(1,128)} custom-call(f32[1]{0:T(128)S(6)} %copy.15.utility_ref, bf16[1,4096]{1,0:T(2,128)(2,1)} %noise_in_ref.1, bf16[1,1024]{1,0:T(2,128)(2,1)} %noise_ref.1), custom_call_target="tpu_custom_call" | custom-call | bytes 524288 | tf_op jit(solution)/shard_map/noise_message/pallas_call | solution.py:258
  11.8 7.8 %decayed_scores.1.scores_ref = bf16[8,1024,256]{2,1,0:T(8,128)(2,1)} custom-call(s32[1]{0:T(128)S(6)} %copy.16.live_ref, bf16[256,1024]{1,0:T(8,128)(2,1)} %bitcast.10, bf16[256,1024]{1,0:T(8,128)(2,1)} %bitcast.11, bf16[256,1024]{1,0:T(8,128)(2,1)} %bitcast.12), custom_call_target="tpu_custom_call" | custom-call | bytes 20971520 | tf_op jit(solution)/shard_map/decayed_scores/pallas_call | solution.py:230
  19.6 0.0 collective-permute-done
  19.6 0.0 collective-permute-done.1
  19.7 0.0 collective-permute-done.3.t1
  19.7 0.0 copy-start.7
  19.7 3.1 %collective-permute-start.14 = (bf16[256,256]{1,0:T(8,128)(2,1)S(1)}, bf16[256,256]{1,0:T(8,128)(2,1)S(1)}, u32[]{:S(2)}, u32[]{:S(2)}) collective-permute-start(bf16[256,256]{1,0:T(8,128)(2,1)S(1)} %get-tuple-element.26), channel_id=1, source_target_pairs={{0,192},{64,128},{128,64},{192,0},{1,193},{65,129},{129,65},{193,1... | collective-permute-start | bytes 393224 | tf_op jit(solution)/shard_map/ppermute | solution.py:33
  22.8 2.8 %collective-permute-start.11 = (bf16[256,256]{1,0:T(8,128)(2,1)S(1)}, bf16[256,256]{1,0:T(8,128)(2,1)S(1)}, u32[]{:S(2)}, u32[]{:S(2)}) collective-permute-start(bf16[256,256]{1,0:T(8,128)(2,1)S(1)} %get-tuple-element.27), channel_id=1, source_target_pairs={{0,48},{16,32},{32,16},{48,0},{1,49},{17,33},{33,17},{49,1},{2,50}... | collective-permute-start | bytes 393224 | tf_op jit(solution)/shard_map/ppermute | solution.py:33
  25.6 0.1 collective-permute-start.8
  25.7 0.2 collective-permute-start.5
  25.9 4.5 %collective-permute-start.4 = (bf16[256,1024]{1,0:T(8,128)(2,1)S(1)}, bf16[256,1024]{1,0:T(8,128)(2,1)S(1)}, u32[]{:S(2)}, u32[]{:S(2)}) collective-permute-start(bf16[256,1024]{1,0:T(8,128)(2,1)S(1)} %bitcast.15), channel_id=1, source_target_pairs={{0,2},{2,0},{1,3},{3,1},{4,6},{6,4},{5,7},{7,5},{8,10},{10,8},{9,1... | collective-permute-start | bytes 1572872 | tf_op jit(solution)/shard_map/ppermute | solution.py:33
  30.5 1.2 %collective-permute-start.15 = (bf16[512,256]{1,0:T(8,128)(2,1)S(1)}, bf16[512,256]{1,0:T(8,128)(2,1)S(1)}, u32[]{:S(2)}, u32[]{:S(2)}) collective-permute-start(bf16[512,256]{1,0:T(8,128)(2,1)S(1)} %pad_maximum_fusion.7), channel_id=1, source_target_pairs={{0,48},{16,32},{32,16},{48,0},{1,49},{17,33},{33,17},{49,1},{2,50}... | collective-permute-start | bytes 786440 | tf_op jit(solution)/shard_map/ppermute | solution.py:33
  31.7 1.1 %collective-permute-start.12 = (bf16[512,256]{1,0:T(8,128)(2,1)S(1)}, bf16[512,256]{1,0:T(8,128)(2,1)S(1)}, u32[]{:S(2)}, u32[]{:S(2)}) collective-permute-start(bf16[512,256]{1,0:T(8,128)(2,1)S(1)} %pad_maximum_fusion.6), channel_id=1, source_target_pairs={{0,192},{64,128},{128,64},{192,0},{1,193},{65,129},{129,65},{193,1... | collective-permute-start | bytes 786440 | tf_op jit(solution)/shard_map/ppermute | solution.py:33
  32.9 0.8 collective-permute-start.9
  33.7 0.0 collective-permute-done.5
  33.7 0.9 collective-permute-start.6
  34.6 3.8 %collective-permute-done.15 = bf16[512,256]{1,0:T(8,128)(2,1)S(1)} collective-permute-done((bf16[512,256]{1,0:T(8,128)(2,1)S(1)}, bf16[512,256]{1,0:T(8,128)(2,1)S(1)}, u32[]{:S(2)}, u32[]{:S(2)}) %collective-permute-start.15) | collective-permute-done | bytes 262176 | tf_op jit(solution)/shard_map/ppermute | solution.py:33
  38.5 0.9 pad_maximum_fusion.3.refs_6_
  39.3 1.7 %collective-permute-start.16 = (bf16[1024,256]{1,0:T(8,128)(2,1)}, bf16[1024,256]{1,0:T(8,128)(2,1)}, u32[]{:S(2)}, u32[]{:S(2)}) collective-permute-start(bf16[1024,256]{1,0:T(8,128)(2,1)} %pad_maximum_fusion.3.refs_6_), channel_id=1, source_target_pairs={{0,64},{64,0},{128,192},{192,128},{1,65},{65,1},{129,193},{193,129... | collective-permute-start | bytes 1572872 | tf_op jit(solution)/shard_map/ppermute | solution.py:33
  41.0 0.0 collective-permute-done.12
  41.0 0.8 pad_maximum_fusion.2.refs_4_
  41.8 0.5 collective-permute-start.13
  42.4 0.0 collective-permute-done.9
  42.4 0.8 pad_maximum_fusion.1.refs_2_
  43.2 0.4 collective-permute-start.10
  43.6 0.9 pad_maximum_fusion.refs_0_
  44.4 1.8 %collective-permute-start.7 = (bf16[1024,256]{1,0:T(8,128)(2,1)}, bf16[1024,256]{1,0:T(8,128)(2,1)}, u32[]{:S(2)}, u32[]{:S(2)}) collective-permute-start(bf16[1024,256]{1,0:T(8,128)(2,1)} %pad_maximum_fusion.refs_0_), channel_id=1, source_target_pairs={{0,48},{16,32},{32,16},{48,0},{1,49},{17,33},{33,17},{49,1},{2,50}... | collective-permute-start | bytes 1572872 | tf_op jit(solution)/shard_map/ppermute | solution.py:33
  46.3 7.3 %all-to-all-start = ((f32[64,1,1152]{2,1,0:T(1,128)}), f32[64,1,1152]{2,1,0:T(1,128)S(1)}, u32[]{:S(2)}, u32[]{:S(2)}) async-start(f32[64,1,1152]{2,1,0:T(1,128)} %noise_message.1), calls=%async_computation | async-start | bytes 589824 | tf_op jit(solution)/shard_map/all_to_all | solution.py:276
  53.6 0.0 collective-permute-done.4.t2
  53.6 0.0 collective-permute-done.13.refs_5_
  53.6 2.0 %collective-permute-done.10.refs_3_ = bf16[1024,256]{1,0:T(8,128)(2,1)} collective-permute-done((bf16[1024,256]{1,0:T(8,128)(2,1)}, bf16[1024,256]{1,0:T(8,128)(2,1)}, u32[]{:S(2)}, u32[]{:S(2)}) %collective-permute-start.10) | collective-permute-done | bytes 524320 | tf_op jit(solution)/shard_map/ppermute | solution.py:33
  55.6 2.3 %collective-permute-done.7.refs_1_ = bf16[1024,256]{1,0:T(8,128)(2,1)} collective-permute-done((bf16[1024,256]{1,0:T(8,128)(2,1)}, bf16[1024,256]{1,0:T(8,128)(2,1)}, u32[]{:S(2)}, u32[]{:S(2)}) %collective-permute-start.7) | collective-permute-done | bytes 524320 | tf_op jit(solution)/shard_map/ppermute | solution.py:33
  58.0 0.0 collective-permute-start.17
  58.0 0.4 collective-permute-start.21
  58.4 0.0 collective-permute-start.20
  58.4 2.1 %collective-permute-start.19 = (bf16[1024,256]{1,0:T(8,128)(2,1)}, bf16[1024,256]{1,0:T(8,128)(2,1)}, u32[]{:S(2)}, u32[]{:S(2)}) collective-permute-start(bf16[1024,256]{1,0:T(8,128)(2,1)} %pad_maximum_fusion.1.refs_2_), channel_id=1, source_target_pairs={{0,48},{16,32},{32,16},{48,0},{1,49},{17,33},{33,17},{49,1},{2,50}... | collective-permute-start | bytes 1572872 | tf_op jit(solution)/shard_map/ppermute | solution.py:33
  60.5 0.1 pad_add_fusion.at_ref
  60.6 1.8 %collective-permute-start.18 = (bf16[1024,256]{1,0:T(8,128)(2,1)}, bf16[1024,256]{1,0:T(8,128)(2,1)}, u32[]{:S(2)}, u32[]{:S(2)}) collective-permute-start(bf16[1024,256]{1,0:T(8,128)(2,1)} %pad_maximum_fusion.refs_0_), channel_id=1, source_target_pairs={{0,192},{64,128},{128,64},{192,0},{1,193},{65,129},{129,65},{193,1... | collective-permute-start | bytes 1572872 | tf_op jit(solution)/shard_map/ppermute | solution.py:33
  62.4 2.0 %all-to-all-done.message_ref = f32[64,1,1152]{2,1,0:T(1,128)S(1)} async-done(((f32[64,1,1152]{2,1,0:T(1,128)}), f32[64,1,1152]{2,1,0:T(1,128)S(1)}, u32[]{:S(2)}, u32[]{:S(2)}) %all-to-all-start) | async-done | bytes 294944 | tf_op jit(solution)/shard_map/all_to_all | solution.py:276
  64.4 0.6 collective-permute-start.24
  65.0 0.2 copy-done.9
  65.2 3.5 %member_tokens.1 = (bf16[4,256,1024]{2,1,0:T(8,128)(2,1)}, f32[256,8]{1,0:T(8,128)}) custom-call(s32[1]{0:T(128)} %bitcast.2.at_ref, bf16[256,1024]{1,0:T(8,128)(2,1)} %bitcast.14, bf16[256,1024]{1,0:T(8,128)(2,1)} %copy-done.7, bf16[256,1024]{1,0:T(8,128)(2,1)} %copy-done.8, bf16[256,1024]{1,0:T(8,128)(2,1)} %copy-done.9, bf16[4,1,1024]{2,1,0:T(2,128)(2,1)} %bitcast.17), custom_call_target="tpu_custom_call" | custom-call | bytes 8388608 | tf_op jit(solution)/shard_map/member_tokens/pallas_call | solution.py:284
  68.7 1.6 %copy-done = bf16[4,256,1024]{2,1,0:T(8,128)(2,1)S(1)} copy-done((bf16[4,256,1024]{2,1,0:T(8,128)(2,1)S(1)}, bf16[4,256,1024]{2,1,0:T(8,128)(2,1)}, u32[]{:S(2)}) %copy-start) | copy-done | bytes 2097176
  70.3 4.9 %products.2.refs_0_ = f32[256,1024]{1,0:T(8,128)S(1)} custom-call(s32[2]{0:T(128)S(1)} %pad_add_fusion.at_ref, bf16[4,256,1024]{2,1,0:T(8,128)(2,1)S(1)} %copy-done, bf16[1024,256]{1,0:T(8,128)(2,1)} %pad_maximum_fusion.refs_0_, bf16[1024,256]{1,0:T(8,128)(2,1)} %collective-permute-done.7.refs_1_, bf16[1024,256]{1,0:T(8,128)(2,1)} %pad_maximum_fusion.1.refs_2_, ...), custom_call_target="tpu_custom_call" | custom-call | flops 1073741824 | bytes 8388608 | tf_op jit(solution)/shard_map/products/pallas_call | solution.py:150
  75.3 0.0 copy-start.4
  75.3 0.0 collective-permute-done.21.refs_4_
  75.3 0.7 collective-permute-start.25
  76.0 0.0 collective-permute-done.20.refs_3_
  76.0 1.0 collective-permute-start.23
  77.0 1.1 %collective-permute-start.22 = (bf16[1024,256]{1,0:T(8,128)(2,1)}, bf16[1024,256]{1,0:T(8,128)(2,1)}, u32[]{:S(2)}, u32[]{:S(2)}) collective-permute-start(bf16[1024,256]{1,0:T(8,128)(2,1)} %collective-permute-done.7.refs_1_), channel_id=1, source_target_pairs={{0,192},{64,128},{128,64},{192,0},{1,193},{65,129},{129,65},{193,1... | collective-permute-start | bytes 1572872 | tf_op jit(solution)/shard_map/ppermute | solution.py:33
  78.1 2.3 %update_product.1 = f32[64,1024]{1,0:T(8,128)} custom-call(s32[1]{0:T(128)} %bitcast.9.z_ref, f32[64,1,1152]{2,1,0:T(1,128)} %copy-done.5), custom_call_target="tpu_custom_call" | custom-call | bytes 1048576 | tf_op jit(solution)/shard_map/update_product/pallas_call | solution.py:297
  80.5 3.6 %products.3.sum_ref = f32[256,1024]{1,0:T(8,128)S(1)} custom-call(s32[2]{0:T(128)S(1)} %pad_add_fusion.at_ref, bf16[4,256,1024]{2,1,0:T(8,128)(2,1)S(1)} %copy-done.1, f32[256,1024]{1,0:T(8,128)S(1)} %products.2.refs_0_, bf16[1024,256]{1,0:T(8,128)(2,1)} %collective-permute-done.18.refs_1_, bf16[1024,256]{1,0:T(8,128)(2,1)} %collective-permute-done.19.refs_2_, ...), custom_call_target="tpu_custom_call" | custom-call | flops 536870912 | bytes 8388608 | tf_op jit(solution)/shard_map/products/pallas_call | solution.py:150
  84.1 0.1 collective-permute-done.24.refs_2_
  84.2 3.4 %collective-permute-done.25.refs_3_ = bf16[1024,256]{1,0:T(8,128)(2,1)} collective-permute-done((bf16[1024,256]{1,0:T(8,128)(2,1)}, bf16[1024,256]{1,0:T(8,128)(2,1)}, u32[]{:S(2)}, u32[]{:S(2)}) %collective-permute-start.25) | collective-permute-done | bytes 524320 | tf_op jit(solution)/shard_map/ppermute | solution.py:33
  87.5 2.1 %collective-permute-done.23.refs_1_ = bf16[1024,256]{1,0:T(8,128)(2,1)} collective-permute-done((bf16[1024,256]{1,0:T(8,128)(2,1)}, bf16[1024,256]{1,0:T(8,128)(2,1)}, u32[]{:S(2)}, u32[]{:S(2)}) %collective-permute-start.23) | collective-permute-done | bytes 524320 | tf_op jit(solution)/shard_map/ppermute | solution.py:33
  89.6 1.2 %collective-permute-done.22.refs_0_ = bf16[1024,256]{1,0:T(8,128)(2,1)} collective-permute-done((bf16[1024,256]{1,0:T(8,128)(2,1)}, bf16[1024,256]{1,0:T(8,128)(2,1)}, u32[]{:S(2)}, u32[]{:S(2)}) %collective-permute-start.22) | collective-permute-done | bytes 524320 | tf_op jit(solution)/shard_map/ppermute | solution.py:33
  90.9 5.7 %values_readout.1 = bf16[256,1024]{1,0:T(8,128)(2,1)} custom-call(s32[2]{0:T(128)S(1)} %pad_add_fusion.at_ref, bf16[4,256,1024]{2,1,0:T(8,128)(2,1)S(1)} %copy-done.1, f32[256,1024]{1,0:T(8,128)S(1)} %products.3.sum_ref, f32[256,8]{1,0:T(8,128)S(1)} %copy-done.3, bf16[1,1024]{1,0:T(2,128)(2,1)S(1)} %copy-done.4, bf16[8,1024,256]{2,1,0:T(8,128)(2,1)S(1)} %copy-done.2, ...), custom_call_target="tpu_custom_call" | custom-call | flops 536870912 | bytes 12582912 | tf_op jit(solution)/shard_map/values_readout/pallas_call | solution.py:314
  (32 shorter events, 0.2 us)
Async XLA Ops:
  0.6 19.0 %collective-permute-start.3 = (bf16[256,1024]{1,0:T(8,128)(2,1)}, bf16[256,1024]{1,0:T(8,128)(2,1)S(1)}, u32[]{:S(2)}, u32[]{:S(2)}) collective-permute-start(bf16[256,1024]{1,0:T(8,128)(2,1)} %bitcast.13), channel_id=1, source_target_pairs={{0,1},{1,0},{2,3},{3,2},{4,5},{5,4},{6,7},{7,6},{8,9},{9,8},{10,11... | collective-permute-start | bytes 1572872 | tf_op jit(solution)/shard_map/ppermute | solution.py:33
  0.7 18.8 %collective-permute-start = (bf16[64,1024]{1,0:T(8,128)(2,1)}, bf16[64,1024]{1,0:T(8,128)(2,1)S(1)}, u32[]{:S(2)}, u32[]{:S(2)}) collective-permute-start(bf16[64,1024]{1,0:T(8,128)(2,1)} %param.13), channel_id=1, source_target_pairs={{4,0},{8,4},{12,8},{0,12},{5,1},{9,5},{13,9},{1,13},{6,2},{10,6},{... | collective-permute-start | bytes 393224 | tf_op jit(solution)/shard_map/ppermute | solution.py:38
  2.7 16.9 %collective-permute-start.1 = (bf16[64,1024]{1,0:T(8,128)(2,1)}, bf16[64,1024]{1,0:T(8,128)(2,1)S(1)}, u32[]{:S(2)}, u32[]{:S(2)}) collective-permute-start(bf16[64,1024]{1,0:T(8,128)(2,1)} %param.13), channel_id=1, source_target_pairs={{12,0},{0,4},{4,8},{8,12},{13,1},{1,5},{5,9},{9,13},{14,2},{2,6},{... | collective-permute-start | bytes 393224 | tf_op jit(solution)/shard_map/ppermute | solution.py:38
  2.8 16.8 %collective-permute-start.2 = (bf16[64,1024]{1,0:T(8,128)(2,1)}, bf16[64,1024]{1,0:T(8,128)(2,1)S(1)}, u32[]{:S(2)}, u32[]{:S(2)}) collective-permute-start(bf16[64,1024]{1,0:T(8,128)(2,1)} %param.13), channel_id=1, source_target_pairs={{8,0},{12,4},{0,8},{4,12},{9,1},{13,5},{1,9},{5,13},{10,2},{14,6},... | collective-permute-start | bytes 393224 | tf_op jit(solution)/shard_map/ppermute | solution.py:38
  8.0 18.0 %copy-start.6 = (bf16[1,256,1024]{2,1,0:T(8,128)(2,1)S(1)}, bf16[1,256,1024]{2,1,0:T(8,128)(2,1)}, u32[]{:S(2)}) copy-start(bf16[1,256,1024]{2,1,0:T(8,128)(2,1)} %param.9) | copy-start | bytes 1572868
  19.7 45.3 %copy-start.7 = (bf16[256,1024]{1,0:T(8,128)(2,1)}, bf16[256,1024]{1,0:T(8,128)(2,1)S(1)}, u32[]{:S(2)}) copy-start(bf16[256,1024]{1,0:T(8,128)(2,1)S(1)} %collective-permute-done.3.t1) | copy-start | bytes 1572868
  19.7 10.7 %collective-permute-start.14 = (bf16[256,256]{1,0:T(8,128)(2,1)S(1)}, bf16[256,256]{1,0:T(8,128)(2,1)S(1)}, u32[]{:S(2)}, u32[]{:S(2)}) collective-permute-start(bf16[256,256]{1,0:T(8,128)(2,1)S(1)} %get-tuple-element.26), channel_id=1, source_target_pairs={{0,192},{64,128},{128,64},{192,0},{1,193},{65,129},{129,65},{193,1... | collective-permute-start | bytes 393224 | tf_op jit(solution)/shard_map/ppermute | solution.py:33
  22.8 8.9 %collective-permute-start.11 = (bf16[256,256]{1,0:T(8,128)(2,1)S(1)}, bf16[256,256]{1,0:T(8,128)(2,1)S(1)}, u32[]{:S(2)}, u32[]{:S(2)}) collective-permute-start(bf16[256,256]{1,0:T(8,128)(2,1)S(1)} %get-tuple-element.27), channel_id=1, source_target_pairs={{0,48},{16,32},{32,16},{48,0},{1,49},{17,33},{33,17},{49,1},{2,50}... | collective-permute-start | bytes 393224 | tf_op jit(solution)/shard_map/ppermute | solution.py:33
  25.6 7.3 %collective-permute-start.8 = (bf16[256,256]{1,0:T(8,128)(2,1)S(1)}, bf16[256,256]{1,0:T(8,128)(2,1)S(1)}, u32[]{:S(2)}, u32[]{:S(2)}) collective-permute-start(bf16[256,256]{1,0:T(8,128)(2,1)S(1)} %get-tuple-element.28), channel_id=1, source_target_pairs={{0,64},{64,0},{128,192},{192,128},{1,65},{65,1},{129,193},{193,129... | collective-permute-start | bytes 393224 | tf_op jit(solution)/shard_map/ppermute | solution.py:33
  25.7 7.9 %collective-permute-start.5 = (bf16[256,256]{1,0:T(8,128)(2,1)S(1)}, bf16[256,256]{1,0:T(8,128)(2,1)S(1)}, u32[]{:S(2)}, u32[]{:S(2)}) collective-permute-start(bf16[256,256]{1,0:T(8,128)(2,1)S(1)} %get-tuple-element.29), channel_id=1, source_target_pairs={{0,16},{16,0},{32,48},{48,32},{1,17},{17,1},{33,49},{49,33},{2,18}... | collective-permute-start | bytes 393224 | tf_op jit(solution)/shard_map/ppermute | solution.py:33
  25.9 27.7 %collective-permute-start.4 = (bf16[256,1024]{1,0:T(8,128)(2,1)S(1)}, bf16[256,1024]{1,0:T(8,128)(2,1)S(1)}, u32[]{:S(2)}, u32[]{:S(2)}) collective-permute-start(bf16[256,1024]{1,0:T(8,128)(2,1)S(1)} %bitcast.15), channel_id=1, source_target_pairs={{0,2},{2,0},{1,3},{3,1},{4,6},{6,4},{5,7},{7,5},{8,10},{10,8},{9,1... | collective-permute-start | bytes 1572872 | tf_op jit(solution)/shard_map/ppermute | solution.py:33
  30.5 8.0 %collective-permute-start.15 = (bf16[512,256]{1,0:T(8,128)(2,1)S(1)}, bf16[512,256]{1,0:T(8,128)(2,1)S(1)}, u32[]{:S(2)}, u32[]{:S(2)}) collective-permute-start(bf16[512,256]{1,0:T(8,128)(2,1)S(1)} %pad_maximum_fusion.7), channel_id=1, source_target_pairs={{0,48},{16,32},{32,16},{48,0},{1,49},{17,33},{33,17},{49,1},{2,50}... | collective-permute-start | bytes 786440 | tf_op jit(solution)/shard_map/ppermute | solution.py:33
  31.7 9.3 %collective-permute-start.12 = (bf16[512,256]{1,0:T(8,128)(2,1)S(1)}, bf16[512,256]{1,0:T(8,128)(2,1)S(1)}, u32[]{:S(2)}, u32[]{:S(2)}) collective-permute-start(bf16[512,256]{1,0:T(8,128)(2,1)S(1)} %pad_maximum_fusion.6), channel_id=1, source_target_pairs={{0,192},{64,128},{128,64},{192,0},{1,193},{65,129},{129,65},{193,1... | collective-permute-start | bytes 786440 | tf_op jit(solution)/shard_map/ppermute | solution.py:33
  32.9 9.5 %collective-permute-start.9 = (bf16[512,256]{1,0:T(8,128)(2,1)S(1)}, bf16[512,256]{1,0:T(8,128)(2,1)S(1)}, u32[]{:S(2)}, u32[]{:S(2)}) collective-permute-start(bf16[512,256]{1,0:T(8,128)(2,1)S(1)} %pad_maximum_fusion.5), channel_id=1, source_target_pairs={{0,16},{16,0},{32,48},{48,32},{1,17},{17,1},{33,49},{49,33},{2,18}... | collective-permute-start | bytes 786440 | tf_op jit(solution)/shard_map/ppermute | solution.py:33
  33.7 9.9 %collective-permute-start.6 = (bf16[512,256]{1,0:T(8,128)(2,1)S(1)}, bf16[512,256]{1,0:T(8,128)(2,1)S(1)}, u32[]{:S(2)}, u32[]{:S(2)}) collective-permute-start(bf16[512,256]{1,0:T(8,128)(2,1)S(1)} %pad_maximum_fusion.4), channel_id=1, source_target_pairs={{0,64},{64,0},{128,192},{192,128},{1,65},{65,1},{129,193},{193,129... | collective-permute-start | bytes 786440 | tf_op jit(solution)/shard_map/ppermute | solution.py:33
  39.3 14.3 %collective-permute-start.16 = (bf16[1024,256]{1,0:T(8,128)(2,1)}, bf16[1024,256]{1,0:T(8,128)(2,1)}, u32[]{:S(2)}, u32[]{:S(2)}) collective-permute-start(bf16[1024,256]{1,0:T(8,128)(2,1)} %pad_maximum_fusion.3.refs_6_), channel_id=1, source_target_pairs={{0,64},{64,0},{128,192},{192,128},{1,65},{65,1},{129,193},{193,129... | collective-permute-start | bytes 1572872 | tf_op jit(solution)/shard_map/ppermute | solution.py:33
  41.8 11.8 %collective-permute-start.13 = (bf16[1024,256]{1,0:T(8,128)(2,1)}, bf16[1024,256]{1,0:T(8,128)(2,1)}, u32[]{:S(2)}, u32[]{:S(2)}) collective-permute-start(bf16[1024,256]{1,0:T(8,128)(2,1)} %pad_maximum_fusion.2.refs_4_), channel_id=1, source_target_pairs={{0,16},{16,0},{32,48},{48,32},{1,17},{17,1},{33,49},{49,33},{2,18}... | collective-permute-start | bytes 1572872 | tf_op jit(solution)/shard_map/ppermute | solution.py:33
  43.2 12.4 %collective-permute-start.10 = (bf16[1024,256]{1,0:T(8,128)(2,1)}, bf16[1024,256]{1,0:T(8,128)(2,1)}, u32[]{:S(2)}, u32[]{:S(2)}) collective-permute-start(bf16[1024,256]{1,0:T(8,128)(2,1)} %pad_maximum_fusion.1.refs_2_), channel_id=1, source_target_pairs={{0,192},{64,128},{128,64},{192,0},{1,193},{65,129},{129,65},{193,1... | collective-permute-start | bytes 1572872 | tf_op jit(solution)/shard_map/ppermute | solution.py:33
  44.4 13.5 %collective-permute-start.7 = (bf16[1024,256]{1,0:T(8,128)(2,1)}, bf16[1024,256]{1,0:T(8,128)(2,1)}, u32[]{:S(2)}, u32[]{:S(2)}) collective-permute-start(bf16[1024,256]{1,0:T(8,128)(2,1)} %pad_maximum_fusion.refs_0_), channel_id=1, source_target_pairs={{0,48},{16,32},{32,16},{48,0},{1,49},{17,33},{33,17},{49,1},{2,50}... | collective-permute-start | bytes 1572872 | tf_op jit(solution)/shard_map/ppermute | solution.py:33
  46.3 18.1 %all-to-all-start = ((f32[64,1,1152]{2,1,0:T(1,128)}), f32[64,1,1152]{2,1,0:T(1,128)S(1)}, u32[]{:S(2)}, u32[]{:S(2)}) async-start(f32[64,1,1152]{2,1,0:T(1,128)} %noise_message.1), calls=%async_computation | async-start | bytes 589824 | tf_op jit(solution)/shard_map/all_to_all | solution.py:276
  53.6 11.4 %copy-start.8 = (bf16[256,1024]{1,0:T(8,128)(2,1)}, bf16[256,1024]{1,0:T(8,128)(2,1)S(1)}, u32[]{:S(2)}) copy-start(bf16[256,1024]{1,0:T(8,128)(2,1)S(1)} %collective-permute-done.4.t2) | copy-start | bytes 1572868
  58.0 6.4 %collective-permute-start.17 = (bf16[256,1024]{1,0:T(8,128)(2,1)S(1)}, bf16[256,1024]{1,0:T(8,128)(2,1)S(1)}, u32[]{:S(2)}, u32[]{:S(2)}) collective-permute-start(bf16[256,1024]{1,0:T(8,128)(2,1)S(1)} %collective-permute-done.4.t2), channel_id=1, source_target_pairs={{0,1},{1,0},{2,3},{3,2},{4,5},{5,4},{6,7},{7,6},{8,9},{9,8},{10,11... | collective-permute-start | bytes 1572872 | tf_op jit(solution)/shard_map/ppermute | solution.py:33
  58.0 17.3 %collective-permute-start.21 = (bf16[1024,256]{1,0:T(8,128)(2,1)}, bf16[1024,256]{1,0:T(8,128)(2,1)}, u32[]{:S(2)}, u32[]{:S(2)}) collective-permute-start(bf16[1024,256]{1,0:T(8,128)(2,1)} %pad_maximum_fusion.3.refs_6_), channel_id=1, source_target_pairs={{0,16},{16,0},{32,48},{48,32},{1,17},{17,1},{33,49},{49,33},{2,18}... | collective-permute-start | bytes 1572872 | tf_op jit(solution)/shard_map/ppermute | solution.py:33
  58.4 17.6 %collective-permute-start.20 = (bf16[1024,256]{1,0:T(8,128)(2,1)}, bf16[1024,256]{1,0:T(8,128)(2,1)}, u32[]{:S(2)}, u32[]{:S(2)}) collective-permute-start(bf16[1024,256]{1,0:T(8,128)(2,1)} %pad_maximum_fusion.2.refs_4_), channel_id=1, source_target_pairs={{0,64},{64,0},{128,192},{192,128},{1,65},{65,1},{129,193},{193,129... | collective-permute-start | bytes 1572872 | tf_op jit(solution)/shard_map/ppermute | solution.py:33
  58.4 18.6 %collective-permute-start.19 = (bf16[1024,256]{1,0:T(8,128)(2,1)}, bf16[1024,256]{1,0:T(8,128)(2,1)}, u32[]{:S(2)}, u32[]{:S(2)}) collective-permute-start(bf16[1024,256]{1,0:T(8,128)(2,1)} %pad_maximum_fusion.1.refs_2_), channel_id=1, source_target_pairs={{0,48},{16,32},{32,16},{48,0},{1,49},{17,33},{33,17},{49,1},{2,50}... | collective-permute-start | bytes 1572872 | tf_op jit(solution)/shard_map/ppermute | solution.py:33
  60.6 19.9 %collective-permute-start.18 = (bf16[1024,256]{1,0:T(8,128)(2,1)}, bf16[1024,256]{1,0:T(8,128)(2,1)}, u32[]{:S(2)}, u32[]{:S(2)}) collective-permute-start(bf16[1024,256]{1,0:T(8,128)(2,1)} %pad_maximum_fusion.refs_0_), channel_id=1, source_target_pairs={{0,192},{64,128},{128,64},{192,0},{1,193},{65,129},{129,65},{193,1... | collective-permute-start | bytes 1572872 | tf_op jit(solution)/shard_map/ppermute | solution.py:33
  64.4 4.3 %copy-start.5 = (f32[64,1,1152]{2,1,0:T(1,128)}, f32[64,1,1152]{2,1,0:T(1,128)S(1)}, u32[]{:S(2)}) copy-start(f32[64,1,1152]{2,1,0:T(1,128)S(1)} %all-to-all-done.message_ref) | copy-start | bytes 884740
  64.4 0.8 copy-start.9
  64.4 19.8 %collective-permute-start.24 = (bf16[1024,256]{1,0:T(8,128)(2,1)}, bf16[1024,256]{1,0:T(8,128)(2,1)}, u32[]{:S(2)}, u32[]{:S(2)}) collective-permute-start(bf16[1024,256]{1,0:T(8,128)(2,1)} %collective-permute-done.13.refs_5_), channel_id=1, source_target_pairs={{0,64},{64,0},{128,192},{192,128},{1,65},{65,1},{129,193},{193,129... | collective-permute-start | bytes 1572872 | tf_op jit(solution)/shard_map/ppermute | solution.py:33
  68.7 1.6 %copy-start = (bf16[4,256,1024]{2,1,0:T(8,128)(2,1)S(1)}, bf16[4,256,1024]{2,1,0:T(8,128)(2,1)}, u32[]{:S(2)}) copy-start(bf16[4,256,1024]{2,1,0:T(8,128)(2,1)} %get-tuple-element.18.tokens_ref) | copy-start | bytes 6291460
  70.3 10.1 %copy-start.1 = (bf16[4,256,1024]{2,1,0:T(8,128)(2,1)S(1)}, bf16[4,256,1024]{2,1,0:T(8,128)(2,1)}, u32[]{:S(2)}) copy-start(bf16[4,256,1024]{2,1,0:T(8,128)(2,1)} %get-tuple-element.18.tokens_ref) | copy-start | bytes 6291460
  75.3 15.6 %copy-start.3 = (f32[256,8]{1,0:T(8,128)S(1)}, f32[256,8]{1,0:T(8,128)}, u32[]{:S(2)}) copy-start(f32[256,8]{1,0:T(8,128)} %get-tuple-element.19.projected_ref) | copy-start | bytes 24580
  75.3 15.6 %copy-start.4 = (bf16[1,1024]{1,0:T(2,128)(2,1)S(1)}, bf16[1,1024]{1,0:T(2,128)(2,1)}, u32[]{:S(2)}) copy-start(bf16[1,1024]{1,0:T(2,128)(2,1)} %noise_ref.1) | copy-start | bytes 6148
  75.3 12.2 %collective-permute-start.25 = (bf16[1024,256]{1,0:T(8,128)(2,1)}, bf16[1024,256]{1,0:T(8,128)(2,1)}, u32[]{:S(2)}, u32[]{:S(2)}) collective-permute-start(bf16[1024,256]{1,0:T(8,128)(2,1)} %collective-permute-done.16.refs_7_), channel_id=1, source_target_pairs={{0,16},{16,0},{32,48},{48,32},{1,17},{17,1},{33,49},{49,33},{2,18}... | collective-permute-start | bytes 1572872 | tf_op jit(solution)/shard_map/ppermute | solution.py:33
  76.0 13.6 %collective-permute-start.23 = (bf16[1024,256]{1,0:T(8,128)(2,1)}, bf16[1024,256]{1,0:T(8,128)(2,1)}, u32[]{:S(2)}, u32[]{:S(2)}) collective-permute-start(bf16[1024,256]{1,0:T(8,128)(2,1)} %collective-permute-done.10.refs_3_), channel_id=1, source_target_pairs={{0,48},{16,32},{32,16},{48,0},{1,49},{17,33},{33,17},{49,1},{2,50}... | collective-permute-start | bytes 1572872 | tf_op jit(solution)/shard_map/ppermute | solution.py:33
  77.0 13.9 %collective-permute-start.22 = (bf16[1024,256]{1,0:T(8,128)(2,1)}, bf16[1024,256]{1,0:T(8,128)(2,1)}, u32[]{:S(2)}, u32[]{:S(2)}) collective-permute-start(bf16[1024,256]{1,0:T(8,128)(2,1)} %collective-permute-done.7.refs_1_), channel_id=1, source_target_pairs={{0,192},{64,128},{128,64},{192,0},{1,193},{65,129},{129,65},{193,1... | collective-permute-start | bytes 1572872 | tf_op jit(solution)/shard_map/ppermute | solution.py:33
  80.4 10.4 %copy-start.2 = (bf16[8,1024,256]{2,1,0:T(8,128)(2,1)S(1)}, bf16[8,1024,256]{2,1,0:T(8,128)(2,1)}, u32[]{:S(2)}) copy-start(bf16[8,1024,256]{2,1,0:T(8,128)(2,1)} %decayed_scores.1.scores_ref) | copy-start | bytes 12582916

commit v9 on v7

--- a/solution.py
+++ b/solution.py
@@ -278,8 +278,17 @@
     )
     third = [swap(held[c], *LINKS[ROUTES[c][2]]) for c in chunks]
     fourth = [swap(held[c], *LINKS[ROUTES[c][3]]) for c in chunks]
+    update = pl.pallas_call(
+        update_kernel,
+        out_shape=jax.ShapeDtypeStruct((rows, width), F32),
+        in_specs=[SMEM, VMEM],
+        out_specs=VMEM,
+        cost_estimate=cost(0, 1 << 20),
+        name="update_product",
+    )(z.reshape(1), message)
+
     ready = list(third)
-    ready[3] = after(third[3], message)
+    ready[3] = after(third[3], update)
     last = [swap(ready[c], *LINKS[ROUTES[c][3]]) for c in chunks]
 
     both = swap(after(twin, *third), "core", 1)
@@ -296,15 +305,6 @@
         compiler_params=params(16),
         name="member_tokens",
     )(tp, tokens, mate, twin, both, noise_in.reshape(4, 1, width))
-
-    update = pl.pallas_call(
-        update_kernel,
-        out_shape=jax.ShapeDtypeStruct((rows, width), F32),
-        in_specs=[SMEM, VMEM],
-        out_specs=VMEM,
-        cost_estimate=cost(0, 1 << 20),
-        name="update_product",
-    )(z.reshape(1), message)
 
     at = jnp.stack([lax.axis_index("y"), lax.axis_index("x")])
     total = product(

time: 92.9 us -> 92.8 us (level)
  transfers between devices with their start and end apart: 27 -> 27, of which waited for: 5 -> 6; matrix products, arithmetic and copies ran while one was open for 1% -> 1% of each run, Pallas kernels for 24% -> 24%
where the time goes in v9:
time: 92.8 us; the launch traced here: 92.1 us
  starting transfers between devices  45.7 us (49%)
  Pallas kernels  27.7 us (30%)
  waiting for transfers between devices  14.2 us (15%)
  between operations  2.33 us (3%)
  local copies, waits for them, and re-layouts  1.85 us (2%)
    ppermute x23, starting transfers between devices, swap(): return lax.ppermute(array, axis, [(i, i ^ mask) for i in range(size)])  32 us
    ppermute x23, waiting for transfers between devices, swap(): return lax.ppermute(array, axis, [(i, i ^ mask) for i in range(size)])  11 us
    pallas_call x2, Pallas kernels, product(): pl.pallas_call(functools.partial(product_kernel, ways, before is not None...  8.38 us
    pallas_call x1, Pallas kernels, score_heads(): pl.pallas_call(score_kernel, out_shape=jax.ShapeDtypeStruct((count, 4 * l...  7.8 us
    ppermute x3, starting transfers between devices, fetch(): lax.ppermute(array, axis, [((i + step) % size, i) for i in range(size)])  7.17 us
    all_to_all x1, starting transfers between devices, body(): lax.all_to_all(after(message, *held), POP, split_axis=0, concat_axis=0, t...  6.58 us
    pallas_call x1, Pallas kernels, body(): pl.pallas_call(readout_kernel, out_shape=jax.ShapeDtypeStruct((length, wi...  5.76 us
    all_to_all x1, waiting for transfers between devices, body(): lax.all_to_all(after(message, *held), POP, split_axis=0, concat_axis=0, t...  3.21 us
  transfers between devices with their start and end apart: 27, of which 6 were waited for; matrix products, arithmetic and copies ran while one was open for 1% of the time, Pallas kernels for 24%

profile of v9, /device:TPU:32, one launch (start us, length us, event | category | flops | bytes accessed | tf_op | source)
XLA Modules:
  0.0 92.1 jit_solution(11935129213324100057)
XLA Ops:
  0.6 0.1 collective-permute-start.3
  0.7 1.9 %collective-permute-start = (bf16[64,1024]{1,0:T(8,128)(2,1)}, bf16[64,1024]{1,0:T(8,128)(2,1)S(1)}, u32[]{:S(2)}, u32[]{:S(2)}) collective-permute-start(bf16[64,1024]{1,0:T(8,128)(2,1)} %param.13), channel_id=1, source_target_pairs={{4,0},{8,4},{12,8},{0,12},{5,1},{9,5},{13,9},{1,13},{6,2},{10,6},{... | collective-permute-start | bytes 393224 | tf_op jit(solution)/shard_map/ppermute | solution.py:38
  2.7 0.2 collective-permute-start.1
  2.8 5.1 %collective-permute-start.2 = (bf16[64,1024]{1,0:T(8,128)(2,1)}, bf16[64,1024]{1,0:T(8,128)(2,1)S(1)}, u32[]{:S(2)}, u32[]{:S(2)}) collective-permute-start(bf16[64,1024]{1,0:T(8,128)(2,1)} %param.13), channel_id=1, source_target_pairs={{8,0},{12,4},{0,8},{4,12},{9,1},{13,5},{1,9},{5,13},{10,2},{14,6},... | collective-permute-start | bytes 393224 | tf_op jit(solution)/shard_map/ppermute | solution.py:38
  7.9 0.1 broadcast_in_dim.3
  8.0 0.0 copy-start.1
  8.0 1.0 %constant_dynamic-update-slice_fusion.3 = bf16[256,1024]{1,0:T(8,128)(2,1)S(1)} fusion(bf16[256,1024]{1,0:T(8,128)(2,1)S(1)} %broadcast_in_dim.3, bf16[64,1024]{1,0:T(8,128)(2,1)} %param.13, s32[]{:T(128)S(6)} %select_n.12), kind=kLoop, calls=%fused_computation.11 | loop fusion | bytes 262148 | tf_op jit(solution)/shard_map/dynamic_update_slice | solution.py:255
  10.3 1.5 %noise_message.1 = f32[64,1,1152]{2,1,0:T(1,128)} custom-call(f32[1]{0:T(128)S(6)} %copy.15.utility_ref, bf16[1,4096]{1,0:T(2,128)(2,1)} %noise_in_ref.1, bf16[1,1024]{1,0:T(2,128)(2,1)} %noise_ref.1), custom_call_target="tpu_custom_call" | custom-call | bytes 524288 | tf_op jit(solution)/shard_map/noise_message/pallas_call | solution.py:258
  11.7 7.8 %decayed_scores.1.scores_ref = bf16[8,1024,256]{2,1,0:T(8,128)(2,1)} custom-call(s32[1]{0:T(128)S(6)} %copy.16.live_ref, bf16[256,1024]{1,0:T(8,128)(2,1)} %bitcast.14, bf16[256,1024]{1,0:T(8,128)(2,1)} %bitcast.15, bf16[256,1024]{1,0:T(8,128)(2,1)} %bitcast.16), custom_call_target="tpu_custom_call" | custom-call | bytes 20971520 | tf_op jit(solution)/shard_map/decayed_scores/pallas_call | solution.py:230
  19.5 0.0 collective-permute-done
  19.6 0.0 collective-permute-done.1
  19.6 0.0 collective-permute-done.2
  19.6 0.0 copy-start.2
  19.6 0.0 collective-permute-done.3.t1
  19.7 3.1 %collective-permute-start.14 = (bf16[256,256]{1,0:T(8,128)(2,1)S(1)}, bf16[256,256]{1,0:T(8,128)(2,1)S(1)}, u32[]{:S(2)}, u32[]{:S(2)}) collective-permute-start(bf16[256,256]{1,0:T(8,128)(2,1)S(1)} %get-tuple-element.22), channel_id=1, source_target_pairs={{0,192},{64,128},{128,64},{192,0},{1,193},{65,129},{129,65},{193,1... | collective-permute-start | bytes 393224 | tf_op jit(solution)/shard_map/ppermute | solution.py:33
  22.8 2.8 %collective-permute-start.11 = (bf16[256,256]{1,0:T(8,128)(2,1)S(1)}, bf16[256,256]{1,0:T(8,128)(2,1)S(1)}, u32[]{:S(2)}, u32[]{:S(2)}) collective-permute-start(bf16[256,256]{1,0:T(8,128)(2,1)S(1)} %get-tuple-element.23), channel_id=1, source_target_pairs={{0,48},{16,32},{32,16},{48,0},{1,49},{17,33},{33,17},{49,1},{2,50}... | collective-permute-start | bytes 393224 | tf_op jit(solution)/shard_map/ppermute | solution.py:33
  25.6 0.1 collective-permute-start.8
  25.7 0.2 collective-permute-start.5
  25.9 4.5 %collective-permute-start.4 = (bf16[256,1024]{1,0:T(8,128)(2,1)S(1)}, bf16[256,1024]{1,0:T(8,128)(2,1)}, u32[]{:S(2)}, u32[]{:S(2)}) collective-permute-start(bf16[256,1024]{1,0:T(8,128)(2,1)S(1)} %bitcast.11), channel_id=1, source_target_pairs={{0,2},{2,0},{1,3},{3,1},{4,6},{6,4},{5,7},{7,5},{8,10},{10,8},{9,1... | collective-permute-start | bytes 1572872 | tf_op jit(solution)/shard_map/ppermute | solution.py:33
  30.4 0.0 collective-permute-done.14
  30.5 1.2 %collective-permute-start.15 = (bf16[512,256]{1,0:T(8,128)(2,1)S(1)}, bf16[512,256]{1,0:T(8,128)(2,1)S(1)}, u32[]{:S(2)}, u32[]{:S(2)}) collective-permute-start(bf16[512,256]{1,0:T(8,128)(2,1)S(1)} %pad_maximum_fusion.7), channel_id=1, source_target_pairs={{0,48},{16,32},{32,16},{48,0},{1,49},{17,33},{33,17},{49,1},{2,50}... | collective-permute-start | bytes 786440 | tf_op jit(solution)/shard_map/ppermute | solution.py:33
  31.7 0.0 collective-permute-done.11
  31.7 1.1 %collective-permute-start.12 = (bf16[512,256]{1,0:T(8,128)(2,1)S(1)}, bf16[512,256]{1,0:T(8,128)(2,1)S(1)}, u32[]{:S(2)}, u32[]{:S(2)}) collective-permute-start(bf16[512,256]{1,0:T(8,128)(2,1)S(1)} %pad_maximum_fusion.6), channel_id=1, source_target_pairs={{0,192},{64,128},{128,64},{192,0},{1,193},{65,129},{129,65},{193,1... | collective-permute-start | bytes 786440 | tf_op jit(solution)/shard_map/ppermute | solution.py:33
  32.8 0.0 collective-permute-done.8
  32.9 0.8 collective-permute-start.9
  33.6 0.0 collective-permute-done.5
  33.7 0.9 %collective-permute-start.6 = (bf16[512,256]{1,0:T(8,128)(2,1)S(1)}, bf16[512,256]{1,0:T(8,128)(2,1)S(1)}, u32[]{:S(2)}, u32[]{:S(2)}) collective-permute-start(bf16[512,256]{1,0:T(8,128)(2,1)S(1)} %pad_maximum_fusion.4), channel_id=1, source_target_pairs={{0,64},{64,0},{128,192},{192,128},{1,65},{65,1},{129,193},{193,129... | collective-permute-start | bytes 786440 | tf_op jit(solution)/shard_map/ppermute | solution.py:33
  34.6 3.8 %collective-permute-done.15 = bf16[512,256]{1,0:T(8,128)(2,1)S(1)} collective-permute-done((bf16[512,256]{1,0:T(8,128)(2,1)S(1)}, bf16[512,256]{1,0:T(8,128)(2,1)S(1)}, u32[]{:S(2)}, u32[]{:S(2)}) %collective-permute-start.15) | collective-permute-done | bytes 262176 | tf_op jit(solution)/shard_map/ppermute | solution.py:33
  38.5 1.7 %collective-permute-start.16 = (bf16[1024,256]{1,0:T(8,128)(2,1)S(1)}, bf16[1024,256]{1,0:T(8,128)(2,1)}, u32[]{:S(2)}, u32[]{:S(2)}) collective-permute-start(bf16[1024,256]{1,0:T(8,128)(2,1)S(1)} %pad_maximum_fusion.3.refs_6_), channel_id=1, source_target_pairs={{0,64},{64,0},{128,192},{192,128},{1,65},{65,1},{129,193},{193,129... | collective-permute-start | bytes 1572872 | tf_op jit(solution)/shard_map/ppermute | solution.py:33
  40.2 0.0 collective-permute-done.12
  40.3 0.6 collective-permute-start.13
  40.9 1.5 %collective-permute-start.10 = (bf16[1024,256]{1,0:T(8,128)(2,1)S(1)}, bf16[1024,256]{1,0:T(8,128)(2,1)}, u32[]{:S(2)}, u32[]{:S(2)}) collective-permute-start(bf16[1024,256]{1,0:T(8,128)(2,1)S(1)} %pad_maximum_fusion.1.refs_2_), channel_id=1, source_target_pairs={{0,192},{64,128},{128,64},{192,0},{1,193},{65,129},{129,65},{193,1... | collective-permute-start | bytes 1572872 | tf_op jit(solution)/shard_map/ppermute | solution.py:33
  42.5 3.1 %collective-permute-start.7 = (bf16[1024,256]{1,0:T(8,128)(2,1)S(1)}, bf16[1024,256]{1,0:T(8,128)(2,1)}, u32[]{:S(2)}, u32[]{:S(2)}) collective-permute-start(bf16[1024,256]{1,0:T(8,128)(2,1)S(1)} %pad_maximum_fusion.refs_0_), channel_id=1, source_target_pairs={{0,48},{16,32},{32,16},{48,0},{1,49},{17,33},{33,17},{49,1},{2,50}... | collective-permute-start | bytes 1572872 | tf_op jit(solution)/shard_map/ppermute | solution.py:33
  45.6 6.6 %all-to-all-start = ((f32[64,1,1152]{2,1,0:T(1,128)}), f32[64,1,1152]{2,1,0:T(1,128)S(1)}, u32[]{:S(2)}, u32[]{:S(2)}) async-start(f32[64,1,1152]{2,1,0:T(1,128)} %noise_message.1), calls=%async_computation | async-start | bytes 589824 | tf_op jit(solution)/shard_map/all_to_all | solution.py:276
  52.2 1.6 %collective-permute-done.4.t2 = bf16[256,1024]{1,0:T(8,128)(2,1)} collective-permute-done((bf16[256,1024]{1,0:T(8,128)(2,1)S(1)}, bf16[256,1024]{1,0:T(8,128)(2,1)}, u32[]{:S(2)}, u32[]{:S(2)}) %collective-permute-start.4) | collective-permute-done | bytes 524320 | tf_op jit(solution)/shard_map/ppermute | solution.py:33
  53.7 1.7 %collective-permute-start.21 = (bf16[1024,256]{1,0:T(8,128)(2,1)S(1)}, bf16[1024,256]{1,0:T(8,128)(2,1)}, u32[]{:S(2)}, u32[]{:S(2)}) collective-permute-start(bf16[1024,256]{1,0:T(8,128)(2,1)S(1)} %pad_maximum_fusion.3.refs_6_), channel_id=1, source_target_pairs={{0,16},{16,0},{32,48},{48,32},{1,17},{17,1},{33,49},{49,33},{2,18}... | collective-permute-start | bytes 1572872 | tf_op jit(solution)/shard_map/ppermute | solution.py:33
  55.4 0.0 collective-permute-done.16.refs_7_
  55.4 1.7 %collective-permute-start.20 = (bf16[1024,256]{1,0:T(8,128)(2,1)S(1)}, bf16[1024,256]{1,0:T(8,128)(2,1)}, u32[]{:S(2)}, u32[]{:S(2)}) collective-permute-start(bf16[1024,256]{1,0:T(8,128)(2,1)S(1)} %pad_maximum_fusion.2.refs_4_), channel_id=1, source_target_pairs={{0,64},{64,0},{128,192},{192,128},{1,65},{65,1},{129,193},{193,129... | collective-permute-start | bytes 1572872 | tf_op jit(solution)/shard_map/ppermute | solution.py:33
  57.1 0.0 collective-permute-done.13.refs_5_
  57.1 0.5 collective-permute-start.19
  57.6 0.0 collective-permute-done.10.refs_3_
  57.6 0.0 collective-permute-done.7.refs_1_
  57.6 0.0 collective-permute-start.17
  57.6 2.1 %collective-permute-start.18 = (bf16[1024,256]{1,0:T(8,128)(2,1)S(1)}, bf16[1024,256]{1,0:T(8,128)(2,1)}, u32[]{:S(2)}, u32[]{:S(2)}) collective-permute-start(bf16[1024,256]{1,0:T(8,128)(2,1)S(1)} %pad_maximum_fusion.refs_0_), channel_id=1, source_target_pairs={{0,192},{64,128},{128,64},{192,0},{1,193},{65,129},{129,65},{193,1... | collective-permute-start | bytes 1572872 | tf_op jit(solution)/shard_map/ppermute | solution.py:33
  59.8 3.2 %all-to-all-done.message_ref = f32[64,1,1152]{2,1,0:T(1,128)S(1)} async-done(((f32[64,1,1152]{2,1,0:T(1,128)}), f32[64,1,1152]{2,1,0:T(1,128)S(1)}, u32[]{:S(2)}, u32[]{:S(2)}) %all-to-all-start) | async-done | bytes 294944 | tf_op jit(solution)/shard_map/all_to_all | solution.py:276
  63.0 0.7 copy-done.4
  63.7 2.3 %update_product.1 = f32[64,1024]{1,0:T(8,128)} custom-call(s32[1]{0:T(128)} %bitcast.8.z_ref, f32[64,1,1152]{2,1,0:T(1,128)} %copy-done.4), custom_call_target="tpu_custom_call" | custom-call | bytes 1048576 | tf_op jit(solution)/shard_map/update_product/pallas_call | solution.py:281
  66.0 2.8 %collective-permute-done.21.refs_4_ = bf16[1024,256]{1,0:T(8,128)(2,1)} collective-permute-done((bf16[1024,256]{1,0:T(8,128)(2,1)S(1)}, bf16[1024,256]{1,0:T(8,128)(2,1)}, u32[]{:S(2)}, u32[]{:S(2)}) %collective-permute-start.21) | collective-permute-done | bytes 524320 | tf_op jit(solution)/shard_map/ppermute | solution.py:33
  68.8 1.8 %collective-permute-start.24 = (bf16[1024,256]{1,0:T(8,128)(2,1)}, bf16[1024,256]{1,0:T(8,128)(2,1)}, u32[]{:S(2)}, u32[]{:S(2)}) collective-permute-start(bf16[1024,256]{1,0:T(8,128)(2,1)} %collective-permute-done.13.refs_5_), channel_id=1, source_target_pairs={{0,64},{64,0},{128,192},{192,128},{1,65},{65,1},{129,193},{193,129... | collective-permute-start | bytes 1572872 | tf_op jit(solution)/shard_map/ppermute | solution.py:33
  70.6 0.0 collective-permute-done.20.refs_3_
  70.6 1.3 %collective-permute-start.23 = (bf16[1024,256]{1,0:T(8,128)(2,1)}, bf16[1024,256]{1,0:T(8,128)(2,1)}, u32[]{:S(2)}, u32[]{:S(2)}) collective-permute-start(bf16[1024,256]{1,0:T(8,128)(2,1)} %collective-permute-done.10.refs_3_), channel_id=1, source_target_pairs={{0,48},{16,32},{32,16},{48,0},{1,49},{17,33},{33,17},{49,1},{2,50}... | collective-permute-start | bytes 1572872 | tf_op jit(solution)/shard_map/ppermute | solution.py:33
  71.9 0.0 collective-permute-done.19.refs_2_
  71.9 1.0 %collective-permute-start.22 = (bf16[1024,256]{1,0:T(8,128)(2,1)}, bf16[1024,256]{1,0:T(8,128)(2,1)}, u32[]{:S(2)}, u32[]{:S(2)}) collective-permute-start(bf16[1024,256]{1,0:T(8,128)(2,1)} %collective-permute-done.7.refs_1_), channel_id=1, source_target_pairs={{0,192},{64,128},{128,64},{192,0},{1,193},{65,129},{129,65},{193,1... | collective-permute-start | bytes 1572872 | tf_op jit(solution)/shard_map/ppermute | solution.py:33
  72.8 0.0 collective-permute-start.25
  72.9 0.1 pad_add_fusion.at_ref
  73.0 2.0 %member_tokens.1 = (bf16[4,256,1024]{2,1,0:T(8,128)(2,1)S(1)}, f32[256,8]{1,0:T(8,128)S(1)}) custom-call(s32[1]{0:T(128)} %bitcast.2.at_ref, bf16[256,1024]{1,0:T(8,128)(2,1)S(1)} %bitcast.12, bf16[256,1024]{1,0:T(8,128)(2,1)S(1)} %collective-permute-done.3.t1, bf16[256,1024]{1,0:T(8,128)(2,1)} %collective-permute-done.4.t2, ...), custom_call_target="tpu_custom_call" | custom-call | bytes 8388608 | tf_op jit(solution)/shard_map/member_tokens/pallas_call | solution.py:296
  74.9 4.7 %products.2.refs_0_ = f32[256,1024]{1,0:T(8,128)S(1)} custom-call(s32[2]{0:T(128)S(1)} %pad_add_fusion.at_ref, bf16[4,256,1024]{2,1,0:T(8,128)(2,1)S(1)} %get-tuple-element.16.tokens_ref, bf16[1024,256]{1,0:T(8,128)(2,1)S(1)} %pad_maximum_fusion.refs_0_, bf16[1024,256]{1,0:T(8,128)(2,1)} %collective-permute-done.7.refs_1_, ...), custom_call_target="tpu_custom_call" | custom-call | flops 1073741824 | bytes 8388608 | tf_op jit(solution)/shard_map/products/pallas_call | solution.py:150
  79.7 0.0 copy-start.3
  79.7 3.6 %products.3.sum_ref = f32[256,1024]{1,0:T(8,128)S(1)} custom-call(s32[2]{0:T(128)S(1)} %pad_add_fusion.at_ref, bf16[4,256,1024]{2,1,0:T(8,128)(2,1)S(1)} %get-tuple-element.16.tokens_ref, f32[256,1024]{1,0:T(8,128)S(1)} %products.2.refs_0_, bf16[1024,256]{1,0:T(8,128)(2,1)} %collective-permute-done.18.refs_1_, ...), custom_call_target="tpu_custom_call" | custom-call | flops 536870912 | bytes 8388608 | tf_op jit(solution)/shard_map/products/pallas_call | solution.py:150
  83.4 0.0 collective-permute-done.24.refs_2_
  83.4 1.8 %collective-permute-done.23.refs_1_ = bf16[1024,256]{1,0:T(8,128)(2,1)} collective-permute-done((bf16[1024,256]{1,0:T(8,128)(2,1)}, bf16[1024,256]{1,0:T(8,128)(2,1)}, u32[]{:S(2)}, u32[]{:S(2)}) %collective-permute-start.23) | collective-permute-done | bytes 524320 | tf_op jit(solution)/shard_map/ppermute | solution.py:33
  85.2 1.0 %collective-permute-done.22.refs_0_ = bf16[1024,256]{1,0:T(8,128)(2,1)} collective-permute-done((bf16[1024,256]{1,0:T(8,128)(2,1)}, bf16[1024,256]{1,0:T(8,128)(2,1)}, u32[]{:S(2)}, u32[]{:S(2)}) %collective-permute-start.22) | collective-permute-done | bytes 524320 | tf_op jit(solution)/shard_map/ppermute | solution.py:33
  86.1 0.0 collective-permute-done.25.refs_3_
  86.2 5.8 %values_readout.1 = bf16[256,1024]{1,0:T(8,128)(2,1)} custom-call(s32[2]{0:T(128)S(1)} %pad_add_fusion.at_ref, bf16[4,256,1024]{2,1,0:T(8,128)(2,1)S(1)} %get-tuple-element.16.tokens_ref, f32[256,1024]{1,0:T(8,128)S(1)} %products.3.sum_ref, f32[256,8]{1,0:T(8,128)S(1)} %get-tuple-element.17.projected_ref, bf16[1,1024]{1,0:T(2,128)(2,1)S(1)} %copy-done.3, ...), custom_call_target="tpu_custom_call" | custom-call | flops 536870912 | bytes 12582912 | tf_op jit(solution)/shard_map/values_readout/pallas_call | solution.py:314
  (22 shorter events, 0.3 us)
Async XLA Ops:
  0.6 19.0 %collective-permute-start.3 = (bf16[256,1024]{1,0:T(8,128)(2,1)}, bf16[256,1024]{1,0:T(8,128)(2,1)S(1)}, u32[]{:S(2)}, u32[]{:S(2)}) collective-permute-start(bf16[256,1024]{1,0:T(8,128)(2,1)} %bitcast.10), channel_id=1, source_target_pairs={{0,1},{1,0},{2,3},{3,2},{4,5},{5,4},{6,7},{7,6},{8,9},{9,8},{10,11... | collective-permute-start | bytes 1572872 | tf_op jit(solution)/shard_map/ppermute | solution.py:33
  0.7 18.8 %collective-permute-start = (bf16[64,1024]{1,0:T(8,128)(2,1)}, bf16[64,1024]{1,0:T(8,128)(2,1)S(1)}, u32[]{:S(2)}, u32[]{:S(2)}) collective-permute-start(bf16[64,1024]{1,0:T(8,128)(2,1)} %param.13), channel_id=1, source_target_pairs={{4,0},{8,4},{12,8},{0,12},{5,1},{9,5},{13,9},{1,13},{6,2},{10,6},{... | collective-permute-start | bytes 393224 | tf_op jit(solution)/shard_map/ppermute | solution.py:38
  2.7 16.9 %collective-permute-start.1 = (bf16[64,1024]{1,0:T(8,128)(2,1)}, bf16[64,1024]{1,0:T(8,128)(2,1)S(1)}, u32[]{:S(2)}, u32[]{:S(2)}) collective-permute-start(bf16[64,1024]{1,0:T(8,128)(2,1)} %param.13), channel_id=1, source_target_pairs={{12,0},{0,4},{4,8},{8,12},{13,1},{1,5},{5,9},{9,13},{14,2},{2,6},{... | collective-permute-start | bytes 393224 | tf_op jit(solution)/shard_map/ppermute | solution.py:38
  2.8 16.8 %collective-permute-start.2 = (bf16[64,1024]{1,0:T(8,128)(2,1)}, bf16[64,1024]{1,0:T(8,128)(2,1)S(1)}, u32[]{:S(2)}, u32[]{:S(2)}) collective-permute-start(bf16[64,1024]{1,0:T(8,128)(2,1)} %param.13), channel_id=1, source_target_pairs={{8,0},{12,4},{0,8},{4,12},{9,1},{13,5},{1,9},{5,13},{10,2},{14,6},... | collective-permute-start | bytes 393224 | tf_op jit(solution)/shard_map/ppermute | solution.py:38
  8.0 18.0 %copy-start.1 = (bf16[1,256,1024]{2,1,0:T(8,128)(2,1)S(1)}, bf16[1,256,1024]{2,1,0:T(8,128)(2,1)}, u32[]{:S(2)}) copy-start(bf16[1,256,1024]{2,1,0:T(8,128)(2,1)} %param.9) | copy-start | bytes 1572868
  19.6 53.3 %copy-start.2 = (bf16[1,4096]{1,0:T(2,128)(2,1)S(1)}, bf16[1,4096]{1,0:T(2,128)(2,1)}, u32[]{:S(2)}) copy-start(bf16[1,4096]{1,0:T(2,128)(2,1)} %noise_in_ref.1) | copy-start | bytes 24580
  19.7 10.7 %collective-permute-start.14 = (bf16[256,256]{1,0:T(8,128)(2,1)S(1)}, bf16[256,256]{1,0:T(8,128)(2,1)S(1)}, u32[]{:S(2)}, u32[]{:S(2)}) collective-permute-start(bf16[256,256]{1,0:T(8,128)(2,1)S(1)} %get-tuple-element.22), channel_id=1, source_target_pairs={{0,192},{64,128},{128,64},{192,0},{1,193},{65,129},{129,65},{193,1... | collective-permute-start | bytes 393224 | tf_op jit(solution)/shard_map/ppermute | solution.py:33
  22.8 8.9 %collective-permute-start.11 = (bf16[256,256]{1,0:T(8,128)(2,1)S(1)}, bf16[256,256]{1,0:T(8,128)(2,1)S(1)}, u32[]{:S(2)}, u32[]{:S(2)}) collective-permute-start(bf16[256,256]{1,0:T(8,128)(2,1)S(1)} %get-tuple-element.23), channel_id=1, source_target_pairs={{0,48},{16,32},{32,16},{48,0},{1,49},{17,33},{33,17},{49,1},{2,50}... | collective-permute-start | bytes 393224 | tf_op jit(solution)/shard_map/ppermute | solution.py:33
  25.6 7.3 %collective-permute-start.8 = (bf16[256,256]{1,0:T(8,128)(2,1)S(1)}, bf16[256,256]{1,0:T(8,128)(2,1)S(1)}, u32[]{:S(2)}, u32[]{:S(2)}) collective-permute-start(bf16[256,256]{1,0:T(8,128)(2,1)S(1)} %get-tuple-element.24), channel_id=1, source_target_pairs={{0,64},{64,0},{128,192},{192,128},{1,65},{65,1},{129,193},{193,129... | collective-permute-start | bytes 393224 | tf_op jit(solution)/shard_map/ppermute | solution.py:33
  25.7 7.9 %collective-permute-start.5 = (bf16[256,256]{1,0:T(8,128)(2,1)S(1)}, bf16[256,256]{1,0:T(8,128)(2,1)S(1)}, u32[]{:S(2)}, u32[]{:S(2)}) collective-permute-start(bf16[256,256]{1,0:T(8,128)(2,1)S(1)} %get-tuple-element.25), channel_id=1, source_target_pairs={{0,16},{16,0},{32,48},{48,32},{1,17},{17,1},{33,49},{49,33},{2,18}... | collective-permute-start | bytes 393224 | tf_op jit(solution)/shard_map/ppermute | solution.py:33
  25.9 27.8 %collective-permute-start.4 = (bf16[256,1024]{1,0:T(8,128)(2,1)S(1)}, bf16[256,1024]{1,0:T(8,128)(2,1)}, u32[]{:S(2)}, u32[]{:S(2)}) collective-permute-start(bf16[256,1024]{1,0:T(8,128)(2,1)S(1)} %bitcast.11), channel_id=1, source_target_pairs={{0,2},{2,0},{1,3},{3,1},{4,6},{6,4},{5,7},{7,5},{8,10},{10,8},{9,1... | collective-permute-start | bytes 1572872 | tf_op jit(solution)/shard_map/ppermute | solution.py:33
  30.5 8.0 %collective-permute-start.15 = (bf16[512,256]{1,0:T(8,128)(2,1)S(1)}, bf16[512,256]{1,0:T(8,128)(2,1)S(1)}, u32[]{:S(2)}, u32[]{:S(2)}) collective-permute-start(bf16[512,256]{1,0:T(8,128)(2,1)S(1)} %pad_maximum_fusion.7), channel_id=1, source_target_pairs={{0,48},{16,32},{32,16},{48,0},{1,49},{17,33},{33,17},{49,1},{2,50}... | collective-permute-start | bytes 786440 | tf_op jit(solution)/shard_map/ppermute | solution.py:33
  31.7 8.5 %collective-permute-start.12 = (bf16[512,256]{1,0:T(8,128)(2,1)S(1)}, bf16[512,256]{1,0:T(8,128)(2,1)S(1)}, u32[]{:S(2)}, u32[]{:S(2)}) collective-permute-start(bf16[512,256]{1,0:T(8,128)(2,1)S(1)} %pad_maximum_fusion.6), channel_id=1, source_target_pairs={{0,192},{64,128},{128,64},{192,0},{1,193},{65,129},{129,65},{193,1... | collective-permute-start | bytes 786440 | tf_op jit(solution)/shard_map/ppermute | solution.py:33
  32.9 8.0 %collective-permute-start.9 = (bf16[512,256]{1,0:T(8,128)(2,1)S(1)}, bf16[512,256]{1,0:T(8,128)(2,1)S(1)}, u32[]{:S(2)}, u32[]{:S(2)}) collective-permute-start(bf16[512,256]{1,0:T(8,128)(2,1)S(1)} %pad_maximum_fusion.5), channel_id=1, source_target_pairs={{0,16},{16,0},{32,48},{48,32},{1,17},{17,1},{33,49},{49,33},{2,18}... | collective-permute-start | bytes 786440 | tf_op jit(solution)/shard_map/ppermute | solution.py:33
  33.7 8.8 %collective-permute-start.6 = (bf16[512,256]{1,0:T(8,128)(2,1)S(1)}, bf16[512,256]{1,0:T(8,128)(2,1)S(1)}, u32[]{:S(2)}, u32[]{:S(2)}) collective-permute-start(bf16[512,256]{1,0:T(8,128)(2,1)S(1)} %pad_maximum_fusion.4), channel_id=1, source_target_pairs={{0,64},{64,0},{128,192},{192,128},{1,65},{65,1},{129,193},{193,129... | collective-permute-start | bytes 786440 | tf_op jit(solution)/shard_map/ppermute | solution.py:33
  38.5 16.9 %collective-permute-start.16 = (bf16[1024,256]{1,0:T(8,128)(2,1)S(1)}, bf16[1024,256]{1,0:T(8,128)(2,1)}, u32[]{:S(2)}, u32[]{:S(2)}) collective-permute-start(bf16[1024,256]{1,0:T(8,128)(2,1)S(1)} %pad_maximum_fusion.3.refs_6_), channel_id=1, source_target_pairs={{0,64},{64,0},{128,192},{192,128},{1,65},{65,1},{129,193},{193,129... | collective-permute-start | bytes 1572872 | tf_op jit(solution)/shard_map/ppermute | solution.py:33
  40.3 16.9 %collective-permute-start.13 = (bf16[1024,256]{1,0:T(8,128)(2,1)S(1)}, bf16[1024,256]{1,0:T(8,128)(2,1)}, u32[]{:S(2)}, u32[]{:S(2)}) collective-permute-start(bf16[1024,256]{1,0:T(8,128)(2,1)S(1)} %pad_maximum_fusion.2.refs_4_), channel_id=1, source_target_pairs={{0,16},{16,0},{32,48},{48,32},{1,17},{17,1},{33,49},{49,33},{2,18}... | collective-permute-start | bytes 1572872 | tf_op jit(solution)/shard_map/ppermute | solution.py:33
  40.9 16.7 %collective-permute-start.10 = (bf16[1024,256]{1,0:T(8,128)(2,1)S(1)}, bf16[1024,256]{1,0:T(8,128)(2,1)}, u32[]{:S(2)}, u32[]{:S(2)}) collective-permute-start(bf16[1024,256]{1,0:T(8,128)(2,1)S(1)} %pad_maximum_fusion.1.refs_2_), channel_id=1, source_target_pairs={{0,192},{64,128},{128,64},{192,0},{1,193},{65,129},{129,65},{193,1... | collective-permute-start | bytes 1572872 | tf_op jit(solution)/shard_map/ppermute | solution.py:33
  42.5 15.1 %collective-permute-start.7 = (bf16[1024,256]{1,0:T(8,128)(2,1)S(1)}, bf16[1024,256]{1,0:T(8,128)(2,1)}, u32[]{:S(2)}, u32[]{:S(2)}) collective-permute-start(bf16[1024,256]{1,0:T(8,128)(2,1)S(1)} %pad_maximum_fusion.refs_0_), channel_id=1, source_target_pairs={{0,48},{16,32},{32,16},{48,0},{1,49},{17,33},{33,17},{49,1},{2,50}... | collective-permute-start | bytes 1572872 | tf_op jit(solution)/shard_map/ppermute | solution.py:33
  45.6 17.4 %all-to-all-start = ((f32[64,1,1152]{2,1,0:T(1,128)}), f32[64,1,1152]{2,1,0:T(1,128)S(1)}, u32[]{:S(2)}, u32[]{:S(2)}) async-start(f32[64,1,1152]{2,1,0:T(1,128)} %noise_message.1), calls=%async_computation | async-start | bytes 589824 | tf_op jit(solution)/shard_map/all_to_all | solution.py:276
  53.7 15.1 %collective-permute-start.21 = (bf16[1024,256]{1,0:T(8,128)(2,1)S(1)}, bf16[1024,256]{1,0:T(8,128)(2,1)}, u32[]{:S(2)}, u32[]{:S(2)}) collective-permute-start(bf16[1024,256]{1,0:T(8,128)(2,1)S(1)} %pad_maximum_fusion.3.refs_6_), channel_id=1, source_target_pairs={{0,16},{16,0},{32,48},{48,32},{1,17},{17,1},{33,49},{49,33},{2,18}... | collective-permute-start | bytes 1572872 | tf_op jit(solution)/shard_map/ppermute | solution.py:33
  55.4 15.2 %collective-permute-start.20 = (bf16[1024,256]{1,0:T(8,128)(2,1)S(1)}, bf16[1024,256]{1,0:T(8,128)(2,1)}, u32[]{:S(2)}, u32[]{:S(2)}) collective-permute-start(bf16[1024,256]{1,0:T(8,128)(2,1)S(1)} %pad_maximum_fusion.2.refs_4_), channel_id=1, source_target_pairs={{0,64},{64,0},{128,192},{192,128},{1,65},{65,1},{129,193},{193,129... | collective-permute-start | bytes 1572872 | tf_op jit(solution)/shard_map/ppermute | solution.py:33
  57.1 14.7 %collective-permute-start.19 = (bf16[1024,256]{1,0:T(8,128)(2,1)S(1)}, bf16[1024,256]{1,0:T(8,128)(2,1)}, u32[]{:S(2)}, u32[]{:S(2)}) collective-permute-start(bf16[1024,256]{1,0:T(8,128)(2,1)S(1)} %pad_maximum_fusion.1.refs_2_), channel_id=1, source_target_pairs={{0,48},{16,32},{32,16},{48,0},{1,49},{17,33},{33,17},{49,1},{2,50}... | collective-permute-start | bytes 1572872 | tf_op jit(solution)/shard_map/ppermute | solution.py:33
  57.6 15.2 %collective-permute-start.17 = (bf16[256,1024]{1,0:T(8,128)(2,1)}, bf16[256,1024]{1,0:T(8,128)(2,1)}, u32[]{:S(2)}, u32[]{:S(2)}) collective-permute-start(bf16[256,1024]{1,0:T(8,128)(2,1)} %collective-permute-done.4.t2), channel_id=1, source_target_pairs={{0,1},{1,0},{2,3},{3,2},{4,5},{5,4},{6,7},{7,6},{8,9},{9,8},{10,11... | collective-permute-start | bytes 1572872 | tf_op jit(solution)/shard_map/ppermute | solution.py:33
  57.6 22.1 %collective-permute-start.18 = (bf16[1024,256]{1,0:T(8,128)(2,1)S(1)}, bf16[1024,256]{1,0:T(8,128)(2,1)}, u32[]{:S(2)}, u32[]{:S(2)}) collective-permute-start(bf16[1024,256]{1,0:T(8,128)(2,1)S(1)} %pad_maximum_fusion.refs_0_), channel_id=1, source_target_pairs={{0,192},{64,128},{128,64},{192,0},{1,193},{65,129},{129,65},{193,1... | collective-permute-start | bytes 1572872 | tf_op jit(solution)/shard_map/ppermute | solution.py:33
  63.0 0.7 copy-start.4
  68.8 14.6 %collective-permute-start.24 = (bf16[1024,256]{1,0:T(8,128)(2,1)}, bf16[1024,256]{1,0:T(8,128)(2,1)}, u32[]{:S(2)}, u32[]{:S(2)}) collective-permute-start(bf16[1024,256]{1,0:T(8,128)(2,1)} %collective-permute-done.13.refs_5_), channel_id=1, source_target_pairs={{0,64},{64,0},{128,192},{192,128},{1,65},{65,1},{129,193},{193,129... | collective-permute-start | bytes 1572872 | tf_op jit(solution)/shard_map/ppermute | solution.py:33
  70.6 14.6 %collective-permute-start.23 = (bf16[1024,256]{1,0:T(8,128)(2,1)}, bf16[1024,256]{1,0:T(8,128)(2,1)}, u32[]{:S(2)}, u32[]{:S(2)}) collective-permute-start(bf16[1024,256]{1,0:T(8,128)(2,1)} %collective-permute-done.10.refs_3_), channel_id=1, source_target_pairs={{0,48},{16,32},{32,16},{48,0},{1,49},{17,33},{33,17},{49,1},{2,50}... | collective-permute-start | bytes 1572872 | tf_op jit(solution)/shard_map/ppermute | solution.py:33
  71.9 14.3 %collective-permute-start.22 = (bf16[1024,256]{1,0:T(8,128)(2,1)}, bf16[1024,256]{1,0:T(8,128)(2,1)}, u32[]{:S(2)}, u32[]{:S(2)}) collective-permute-start(bf16[1024,256]{1,0:T(8,128)(2,1)} %collective-permute-done.7.refs_1_), channel_id=1, source_target_pairs={{0,192},{64,128},{128,64},{192,0},{1,193},{65,129},{129,65},{193,1... | collective-permute-start | bytes 1572872 | tf_op jit(solution)/shard_map/ppermute | solution.py:33
  72.8 13.3 %collective-permute-start.25 = (bf16[1024,256]{1,0:T(8,128)(2,1)}, bf16[1024,256]{1,0:T(8,128)(2,1)}, u32[]{:S(2)}, u32[]{:S(2)}) collective-permute-start(bf16[1024,256]{1,0:T(8,128)(2,1)} %collective-permute-done.16.refs_7_), channel_id=1, source_target_pairs={{0,16},{16,0},{32,48},{48,32},{1,17},{17,1},{33,49},{49,33},{2,18}... | collective-permute-start | bytes 1572872 | tf_op jit(solution)/shard_map/ppermute | solution.py:33
  79.7 6.4 %copy-start = (bf16[8,1024,256]{2,1,0:T(8,128)(2,1)S(1)}, bf16[8,1024,256]{2,1,0:T(8,128)(2,1)}, u32[]{:S(2)}) copy-start(bf16[8,1024,256]{2,1,0:T(8,128)(2,1)} %decayed_scores.1.scores_ref) | copy-start | bytes 12582916
  79.7 6.4 %copy-start.3 = (bf16[1,1024]{1,0:T(2,128)(2,1)S(1)}, bf16[1,1024]{1,0:T(2,128)(2,1)}, u32[]{:S(2)}) copy-start(bf16[1,1024]{1,0:T(2,128)(2,1)} %noise_ref.1) | copy-start | bytes 6148

commit v10 on v9

--- a/solution.py
+++ b/solution.py
@@ -103,12 +103,11 @@
         there = lax.broadcasted_iota(jnp.int32, (SPAN, last), 1)
         kept = (here >= there) & (here < live)
         for head in range(2):
-            parts = halves(jnp.where(kept, scores[head * SPAN : (head + 1) * SPAN], 0.0))
-            for i, part in enumerate(parts):
-                start = (2 * i + head) * length + first
-                out_ref[0, start : start + SPAN, :last] = part
-                if last < length:
-                    out_ref[0, start : start + SPAN, last:] = jnp.zeros((SPAN, length - last), BF16)
+            start = head * length + first
+            mine = jnp.where(kept, scores[head * SPAN : (head + 1) * SPAN], 0.0)
+            out_ref[0, start : start + SPAN, :last] = mine.astype(BF16)
+            if last < length:
+                out_ref[0, start : start + SPAN, last:] = jnp.zeros((SPAN, length - last), BF16)
 
 
 def chunk_product(at_ref, tokens_ref, piece, blocks):
@@ -182,7 +181,6 @@
             outs = jnp.dot(
                 scores_ref[c * (wide // LANES) + pair], mine, preferred_element_type=F32
             )
-            outs = outs[: 2 * length] + outs[2 * length :]
             start = c * wide + pair * LANES
             out_ref[:, start : start + LANES] = jnp.where(
                 lane < HEAD, outs[:length], outs[length:]
@@ -229,10 +227,10 @@
     strip = pl.BlockSpec((length, LANES), lambda i: (0, i))
     return pl.pallas_call(
         score_kernel,
-        out_shape=jax.ShapeDtypeStruct((count, 4 * length, length), BF16),
+        out_shape=jax.ShapeDtypeStruct((count, 2 * length, length), BF16),
         grid=(count,),
         in_specs=[SMEM, strip, strip, strip],
-        out_specs=pl.BlockSpec((1, 4 * length, length), lambda i: (i, 0, 0)),
+        out_specs=pl.BlockSpec((1, 2 * length, length), lambda i: (i, 0, 0)),
         cost_estimate=cost(0, 20 << 20),
         name="decayed_scores",
     )(live_length, receptance, keys, log_decay)

time: 92.8 us -> 92.3 us (level)
  transfers between devices with their start and end apart: 27 -> 27, of which waited for: 6 -> 6; matrix products, arithmetic and copies ran while one was open for 1% -> 1% of each run, Pallas kernels for 24% -> 23%
where the time goes in v10:
time: 92.3 us; the launch traced here: 91.6 us
  starting transfers between devices  45.7 us (50%)
  Pallas kernels  27.2 us (29%)
  waiting for transfers between devices  14.4 us (16%)
  between operations  2.32 us (3%)
  local copies, waits for them, and re-layouts  1.79 us (2%)
    ppermute x23, starting transfers between devices, swap(): return lax.ppermute(array, axis, [(i, i ^ mask) for i in range(size)])  32 us
    ppermute x23, waiting for transfers between devices, swap(): return lax.ppermute(array, axis, [(i, i ^ mask) for i in range(size)])  11.2 us
    pallas_call x2, Pallas kernels, product(): pl.pallas_call(functools.partial(product_kernel, ways, before is not None...  8.18 us
    pallas_call x1, Pallas kernels, score_heads(): pl.pallas_call(score_kernel, out_shape=jax.ShapeDtypeStruct((count, 2 * l...  7.49 us
    ppermute x3, starting transfers between devices, fetch(): lax.ppermute(array, axis, [((i + step) % size, i) for i in range(size)])  7.17 us
    all_to_all x1, starting transfers between devices, body(): lax.all_to_all(after(message, *held), POP, split_axis=0, concat_axis=0, t...  6.49 us
    pallas_call x1, Pallas kernels, body(): pl.pallas_call(readout_kernel, out_shape=jax.ShapeDtypeStruct((length, wi...  5.72 us
    all_to_all x1, waiting for transfers between devices, body(): lax.all_to_all(after(message, *held), POP, split_axis=0, concat_axis=0, t...  3.2 us
  transfers between devices with their start and end apart: 27, of which 6 were waited for; matrix products, arithmetic and copies ran while one was open for 1% of the time, Pallas kernels for 23%

profile of v10, /device:TPU:32, one launch (start us, length us, event | category | flops | bytes accessed | tf_op | source)
XLA Modules:
  0.0 91.6 jit_solution(14797859510840469797)
XLA Ops:
  0.6 0.1 collective-permute-start.3
  0.7 1.9 %collective-permute-start = (bf16[64,1024]{1,0:T(8,128)(2,1)}, bf16[64,1024]{1,0:T(8,128)(2,1)S(1)}, u32[]{:S(2)}, u32[]{:S(2)}) collective-permute-start(bf16[64,1024]{1,0:T(8,128)(2,1)} %param.13), channel_id=1, source_target_pairs={{4,0},{8,4},{12,8},{0,12},{5,1},{9,5},{13,9},{1,13},{6,2},{10,6},{... | collective-permute-start | bytes 393224 | tf_op jit(solution)/shard_map/ppermute | solution.py:38
  2.7 0.2 collective-permute-start.1
  2.8 5.1 %collective-permute-start.2 = (bf16[64,1024]{1,0:T(8,128)(2,1)}, bf16[64,1024]{1,0:T(8,128)(2,1)S(1)}, u32[]{:S(2)}, u32[]{:S(2)}) collective-permute-start(bf16[64,1024]{1,0:T(8,128)(2,1)} %param.13), channel_id=1, source_target_pairs={{8,0},{12,4},{0,8},{4,12},{9,1},{13,5},{1,9},{5,13},{10,2},{14,6},... | collective-permute-start | bytes 393224 | tf_op jit(solution)/shard_map/ppermute | solution.py:38
  7.9 0.1 broadcast_in_dim.3
  8.0 0.9 %constant_dynamic-update-slice_fusion.3 = bf16[256,1024]{1,0:T(8,128)(2,1)S(1)} fusion(bf16[256,1024]{1,0:T(8,128)(2,1)S(1)} %broadcast_in_dim.3, bf16[64,1024]{1,0:T(8,128)(2,1)} %param.13, s32[]{:T(128)S(6)} %select_n.12), kind=kLoop, calls=%fused_computation.11 | loop fusion | bytes 262148 | tf_op jit(solution)/shard_map/dynamic_update_slice | solution.py:253
  10.2 1.5 %noise_message.1 = f32[64,1,1152]{2,1,0:T(1,128)} custom-call(f32[1]{0:T(128)S(6)} %copy.15.utility_ref, bf16[1,4096]{1,0:T(2,128)(2,1)} %noise_in_ref.1, bf16[1,1024]{1,0:T(2,128)(2,1)} %noise_ref.1), custom_call_target="tpu_custom_call" | custom-call | bytes 524288 | tf_op jit(solution)/shard_map/noise_message/pallas_call | solution.py:256
  11.7 7.5 %decayed_scores.1.scores_ref = bf16[8,512,256]{2,1,0:T(8,128)(2,1)} custom-call(s32[1]{0:T(128)S(6)} %copy.16.live_ref, bf16[256,1024]{1,0:T(8,128)(2,1)} %bitcast.15, bf16[256,1024]{1,0:T(8,128)(2,1)} %bitcast.16, bf16[256,1024]{1,0:T(8,128)(2,1)} %bitcast.17), custom_call_target="tpu_custom_call" | custom-call | bytes 20971520 | tf_op jit(solution)/shard_map/decayed_scores/pallas_call | solution.py:228
  19.2 0.0 collective-permute-done
  19.2 0.0 collective-permute-done.1
  19.2 0.0 collective-permute-done.2
  19.3 0.0 collective-permute-done.3.t1
  19.3 3.1 %collective-permute-start.14 = (bf16[256,256]{1,0:T(8,128)(2,1)S(1)}, bf16[256,256]{1,0:T(8,128)(2,1)S(1)}, u32[]{:S(2)}, u32[]{:S(2)}) collective-permute-start(bf16[256,256]{1,0:T(8,128)(2,1)S(1)} %get-tuple-element.22), channel_id=1, source_target_pairs={{0,192},{64,128},{128,64},{192,0},{1,193},{65,129},{129,65},{193,1... | collective-permute-start | bytes 393224 | tf_op jit(solution)/shard_map/ppermute | solution.py:33
  22.4 2.8 %collective-permute-start.11 = (bf16[256,256]{1,0:T(8,128)(2,1)S(1)}, bf16[256,256]{1,0:T(8,128)(2,1)S(1)}, u32[]{:S(2)}, u32[]{:S(2)}) collective-permute-start(bf16[256,256]{1,0:T(8,128)(2,1)S(1)} %get-tuple-element.23), channel_id=1, source_target_pairs={{0,48},{16,32},{32,16},{48,0},{1,49},{17,33},{33,17},{49,1},{2,50}... | collective-permute-start | bytes 393224 | tf_op jit(solution)/shard_map/ppermute | solution.py:33
  25.2 0.1 collective-permute-start.8
  25.3 0.2 collective-permute-start.5
  25.5 4.5 %collective-permute-start.4 = (bf16[256,1024]{1,0:T(8,128)(2,1)S(1)}, bf16[256,1024]{1,0:T(8,128)(2,1)}, u32[]{:S(2)}, u32[]{:S(2)}) collective-permute-start(bf16[256,1024]{1,0:T(8,128)(2,1)S(1)} %bitcast.11), channel_id=1, source_target_pairs={{0,2},{2,0},{1,3},{3,1},{4,6},{6,4},{5,7},{7,5},{8,10},{10,8},{9,1... | collective-permute-start | bytes 1572872 | tf_op jit(solution)/shard_map/ppermute | solution.py:33
  30.0 0.0 collective-permute-done.14
  30.1 1.2 %collective-permute-start.15 = (bf16[512,256]{1,0:T(8,128)(2,1)S(1)}, bf16[512,256]{1,0:T(8,128)(2,1)S(1)}, u32[]{:S(2)}, u32[]{:S(2)}) collective-permute-start(bf16[512,256]{1,0:T(8,128)(2,1)S(1)} %pad_maximum_fusion.7), channel_id=1, source_target_pairs={{0,48},{16,32},{32,16},{48,0},{1,49},{17,33},{33,17},{49,1},{2,50}... | collective-permute-start | bytes 786440 | tf_op jit(solution)/shard_map/ppermute | solution.py:33
  31.3 0.0 collective-permute-done.11
  31.3 1.2 %collective-permute-start.12 = (bf16[512,256]{1,0:T(8,128)(2,1)S(1)}, bf16[512,256]{1,0:T(8,128)(2,1)S(1)}, u32[]{:S(2)}, u32[]{:S(2)}) collective-permute-start(bf16[512,256]{1,0:T(8,128)(2,1)S(1)} %pad_maximum_fusion.6), channel_id=1, source_target_pairs={{0,192},{64,128},{128,64},{192,0},{1,193},{65,129},{129,65},{193,1... | collective-permute-start | bytes 786440 | tf_op jit(solution)/shard_map/ppermute | solution.py:33
  32.5 0.0 collective-permute-done.8
  32.5 0.8 collective-permute-start.9
  33.3 0.0 collective-permute-done.5
  33.3 0.9 %collective-permute-start.6 = (bf16[512,256]{1,0:T(8,128)(2,1)S(1)}, bf16[512,256]{1,0:T(8,128)(2,1)S(1)}, u32[]{:S(2)}, u32[]{:S(2)}) collective-permute-start(bf16[512,256]{1,0:T(8,128)(2,1)S(1)} %pad_maximum_fusion.4), channel_id=1, source_target_pairs={{0,64},{64,0},{128,192},{192,128},{1,65},{65,1},{129,193},{193,129... | collective-permute-start | bytes 786440 | tf_op jit(solution)/shard_map/ppermute | solution.py:33
  34.2 3.8 %collective-permute-done.15 = bf16[512,256]{1,0:T(8,128)(2,1)S(1)} collective-permute-done((bf16[512,256]{1,0:T(8,128)(2,1)S(1)}, bf16[512,256]{1,0:T(8,128)(2,1)S(1)}, u32[]{:S(2)}, u32[]{:S(2)}) %collective-permute-start.15) | collective-permute-done | bytes 262176 | tf_op jit(solution)/shard_map/ppermute | solution.py:33
  38.1 0.0 copy-start.2
  38.1 1.7 %collective-permute-start.16 = (bf16[1024,256]{1,0:T(8,128)(2,1)S(1)}, bf16[1024,256]{1,0:T(8,128)(2,1)}, u32[]{:S(2)}, u32[]{:S(2)}) collective-permute-start(bf16[1024,256]{1,0:T(8,128)(2,1)S(1)} %pad_maximum_fusion.3.refs_6_), channel_id=1, source_target_pairs={{0,64},{64,0},{128,192},{192,128},{1,65},{65,1},{129,193},{193,129... | collective-permute-start | bytes 1572872 | tf_op jit(solution)/shard_map/ppermute | solution.py:33
  39.8 0.0 collective-permute-done.12
  39.9 0.6 collective-permute-start.13
  40.5 0.0 collective-permute-done.9
  40.6 1.5 %collective-permute-start.10 = (bf16[1024,256]{1,0:T(8,128)(2,1)S(1)}, bf16[1024,256]{1,0:T(8,128)(2,1)}, u32[]{:S(2)}, u32[]{:S(2)}) collective-permute-start(bf16[1024,256]{1,0:T(8,128)(2,1)S(1)} %pad_maximum_fusion.1.refs_2_), channel_id=1, source_target_pairs={{0,192},{64,128},{128,64},{192,0},{1,193},{65,129},{129,65},{193,1... | collective-permute-start | bytes 1572872 | tf_op jit(solution)/shard_map/ppermute | solution.py:33
  42.0 0.0 collective-permute-done.6
  42.1 3.2 %collective-permute-start.7 = (bf16[1024,256]{1,0:T(8,128)(2,1)S(1)}, bf16[1024,256]{1,0:T(8,128)(2,1)}, u32[]{:S(2)}, u32[]{:S(2)}) collective-permute-start(bf16[1024,256]{1,0:T(8,128)(2,1)S(1)} %pad_maximum_fusion.refs_0_), channel_id=1, source_target_pairs={{0,48},{16,32},{32,16},{48,0},{1,49},{17,33},{33,17},{49,1},{2,50}... | collective-permute-start | bytes 1572872 | tf_op jit(solution)/shard_map/ppermute | solution.py:33
  45.3 6.5 %all-to-all-start = ((f32[64,1,1152]{2,1,0:T(1,128)}), f32[64,1,1152]{2,1,0:T(1,128)S(1)}, u32[]{:S(2)}, u32[]{:S(2)}) async-start(f32[64,1,1152]{2,1,0:T(1,128)} %noise_message.1), calls=%async_computation | async-start | bytes 589824 | tf_op jit(solution)/shard_map/all_to_all | solution.py:274
  51.8 1.6 %collective-permute-done.4.t2 = bf16[256,1024]{1,0:T(8,128)(2,1)} collective-permute-done((bf16[256,1024]{1,0:T(8,128)(2,1)S(1)}, bf16[256,1024]{1,0:T(8,128)(2,1)}, u32[]{:S(2)}, u32[]{:S(2)}) %collective-permute-start.4) | collective-permute-done | bytes 524320 | tf_op jit(solution)/shard_map/ppermute | solution.py:33
  53.3 1.7 %collective-permute-start.21 = (bf16[1024,256]{1,0:T(8,128)(2,1)S(1)}, bf16[1024,256]{1,0:T(8,128)(2,1)}, u32[]{:S(2)}, u32[]{:S(2)}) collective-permute-start(bf16[1024,256]{1,0:T(8,128)(2,1)S(1)} %pad_maximum_fusion.3.refs_6_), channel_id=1, source_target_pairs={{0,16},{16,0},{32,48},{48,32},{1,17},{17,1},{33,49},{49,33},{2,18}... | collective-permute-start | bytes 1572872 | tf_op jit(solution)/shard_map/ppermute | solution.py:33
  55.0 0.0 collective-permute-done.16.refs_7_
  55.0 1.7 %collective-permute-start.20 = (bf16[1024,256]{1,0:T(8,128)(2,1)S(1)}, bf16[1024,256]{1,0:T(8,128)(2,1)}, u32[]{:S(2)}, u32[]{:S(2)}) collective-permute-start(bf16[1024,256]{1,0:T(8,128)(2,1)S(1)} %pad_maximum_fusion.2.refs_4_), channel_id=1, source_target_pairs={{0,64},{64,0},{128,192},{192,128},{1,65},{65,1},{129,193},{193,129... | collective-permute-start | bytes 1572872 | tf_op jit(solution)/shard_map/ppermute | solution.py:33
  56.7 0.0 collective-permute-done.13.refs_5_
  56.7 0.5 collective-permute-start.19
  57.2 0.0 collective-permute-done.10.refs_3_
  57.2 0.0 collective-permute-done.7.refs_1_
  57.2 0.0 collective-permute-start.17
  57.2 2.1 %collective-permute-start.18 = (bf16[1024,256]{1,0:T(8,128)(2,1)S(1)}, bf16[1024,256]{1,0:T(8,128)(2,1)}, u32[]{:S(2)}, u32[]{:S(2)}) collective-permute-start(bf16[1024,256]{1,0:T(8,128)(2,1)S(1)} %pad_maximum_fusion.refs_0_), channel_id=1, source_target_pairs={{0,192},{64,128},{128,64},{192,0},{1,193},{65,129},{129,65},{193,1... | collective-permute-start | bytes 1572872 | tf_op jit(solution)/shard_map/ppermute | solution.py:33
  59.4 3.2 %all-to-all-done.message_ref = f32[64,1,1152]{2,1,0:T(1,128)S(1)} async-done(((f32[64,1,1152]{2,1,0:T(1,128)}), f32[64,1,1152]{2,1,0:T(1,128)S(1)}, u32[]{:S(2)}, u32[]{:S(2)}) %all-to-all-start) | async-done | bytes 294944 | tf_op jit(solution)/shard_map/all_to_all | solution.py:274
  62.6 0.7 copy-done.4
  63.3 2.3 %update_product.1 = f32[64,1024]{1,0:T(8,128)} custom-call(s32[1]{0:T(128)} %bitcast.8.z_ref, f32[64,1,1152]{2,1,0:T(1,128)} %copy-done.4), custom_call_target="tpu_custom_call" | custom-call | bytes 1048576 | tf_op jit(solution)/shard_map/update_product/pallas_call | solution.py:279
  65.6 2.8 %collective-permute-done.21.refs_4_ = bf16[1024,256]{1,0:T(8,128)(2,1)} collective-permute-done((bf16[1024,256]{1,0:T(8,128)(2,1)S(1)}, bf16[1024,256]{1,0:T(8,128)(2,1)}, u32[]{:S(2)}, u32[]{:S(2)}) %collective-permute-start.21) | collective-permute-done | bytes 524320 | tf_op jit(solution)/shard_map/ppermute | solution.py:33
  68.4 1.8 %collective-permute-start.24 = (bf16[1024,256]{1,0:T(8,128)(2,1)}, bf16[1024,256]{1,0:T(8,128)(2,1)}, u32[]{:S(2)}, u32[]{:S(2)}) collective-permute-start(bf16[1024,256]{1,0:T(8,128)(2,1)} %collective-permute-done.13.refs_5_), channel_id=1, source_target_pairs={{0,64},{64,0},{128,192},{192,128},{1,65},{65,1},{129,193},{193,129... | collective-permute-start | bytes 1572872 | tf_op jit(solution)/shard_map/ppermute | solution.py:33
  70.2 0.0 collective-permute-done.20.refs_3_
  70.2 1.2 %collective-permute-start.23 = (bf16[1024,256]{1,0:T(8,128)(2,1)}, bf16[1024,256]{1,0:T(8,128)(2,1)}, u32[]{:S(2)}, u32[]{:S(2)}) collective-permute-start(bf16[1024,256]{1,0:T(8,128)(2,1)} %collective-permute-done.10.refs_3_), channel_id=1, source_target_pairs={{0,48},{16,32},{32,16},{48,0},{1,49},{17,33},{33,17},{49,1},{2,50}... | collective-permute-start | bytes 1572872 | tf_op jit(solution)/shard_map/ppermute | solution.py:33
  71.5 0.0 collective-permute-done.19.refs_2_
  71.5 1.0 %collective-permute-start.22 = (bf16[1024,256]{1,0:T(8,128)(2,1)}, bf16[1024,256]{1,0:T(8,128)(2,1)}, u32[]{:S(2)}, u32[]{:S(2)}) collective-permute-start(bf16[1024,256]{1,0:T(8,128)(2,1)} %collective-permute-done.7.refs_1_), channel_id=1, source_target_pairs={{0,192},{64,128},{128,64},{192,0},{1,193},{65,129},{129,65},{193,1... | collective-permute-start | bytes 1572872 | tf_op jit(solution)/shard_map/ppermute | solution.py:33
  72.5 0.0 collective-permute-start.25
  72.5 0.1 pad_add_fusion.at_ref
  72.6 2.0 %member_tokens.1 = (bf16[4,256,1024]{2,1,0:T(8,128)(2,1)S(1)}, f32[256,8]{1,0:T(8,128)S(1)}) custom-call(s32[1]{0:T(128)} %bitcast.2.at_ref, bf16[256,1024]{1,0:T(8,128)(2,1)S(1)} %bitcast.12, bf16[256,1024]{1,0:T(8,128)(2,1)S(1)} %collective-permute-done.3.t1, bf16[256,1024]{1,0:T(8,128)(2,1)} %collective-permute-done.4.t2, ...), custom_call_target="tpu_custom_call" | custom-call | bytes 8388608 | tf_op jit(solution)/shard_map/member_tokens/pallas_call | solution.py:294
  74.6 4.7 %products.2.refs_0_ = f32[256,1024]{1,0:T(8,128)S(1)} custom-call(s32[2]{0:T(128)S(1)} %pad_add_fusion.at_ref, bf16[4,256,1024]{2,1,0:T(8,128)(2,1)S(1)} %get-tuple-element.16.tokens_ref, bf16[1024,256]{1,0:T(8,128)(2,1)S(1)} %pad_maximum_fusion.refs_0_, bf16[1024,256]{1,0:T(8,128)(2,1)} %collective-permute-done.7.refs_1_, ...), custom_call_target="tpu_custom_call" | custom-call | flops 1073741824 | bytes 8388608 | tf_op jit(solution)/shard_map/products/pallas_call | solution.py:149
  79.3 0.0 copy-start.3
  79.3 0.0 collective-permute-done.18.refs_1_
  79.3 3.4 %products.3.sum_ref = f32[256,1024]{1,0:T(8,128)S(1)} custom-call(s32[2]{0:T(128)S(1)} %pad_add_fusion.at_ref, bf16[4,256,1024]{2,1,0:T(8,128)(2,1)S(1)} %get-tuple-element.16.tokens_ref, f32[256,1024]{1,0:T(8,128)S(1)} %products.2.refs_0_, bf16[1024,256]{1,0:T(8,128)(2,1)} %collective-permute-done.18.refs_1_, ...), custom_call_target="tpu_custom_call" | custom-call | flops 536870912 | bytes 8388608 | tf_op jit(solution)/shard_map/products/pallas_call | solution.py:149
  82.8 2.1 %collective-permute-done.23.refs_1_ = bf16[1024,256]{1,0:T(8,128)(2,1)} collective-permute-done((bf16[1024,256]{1,0:T(8,128)(2,1)}, bf16[1024,256]{1,0:T(8,128)(2,1)}, u32[]{:S(2)}, u32[]{:S(2)}) %collective-permute-start.23) | collective-permute-done | bytes 524320 | tf_op jit(solution)/shard_map/ppermute | solution.py:33
  84.8 0.9 collective-permute-done.22.refs_0_
  85.8 5.7 %values_readout.1 = bf16[256,1024]{1,0:T(8,128)(2,1)} custom-call(s32[2]{0:T(128)S(1)} %pad_add_fusion.at_ref, bf16[4,256,1024]{2,1,0:T(8,128)(2,1)S(1)} %get-tuple-element.16.tokens_ref, f32[256,1024]{1,0:T(8,128)S(1)} %products.3.sum_ref, f32[256,8]{1,0:T(8,128)S(1)} %get-tuple-element.17.projected_ref, bf16[1,1024]{1,0:T(2,128)(2,1)S(1)} %copy-done.3, ...), custom_call_target="tpu_custom_call" | custom-call | flops 536870912 | bytes 12582912 | tf_op jit(solution)/shard_map/values_readout/pallas_call | solution.py:312
  (22 shorter events, 0.3 us)
Async XLA Ops:
  0.6 18.6 %collective-permute-start.3 = (bf16[256,1024]{1,0:T(8,128)(2,1)}, bf16[256,1024]{1,0:T(8,128)(2,1)S(1)}, u32[]{:S(2)}, u32[]{:S(2)}) collective-permute-start(bf16[256,1024]{1,0:T(8,128)(2,1)} %bitcast.10), channel_id=1, source_target_pairs={{0,1},{1,0},{2,3},{3,2},{4,5},{5,4},{6,7},{7,6},{8,9},{9,8},{10,11... | collective-permute-start | bytes 1572872 | tf_op jit(solution)/shard_map/ppermute | solution.py:33
  0.7 18.4 %collective-permute-start = (bf16[64,1024]{1,0:T(8,128)(2,1)}, bf16[64,1024]{1,0:T(8,128)(2,1)S(1)}, u32[]{:S(2)}, u32[]{:S(2)}) collective-permute-start(bf16[64,1024]{1,0:T(8,128)(2,1)} %param.13), channel_id=1, source_target_pairs={{4,0},{8,4},{12,8},{0,12},{5,1},{9,5},{13,9},{1,13},{6,2},{10,6},{... | collective-permute-start | bytes 393224 | tf_op jit(solution)/shard_map/ppermute | solution.py:38
  2.7 16.5 %collective-permute-start.1 = (bf16[64,1024]{1,0:T(8,128)(2,1)}, bf16[64,1024]{1,0:T(8,128)(2,1)S(1)}, u32[]{:S(2)}, u32[]{:S(2)}) collective-permute-start(bf16[64,1024]{1,0:T(8,128)(2,1)} %param.13), channel_id=1, source_target_pairs={{12,0},{0,4},{4,8},{8,12},{13,1},{1,5},{5,9},{9,13},{14,2},{2,6},{... | collective-permute-start | bytes 393224 | tf_op jit(solution)/shard_map/ppermute | solution.py:38
  2.8 16.4 %collective-permute-start.2 = (bf16[64,1024]{1,0:T(8,128)(2,1)}, bf16[64,1024]{1,0:T(8,128)(2,1)S(1)}, u32[]{:S(2)}, u32[]{:S(2)}) collective-permute-start(bf16[64,1024]{1,0:T(8,128)(2,1)} %param.13), channel_id=1, source_target_pairs={{8,0},{12,4},{0,8},{4,12},{9,1},{13,5},{1,9},{5,13},{10,2},{14,6},... | collective-permute-start | bytes 393224 | tf_op jit(solution)/shard_map/ppermute | solution.py:38
  11.7 13.9 %copy-start.1 = (bf16[1,256,1024]{2,1,0:T(8,128)(2,1)S(1)}, bf16[1,256,1024]{2,1,0:T(8,128)(2,1)}, u32[]{:S(2)}) copy-start(bf16[1,256,1024]{2,1,0:T(8,128)(2,1)} %param.9) | copy-start | bytes 1572868
  19.3 10.7 %collective-permute-start.14 = (bf16[256,256]{1,0:T(8,128)(2,1)S(1)}, bf16[256,256]{1,0:T(8,128)(2,1)S(1)}, u32[]{:S(2)}, u32[]{:S(2)}) collective-permute-start(bf16[256,256]{1,0:T(8,128)(2,1)S(1)} %get-tuple-element.22), channel_id=1, source_target_pairs={{0,192},{64,128},{128,64},{192,0},{1,193},{65,129},{129,65},{193,1... | collective-permute-start | bytes 393224 | tf_op jit(solution)/shard_map/ppermute | solution.py:33
  22.4 8.9 %collective-permute-start.11 = (bf16[256,256]{1,0:T(8,128)(2,1)S(1)}, bf16[256,256]{1,0:T(8,128)(2,1)S(1)}, u32[]{:S(2)}, u32[]{:S(2)}) collective-permute-start(bf16[256,256]{1,0:T(8,128)(2,1)S(1)} %get-tuple-element.23), channel_id=1, source_target_pairs={{0,48},{16,32},{32,16},{48,0},{1,49},{17,33},{33,17},{49,1},{2,50}... | collective-permute-start | bytes 393224 | tf_op jit(solution)/shard_map/ppermute | solution.py:33
  25.2 7.3 %collective-permute-start.8 = (bf16[256,256]{1,0:T(8,128)(2,1)S(1)}, bf16[256,256]{1,0:T(8,128)(2,1)S(1)}, u32[]{:S(2)}, u32[]{:S(2)}) collective-permute-start(bf16[256,256]{1,0:T(8,128)(2,1)S(1)} %get-tuple-element.24), channel_id=1, source_target_pairs={{0,64},{64,0},{128,192},{192,128},{1,65},{65,1},{129,193},{193,129... | collective-permute-start | bytes 393224 | tf_op jit(solution)/shard_map/ppermute | solution.py:33
  25.3 7.9 %collective-permute-start.5 = (bf16[256,256]{1,0:T(8,128)(2,1)S(1)}, bf16[256,256]{1,0:T(8,128)(2,1)S(1)}, u32[]{:S(2)}, u32[]{:S(2)}) collective-permute-start(bf16[256,256]{1,0:T(8,128)(2,1)S(1)} %get-tuple-element.25), channel_id=1, source_target_pairs={{0,16},{16,0},{32,48},{48,32},{1,17},{17,1},{33,49},{49,33},{2,18}... | collective-permute-start | bytes 393224 | tf_op jit(solution)/shard_map/ppermute | solution.py:33
  25.5 27.8 %collective-permute-start.4 = (bf16[256,1024]{1,0:T(8,128)(2,1)S(1)}, bf16[256,1024]{1,0:T(8,128)(2,1)}, u32[]{:S(2)}, u32[]{:S(2)}) collective-permute-start(bf16[256,1024]{1,0:T(8,128)(2,1)S(1)} %bitcast.11), channel_id=1, source_target_pairs={{0,2},{2,0},{1,3},{3,1},{4,6},{6,4},{5,7},{7,5},{8,10},{10,8},{9,1... | collective-permute-start | bytes 1572872 | tf_op jit(solution)/shard_map/ppermute | solution.py:33
  30.1 8.0 %collective-permute-start.15 = (bf16[512,256]{1,0:T(8,128)(2,1)S(1)}, bf16[512,256]{1,0:T(8,128)(2,1)S(1)}, u32[]{:S(2)}, u32[]{:S(2)}) collective-permute-start(bf16[512,256]{1,0:T(8,128)(2,1)S(1)} %pad_maximum_fusion.7), channel_id=1, source_target_pairs={{0,48},{16,32},{32,16},{48,0},{1,49},{17,33},{33,17},{49,1},{2,50}... | collective-permute-start | bytes 786440 | tf_op jit(solution)/shard_map/ppermute | solution.py:33
  31.3 8.5 %collective-permute-start.12 = (bf16[512,256]{1,0:T(8,128)(2,1)S(1)}, bf16[512,256]{1,0:T(8,128)(2,1)S(1)}, u32[]{:S(2)}, u32[]{:S(2)}) collective-permute-start(bf16[512,256]{1,0:T(8,128)(2,1)S(1)} %pad_maximum_fusion.6), channel_id=1, source_target_pairs={{0,192},{64,128},{128,64},{192,0},{1,193},{65,129},{129,65},{193,1... | collective-permute-start | bytes 786440 | tf_op jit(solution)/shard_map/ppermute | solution.py:33
  32.5 8.0 %collective-permute-start.9 = (bf16[512,256]{1,0:T(8,128)(2,1)S(1)}, bf16[512,256]{1,0:T(8,128)(2,1)S(1)}, u32[]{:S(2)}, u32[]{:S(2)}) collective-permute-start(bf16[512,256]{1,0:T(8,128)(2,1)S(1)} %pad_maximum_fusion.5), channel_id=1, source_target_pairs={{0,16},{16,0},{32,48},{48,32},{1,17},{17,1},{33,49},{49,33},{2,18}... | collective-permute-start | bytes 786440 | tf_op jit(solution)/shard_map/ppermute | solution.py:33
  33.3 8.7 %collective-permute-start.6 = (bf16[512,256]{1,0:T(8,128)(2,1)S(1)}, bf16[512,256]{1,0:T(8,128)(2,1)S(1)}, u32[]{:S(2)}, u32[]{:S(2)}) collective-permute-start(bf16[512,256]{1,0:T(8,128)(2,1)S(1)} %pad_maximum_fusion.4), channel_id=1, source_target_pairs={{0,64},{64,0},{128,192},{192,128},{1,65},{65,1},{129,193},{193,129... | collective-permute-start | bytes 786440 | tf_op jit(solution)/shard_map/ppermute | solution.py:33
  38.1 34.5 %copy-start.2 = (bf16[1,4096]{1,0:T(2,128)(2,1)S(1)}, bf16[1,4096]{1,0:T(2,128)(2,1)}, u32[]{:S(2)}) copy-start(bf16[1,4096]{1,0:T(2,128)(2,1)} %noise_in_ref.1) | copy-start | bytes 24580
  38.1 16.9 %collective-permute-start.16 = (bf16[1024,256]{1,0:T(8,128)(2,1)S(1)}, bf16[1024,256]{1,0:T(8,128)(2,1)}, u32[]{:S(2)}, u32[]{:S(2)}) collective-permute-start(bf16[1024,256]{1,0:T(8,128)(2,1)S(1)} %pad_maximum_fusion.3.refs_6_), channel_id=1, source_target_pairs={{0,64},{64,0},{128,192},{192,128},{1,65},{65,1},{129,193},{193,129... | collective-permute-start | bytes 1572872 | tf_op jit(solution)/shard_map/ppermute | solution.py:33
  39.9 16.9 %collective-permute-start.13 = (bf16[1024,256]{1,0:T(8,128)(2,1)S(1)}, bf16[1024,256]{1,0:T(8,128)(2,1)}, u32[]{:S(2)}, u32[]{:S(2)}) collective-permute-start(bf16[1024,256]{1,0:T(8,128)(2,1)S(1)} %pad_maximum_fusion.2.refs_4_), channel_id=1, source_target_pairs={{0,16},{16,0},{32,48},{48,32},{1,17},{17,1},{33,49},{49,33},{2,18}... | collective-permute-start | bytes 1572872 | tf_op jit(solution)/shard_map/ppermute | solution.py:33
  40.6 16.7 %collective-permute-start.10 = (bf16[1024,256]{1,0:T(8,128)(2,1)S(1)}, bf16[1024,256]{1,0:T(8,128)(2,1)}, u32[]{:S(2)}, u32[]{:S(2)}) collective-permute-start(bf16[1024,256]{1,0:T(8,128)(2,1)S(1)} %pad_maximum_fusion.1.refs_2_), channel_id=1, source_target_pairs={{0,192},{64,128},{128,64},{192,0},{1,193},{65,129},{129,65},{193,1... | collective-permute-start | bytes 1572872 | tf_op jit(solution)/shard_map/ppermute | solution.py:33
  42.1 15.2 %collective-permute-start.7 = (bf16[1024,256]{1,0:T(8,128)(2,1)S(1)}, bf16[1024,256]{1,0:T(8,128)(2,1)}, u32[]{:S(2)}, u32[]{:S(2)}) collective-permute-start(bf16[1024,256]{1,0:T(8,128)(2,1)S(1)} %pad_maximum_fusion.refs_0_), channel_id=1, source_target_pairs={{0,48},{16,32},{32,16},{48,0},{1,49},{17,33},{33,17},{49,1},{2,50}... | collective-permute-start | bytes 1572872 | tf_op jit(solution)/shard_map/ppermute | solution.py:33
  45.3 17.3 %all-to-all-start = ((f32[64,1,1152]{2,1,0:T(1,128)}), f32[64,1,1152]{2,1,0:T(1,128)S(1)}, u32[]{:S(2)}, u32[]{:S(2)}) async-start(f32[64,1,1152]{2,1,0:T(1,128)} %noise_message.1), calls=%async_computation | async-start | bytes 589824 | tf_op jit(solution)/shard_map/all_to_all | solution.py:274
  53.3 15.1 %collective-permute-start.21 = (bf16[1024,256]{1,0:T(8,128)(2,1)S(1)}, bf16[1024,256]{1,0:T(8,128)(2,1)}, u32[]{:S(2)}, u32[]{:S(2)}) collective-permute-start(bf16[1024,256]{1,0:T(8,128)(2,1)S(1)} %pad_maximum_fusion.3.refs_6_), channel_id=1, source_target_pairs={{0,16},{16,0},{32,48},{48,32},{1,17},{17,1},{33,49},{49,33},{2,18}... | collective-permute-start | bytes 1572872 | tf_op jit(solution)/shard_map/ppermute | solution.py:33
  55.0 15.2 %collective-permute-start.20 = (bf16[1024,256]{1,0:T(8,128)(2,1)S(1)}, bf16[1024,256]{1,0:T(8,128)(2,1)}, u32[]{:S(2)}, u32[]{:S(2)}) collective-permute-start(bf16[1024,256]{1,0:T(8,128)(2,1)S(1)} %pad_maximum_fusion.2.refs_4_), channel_id=1, source_target_pairs={{0,64},{64,0},{128,192},{192,128},{1,65},{65,1},{129,193},{193,129... | collective-permute-start | bytes 1572872 | tf_op jit(solution)/shard_map/ppermute | solution.py:33
  56.7 14.7 %collective-permute-start.19 = (bf16[1024,256]{1,0:T(8,128)(2,1)S(1)}, bf16[1024,256]{1,0:T(8,128)(2,1)}, u32[]{:S(2)}, u32[]{:S(2)}) collective-permute-start(bf16[1024,256]{1,0:T(8,128)(2,1)S(1)} %pad_maximum_fusion.1.refs_2_), channel_id=1, source_target_pairs={{0,48},{16,32},{32,16},{48,0},{1,49},{17,33},{33,17},{49,1},{2,50}... | collective-permute-start | bytes 1572872 | tf_op jit(solution)/shard_map/ppermute | solution.py:33
  57.2 15.2 %collective-permute-start.17 = (bf16[256,1024]{1,0:T(8,128)(2,1)}, bf16[256,1024]{1,0:T(8,128)(2,1)}, u32[]{:S(2)}, u32[]{:S(2)}) collective-permute-start(bf16[256,1024]{1,0:T(8,128)(2,1)} %collective-permute-done.4.t2), channel_id=1, source_target_pairs={{0,1},{1,0},{2,3},{3,2},{4,5},{5,4},{6,7},{7,6},{8,9},{9,8},{10,11... | collective-permute-start | bytes 1572872 | tf_op jit(solution)/shard_map/ppermute | solution.py:33
  57.2 22.1 %collective-permute-start.18 = (bf16[1024,256]{1,0:T(8,128)(2,1)S(1)}, bf16[1024,256]{1,0:T(8,128)(2,1)}, u32[]{:S(2)}, u32[]{:S(2)}) collective-permute-start(bf16[1024,256]{1,0:T(8,128)(2,1)S(1)} %pad_maximum_fusion.refs_0_), channel_id=1, source_target_pairs={{0,192},{64,128},{128,64},{192,0},{1,193},{65,129},{129,65},{193,1... | collective-permute-start | bytes 1572872 | tf_op jit(solution)/shard_map/ppermute | solution.py:33
  62.6 0.7 copy-start.4
  68.4 14.3 %collective-permute-start.24 = (bf16[1024,256]{1,0:T(8,128)(2,1)}, bf16[1024,256]{1,0:T(8,128)(2,1)}, u32[]{:S(2)}, u32[]{:S(2)}) collective-permute-start(bf16[1024,256]{1,0:T(8,128)(2,1)} %collective-permute-done.13.refs_5_), channel_id=1, source_target_pairs={{0,64},{64,0},{128,192},{192,128},{1,65},{65,1},{129,193},{193,129... | collective-permute-start | bytes 1572872 | tf_op jit(solution)/shard_map/ppermute | solution.py:33
  70.2 14.6 %collective-permute-start.23 = (bf16[1024,256]{1,0:T(8,128)(2,1)}, bf16[1024,256]{1,0:T(8,128)(2,1)}, u32[]{:S(2)}, u32[]{:S(2)}) collective-permute-start(bf16[1024,256]{1,0:T(8,128)(2,1)} %collective-permute-done.10.refs_3_), channel_id=1, source_target_pairs={{0,48},{16,32},{32,16},{48,0},{1,49},{17,33},{33,17},{49,1},{2,50}... | collective-permute-start | bytes 1572872 | tf_op jit(solution)/shard_map/ppermute | solution.py:33
  71.5 14.3 %collective-permute-start.22 = (bf16[1024,256]{1,0:T(8,128)(2,1)}, bf16[1024,256]{1,0:T(8,128)(2,1)}, u32[]{:S(2)}, u32[]{:S(2)}) collective-permute-start(bf16[1024,256]{1,0:T(8,128)(2,1)} %collective-permute-done.7.refs_1_), channel_id=1, source_target_pairs={{0,192},{64,128},{128,64},{192,0},{1,193},{65,129},{129,65},{193,1... | collective-permute-start | bytes 1572872 | tf_op jit(solution)/shard_map/ppermute | solution.py:33
  72.5 13.3 %collective-permute-start.25 = (bf16[1024,256]{1,0:T(8,128)(2,1)}, bf16[1024,256]{1,0:T(8,128)(2,1)}, u32[]{:S(2)}, u32[]{:S(2)}) collective-permute-start(bf16[1024,256]{1,0:T(8,128)(2,1)} %collective-permute-done.16.refs_7_), channel_id=1, source_target_pairs={{0,16},{16,0},{32,48},{48,32},{1,17},{17,1},{33,49},{49,33},{2,18}... | collective-permute-start | bytes 1572872 | tf_op jit(solution)/shard_map/ppermute | solution.py:33
  79.3 6.5 %copy-start = (bf16[8,512,256]{2,1,0:T(8,128)(2,1)S(1)}, bf16[8,512,256]{2,1,0:T(8,128)(2,1)}, u32[]{:S(2)}) copy-start(bf16[8,512,256]{2,1,0:T(8,128)(2,1)} %decayed_scores.1.scores_ref) | copy-start | bytes 6291460
  79.3 6.4 %copy-start.3 = (bf16[1,1024]{1,0:T(2,128)(2,1)S(1)}, bf16[1,1024]{1,0:T(2,128)(2,1)}, u32[]{:S(2)}) copy-start(bf16[1,1024]{1,0:T(2,128)(2,1)} %noise_ref.1) | copy-start | bytes 6148
